TPU v7x, 128 devices: a whole 4x4x4 slice. The times are simulated.
128 devices in a mesh: dom: 16 (over x, y), grp: 8 (over z, core).
Axes of the slice: x: 4, y: 4, z: 4, core: 2. Of those that a mesh axis runs over, the one named last changes fastest.
Arguments:
- blocks: bfloat16 [4096, 128, 256], P(('dom', 'grp')), may hold values from -6 to 6
- tile_values: bfloat16 [4096, 16, 128, 128], P(('dom', 'grp')), may hold values from -0.125 to 0.125
- tile_cols: int32 [4096, 16], P(('dom', 'grp')), may hold values from 0 to 103, as said below
- halo_send: int32 [128, 16, 4], P(('dom', 'grp')), may hold values from 0 to 31
- halo_counts: int32 [128, 16], P(('dom', 'grp')), may hold values from 0 to 4, as said below
- grp_send: int32 [128, 2, 4], P(('dom', 'grp')), may hold values from 0 to 31
- well_send: int32 [128, 16, 4], P(('dom', 'grp')), may hold values from 0 to 31
- well_slot: int32 [2048, 4], P(('dom', 'grp')), may hold values from 0 to 63, as said below
- well_count: int32 [128], P(('dom', 'grp')), may hold values from 1 to 16
- couple_in: bfloat16 [2048, 4, 32, 128], P(('dom', 'grp')), may hold values from -0.25 to 0.25
- couple_out: bfloat16 [2048, 4, 32, 128], P(('dom', 'grp')), may hold values from -1 to 1
- well_inverse: float32 [2048, 32, 32], P(('dom', 'grp')), may hold values from -1 to 1
Outputs:
- pressure_image: bfloat16 [4096, 128, 256], P(('dom', 'grp'))
Inputs may be any that keep to these rules, and one draw needn't show every extreme that they name: Column 0 of every row of tile_cols is that block row's own local index (row modulo 32). halo_counts[d, j] is 0 where j is d's own dom index; some device receives 4 from every other partition. `well_slot`: the 64 entries of each device's rows are a permutation of 0 to 63.
All inputs are finite; a program needn't handle non-finite values.
Results may differ from a plain program's by a relative error of at most 0.005.
Values may be sent and summed in bfloat16 or wider, within the bound.
A program may use at most 192 MiB of HBM per device.

v0:
```python
import jax
import jax.numpy as jnp
from jax import lax
from jax.sharding import PartitionSpec as P


def padded(value, sides, width):
    for axis, dim in sides:
        devices, length = (lax.axis_size(axis), value.shape[dim])
        up = [(i, (i + 1) % devices) for i in range(devices - 1)]
        down = [(j, i) for i, j in up]
        last = lax.slice_in_dim(value, length - width, length, axis=dim)
        leading = lax.slice_in_dim(value, 0, width, axis=dim)
        before = lax.ppermute(last, axis, up)
        after = lax.ppermute(leading, axis, down)
        value = jnp.concatenate([before, value, after], axis=dim)
    return value


def local_product(extended, tile_values, tile_cols):
    gathered = extended[tile_cols]
    return jnp.einsum("btij,btjv->biv", tile_values, gathered, preferred_element_type=jnp.float32)


def well_states_of(summed, well_inverse, well_count):
    wells = summed.shape[0]
    live_mask = (jnp.arange(wells) < well_count[0]).astype(jnp.float32)
    solved = jnp.einsum("wst,wtv->wsv", well_inverse, summed, precision=lax.Precision.HIGHEST)
    return (solved * live_mask[:, None, None]).astype(jnp.bfloat16)


def subtract_incoming(product, well_send, incoming):
    targets = well_send[0].reshape(-1)
    selector = (targets[None, :] == jnp.arange(product.shape[0])[:, None]).astype(jnp.bfloat16)
    flat_rows = incoming.reshape(targets.shape[0], product.shape[1], product.shape[2])
    return product - jnp.einsum(
        "bq,qkv->bkv", selector, flat_rows, preferred_element_type=jnp.float32
    )


def on_device(
    blocks,
    tile_values,
    tile_cols,
    halo_send,
    halo_counts,
    grp_send,
    well_send,
    well_slot,
    well_count,
    couple_in,
    couple_out,
    well_inverse,
):
    dom_count = lax.axis_size("dom")
    halo_width = halo_send.shape[2]
    rim_width = grp_send.shape[2]
    slot_width = well_send.shape[2]
    cell_count = blocks.shape[1]
    vec_count = blocks.shape[2]
    wells, couplings = well_slot.shape
    slot_total = dom_count * slot_width
    halo_pack = blocks[halo_send[0]]
    rim_pack = blocks[grp_send[0].reshape(-1)]
    rim_ext = padded(rim_pack, (("grp", 0),), rim_width)
    rim_rows = jnp.concatenate([rim_ext[:rim_width], rim_ext[rim_ext.shape[0] - rim_width :]], 0)
    slot_order = jnp.argsort(well_slot.reshape(-1))
    well_pack = blocks[well_send[0]]
    halo_rows = lax.all_to_all(halo_pack, "dom", split_axis=0, concat_axis=0, tiled=True)
    well_rows = lax.all_to_all(well_pack, "dom", split_axis=0, concat_axis=0, tiled=True)
    coupled = well_rows.reshape(slot_total, cell_count, vec_count)[well_slot.reshape(-1)]
    coupled = coupled.reshape(wells, couplings, cell_count, vec_count)
    summed = jnp.einsum("wcsk,wckv->wsv", couple_in, coupled, preferred_element_type=jnp.float32)
    well_state = well_states_of(summed, well_inverse, well_count)
    contrib = jnp.einsum(
        "wcsk,wsv->wckv", couple_out, well_state, preferred_element_type=jnp.float32
    ).astype(jnp.bfloat16)
    contrib_slots = contrib.reshape(wells * couplings, cell_count, vec_count)[slot_order]
    contrib_slots = contrib_slots.reshape(dom_count, slot_width, cell_count, vec_count)
    incoming = lax.all_to_all(contrib_slots, "dom", split_axis=0, concat_axis=0, tiled=True)
    live_halo = jnp.arange(halo_width)[None, :] < halo_counts[0][:, None]
    halo_rows = jnp.where(live_halo[:, :, None, None], halo_rows, jnp.zeros_like(halo_rows))
    extended = jnp.concatenate(
        [blocks, halo_rows.reshape(dom_count * halo_width, cell_count, vec_count), rim_rows], 0
    )
    product = local_product(extended, tile_values, tile_cols)
    return subtract_incoming(product, well_send, incoming).astype(jnp.bfloat16)


def solution(mesh):
    in_specs = (
        P(("dom", "grp"), None, None),
        P(("dom", "grp"), None, None, None),
        P(("dom", "grp"), None),
        P(("dom", "grp"), None, None),
        P(("dom", "grp"), None),
        P(("dom", "grp"), None, None),
        P(("dom", "grp"), None, None),
        P(("dom", "grp"), None),
        P(("dom", "grp")),
        P(("dom", "grp"), None, None, None),
        P(("dom", "grp"), None, None, None),
        P(("dom", "grp"), None, None),
    )
    out_specs = P(("dom", "grp"), None, None)
    return jax.shard_map(
        on_device, mesh=mesh, in_specs=in_specs, out_specs=out_specs, check_vma=False
    )
```

profile of v0, /device:TPU:66, one launch (start us, length us, event | category | flops | bytes accessed | tf_op | source)
XLA Modules:
  0.0 238.7 jit_solution(15428076810765388917)
XLA Ops:
  0.0 0.7 compare_select_fusion.1
  0.9 4.4 %gather_fusion.3 = bf16[64,128,256]{2,1,0:T(8,128)(2,1)} fusion(bf16[32,128,256]{2,1,0:T(8,128)(2,1)} %param.12, s32[1024]{0:T(1024)S(1)} %pad_clamp_fusion.2), kind=kCustom, calls=%fused_computation.3 | custom fusion | bytes 8388864 | tf_op jit(solution)/shard_map/gather | solution.py:68
  5.3 7.6 %all-to-all-start.1 = ((bf16[16,4,128,256]{3,2,1,0:T(8,128)(2,1)}), bf16[16,4,128,256]{3,2,1,0:T(8,128)(2,1)}, u32[]{:S(2)}, u32[]{:S(2)}) async-start(bf16[16,4,128,256]{3,2,1,0:T(8,128)(2,1)} %bitcast.55), calls=%async_computation.1 | async-start | bytes 8388608 | tf_op jit(solution)/shard_map/all_to_all | solution.py:70
  13.1 2.8 %gather_fusion = bf16[64,128,256]{2,1,0:T(8,128)(2,1)} fusion(bf16[32,128,256]{2,1,0:T(8,128)(2,1)S(1)} %copy-done.2, s32[1024]{0:T(1024)S(1)} %pad_clamp_fusion.5), kind=kCustom, calls=%fused_computation | custom fusion | bytes 8388864 | tf_op jit(solution)/shard_map/gather | solution.py:63
  15.9 51.3 %all-to-all-done.1 = bf16[16,4,128,256]{3,2,1,0:T(8,128)(2,1)} async-done(((bf16[16,4,128,256]{3,2,1,0:T(8,128)(2,1)}), bf16[16,4,128,256]{3,2,1,0:T(8,128)(2,1)}, u32[]{:S(2)}, u32[]{:S(2)}) %all-to-all-start.1) | async-done | bytes 4194336 | tf_op jit(solution)/shard_map/all_to_all | solution.py:70
  67.2 19.0 %all-to-all-start = ((bf16[16,4,128,256]{3,2,1,0:T(8,128)(2,1)}), bf16[16,4,128,256]{3,2,1,0:T(8,128)(2,1)}, u32[]{:S(2)}, u32[]{:S(2)}) async-start(bf16[16,4,128,256]{3,2,1,0:T(8,128)(2,1)} %bitcast.54), calls=%async_computation | async-start | bytes 8388608 | tf_op jit(solution)/shard_map/all_to_all | solution.py:69
  86.4 0.1 reshape.171
  87.1 2.1 sort.17
  89.2 5.0 %gather_fusion.4 = bf16[64,128,256]{2,1,0:T(8,128)(2,1)} fusion(bf16[64,128,256]{2,1,0:T(8,128)(2,1)} %bitcast.12, s32[1024]{0:T(1024)S(1)} %pad_clamp_fusion.1), kind=kCustom, calls=%fused_computation.4 | custom fusion | bytes 8388864 | tf_op jit(solution)/shard_map/gather | solution.py:71
  94.2 3.0 %convolution_bitcast_fusion = f32[16,256,32]{1,2,0:T(8,128)S(1)} fusion(bf16[16,4,32,128]{3,2,1,0:T(8,128)(2,1)S(1)} %copy-done.3, bf16[16,4,128,256]{3,2,1,0:T(8,128)(2,1)} %bitcast.57), kind=kOutput, calls=%fused_computation.11 | convolution fusion | flops 134217728 | bytes 5242880 | tf_op jit(solution)/shard_map/wcsk,wckv->wsv/dot_general | solution.py:73
  97.3 0.6 fusion.2
  97.9 3.2 %convolution_convert_fusion = bf16[16,256,4,128]{3,1,2,0:T(8,128)(2,1)} fusion(bf16[16,256,32,1]{1,2,3,0:T(8,128)(2,1)S(1)} %fusion.2, bf16[16,4,32,128]{3,2,1,0:T(8,128)(2,1)S(1)} %copy-done), kind=kOutput, calls=%fused_computation.10 | convolution fusion | flops 136314880 | bytes 4980736 | tf_op jit(solution)/shard_map/wcsk,wsv->wckv/dot_general | solution.py:75
  101.1 6.4 %copy.59 = bf16[64,128,256]{2,1,0:T(8,128)(2,1)} copy(bf16[64,128,256]{1,2,0:T(8,128)(2,1)} %bitcast.59) | data formatting | bytes 8388608 | tf_op jit(solution)/shard_map/reshape | solution.py:78
  107.5 4.9 %gather_fusion.5 = bf16[64,128,256]{2,1,0:T(8,128)(2,1)} fusion(bf16[64,128,256]{2,1,0:T(8,128)(2,1)} %copy.59, s32[1024]{0:T(1024)S(1)} %pad_clamp_fusion), kind=kCustom, calls=%fused_computation.5 | custom fusion | bytes 8388864 | tf_op jit(solution)/shard_map/gather | solution.py:78
  112.4 7.7 %copy.60 = bf16[16,4,128,256]{3,1,2,0:T(4,128)(2,1)} copy(bf16[16,4,128,256]{3,2,1,0:T(8,128)(2,1)} %bitcast.58) | data formatting | bytes 8388608 | tf_op jit(solution)/shard_map/reshape | solution.py:79
  120.1 15.4 %all-to-all-done = bf16[16,4,128,256]{3,2,1,0:T(8,128)(2,1)} async-done(((bf16[16,4,128,256]{3,2,1,0:T(8,128)(2,1)}), bf16[16,4,128,256]{3,2,1,0:T(8,128)(2,1)}, u32[]{:S(2)}, u32[]{:S(2)}) %all-to-all-start) | async-done | bytes 4194336 | tf_op jit(solution)/shard_map/all_to_all | solution.py:69
  135.5 8.5 %all-to-all-start.2 = ((bf16[16,4,128,256]{3,1,2,0:T(4,128)(2,1)}), bf16[16,4,128,256]{3,1,2,0:T(4,128)(2,1)}, u32[]{:S(2)}, u32[]{:S(2)}) async-start(bf16[16,4,128,256]{3,1,2,0:T(4,128)(2,1)} %copy.60), calls=%async_computation.2 | async-start | bytes 8388608 | tf_op jit(solution)/shard_map/all_to_all | solution.py:80
  144.1 0.6 gather_fusion.1
  144.8 1.9 collective-permute-start
  146.7 3.8 %collective-permute-start.1 = (bf16[4,128,256]{2,1,0:T(8,128)(2,1)S(1)}, bf16[4,128,256]{2,1,0:T(8,128)(2,1)S(1)}, u32[]{:S(2)}, u32[]{:S(2)}) collective-permute-start(bf16[4,128,256]{2,1,0:T(8,128)(2,1)S(1)} %get-tuple-element.8), channel_id=1, source_target_pairs={{1,0},{2,1},{3,2},{4,3},{5,4},{6,5},{7,6},{9,8},{10,9},{11,10},{12... | collective-permute-start | bytes 786440 | tf_op jit(solution)/shard_map/ppermute | solution.py:15
  150.8 0.1 eq.15
  151.0 2.5 %broadcast_select_fusion = bf16[16,4,128,256]{3,2,1,0:T(8,128)(2,1)S(1)} fusion(bf16[16,4,128,256]{3,2,1,0:T(8,128)(2,1)} %all-to-all-done, pred[16,4]{1,0:T(8,128)(4,1)S(1)} %iota_compare_fusion.1), kind=kLoop, calls=%fused_computation.9 | loop fusion | flops 2097152 | bytes 8388672 | tf_op jit(solution)/shard_map/jit(_where)/select_n | solution.py:82
  153.5 0.7 collective-permute-done.1
  154.2 3.7 %pad_maximum_fusion = bf16[104,128,256]{2,1,0:T(8,128)(2,1)} fusion(bf16[4,128,256]{2,1,0:T(8,128)(2,1)S(1)} %collective-permute-done.1, bf16[4,128,256]{2,1,0:T(8,128)(2,1)S(1)} %collective-permute-done, bf16[64,128,256]{2,1,0:T(8,128)(2,1)S(1)} %bitcast.56, bf16[32,128,256]{2,1,0:T(8,128)(2,1)S(1)} %copy-done.2), kind=kLoop, calls=%fused_computation.6 | loop fusion | flops 10223616 | bytes 13631488 | tf_op jit(solution)/shard_map/concatenate | solution.py:83
  157.9 19.1 %gather_fusion.2 = bf16[512,128,256]{2,1,0:T(8,128)(2,1)} fusion(bf16[104,128,256]{2,1,0:T(8,128)(2,1)} %pad_maximum_fusion, s32[1024]{0:T(1024)S(1)} %pad_clamp_fusion.3), kind=kCustom, calls=%fused_computation.2 | custom fusion | bytes 67110912 | tf_op jit(solution)/shard_map/gather | solution.py:21
  177.0 15.2 %all-to-all-done.2 = bf16[16,4,128,256]{3,1,2,0:T(4,128)(2,1)} async-done(((bf16[16,4,128,256]{3,1,2,0:T(4,128)(2,1)}), bf16[16,4,128,256]{3,1,2,0:T(4,128)(2,1)}, u32[]{:S(2)}, u32[]{:S(2)}) %all-to-all-start.2) | async-done | bytes 4194336 | tf_op jit(solution)/shard_map/all_to_all | solution.py:80
  192.2 6.6 %copy.61 = bf16[16,4,128,256]{3,1,0,2:T(4,128)(2,1)} copy(bf16[16,4,128,256]{3,1,2,0:T(4,128)(2,1)} %all-to-all-done.2) | data formatting | bytes 8388608 | tf_op jit(solution)/shard_map/all_to_all | solution.py:80
  198.8 7.0 %reshape.173 = bf16[64,128,256]{2,0,1:T(8,128)(2,1)} reshape(bf16[16,4,128,256]{3,1,0,2:T(4,128)(2,1)} %copy.61) | data formatting | bytes 8388608 | tf_op jit(solution)/shard_map/reshape | solution.py:35
  205.8 5.0 %fusion.4 = f32[32,128,256]{2,0,1:T(8,128)} fusion(bf16[64,128,256]{2,0,1:T(8,128)(2,1)} %reshape.173, s32[64]{0:T(128)S(1)} %eq.15), kind=kOutput, calls=%fused_computation.18 | convolution fusion | flops 134219776 | bytes 8388864 | tf_op jit(solution)/shard_map/bq,qkv->bkv/dot_general | solution.py:36
  210.8 5.3 %copy.62 = f32[32,128,256]{1,2,0:T(8,128)} copy(f32[32,128,256]{2,0,1:T(8,128)} %fusion.4) | data formatting | bytes 8388608 | tf_op jit(solution)/shard_map/bq,qkv->bkv/dot_general | solution.py:36
  216.1 19.7 %fusion = bf16[32,128,256]{1,2,0:T(8,128)(2,1)S(1)} fusion(f32[32,128,256]{1,2,0:T(8,128)} %copy.62, bf16[32,16,128,256]{3,2,1,0:T(8,128)(2,1)} %bitcast.53, bf16[32,16,128,128]{3,2,1,0:T(8,128)(2,1)} %param.13), kind=kOutput, calls=%fused_computation.8 | convolution fusion | flops 4297064448 | bytes 56623104 | tf_op jit(solution)/shard_map/btij,btjv->biv/dot_general | solution.py:22
  235.8 2.9 %copy.63 = bf16[32,128,256]{2,1,0:T(8,128)(2,1)} copy(bf16[32,128,256]{1,2,0:T(8,128)(2,1)S(1)} %fusion) | data formatting | bytes 4194304 | tf_op jit(solution)/shard_map/convert_element_type | solution.py:87
  (48 shorter events, 1.1 us)
Async XLA Ops:
  0.0 97.9 %copy-start = (bf16[16,4,32,128]{3,2,1,0:T(8,128)(2,1)S(1)}, bf16[16,4,32,128]{3,2,1,0:T(8,128)(2,1)}, u32[]{:S(2)}) copy-start(bf16[16,4,32,128]{3,2,1,0:T(8,128)(2,1)} %param.22) | copy-start | bytes 1572868
  5.3 7.6 %copy-start.8 = (s32[1,16,4]{1,2,0:T(4,128)S(1)}, s32[1,16,4]{1,2,0:T(4,128)}, u32[]{:S(2)}) copy-start(s32[1,16,4]{1,2,0:T(4,128)} %param.15) | copy-start | bytes 772
  5.3 7.8 %copy-start.2 = (bf16[32,128,256]{2,1,0:T(8,128)(2,1)S(1)}, bf16[32,128,256]{2,1,0:T(8,128)(2,1)}, u32[]{:S(2)}) copy-start(bf16[32,128,256]{2,1,0:T(8,128)(2,1)} %param.12) | copy-start | bytes 6291460
  5.3 61.9 %all-to-all-start.1 = ((bf16[16,4,128,256]{3,2,1,0:T(8,128)(2,1)}), bf16[16,4,128,256]{3,2,1,0:T(8,128)(2,1)}, u32[]{:S(2)}, u32[]{:S(2)}) async-start(bf16[16,4,128,256]{3,2,1,0:T(8,128)(2,1)} %bitcast.55), calls=%async_computation.1 | async-start | bytes 8388608 | tf_op jit(solution)/shard_map/all_to_all | solution.py:70
  67.2 19.0 %copy-start.7 = (s32[16,4]{0,1:T(4,128)S(1)}, s32[16,4]{0,1:T(4,128)}, u32[]{:S(2)}) copy-start(s32[16,4]{0,1:T(4,128)} %param.19) | copy-start | bytes 772
  67.2 68.4 %all-to-all-start = ((bf16[16,4,128,256]{3,2,1,0:T(8,128)(2,1)}), bf16[16,4,128,256]{3,2,1,0:T(8,128)(2,1)}, u32[]{:S(2)}, u32[]{:S(2)}) async-start(bf16[16,4,128,256]{3,2,1,0:T(8,128)(2,1)} %bitcast.54), calls=%async_computation | async-start | bytes 8388608 | tf_op jit(solution)/shard_map/all_to_all | solution.py:69
  89.2 5.0 %copy-start.3 = (bf16[16,4,32,128]{3,2,1,0:T(8,128)(2,1)S(1)}, bf16[16,4,32,128]{3,2,1,0:T(8,128)(2,1)}, u32[]{:S(2)}) copy-start(bf16[16,4,32,128]{3,2,1,0:T(8,128)(2,1)} %param.21) | copy-start | bytes 1572868
  94.2 3.1 %copy-start.4 = (f32[16,32,32]{2,1,0:T(8,128)S(1)}, f32[16,32,32]{2,1,0:T(8,128)}, u32[]{:S(2)}) copy-start(f32[16,32,32]{2,1,0:T(8,128)} %param.23) | copy-start | bytes 196612
  120.1 23.9 %copy-start.10 = (s32[1,2,4]{2,1,0:T(2,128)S(1)}, s32[1,2,4]{2,1,0:T(2,128)}, u32[]{:S(2)}) copy-start(s32[1,2,4]{2,1,0:T(2,128)} %param.17) | copy-start | bytes 100
  120.1 30.4 %copy-start.5 = (s32[1,16,4]{1,2,0:T(4,128)S(1)}, s32[1,16,4]{1,2,0:T(4,128)}, u32[]{:S(2)}) copy-start(s32[1,16,4]{1,2,0:T(4,128)} %param.18) | copy-start | bytes 772
  120.1 30.5 %copy-start.6 = (s32[32,16]{0,1:T(8,128)S(1)}, s32[32,16]{0,1:T(8,128)}, u32[]{:S(2)}) copy-start(s32[32,16]{0,1:T(8,128)} %param.14) | copy-start | bytes 6148
  120.1 30.8 %copy-start.9 = (s32[1,16]{1,0:T(1,128)S(1)}, s32[1,16]{1,0:T(1,128)}, u32[]{:S(2)}) copy-start(s32[1,16]{1,0:T(1,128)} %param.16) | copy-start | bytes 196
  135.5 56.7 %all-to-all-start.2 = ((bf16[16,4,128,256]{3,1,2,0:T(4,128)(2,1)}), bf16[16,4,128,256]{3,1,2,0:T(4,128)(2,1)}, u32[]{:S(2)}, u32[]{:S(2)}) async-start(bf16[16,4,128,256]{3,1,2,0:T(4,128)(2,1)} %copy.60), calls=%async_computation.2 | async-start | bytes 8388608 | tf_op jit(solution)/shard_map/all_to_all | solution.py:80
  144.8 8.7 %collective-permute-start = (bf16[4,128,256]{2,1,0:T(8,128)(2,1)S(1)}, bf16[4,128,256]{2,1,0:T(8,128)(2,1)S(1)}, u32[]{:S(2)}, u32[]{:S(2)}) collective-permute-start(bf16[4,128,256]{2,1,0:T(8,128)(2,1)S(1)} %get-tuple-element.7), channel_id=1, source_target_pairs={{0,1},{1,2},{2,3},{3,4},{4,5},{5,6},{6,7},{8,9},{9,10},{10,11},{11... | collective-permute-start | bytes 786440 | tf_op jit(solution)/shard_map/ppermute | solution.py:14
  146.7 7.5 %collective-permute-start.1 = (bf16[4,128,256]{2,1,0:T(8,128)(2,1)S(1)}, bf16[4,128,256]{2,1,0:T(8,128)(2,1)S(1)}, u32[]{:S(2)}, u32[]{:S(2)}) collective-permute-start(bf16[4,128,256]{2,1,0:T(8,128)(2,1)S(1)} %get-tuple-element.8), channel_id=1, source_target_pairs={{1,0},{2,1},{3,2},{4,3},{5,4},{6,5},{7,6},{9,8},{10,9},{11,10},{12... | collective-permute-start | bytes 786440 | tf_op jit(solution)/shard_map/ppermute | solution.py:15
  216.1 22.6 %copy-start.1 = (bf16[16,4,32,128]{3,2,1,0:T(8,128)(2,1)S(1)}, bf16[16,4,32,128]{3,2,1,0:T(8,128)(2,1)}, u32[]{:S(2)}) copy-start(bf16[16,4,32,128]{3,2,1,0:T(8,128)(2,1)} %param.22) | copy-start | bytes 1572868
where the time goes:
time: 242 us; the launch traced here: 239 us
  waiting for transfers between devices  82.6 us (34%)
  local copies, waits for them, and re-layouts  73.7 us (30%)
  starting transfers between devices  40.9 us (17%)
  matrix products  31.5 us (13%)
  other arithmetic  9.16 us (4%)
    all_to_all x1, waiting for transfers between devices, on_device(): lax.all_to_all(well_pack, 'dom', split_axis=0, concat_axis=0, tiled=True)  51.3 us
    dot_general x1, matrix products, local_product(): jnp.einsum('btij,btjv->biv', tile_values, gathered, preferred_element_typ...  19.7 us
    gather x1, local copies, waits for them, and re-layouts, local_product(): gathered = extended[tile_cols]  19.1 us
    all_to_all x1, starting transfers between devices, on_device(): lax.all_to_all(halo_pack, 'dom', split_axis=0, concat_axis=0, tiled=True)  19 us
    all_to_all x1, waiting for transfers between devices, on_device(): lax.all_to_all(halo_pack, 'dom', split_axis=0, concat_axis=0, tiled=True)  15.4 us
    all_to_all x1, waiting for transfers between devices, on_device(): lax.all_to_all(contrib_slots, 'dom', split_axis=0, concat_axis=0, tiled=T...  15.2 us
    all_to_all x1, starting transfers between devices, on_device(): lax.all_to_all(contrib_slots, 'dom', split_axis=0, concat_axis=0, tiled=T...  8.49 us
    reshape x1, local copies, waits for them, and re-layouts, on_device(): contrib_slots.reshape(dom_count, slot_width, cell_count, vec_count)  7.72 us
  transfers between devices with their start and end apart: 5, of which 4 were waited for; matrix products, arithmetic and copies ran while one was open for 26% of the time, Pallas kernels for 0%

commit v1 on v0

--- a/solution.py
+++ b/solution.py
@@ -59,6 +59,7 @@
     cell_count = blocks.shape[1]
     vec_count = blocks.shape[2]
     wells, couplings = well_slot.shape
+    seg = couple_in.shape[2]
     slot_total = dom_count * slot_width
     halo_pack = blocks[halo_send[0]]
     rim_pack = blocks[grp_send[0].reshape(-1)]
@@ -66,18 +67,27 @@
     rim_rows = jnp.concatenate([rim_ext[:rim_width], rim_ext[rim_ext.shape[0] - rim_width :]], 0)
     slot_order = jnp.argsort(well_slot.reshape(-1))
     well_pack = blocks[well_send[0]]
-    halo_rows = lax.all_to_all(halo_pack, "dom", split_axis=0, concat_axis=0, tiled=True)
-    well_rows = lax.all_to_all(well_pack, "dom", split_axis=0, concat_axis=0, tiled=True)
+    send_pack = jnp.concatenate([halo_pack, well_pack], 1)
+    recv_pack = lax.all_to_all(send_pack, "dom", split_axis=0, concat_axis=0, tiled=True)
+    halo_rows = recv_pack[:, :halo_width]
+    well_rows = recv_pack[:, halo_width:]
     coupled = well_rows.reshape(slot_total, cell_count, vec_count)[well_slot.reshape(-1)]
     coupled = coupled.reshape(wells, couplings, cell_count, vec_count)
     summed = jnp.einsum("wcsk,wckv->wsv", couple_in, coupled, preferred_element_type=jnp.float32)
     well_state = well_states_of(summed, well_inverse, well_count)
-    contrib = jnp.einsum(
-        "wcsk,wsv->wckv", couple_out, well_state, preferred_element_type=jnp.float32
+    slot_well = slot_order // couplings
+    state_slots = well_state[slot_well]
+    out_slots = couple_out.reshape(wells * couplings, seg, cell_count)[slot_order]
+    state_pack = jnp.concatenate([state_slots, out_slots], 2)
+    state_pack = state_pack.reshape(dom_count, slot_width, seg, vec_count + cell_count)
+    state_in = lax.all_to_all(state_pack, "dom", split_axis=0, concat_axis=0, tiled=True)
+    state_in = state_in.reshape(slot_total, seg, vec_count + cell_count)
+    incoming = jnp.einsum(
+        "qsk,qsv->qkv",
+        state_in[:, :, vec_count:],
+        state_in[:, :, :vec_count],
+        preferred_element_type=jnp.float32,
     ).astype(jnp.bfloat16)
-    contrib_slots = contrib.reshape(wells * couplings, cell_count, vec_count)[slot_order]
-    contrib_slots = contrib_slots.reshape(dom_count, slot_width, cell_count, vec_count)
-    incoming = lax.all_to_all(contrib_slots, "dom", split_axis=0, concat_axis=0, tiled=True)
     live_halo = jnp.arange(halo_width)[None, :] < halo_counts[0][:, None]
     halo_rows = jnp.where(live_halo[:, :, None, None], halo_rows, jnp.zeros_like(halo_rows))
     extended = jnp.concatenate(

time: 242 us -> 273 us (1.13)
  local copies, waits for them, and re-layouts: 73.7 us -> 44.3 us
  starting transfers between devices: 40.9 us -> 64.6 us
  waiting for transfers between devices: 82.6 us -> 103 us
  other arithmetic: 9.16 us -> 25.4 us
    all_to_all x3 -> x2, starting transfers between devices: 35.1 us -> 58.9 us  [the longest x1 51.3 us: on_device(): lax.all_to_all(state_pack, 'dom', split_axis=0, concat_axis=0, tiled=True)]
    reshape x3 -> x0, local copies, waits for them, and re-layouts: 21.1 us -> none  [the longest x1 7.72 us: on_device(): contrib_slots.reshape(dom_count, slot_width, cell_count, vec_count)]
    all_to_all x3 -> x2, waiting for transfers between devices: 81.9 us -> 99.6 us  [the longest x1 99.6 us: on_device(): lax.all_to_all(send_pack, 'dom', split_axis=0, concat_axis=0, tiled=True)]
    concatenate x0 -> x2, other arithmetic: none -> 10.1 us  [the longest x1 7.42 us: on_device(): send_pack = jnp.concatenate([halo_pack, well_pack], 1)]
    all_to_all x1 -> x0, local copies, waits for them, and re-layouts: 6.62 us -> none  [on_device(): lax.all_to_all(contrib_slots, 'dom', split_axis=0, concat_axis=0, tiled=T...]
    select_n x1, other arithmetic: 2.53 us -> 5.76 us  [on_device(): jnp.where(live_halo[:, :, None, None], halo_rows, jnp.zeros_like(halo_rows))]
  transfers between devices with their start and end apart: 5 -> 4, of which waited for: 4 -> 3; matrix products, arithmetic and copies ran while one was open for 26% -> 11% of each run, Pallas kernels for 0% -> 0%
where the time goes in v1:
time: 273 us; the launch traced here: 269 us
  waiting for transfers between devices  103 us (38%)
  starting transfers between devices  64.6 us (24%)
  local copies, waits for them, and re-layouts  44.3 us (16%)
  matrix products  31 us (11%)
  other arithmetic  25.4 us (9%)
    all_to_all x1, waiting for transfers between devices, on_device(): lax.all_to_all(send_pack, 'dom', split_axis=0, concat_axis=0, tiled=True)  99.6 us
    all_to_all x1, starting transfers between devices, on_device(): lax.all_to_all(state_pack, 'dom', split_axis=0, concat_axis=0, tiled=True)  51.3 us
    dot_general x1, matrix products, local_product(): jnp.einsum('btij,btjv->biv', tile_values, gathered, preferred_element_typ...  19.7 us
    gather x1, local copies, waits for them, and re-layouts, local_product(): gathered = extended[tile_cols]  19 us
    all_to_all x1, starting transfers between devices, on_device(): lax.all_to_all(send_pack, 'dom', split_axis=0, concat_axis=0, tiled=True)  7.61 us
    concatenate x1, other arithmetic, on_device(): send_pack = jnp.concatenate([halo_pack, well_pack], 1)  7.42 us
    concatenate x1, other arithmetic, on_device(): jnp.concatenate([blocks, halo_rows.reshape(dom_count * halo_width, cell_c...  5.93 us
    select_n x1, other arithmetic, on_device(): jnp.where(live_halo[:, :, None, None], halo_rows, jnp.zeros_like(halo_rows))  5.76 us
  transfers between devices with their start and end apart: 4, of which 3 were waited for; matrix products, arithmetic and copies ran while one was open for 11% of the time, Pallas kernels for 0%

profile of v1, /device:TPU:66, one launch (start us, length us, event | category | flops | bytes accessed | tf_op | source)
XLA Modules:
  0.0 269.0 jit_solution(9157633568273817968)
XLA Ops:
  0.0 0.7 compare_select_fusion.2
  0.7 0.7 compare_select_fusion.1
  1.7 0.1 reshape.176
  1.8 4.5 %gather_fusion = bf16[64,128,256]{2,1,0:T(8,128)(2,1)} fusion(bf16[32,128,256]{2,1,0:T(8,128)(2,1)} %param.12, s32[1024]{0:T(1024)S(1)} %pad_clamp_fusion.6), kind=kCustom, calls=%fused_computation | custom fusion | bytes 8388864 | tf_op jit(solution)/shard_map/gather | solution.py:64
  6.3 2.8 %gather_fusion.1 = bf16[64,128,256]{2,1,0:T(8,128)(2,1)} fusion(bf16[32,128,256]{2,1,0:T(8,128)(2,1)S(1)} %copy-done.2, s32[1024]{0:T(1024)S(1)} %pad_clamp_fusion.5), kind=kCustom, calls=%fused_computation.1 | custom fusion | bytes 8388864 | tf_op jit(solution)/shard_map/gather | solution.py:69
  9.1 7.4 %pad_maximum_fusion = bf16[16,8,128,256]{3,2,1,0:T(8,128)(2,1)} fusion(bf16[16,4,128,256]{3,2,1,0:T(8,128)(2,1)} %bitcast.51, bf16[16,4,128,256]{3,2,1,0:T(8,128)(2,1)} %bitcast.50), kind=kLoop, calls=%fused_computation.7 | loop fusion | flops 4194304 | bytes 16777216 | tf_op jit(solution)/shard_map/concatenate | solution.py:70
  16.5 7.6 %all-to-all-start = ((bf16[16,8,128,256]{3,2,1,0:T(8,128)(2,1)}), bf16[16,8,128,256]{3,2,1,0:T(8,128)(2,1)}, u32[]{:S(2)}, u32[]{:S(2)}) async-start(bf16[16,8,128,256]{3,2,1,0:T(8,128)(2,1)} %pad_maximum_fusion), calls=%async_computation | async-start | bytes 16777216 | tf_op jit(solution)/shard_map/all_to_all | solution.py:71
  24.2 0.1 reshape.170
  24.3 0.1 reshape.168
  25.2 0.6 gather_fusion.2
  25.8 2.0 sort.17
  27.8 1.4 gather_fusion.6
  29.4 99.6 %all-to-all-done = bf16[16,8,128,256]{3,2,1,0:T(8,128)(2,1)} async-done(((bf16[16,8,128,256]{3,2,1,0:T(8,128)(2,1)}), bf16[16,8,128,256]{3,2,1,0:T(8,128)(2,1)}, u32[]{:S(2)}, u32[]{:S(2)}) %all-to-all-start) | async-done | bytes 8388640 | tf_op jit(solution)/shard_map/all_to_all | solution.py:71
  128.9 5.8 %slice_select_fusion = (bf16[16,4,128,256]{3,2,1,0:T(8,128)(2,1)}, bf16[16,4,128,256]{3,2,1,0:T(8,128)(2,1)}) fusion(bf16[16,8,128,256]{3,2,1,0:T(8,128)(2,1)} %all-to-all-done, pred[16,4]{1,0:T(8,128)(4,1)S(1)} %iota_compare_fusion.1), kind=kLoop, calls=%fused_computation.11 | loop fusion | flops 2097152 | bytes 16777280 | tf_op jit(solution)/shard_map/jit(_where)/select_n | solution.py:92
  134.7 5.0 %gather_fusion.4 = bf16[64,128,256]{2,1,0:T(8,128)(2,1)} fusion(bf16[64,128,256]{2,1,0:T(8,128)(2,1)} %bitcast.48, s32[1024]{0:T(1024)S(1)} %pad_clamp_fusion.2), kind=kCustom, calls=%fused_computation.4 | custom fusion | bytes 8388864 | tf_op jit(solution)/shard_map/gather | solution.py:74
  139.7 3.0 %convolution_bitcast_fusion = f32[16,256,32]{1,2,0:T(8,128)S(1)} fusion(bf16[16,4,32,128]{3,2,1,0:T(8,128)(2,1)S(1)} %copy-done.3, bf16[16,4,128,256]{3,2,1,0:T(8,128)(2,1)} %bitcast.49), kind=kOutput, calls=%fused_computation.15 | convolution fusion | flops 134217728 | bytes 5242880 | tf_op jit(solution)/shard_map/wcsk,wckv->wsv/dot_general | solution.py:76
  142.8 0.6 fusion.3
  143.4 1.6 gather_fusion.5
  145.0 2.7 %pad_maximum_fusion.2 = bf16[64,32,384]{2,1,0:T(8,128)(2,1)} fusion(bf16[64,32,128]{2,1,0:T(8,128)(2,1)} %gather_fusion.6, bf16[64,32,256]{2,1,0:T(8,128)(2,1)} %gather_fusion.5), kind=kLoop, calls=%fused_computation.14 | loop fusion | flops 3145728 | bytes 3145728 | tf_op jit(solution)/shard_map/concatenate | solution.py:81
  147.7 51.3 %all-to-all-start.1 = ((bf16[16,4,32,384]{3,2,1,0:T(8,128)(2,1)}), bf16[16,4,32,384]{3,2,1,0:T(8,128)(2,1)}, u32[]{:S(2)}, u32[]{:S(2)}) async-start(bf16[16,4,32,384]{3,2,1,0:T(8,128)(2,1)} %bitcast.52), calls=%async_computation.1 | async-start | bytes 3145728 | tf_op jit(solution)/shard_map/all_to_all | solution.py:83
  199.0 1.9 collective-permute-start
  200.9 3.8 %collective-permute-start.1 = (bf16[4,128,256]{2,1,0:T(8,128)(2,1)S(1)}, bf16[4,128,256]{2,1,0:T(8,128)(2,1)S(1)}, u32[]{:S(2)}, u32[]{:S(2)}) collective-permute-start(bf16[4,128,256]{2,1,0:T(8,128)(2,1)S(1)} %get-tuple-element.10), channel_id=1, source_target_pairs={{1,0},{2,1},{3,2},{4,3},{5,4},{6,5},{7,6},{9,8},{10,9},{11,10},{12... | collective-permute-start | bytes 786440 | tf_op jit(solution)/shard_map/ppermute | solution.py:15
  205.0 0.1 eq.15
  205.1 1.6 collective-permute-done
  206.7 1.8 collective-permute-done.1
  208.4 5.9 %pad_maximum_fusion.1 = bf16[104,128,256]{2,1,0:T(8,128)(2,1)} fusion(bf16[4,128,256]{2,1,0:T(8,128)(2,1)S(1)} %collective-permute-done.1, bf16[4,128,256]{2,1,0:T(8,128)(2,1)S(1)} %collective-permute-done, bf16[64,128,256]{2,1,0:T(8,128)(2,1)} %bitcast.47, bf16[32,128,256]{2,1,0:T(8,128)(2,1)S(1)} %copy-done.2), kind=kLoop, calls=%fused_computation.9 | loop fusion | flops 10223616 | bytes 13631488 | tf_op jit(solution)/shard_map/concatenate | solution.py:93
  214.3 19.0 %gather_fusion.3 = bf16[512,128,256]{2,1,0:T(8,128)(2,1)} fusion(bf16[104,128,256]{2,1,0:T(8,128)(2,1)} %pad_maximum_fusion.1, s32[1024]{0:T(1024)S(1)} %pad_clamp_fusion.3), kind=kCustom, calls=%fused_computation.3 | custom fusion | bytes 67110912 | tf_op jit(solution)/shard_map/gather | solution.py:21
  233.4 2.7 fusion.4
  236.1 5.0 %fusion = f32[32,128,256]{2,0,1:T(8,128)} fusion(bf16[64,128,256]{2,1,0:T(8,128)(2,1)S(1)} %fusion.4, s32[64]{0:T(128)S(1)} %eq.15), kind=kOutput, calls=%fused_computation.10 | convolution fusion | flops 134219776 | bytes 8388864 | tf_op jit(solution)/shard_map/bq,qkv->bkv/dot_general | solution.py:36
  241.1 5.4 %copy.27 = f32[32,128,256]{1,2,0:T(8,128)} copy(f32[32,128,256]{2,0,1:T(8,128)} %fusion) | data formatting | bytes 8388608 | tf_op jit(solution)/shard_map/bq,qkv->bkv/dot_general | solution.py:36
  246.4 19.7 %fusion.1 = bf16[32,128,256]{1,2,0:T(8,128)(2,1)S(1)} fusion(f32[32,128,256]{1,2,0:T(8,128)} %copy.27, bf16[32,16,128,256]{3,2,1,0:T(8,128)(2,1)} %bitcast.46, bf16[32,16,128,128]{3,2,1,0:T(8,128)(2,1)} %param.13), kind=kOutput, calls=%fused_computation.13 | convolution fusion | flops 4297064448 | bytes 56623104 | tf_op jit(solution)/shard_map/btij,btjv->biv/dot_general | solution.py:22
  266.1 2.9 %copy.28 = bf16[32,128,256]{2,1,0:T(8,128)(2,1)} copy(bf16[32,128,256]{1,2,0:T(8,128)(2,1)S(1)} %fusion.1) | data formatting | bytes 4194304 | tf_op jit(solution)/shard_map/convert_element_type | solution.py:97
  (43 shorter events, 0.9 us)
Async XLA Ops:
  0.0 27.8 %copy-start = (bf16[16,4,32,128]{3,2,1,0:T(8,128)(2,1)S(1)}, bf16[16,4,32,128]{3,2,1,0:T(8,128)(2,1)}, u32[]{:S(2)}) copy-start(bf16[16,4,32,128]{3,2,1,0:T(8,128)(2,1)} %param.22) | copy-start | bytes 1572868
  1.8 4.5 %copy-start.2 = (bf16[32,128,256]{2,1,0:T(8,128)(2,1)S(1)}, bf16[32,128,256]{2,1,0:T(8,128)(2,1)}, u32[]{:S(2)}) copy-start(bf16[32,128,256]{2,1,0:T(8,128)(2,1)} %param.12) | copy-start | bytes 6291460
  16.5 7.6 %copy-start.7 = (s32[16,4]{0,1:T(4,128)S(1)}, s32[16,4]{0,1:T(4,128)}, u32[]{:S(2)}) copy-start(s32[16,4]{0,1:T(4,128)} %param.19) | copy-start | bytes 772
  16.5 8.5 %copy-start.9 = (s32[1,2,4]{2,1,0:T(2,128)S(1)}, s32[1,2,4]{2,1,0:T(2,128)}, u32[]{:S(2)}) copy-start(s32[1,2,4]{2,1,0:T(2,128)} %param.17) | copy-start | bytes 100
  16.5 12.8 %copy-start.8 = (s32[1,16]{1,0:T(1,128)S(1)}, s32[1,16]{1,0:T(1,128)}, u32[]{:S(2)}) copy-start(s32[1,16]{1,0:T(1,128)} %param.16) | copy-start | bytes 196
  16.5 112.4 %all-to-all-start = ((bf16[16,8,128,256]{3,2,1,0:T(8,128)(2,1)}), bf16[16,8,128,256]{3,2,1,0:T(8,128)(2,1)}, u32[]{:S(2)}, u32[]{:S(2)}) async-start(bf16[16,8,128,256]{3,2,1,0:T(8,128)(2,1)} %pad_maximum_fusion), calls=%async_computation | async-start | bytes 16777216 | tf_op jit(solution)/shard_map/all_to_all | solution.py:71
  134.7 5.0 %copy-start.3 = (bf16[16,4,32,128]{3,2,1,0:T(8,128)(2,1)S(1)}, bf16[16,4,32,128]{3,2,1,0:T(8,128)(2,1)}, u32[]{:S(2)}) copy-start(bf16[16,4,32,128]{3,2,1,0:T(8,128)(2,1)} %param.21) | copy-start | bytes 1572868
  139.7 3.1 %copy-start.4 = (f32[16,32,32]{2,1,0:T(8,128)S(1)}, f32[16,32,32]{2,1,0:T(8,128)}, u32[]{:S(2)}) copy-start(f32[16,32,32]{2,1,0:T(8,128)} %param.23) | copy-start | bytes 196612
  145.0 59.8 %copy-start.5 = (s32[1,16,4]{1,2,0:T(4,128)S(1)}, s32[1,16,4]{1,2,0:T(4,128)}, u32[]{:S(2)}) copy-start(s32[1,16,4]{1,2,0:T(4,128)} %param.18) | copy-start | bytes 772
  145.0 59.9 %copy-start.6 = (s32[32,16]{0,1:T(8,128)S(1)}, s32[32,16]{0,1:T(8,128)}, u32[]{:S(2)}) copy-start(s32[32,16]{0,1:T(8,128)} %param.14) | copy-start | bytes 6148
  147.7 85.7 %all-to-all-start.1 = ((bf16[16,4,32,384]{3,2,1,0:T(8,128)(2,1)}), bf16[16,4,32,384]{3,2,1,0:T(8,128)(2,1)}, u32[]{:S(2)}, u32[]{:S(2)}) async-start(bf16[16,4,32,384]{3,2,1,0:T(8,128)(2,1)} %bitcast.52), calls=%async_computation.1 | async-start | bytes 3145728 | tf_op jit(solution)/shard_map/all_to_all | solution.py:83
  199.0 7.7 %collective-permute-start = (bf16[4,128,256]{2,1,0:T(8,128)(2,1)S(1)}, bf16[4,128,256]{2,1,0:T(8,128)(2,1)S(1)}, u32[]{:S(2)}, u32[]{:S(2)}) collective-permute-start(bf16[4,128,256]{2,1,0:T(8,128)(2,1)S(1)} %get-tuple-element.9), channel_id=1, source_target_pairs={{0,1},{1,2},{2,3},{3,4},{4,5},{5,6},{6,7},{8,9},{9,10},{10,11},{11... | collective-permute-start | bytes 786440 | tf_op jit(solution)/shard_map/ppermute | solution.py:14
  200.9 7.5 %collective-permute-start.1 = (bf16[4,128,256]{2,1,0:T(8,128)(2,1)S(1)}, bf16[4,128,256]{2,1,0:T(8,128)(2,1)S(1)}, u32[]{:S(2)}, u32[]{:S(2)}) collective-permute-start(bf16[4,128,256]{2,1,0:T(8,128)(2,1)S(1)} %get-tuple-element.10), channel_id=1, source_target_pairs={{1,0},{2,1},{3,2},{4,3},{5,4},{6,5},{7,6},{9,8},{10,9},{11,10},{12... | collective-permute-start | bytes 786440 | tf_op jit(solution)/shard_map/ppermute | solution.py:15
  246.4 22.6 %copy-start.1 = (bf16[16,4,32,128]{3,2,1,0:T(8,128)(2,1)S(1)}, bf16[16,4,32,128]{3,2,1,0:T(8,128)(2,1)}, u32[]{:S(2)}) copy-start(bf16[16,4,32,128]{3,2,1,0:T(8,128)(2,1)} %param.22) | copy-start | bytes 1572868

commit v2 on v1

--- a/solution.py
+++ b/solution.py
@@ -66,16 +66,20 @@
     rim_ext = padded(rim_pack, (("grp", 0),), rim_width)
     rim_rows = jnp.concatenate([rim_ext[:rim_width], rim_ext[rim_ext.shape[0] - rim_width :]], 0)
     slot_order = jnp.argsort(well_slot.reshape(-1))
+    slot_well = slot_order // couplings
+    in_slots = couple_in.reshape(wells * couplings, seg, cell_count)[slot_order]
+    in_slots = in_slots.reshape(dom_count, slot_width * seg * cell_count // vec_count, vec_count)
+    halo_flat = halo_pack.reshape(dom_count, halo_width * cell_count, vec_count)
+    send_pack = jnp.concatenate([halo_flat, in_slots], 1)
+    recv_pack = lax.all_to_all(send_pack, "dom", split_axis=0, concat_axis=0, tiled=True)
+    halo_rows = recv_pack[:, : halo_width * cell_count].reshape(dom_count, halo_width, cell_count, vec_count)
+    in_recv = recv_pack[:, halo_width * cell_count :].reshape(dom_count, slot_width, seg, cell_count)
     well_pack = blocks[well_send[0]]
-    send_pack = jnp.concatenate([halo_pack, well_pack], 1)
-    recv_pack = lax.all_to_all(send_pack, "dom", split_axis=0, concat_axis=0, tiled=True)
-    halo_rows = recv_pack[:, :halo_width]
-    well_rows = recv_pack[:, halo_width:]
-    coupled = well_rows.reshape(slot_total, cell_count, vec_count)[well_slot.reshape(-1)]
-    coupled = coupled.reshape(wells, couplings, cell_count, vec_count)
-    summed = jnp.einsum("wcsk,wckv->wsv", couple_in, coupled, preferred_element_type=jnp.float32)
+    partial = jnp.einsum("qcsk,qckv->qcsv", in_recv, well_pack, preferred_element_type=jnp.float32)
+    partial_in = lax.all_to_all(partial, "dom", split_axis=0, concat_axis=0, tiled=True)
+    partial_in = partial_in.reshape(slot_total, seg, vec_count)
+    summed = jnp.sum(partial_in[well_slot.reshape(-1)].reshape(wells, couplings, seg, vec_count), axis=1)
     well_state = well_states_of(summed, well_inverse, well_count)
-    slot_well = slot_order // couplings
     state_slots = well_state[slot_well]
     out_slots = couple_out.reshape(wells * couplings, seg, cell_count)[slot_order]
     state_pack = jnp.concatenate([state_slots, out_slots], 2)

time: 273 us -> 214 us (0.78); the launches traced: 269 us -> 213 us
  waiting for transfers between devices: 103 us -> 68.4 us
  starting transfers between devices: 64.6 us -> 42.3 us
  other arithmetic: 25.4 us -> 19.6 us
  local copies, waits for them, and re-layouts: 44.3 us -> 49.7 us
    all_to_all x1, starting transfers between devices: 51.3 us -> 6.9 us  [on_device(): lax.all_to_all(state_pack, 'dom', split_axis=0, concat_axis=0, tiled=True)]
    all_to_all x1, waiting for transfers between devices: 99.6 us -> 57.7 us  [on_device(): lax.all_to_all(send_pack, 'dom', split_axis=0, concat_axis=0, tiled=True)]
    all_to_all x0 -> x1, starting transfers between devices: none -> 22.3 us  [on_device(): lax.all_to_all(partial, 'dom', split_axis=0, concat_axis=0, tiled=True)]
    all_to_all x0 -> x1, waiting for transfers between devices: none -> 10.7 us  [on_device(): lax.all_to_all(partial, 'dom', split_axis=0, concat_axis=0, tiled=True)]
    slice x0 -> x2, local copies, waits for them, and re-layouts: none -> 5.67 us  [the longest x1 4.59 us: on_device(): recv_pack[:, :halo_width * cell_count]]
    select_n x1, other arithmetic: 5.76 us -> 2.53 us  [on_device(): jnp.where(live_halo[:, :, None, None], halo_rows, jnp.zeros_like(halo_rows))]
  transfers between devices with their start and end apart: 4 -> 5, of which waited for: 3 -> 2; matrix products, arithmetic and copies ran while one was open for 11% -> 23% of each run, Pallas kernels for 0% -> 0%
where the time goes in v2:
time: 214 us; the launch traced here: 213 us
  waiting for transfers between devices  68.4 us (32%)
  local copies, waits for them, and re-layouts  49.7 us (23%)
  starting transfers between devices  42.3 us (20%)
  matrix products  32.2 us (15%)
  other arithmetic  19.6 us (9%)
    all_to_all x1, waiting for transfers between devices, on_device(): lax.all_to_all(send_pack, 'dom', split_axis=0, concat_axis=0, tiled=True)  57.7 us
    all_to_all x1, starting transfers between devices, on_device(): lax.all_to_all(partial, 'dom', split_axis=0, concat_axis=0, tiled=True)  22.3 us
    dot_general x1, matrix products, local_product(): jnp.einsum('btij,btjv->biv', tile_values, gathered, preferred_element_typ...  19.7 us
    gather x1, local copies, waits for them, and re-layouts, local_product(): gathered = extended[tile_cols]  19.1 us
    all_to_all x1, waiting for transfers between devices, on_device(): lax.all_to_all(partial, 'dom', split_axis=0, concat_axis=0, tiled=True)  10.7 us
    all_to_all x1, starting transfers between devices, on_device(): lax.all_to_all(send_pack, 'dom', split_axis=0, concat_axis=0, tiled=True)  7.61 us
    all_to_all x1, starting transfers between devices, on_device(): lax.all_to_all(state_pack, 'dom', split_axis=0, concat_axis=0, tiled=True)  6.9 us
    dot_general x1, local copies, waits for them, and re-layouts, subtract_incoming(): jnp.einsum('bq,qkv->bkv', selector, flat_rows, preferred_element_type=jnp...  5.37 us
  transfers between devices with their start and end apart: 5, of which 2 were waited for; matrix products, arithmetic and copies ran while one was open for 23% of the time, Pallas kernels for 0%

profile of v2, /device:TPU:66, one launch (start us, length us, event | category | flops | bytes accessed | tf_op | source)
XLA Modules:
  0.0 213.0 jit_solution(6813289489803861685)
XLA Ops:
  0.0 0.8 compare_select_fusion.2
  1.0 0.8 copy.21
  1.9 2.0 sort.17
  4.0 0.7 gather_fusion.1
  4.8 2.8 %gather_fusion = bf16[64,128,256]{2,1,0:T(8,128)(2,1)} fusion(bf16[32,128,256]{2,1,0:T(8,128)(2,1)S(1)} %copy-done.2, s32[1024]{0:T(1024)S(1)} %pad_clamp_fusion.6), kind=kCustom, calls=%fused_computation | custom fusion | bytes 8388864 | tf_op jit(solution)/shard_map/gather | solution.py:64
  7.6 4.8 %pad_maximum_fusion.1 = bf16[16,576,256]{2,1,0:T(8,128)(2,1)} fusion(bf16[16,64,256]{2,1,0:T(8,128)(2,1)S(1)} %reshape.181, bf16[16,512,256]{2,1,0:T(8,128)(2,1)} %bitcast.46), kind=kLoop, calls=%fused_computation.10 | loop fusion | flops 9437184 | bytes 9437184 | tf_op jit(solution)/shard_map/concatenate | solution.py:73
  12.3 7.6 %all-to-all-start = ((bf16[16,576,256]{2,1,0:T(8,128)(2,1)}), bf16[16,576,256]{2,1,0:T(8,128)(2,1)}, u32[]{:S(2)}, u32[]{:S(2)}) async-start(bf16[16,576,256]{2,1,0:T(8,128)(2,1)} %pad_maximum_fusion.1), calls=%async_computation | async-start | bytes 9437184 | tf_op jit(solution)/shard_map/all_to_all | solution.py:74
  20.2 2.9 %gather_fusion.4 = bf16[64,128,256]{2,1,0:T(8,128)(2,1)} fusion(bf16[32,128,256]{2,1,0:T(8,128)(2,1)S(1)} %copy-done.2, s32[1024]{0:T(1024)S(1)} %pad_clamp_fusion.2), kind=kCustom, calls=%fused_computation.4 | custom fusion | bytes 8388864 | tf_op jit(solution)/shard_map/gather | solution.py:77
  23.0 57.7 %all-to-all-done = bf16[16,576,256]{2,1,0:T(8,128)(2,1)} async-done(((bf16[16,576,256]{2,1,0:T(8,128)(2,1)}), bf16[16,576,256]{2,1,0:T(8,128)(2,1)}, u32[]{:S(2)}, u32[]{:S(2)}) %all-to-all-start) | async-done | bytes 4718624 | tf_op jit(solution)/shard_map/all_to_all | solution.py:74
  80.7 1.1 slice.43
  82.0 4.2 %fusion.13 = f32[16,4,32,256]{3,2,1,0:T(8,128)} fusion(bf16[16,4,32,128]{3,2,1,0:T(8,128)(2,1)S(1)} %reshape.183, bf16[16,4,128,256]{3,2,1,0:T(8,128)(2,1)} %bitcast.48), kind=kOutput, calls=%fused_computation.49 | convolution fusion | flops 134217728 | bytes 6815744 | tf_op jit(solution)/shard_map/qcsk,qckv->qcsv/dot_general | solution.py:78
  86.2 22.3 %all-to-all-start.1 = ((f32[16,4,32,256]{3,2,1,0:T(8,128)}), f32[16,4,32,256]{3,2,1,0:T(8,128)}, u32[]{:S(2)}, u32[]{:S(2)}) async-start(f32[16,4,32,256]{3,2,1,0:T(8,128)} %fusion.13), calls=%async_computation.1 | async-start | bytes 4194304 | tf_op jit(solution)/shard_map/all_to_all | solution.py:79
  109.2 0.7 fusion.12
  109.9 1.9 collective-permute-start
  111.9 3.6 %collective-permute-start.1 = (bf16[4,128,256]{2,1,0:T(8,128)(2,1)S(1)}, bf16[4,128,256]{2,1,0:T(8,128)(2,1)}, u32[]{:S(2)}, u32[]{:S(2)}) collective-permute-start(bf16[4,128,256]{2,1,0:T(8,128)(2,1)S(1)} %get-tuple-element.8), channel_id=1, source_target_pairs={{1,0},{2,1},{3,2},{4,3},{5,4},{6,5},{7,6},{9,8},{10,9},{11,10},{12... | collective-permute-start | bytes 786440 | tf_op jit(solution)/shard_map/ppermute | solution.py:15
  116.8 1.7 gather_fusion.7
  118.5 4.6 %slice.40 = bf16[16,512,256]{2,1,0:T(8,128)(2,1)} slice(bf16[16,576,256]{2,1,0:T(8,128)(2,1)} %all-to-all-done), slice={[0:16], [0:512], [0:256]} | slice | bytes 8388608 | tf_op jit(solution)/shard_map/slice | solution.py:75
  123.1 10.7 %all-to-all-done.1 = f32[16,4,32,256]{3,2,1,0:T(8,128)} async-done(((f32[16,4,32,256]{3,2,1,0:T(8,128)}), f32[16,4,32,256]{3,2,1,0:T(8,128)}, u32[]{:S(2)}, u32[]{:S(2)}) %all-to-all-start.1) | async-done | bytes 2097184 | tf_op jit(solution)/shard_map/all_to_all | solution.py:79
  133.8 3.6 %gather_fusion.5 = f32[64,32,256]{2,1,0:T(8,128)} fusion(f32[64,32,256]{2,1,0:T(8,128)} %bitcast.13, s32[1024]{0:T(1024)S(1)} %pad_clamp_fusion.1), kind=kCustom, calls=%fused_computation.5 | custom fusion | bytes 4194560 | tf_op jit(solution)/shard_map/gather | solution.py:81
  137.4 1.8 bitcast_reduce_fusion
  139.3 0.6 fusion.3
  139.9 1.6 gather_fusion.6
  141.5 2.5 %pad_maximum_fusion.2 = bf16[64,32,384]{2,1,0:T(8,128)(2,1)} fusion(bf16[64,32,128]{2,1,0:T(8,128)(2,1)S(1)} %gather_fusion.7, bf16[64,32,256]{2,1,0:T(8,128)(2,1)} %gather_fusion.6), kind=kLoop, calls=%fused_computation.16 | loop fusion | flops 3145728 | bytes 3145728 | tf_op jit(solution)/shard_map/concatenate | solution.py:85
  144.0 6.9 %all-to-all-start.2 = ((bf16[16,4,32,384]{3,2,1,0:T(8,128)(2,1)}), bf16[16,4,32,384]{3,2,1,0:T(8,128)(2,1)}, u32[]{:S(2)}, u32[]{:S(2)}) async-start(bf16[16,4,32,384]{3,2,1,0:T(8,128)(2,1)} %bitcast.49), calls=%async_computation.2 | async-start | bytes 3145728 | tf_op jit(solution)/shard_map/all_to_all | solution.py:87
  150.9 2.5 %broadcast_select_fusion = bf16[64,128,256]{2,1,0:T(8,128)(2,1)S(1)} fusion(bf16[64,128,256]{2,1,0:T(8,128)(2,1)} %bitcast.47, pred[64]{0:T(512)(128)(4,1)S(1)} %lt.89), kind=kLoop, calls=%fused_computation.14 | loop fusion | flops 2097152 | bytes 8388672 | tf_op jit(solution)/shard_map/jit(_where)/select_n | solution.py:96
  153.4 4.9 %pad_maximum_fusion = bf16[104,128,256]{2,1,0:T(8,128)(2,1)} fusion(bf16[4,128,256]{2,1,0:T(8,128)(2,1)} %collective-permute-done.1, bf16[4,128,256]{2,1,0:T(8,128)(2,1)} %collective-permute-done, bf16[64,128,256]{2,1,0:T(8,128)(2,1)S(1)} %broadcast_select_fusion, bf16[32,128,256]{2,1,0:T(8,128)(2,1)S(1)} %copy-done.2), kind=kLoop, calls=%fused_computation.9 | loop fusion | flops 10223616 | bytes 13631488 | tf_op jit(solution)/shard_map/concatenate | solution.py:97
  158.3 19.1 %gather_fusion.3 = bf16[512,128,256]{2,1,0:T(8,128)(2,1)} fusion(bf16[104,128,256]{2,1,0:T(8,128)(2,1)} %pad_maximum_fusion, s32[1024]{0:T(1024)S(1)} %pad_clamp_fusion.3), kind=kCustom, calls=%fused_computation.3 | custom fusion | bytes 67110912 | tf_op jit(solution)/shard_map/gather | solution.py:21
  177.4 2.7 %fusion.4 = bf16[64,128,256]{2,1,0:T(8,128)(2,1)S(1)} fusion(bf16[64,32,384]{2,1,0:T(8,128)(2,1)} %bitcast.20), kind=kOutput, calls=%fused_computation.20 | convolution fusion | flops 134217728 | bytes 5767168 | tf_op jit(solution)/shard_map/qsk,qsv->qkv/dot_general | solution.py:89
  180.1 5.0 %fusion = f32[32,128,256]{2,0,1:T(8,128)} fusion(bf16[64,128,256]{2,1,0:T(8,128)(2,1)S(1)} %fusion.4, s32[64]{0:T(128)S(1)} %eq.15), kind=kOutput, calls=%fused_computation.11 | convolution fusion | flops 134219776 | bytes 8388864 | tf_op jit(solution)/shard_map/bq,qkv->bkv/dot_general | solution.py:36
  185.1 5.4 %copy.27 = f32[32,128,256]{1,2,0:T(8,128)} copy(f32[32,128,256]{2,0,1:T(8,128)} %fusion) | data formatting | bytes 8388608 | tf_op jit(solution)/shard_map/bq,qkv->bkv/dot_general | solution.py:36
  190.5 19.7 %fusion.1 = bf16[32,128,256]{1,2,0:T(8,128)(2,1)S(1)} fusion(f32[32,128,256]{1,2,0:T(8,128)} %copy.27, bf16[32,16,128,256]{3,2,1,0:T(8,128)(2,1)} %bitcast.45, bf16[32,16,128,128]{3,2,1,0:T(8,128)(2,1)} %param.13), kind=kOutput, calls=%fused_computation.13 | convolution fusion | flops 4297064448 | bytes 56623104 | tf_op jit(solution)/shard_map/btij,btjv->biv/dot_general | solution.py:22
  210.1 2.9 %copy.28 = bf16[32,128,256]{2,1,0:T(8,128)(2,1)} copy(bf16[32,128,256]{1,2,0:T(8,128)(2,1)S(1)} %fusion.1) | data formatting | bytes 4194304 | tf_op jit(solution)/shard_map/convert_element_type | solution.py:101
  (48 shorter events, 2.1 us)
Async XLA Ops:
  0.0 4.0 %copy-start = (bf16[16,4,32,128]{3,2,1,0:T(8,128)(2,1)S(1)}, bf16[16,4,32,128]{3,2,1,0:T(8,128)(2,1)}, u32[]{:S(2)}) copy-start(bf16[16,4,32,128]{3,2,1,0:T(8,128)(2,1)} %param.21) | copy-start | bytes 1572868
  0.0 4.8 %copy-start.2 = (bf16[32,128,256]{2,1,0:T(8,128)(2,1)S(1)}, bf16[32,128,256]{2,1,0:T(8,128)(2,1)}, u32[]{:S(2)}) copy-start(bf16[32,128,256]{2,1,0:T(8,128)(2,1)} %param.12) | copy-start | bytes 6291460
  12.3 7.6 %copy-start.4 = (s32[1,16,4]{1,2,0:T(4,128)S(1)}, s32[1,16,4]{1,2,0:T(4,128)}, u32[]{:S(2)}) copy-start(s32[1,16,4]{1,2,0:T(4,128)} %param.18) | copy-start | bytes 772
  12.3 68.4 %all-to-all-start = ((bf16[16,576,256]{2,1,0:T(8,128)(2,1)}), bf16[16,576,256]{2,1,0:T(8,128)(2,1)}, u32[]{:S(2)}, u32[]{:S(2)}) async-start(bf16[16,576,256]{2,1,0:T(8,128)(2,1)} %pad_maximum_fusion.1), calls=%async_computation | async-start | bytes 9437184 | tf_op jit(solution)/shard_map/all_to_all | solution.py:74
  82.0 26.5 %copy-start.7 = (s32[1,2,4]{2,1,0:T(2,128)S(1)}, s32[1,2,4]{2,1,0:T(2,128)}, u32[]{:S(2)}) copy-start(s32[1,2,4]{2,1,0:T(2,128)} %param.17) | copy-start | bytes 100
  86.2 30.1 %copy-start.6 = (s32[1,16]{1,0:T(1,128)S(1)}, s32[1,16]{1,0:T(1,128)}, u32[]{:S(2)}) copy-start(s32[1,16]{1,0:T(1,128)} %param.16) | copy-start | bytes 196
  86.2 30.3 %copy-start.5 = (s32[32,16]{0,1:T(8,128)S(1)}, s32[32,16]{0,1:T(8,128)}, u32[]{:S(2)}) copy-start(s32[32,16]{0,1:T(8,128)} %param.14) | copy-start | bytes 6148
  86.2 47.6 %all-to-all-start.1 = ((f32[16,4,32,256]{3,2,1,0:T(8,128)}), f32[16,4,32,256]{3,2,1,0:T(8,128)}, u32[]{:S(2)}, u32[]{:S(2)}) async-start(f32[16,4,32,256]{3,2,1,0:T(8,128)} %fusion.13), calls=%async_computation.1 | async-start | bytes 4194304 | tf_op jit(solution)/shard_map/all_to_all | solution.py:79
  109.9 43.5 %collective-permute-start = (bf16[4,128,256]{2,1,0:T(8,128)(2,1)}, bf16[4,128,256]{2,1,0:T(8,128)(2,1)}, u32[]{:S(2)}, u32[]{:S(2)}) collective-permute-start(bf16[4,128,256]{2,1,0:T(8,128)(2,1)} %get-tuple-element.7), channel_id=1, source_target_pairs={{0,1},{1,2},{2,3},{3,4},{4,5},{5,6},{6,7},{8,9},{9,10},{10,11},{11... | collective-permute-start | bytes 786440 | tf_op jit(solution)/shard_map/ppermute | solution.py:14
  111.9 41.6 %collective-permute-start.1 = (bf16[4,128,256]{2,1,0:T(8,128)(2,1)S(1)}, bf16[4,128,256]{2,1,0:T(8,128)(2,1)}, u32[]{:S(2)}, u32[]{:S(2)}) collective-permute-start(bf16[4,128,256]{2,1,0:T(8,128)(2,1)S(1)} %get-tuple-element.8), channel_id=1, source_target_pairs={{1,0},{2,1},{3,2},{4,3},{5,4},{6,5},{7,6},{9,8},{10,9},{11,10},{12... | collective-permute-start | bytes 786440 | tf_op jit(solution)/shard_map/ppermute | solution.py:15
  123.1 16.1 %copy-start.3 = (f32[16,32,32]{2,1,0:T(8,128)S(1)}, f32[16,32,32]{2,1,0:T(8,128)}, u32[]{:S(2)}) copy-start(f32[16,32,32]{2,1,0:T(8,128)} %param.23) | copy-start | bytes 196612
  144.0 33.4 %all-to-all-start.2 = ((bf16[16,4,32,384]{3,2,1,0:T(8,128)(2,1)}), bf16[16,4,32,384]{3,2,1,0:T(8,128)(2,1)}, u32[]{:S(2)}, u32[]{:S(2)}) async-start(bf16[16,4,32,384]{3,2,1,0:T(8,128)(2,1)} %bitcast.49), calls=%async_computation.2 | async-start | bytes 3145728 | tf_op jit(solution)/shard_map/all_to_all | solution.py:87
  190.5 22.6 %copy-start.1 = (bf16[16,4,32,128]{3,2,1,0:T(8,128)(2,1)S(1)}, bf16[16,4,32,128]{3,2,1,0:T(8,128)(2,1)}, u32[]{:S(2)}) copy-start(bf16[16,4,32,128]{3,2,1,0:T(8,128)(2,1)} %param.21) | copy-start | bytes 1572868

commit v3 on v2

--- a/solution.py
+++ b/solution.py
@@ -2,6 +2,8 @@
 import jax.numpy as jnp
 from jax import lax
 from jax.sharding import PartitionSpec as P
+from jax.experimental import pallas as pl
+from jax.experimental.pallas import tpu as pltpu
 
 
 def padded(value, sides, width):
@@ -17,9 +19,38 @@
     return value
 
 
+def product_kernel(cols_ref, ext_ref, tiles_ref, out_ref):
+    rows, tiles_per_row = tiles_ref.shape[0], tiles_ref.shape[1]
+    first = pl.program_id(0) * rows
+    for r in range(rows):
+        acc = jnp.zeros(out_ref.shape[1:], jnp.float32)
+        for t in range(tiles_per_row):
+            col = cols_ref[(first + r) * tiles_per_row + t]
+            acc = acc + jnp.dot(tiles_ref[r, t], ext_ref[col], preferred_element_type=jnp.float32)
+        out_ref[r] = acc
+
+
 def local_product(extended, tile_values, tile_cols):
-    gathered = extended[tile_cols]
-    return jnp.einsum("btij,btjv->biv", tile_values, gathered, preferred_element_type=jnp.float32)
+    block_rows, tiles_per_row, cells, _ = tile_values.shape
+    ext_blocks, _, vecs = extended.shape
+    rows = 4
+    grid_spec = pltpu.PrefetchScalarGridSpec(
+        num_scalar_prefetch=1,
+        grid=(block_rows // rows,),
+        in_specs=[
+            pl.BlockSpec((ext_blocks, cells, vecs), lambda k, cols: (0, 0, 0)),
+            pl.BlockSpec((rows, tiles_per_row, cells, cells), lambda k, cols: (k, 0, 0, 0)),
+        ],
+        out_specs=pl.BlockSpec((rows, cells, vecs), lambda k, cols: (k, 0, 0)),
+    )
+    flops = 2 * block_rows * tiles_per_row * cells * cells * vecs
+    moved = tile_values.size * 2 + extended.size * 2 + block_rows * cells * vecs * 4
+    return pl.pallas_call(
+        product_kernel,
+        out_shape=jax.ShapeDtypeStruct((block_rows, cells, vecs), jnp.float32),
+        grid_spec=grid_spec,
+        cost_estimate=pl.CostEstimate(flops=flops, transcendentals=0, bytes_accessed=moved),
+    )(tile_cols.reshape(-1), extended, tile_values)
 
 
 def well_states_of(summed, well_inverse, well_count):

time: 214 us -> 185 us (0.86)
  local copies, waits for them, and re-layouts: 49.7 us -> 20.9 us
  matrix products: 32.2 us -> 10.5 us
  Pallas kernels: 0 us -> 17 us
  other arithmetic: 19.6 us -> 24.3 us
    dot_general x1 -> x0, matrix products: 19.7 us -> none  [local_product(): jnp.einsum('btij,btjv->biv', tile_values, gathered, preferred_element_typ...]
    gather x1 -> x0, local copies, waits for them, and re-layouts: 19.1 us -> none  [local_product(): gathered = extended[tile_cols]]
    pallas_call x0 -> x1, Pallas kernels: none -> 17 us  [local_product(): pl.pallas_call(product_kernel, out_shape=jax.ShapeDtypeStruct((block_rows...]
    dot_general x1 -> x0, local copies, waits for them, and re-layouts: 5.37 us -> none  [subtract_incoming(): jnp.einsum('bq,qkv->bkv', selector, flat_rows, preferred_element_type=jnp...]
    convert_element_type x0 -> x1, other arithmetic: none -> 3.65 us  [on_device(): return subtract_incoming(product, well_send, incoming).astype(jnp.bfloat16)]
    convert_element_type x1 -> x0, local copies, waits for them, and re-layouts: 2.89 us -> none  [on_device(): return subtract_incoming(product, well_send, incoming).astype(jnp.bfloat16)]
  transfers between devices with their start and end apart: 5 -> 5, of which waited for: 2 -> 2; matrix products, arithmetic and copies ran while one was open for 23% -> 16% of each run, Pallas kernels for 0% -> 9%
where the time goes in v3:
time: 185 us; the launch traced here: 183 us
  waiting for transfers between devices  67.3 us (36%)
  starting transfers between devices  42.5 us (23%)
  other arithmetic  24.3 us (13%)
  local copies, waits for them, and re-layouts  20.9 us (11%)
  Pallas kernels  17 us (9%)
  matrix products  10.5 us (6%)
    all_to_all x1, waiting for transfers between devices, on_device(): lax.all_to_all(send_pack, 'dom', split_axis=0, concat_axis=0, tiled=True)  57.7 us
    all_to_all x1, starting transfers between devices, on_device(): lax.all_to_all(partial, 'dom', split_axis=0, concat_axis=0, tiled=True)  22.3 us
    pallas_call x1, Pallas kernels, local_product(): pl.pallas_call(product_kernel, out_shape=jax.ShapeDtypeStruct((block_rows...  17 us
    all_to_all x1, waiting for transfers between devices, on_device(): lax.all_to_all(partial, 'dom', split_axis=0, concat_axis=0, tiled=True)  9.63 us
    all_to_all x1, starting transfers between devices, on_device(): lax.all_to_all(send_pack, 'dom', split_axis=0, concat_axis=0, tiled=True)  7.61 us
    all_to_all x1, starting transfers between devices, on_device(): lax.all_to_all(state_pack, 'dom', split_axis=0, concat_axis=0, tiled=True)  7.07 us
    concatenate x1, other arithmetic, on_device(): jnp.concatenate([blocks, halo_rows.reshape(dom_count * halo_width, cell_c...  6.1 us
    concatenate x1, other arithmetic, on_device(): send_pack = jnp.concatenate([halo_flat, in_slots], 1)  4.78 us
  transfers between devices with their start and end apart: 5, of which 2 were waited for; matrix products, arithmetic and copies ran while one was open for 16% of the time, Pallas kernels for 9%

profile of v3, /device:TPU:66, one launch (start us, length us, event | category | flops | bytes accessed | tf_op | source)
XLA Modules:
  0.0 183.4 jit_solution(10585007503325113643)
XLA Ops:
  0.0 0.8 compare_select_fusion.1
  1.0 0.8 copy.21
  1.9 2.0 %sort.17 = (s32[64]{0:T(128)}, s32[64]{0:T(128)S(1)}) sort(s32[64]{0:T(128)S(1)} %reshape.184, s32[64]{0:T(128)S(1)} %iota.21), dimensions={0}, to_apply=%region_0.0 | sort | flops 384 | bytes 1024 | tf_op jit(solution)/shard_map/jit(argsort)/sort | solution.py:99
  4.0 0.7 gather_fusion.1
  4.8 2.8 %gather_fusion = bf16[64,128,256]{2,1,0:T(8,128)(2,1)} fusion(bf16[32,128,256]{2,1,0:T(8,128)(2,1)S(1)} %copy-done.2, s32[1024]{0:T(1024)S(1)} %pad_clamp_fusion.5), kind=kCustom, calls=%fused_computation | custom fusion | bytes 8388864 | tf_op jit(solution)/shard_map/gather | solution.py:95
  7.6 4.8 %pad_maximum_fusion.1 = bf16[16,576,256]{2,1,0:T(8,128)(2,1)} fusion(bf16[16,64,256]{2,1,0:T(8,128)(2,1)S(1)} %reshape.185, bf16[16,512,256]{2,1,0:T(8,128)(2,1)} %bitcast.35), kind=kLoop, calls=%fused_computation.9 | loop fusion | flops 9437184 | bytes 9437184 | tf_op jit(solution)/shard_map/concatenate | solution.py:104
  12.4 7.6 %all-to-all-start = ((bf16[16,576,256]{2,1,0:T(8,128)(2,1)}), bf16[16,576,256]{2,1,0:T(8,128)(2,1)}, u32[]{:S(2)}, u32[]{:S(2)}) async-start(bf16[16,576,256]{2,1,0:T(8,128)(2,1)} %pad_maximum_fusion.1), calls=%async_computation | async-start | bytes 9437184 | tf_op jit(solution)/shard_map/all_to_all | solution.py:105
  20.2 2.9 %gather_fusion.3 = bf16[64,128,256]{2,1,0:T(8,128)(2,1)} fusion(bf16[32,128,256]{2,1,0:T(8,128)(2,1)S(1)} %copy-done.2, s32[1024]{0:T(1024)S(1)} %pad_clamp_fusion.2), kind=kCustom, calls=%fused_computation.3 | custom fusion | bytes 8388864 | tf_op jit(solution)/shard_map/gather | solution.py:108
  23.1 57.7 %all-to-all-done = bf16[16,576,256]{2,1,0:T(8,128)(2,1)} async-done(((bf16[16,576,256]{2,1,0:T(8,128)(2,1)}), bf16[16,576,256]{2,1,0:T(8,128)(2,1)}, u32[]{:S(2)}, u32[]{:S(2)}) %all-to-all-start) | async-done | bytes 4718624 | tf_op jit(solution)/shard_map/all_to_all | solution.py:105
  80.7 1.1 slice.41
  82.0 4.2 %fusion.13 = f32[16,4,32,256]{3,2,1,0:T(8,128)} fusion(bf16[16,4,32,128]{3,2,1,0:T(8,128)(2,1)S(1)} %reshape.187, bf16[16,4,128,256]{3,2,1,0:T(8,128)(2,1)} %bitcast.36), kind=kOutput, calls=%fused_computation.46 | convolution fusion | flops 134217728 | bytes 6815744 | tf_op jit(solution)/shard_map/qcsk,qckv->qcsv/dot_general | solution.py:109
  86.2 22.3 %all-to-all-start.1 = ((f32[16,4,32,256]{3,2,1,0:T(8,128)}), f32[16,4,32,256]{3,2,1,0:T(8,128)}, u32[]{:S(2)}, u32[]{:S(2)}) async-start(f32[16,4,32,256]{3,2,1,0:T(8,128)} %fusion.13), calls=%async_computation.1 | async-start | bytes 4194304 | tf_op jit(solution)/shard_map/all_to_all | solution.py:110
  108.6 0.6 gather_fusion.2
  109.2 0.8 fusion.12
  110.0 1.9 %collective-permute-start = (bf16[4,128,256]{2,1,0:T(8,128)(2,1)}, bf16[4,128,256]{2,1,0:T(8,128)(2,1)}, u32[]{:S(2)}, u32[]{:S(2)}) collective-permute-start(bf16[4,128,256]{2,1,0:T(8,128)(2,1)} %get-tuple-element.7), channel_id=1, source_target_pairs={{0,1},{1,2},{2,3},{3,4},{4,5},{5,6},{6,7},{8,9},{9,10},{10,11},{11... | collective-permute-start | bytes 786440 | tf_op jit(solution)/shard_map/ppermute | solution.py:16
  111.9 3.6 %collective-permute-start.1 = (bf16[4,128,256]{2,1,0:T(8,128)(2,1)S(1)}, bf16[4,128,256]{2,1,0:T(8,128)(2,1)}, u32[]{:S(2)}, u32[]{:S(2)}) collective-permute-start(bf16[4,128,256]{2,1,0:T(8,128)(2,1)S(1)} %get-tuple-element.8), channel_id=1, source_target_pairs={{1,0},{2,1},{3,2},{4,3},{5,4},{6,5},{7,6},{9,8},{10,9},{11,10},{12... | collective-permute-start | bytes 786440 | tf_op jit(solution)/shard_map/ppermute | solution.py:17
  116.7 0.6 reshape.181.cols_ref
  117.3 1.7 gather_fusion.6
  119.1 2.6 %slice.38 = bf16[16,512,256]{2,1,0:T(8,128)(2,1)S(1)} slice(bf16[16,576,256]{2,1,0:T(8,128)(2,1)} %all-to-all-done), slice={[0:16], [0:512], [0:256]} | slice | bytes 8388608 | tf_op jit(solution)/shard_map/slice | solution.py:106
  121.6 2.4 %broadcast_select_fusion = bf16[64,128,256]{2,1,0:T(8,128)(2,1)} fusion(bf16[64,128,256]{2,1,0:T(8,128)(2,1)S(1)} %bitcast.37, pred[64]{0:T(512)(128)(4,1)S(1)} %lt.83), kind=kLoop, calls=%fused_computation.13 | loop fusion | flops 2097152 | bytes 8388672 | tf_op jit(solution)/shard_map/jit(_where)/select_n | solution.py:127
  124.1 9.6 %all-to-all-done.1 = f32[16,4,32,256]{3,2,1,0:T(8,128)} async-done(((f32[16,4,32,256]{3,2,1,0:T(8,128)}), f32[16,4,32,256]{3,2,1,0:T(8,128)}, u32[]{:S(2)}, u32[]{:S(2)}) %all-to-all-start.1) | async-done | bytes 2097184 | tf_op jit(solution)/shard_map/all_to_all | solution.py:110
  133.7 3.6 %gather_fusion.4 = f32[64,32,256]{2,1,0:T(8,128)} fusion(f32[64,32,256]{2,1,0:T(8,128)} %bitcast.9, s32[1024]{0:T(1024)S(1)} %pad_clamp_fusion.1), kind=kCustom, calls=%fused_computation.4 | custom fusion | bytes 4194560 | tf_op jit(solution)/shard_map/gather | solution.py:112
  137.3 1.8 %bitcast_reduce_fusion = f32[16,32,256]{2,1,0:T(8,128)S(1)} fusion(f32[64,32,256]{2,1,0:T(8,128)} %gather_fusion.4), kind=kLoop, calls=%fused_computation.14 | loop fusion | flops 393216 | bytes 2621440 | tf_op jit(solution)/shard_map/reduce_sum | solution.py:112
  139.1 0.6 fusion.3
  139.7 1.6 gather_fusion.5
  141.3 2.5 %pad_maximum_fusion.2 = bf16[64,32,384]{2,1,0:T(8,128)(2,1)} fusion(bf16[64,32,128]{2,1,0:T(8,128)(2,1)S(1)} %gather_fusion.6, bf16[64,32,256]{2,1,0:T(8,128)(2,1)} %gather_fusion.5), kind=kLoop, calls=%fused_computation.15 | loop fusion | flops 3145728 | bytes 3145728 | tf_op jit(solution)/shard_map/concatenate | solution.py:116
  143.9 7.1 %all-to-all-start.2 = ((bf16[16,4,32,384]{3,2,1,0:T(8,128)(2,1)}), bf16[16,4,32,384]{3,2,1,0:T(8,128)(2,1)}, u32[]{:S(2)}, u32[]{:S(2)}) async-start(bf16[16,4,32,384]{3,2,1,0:T(8,128)(2,1)} %bitcast.38), calls=%async_computation.2 | async-start | bytes 3145728 | tf_op jit(solution)/shard_map/all_to_all | solution.py:118
  150.9 6.1 %pad_maximum_fusion.ext_ref = bf16[104,128,256]{2,1,0:T(8,128)(2,1)} fusion(bf16[4,128,256]{2,1,0:T(8,128)(2,1)} %collective-permute-done.1, bf16[4,128,256]{2,1,0:T(8,128)(2,1)} %collective-permute-done, bf16[64,128,256]{2,1,0:T(8,128)(2,1)} %broadcast_select_fusion, bf16[32,128,256]{2,1,0:T(8,128)(2,1)S(1)} %copy-done.2), kind=kLoop, calls=%fused_computation.8 | loop fusion | flops 10223616 | bytes 13631488 | tf_op jit(solution)/shard_map/concatenate | solution.py:128
  157.0 17.0 %shard_map.118 = f32[32,128,256]{2,1,0:T(8,128)} custom-call(s32[512]{0:T(512)} %reshape.181.cols_ref, bf16[104,128,256]{2,1,0:T(8,128)(2,1)} %pad_maximum_fusion.ext_ref, bf16[32,16,128,128]{3,2,1,0:T(8,128)(2,1)} %tiles_ref.1), custom_call_target="tpu_custom_call" | custom-call | flops 4294967296 | bytes 27787264 | tf_op jit(solution)/shard_map/pallas_call | solution.py:48
  174.0 2.7 %fusion.4 = bf16[64,128,256]{2,1,0:T(8,128)(2,1)S(1)} fusion(bf16[64,32,384]{2,1,0:T(8,128)(2,1)} %bitcast.16), kind=kOutput, calls=%fused_computation.19 | convolution fusion | flops 134217728 | bytes 5767168 | tf_op jit(solution)/shard_map/qsk,qsv->qkv/dot_general | solution.py:120
  176.7 3.0 %fusion = f32[32,128,256]{2,0,1:T(8,128)S(1)} fusion(bf16[64,128,256]{2,1,0:T(8,128)(2,1)S(1)} %fusion.4, s32[64]{0:T(128)S(1)} %eq.15), kind=kOutput, calls=%fused_computation.10 | convolution fusion | flops 134219776 | bytes 8388864 | tf_op jit(solution)/shard_map/bq,qkv->bkv/dot_general | solution.py:67
  179.8 3.7 %fusion.1 = bf16[32,128,256]{2,1,0:T(8,128)(2,1)} fusion(f32[32,128,256]{2,1,0:T(8,128)S(1)} %copy-done.3, f32[32,128,256]{2,0,1:T(8,128)S(1)} %fusion), kind=kLoop, calls=%fused_computation.12 | loop fusion | flops 2097152 | bytes 10485760 | tf_op jit(solution)/shard_map/convert_element_type | solution.py:132
  (46 shorter events, 1.5 us)
Async XLA Ops:
  0.0 4.0 %copy-start = (bf16[16,4,32,128]{3,2,1,0:T(8,128)(2,1)S(1)}, bf16[16,4,32,128]{3,2,1,0:T(8,128)(2,1)}, u32[]{:S(2)}) copy-start(bf16[16,4,32,128]{3,2,1,0:T(8,128)(2,1)} %param.21) | copy-start | bytes 1572868
  0.0 4.8 %copy-start.2 = (bf16[32,128,256]{2,1,0:T(8,128)(2,1)S(1)}, bf16[32,128,256]{2,1,0:T(8,128)(2,1)}, u32[]{:S(2)}) copy-start(bf16[32,128,256]{2,1,0:T(8,128)(2,1)} %param.12) | copy-start | bytes 6291460
  12.4 7.6 %copy-start.6 = (s32[1,16,4]{1,2,0:T(4,128)S(1)}, s32[1,16,4]{1,2,0:T(4,128)}, u32[]{:S(2)}) copy-start(s32[1,16,4]{1,2,0:T(4,128)} %param.18) | copy-start | bytes 772
  12.4 68.4 %all-to-all-start = ((bf16[16,576,256]{2,1,0:T(8,128)(2,1)}), bf16[16,576,256]{2,1,0:T(8,128)(2,1)}, u32[]{:S(2)}, u32[]{:S(2)}) async-start(bf16[16,576,256]{2,1,0:T(8,128)(2,1)} %pad_maximum_fusion.1), calls=%async_computation | async-start | bytes 9437184 | tf_op jit(solution)/shard_map/all_to_all | solution.py:105
  82.0 26.5 %copy-start.8 = (s32[1,2,4]{2,1,0:T(2,128)S(1)}, s32[1,2,4]{2,1,0:T(2,128)}, u32[]{:S(2)}) copy-start(s32[1,2,4]{2,1,0:T(2,128)} %param.17) | copy-start | bytes 100
  86.2 30.2 %copy-start.7 = (s32[1,16]{1,0:T(1,128)S(1)}, s32[1,16]{1,0:T(1,128)}, u32[]{:S(2)}) copy-start(s32[1,16]{1,0:T(1,128)} %param.16) | copy-start | bytes 196
  86.2 30.4 %copy-start.5 = (s32[32,16]{0,1:T(8,128)S(1)}, s32[32,16]{0,1:T(8,128)}, u32[]{:S(2)}) copy-start(s32[32,16]{0,1:T(8,128)} %param.14) | copy-start | bytes 6148
  86.2 47.5 %all-to-all-start.1 = ((f32[16,4,32,256]{3,2,1,0:T(8,128)}), f32[16,4,32,256]{3,2,1,0:T(8,128)}, u32[]{:S(2)}, u32[]{:S(2)}) async-start(f32[16,4,32,256]{3,2,1,0:T(8,128)} %fusion.13), calls=%async_computation.1 | async-start | bytes 4194304 | tf_op jit(solution)/shard_map/all_to_all | solution.py:110
  110.0 41.0 %collective-permute-start = (bf16[4,128,256]{2,1,0:T(8,128)(2,1)}, bf16[4,128,256]{2,1,0:T(8,128)(2,1)}, u32[]{:S(2)}, u32[]{:S(2)}) collective-permute-start(bf16[4,128,256]{2,1,0:T(8,128)(2,1)} %get-tuple-element.7), channel_id=1, source_target_pairs={{0,1},{1,2},{2,3},{3,4},{4,5},{5,6},{6,7},{8,9},{9,10},{10,11},{11... | collective-permute-start | bytes 786440 | tf_op jit(solution)/shard_map/ppermute | solution.py:16
  111.9 39.1 %collective-permute-start.1 = (bf16[4,128,256]{2,1,0:T(8,128)(2,1)S(1)}, bf16[4,128,256]{2,1,0:T(8,128)(2,1)}, u32[]{:S(2)}, u32[]{:S(2)}) collective-permute-start(bf16[4,128,256]{2,1,0:T(8,128)(2,1)S(1)} %get-tuple-element.8), channel_id=1, source_target_pairs={{1,0},{2,1},{3,2},{4,3},{5,4},{6,5},{7,6},{9,8},{10,9},{11,10},{12... | collective-permute-start | bytes 786440 | tf_op jit(solution)/shard_map/ppermute | solution.py:17
  124.1 15.1 %copy-start.4 = (f32[16,32,32]{2,1,0:T(8,128)S(1)}, f32[16,32,32]{2,1,0:T(8,128)}, u32[]{:S(2)}) copy-start(f32[16,32,32]{2,1,0:T(8,128)} %param.23) | copy-start | bytes 196612
  143.9 30.2 %all-to-all-start.2 = ((bf16[16,4,32,384]{3,2,1,0:T(8,128)(2,1)}), bf16[16,4,32,384]{3,2,1,0:T(8,128)(2,1)}, u32[]{:S(2)}, u32[]{:S(2)}) async-start(bf16[16,4,32,384]{3,2,1,0:T(8,128)(2,1)} %bitcast.38), calls=%async_computation.2 | async-start | bytes 3145728 | tf_op jit(solution)/shard_map/all_to_all | solution.py:118
  176.7 3.0 %copy-start.3 = (f32[32,128,256]{2,1,0:T(8,128)S(1)}, f32[32,128,256]{2,1,0:T(8,128)}, u32[]{:S(2)}) copy-start(f32[32,128,256]{2,1,0:T(8,128)} %shard_map.118) | copy-start | bytes 12582916
  176.7 6.7 %copy-start.1 = (bf16[16,4,32,128]{3,2,1,0:T(8,128)(2,1)S(1)}, bf16[16,4,32,128]{3,2,1,0:T(8,128)(2,1)}, u32[]{:S(2)}) copy-start(bf16[16,4,32,128]{3,2,1,0:T(8,128)(2,1)} %param.21) | copy-start | bytes 1572868

commit v4 on v3

--- a/solution.py
+++ b/solution.py
@@ -51,6 +51,55 @@
         grid_spec=grid_spec,
         cost_estimate=pl.CostEstimate(flops=flops, transcendentals=0, bytes_accessed=moved),
     )(tile_cols.reshape(-1), extended, tile_values)
+
+
+def exchange_kernel(send_ref, recv_ref, send_sems, recv_sems, own_sem):
+    count = send_ref.shape[0]
+    me = lax.axis_index("dom")
+    grp = lax.axis_index("grp")
+    barrier = pltpu.get_barrier_semaphore()
+    for step in range(1, count):
+        peer = lax.rem(me + step, count)
+        pl.semaphore_signal(
+            barrier, inc=1, device_id=(peer, grp), device_id_type=pl.DeviceIdType.MESH
+        )
+    pl.semaphore_wait(barrier, count - 1)
+    own = pltpu.make_async_copy(send_ref.at[me], recv_ref.at[me], own_sem)
+    own.start()
+    copies = []
+    for step in range(1, count):
+        peer = lax.rem(me + step, count)
+        copy = pltpu.make_async_remote_copy(
+            src_ref=send_ref.at[peer],
+            dst_ref=recv_ref.at[me],
+            send_sem=send_sems.at[step],
+            recv_sem=recv_sems.at[step],
+            device_id=(peer, grp),
+            device_id_type=pl.DeviceIdType.MESH,
+        )
+        copy.start()
+        copies.append(copy)
+    for copy in copies:
+        copy.wait_send()
+    for copy in copies:
+        copy.wait_recv()
+    own.wait()
+
+
+def dom_exchange(value, collective):
+    count = value.shape[0]
+    return pl.pallas_call(
+        exchange_kernel,
+        out_shape=jax.ShapeDtypeStruct(value.shape, value.dtype),
+        in_specs=[pl.BlockSpec(memory_space=pl.ANY)],
+        out_specs=pl.BlockSpec(memory_space=pl.ANY),
+        scratch_shapes=[
+            pltpu.SemaphoreType.DMA((count,)),
+            pltpu.SemaphoreType.DMA((count,)),
+            pltpu.SemaphoreType.DMA,
+        ],
+        compiler_params=pltpu.CompilerParams(collective_id=collective, has_side_effects=True),
+    )(value)
 
 
 def well_states_of(summed, well_inverse, well_count):
@@ -102,7 +151,7 @@
     in_slots = in_slots.reshape(dom_count, slot_width * seg * cell_count // vec_count, vec_count)
     halo_flat = halo_pack.reshape(dom_count, halo_width * cell_count, vec_count)
     send_pack = jnp.concatenate([halo_flat, in_slots], 1)
-    recv_pack = lax.all_to_all(send_pack, "dom", split_axis=0, concat_axis=0, tiled=True)
+    recv_pack = dom_exchange(send_pack, 0)
     halo_rows = recv_pack[:, : halo_width * cell_count].reshape(dom_count, halo_width, cell_count, vec_count)
     in_recv = recv_pack[:, halo_width * cell_count :].reshape(dom_count, slot_width, seg, cell_count)
     well_pack = blocks[well_send[0]]

time: 185 us -> 212 us (1.15)
  Pallas kernels: 17 us -> 87 us
  waiting for transfers between devices: 67.3 us -> 7.65 us
  starting transfers between devices: 42.5 us -> 55.9 us
  other arithmetic: 24.3 us -> 27.1 us
    pallas_call x0 -> x1, Pallas kernels: none -> 70 us  [dom_exchange(): pl.pallas_call(exchange_kernel, out_shape=jax.ShapeDtypeStruct(value.shap...]
    all_to_all x1 -> x0, waiting for transfers between devices: 57.7 us -> none  [on_device(): lax.all_to_all(send_pack, 'dom', split_axis=0, concat_axis=0, tiled=True)]
    all_to_all x1, starting transfers between devices: 22.3 us -> 43.4 us  [on_device(): lax.all_to_all(partial, 'dom', split_axis=0, concat_axis=0, tiled=True)]
    all_to_all x1 -> x0, starting transfers between devices: 7.61 us -> none  [on_device(): lax.all_to_all(send_pack, 'dom', split_axis=0, concat_axis=0, tiled=True)]
    select_n x1, other arithmetic: 2.43 us -> 4.59 us  [on_device(): jnp.where(live_halo[:, :, None, None], halo_rows, jnp.zeros_like(halo_rows))]
  transfers between devices with their start and end apart: 5 -> 4, of which waited for: 2 -> 1; matrix products, arithmetic and copies ran while one was open for 16% -> 14% of each run, Pallas kernels for 9% -> 8%
where the time goes in v4:
time: 212 us; the launch traced here: 211 us
  Pallas kernels  87 us (41%)
  starting transfers between devices  55.9 us (26%)
  other arithmetic  27.1 us (13%)
  local copies, waits for them, and re-layouts  22 us (10%)
  matrix products  10.5 us (5%)
  waiting for transfers between devices  7.65 us (4%)
    pallas_call x1, Pallas kernels, dom_exchange(): pl.pallas_call(exchange_kernel, out_shape=jax.ShapeDtypeStruct(value.shap...  70 us
    all_to_all x1, starting transfers between devices, on_device(): lax.all_to_all(partial, 'dom', split_axis=0, concat_axis=0, tiled=True)  43.4 us
    pallas_call x1, Pallas kernels, local_product(): pl.pallas_call(product_kernel, out_shape=jax.ShapeDtypeStruct((block_rows...  17 us
    all_to_all x1, waiting for transfers between devices, on_device(): lax.all_to_all(partial, 'dom', split_axis=0, concat_axis=0, tiled=True)  7.64 us
    all_to_all x1, starting transfers between devices, on_device(): lax.all_to_all(state_pack, 'dom', split_axis=0, concat_axis=0, tiled=True)  6.92 us
    concatenate x1, other arithmetic, on_device(): jnp.concatenate([blocks, halo_rows.reshape(dom_count * halo_width, cell_c...  6.05 us
    concatenate x1, other arithmetic, on_device(): send_pack = jnp.concatenate([halo_flat, in_slots], 1)  4.75 us
    slice x1, local copies, waits for them, and re-layouts, on_device(): recv_pack[:, :halo_width * cell_count]  4.67 us
  transfers between devices with their start and end apart: 4, of which 1 were waited for; matrix products, arithmetic and copies ran while one was open for 14% of the time, Pallas kernels for 8%

profile of v4, /device:TPU:66, one launch (start us, length us, event | category | flops | bytes accessed | tf_op | source)
XLA Modules:
  0.0 211.0 jit_solution(14127434785529086067)
XLA Ops:
  0.0 0.8 compare_select_fusion.1
  0.8 0.7 compare_select_fusion
  1.9 0.8 copy.21
  2.8 2.0 sort.17
  4.8 0.7 gather_fusion.1
  5.7 2.8 %gather_fusion = bf16[64,128,256]{2,1,0:T(8,128)(2,1)} fusion(bf16[32,128,256]{2,1,0:T(8,128)(2,1)S(1)} %copy-done.2, s32[1024]{0:T(1024)S(1)} %pad_clamp_fusion.5), kind=kCustom, calls=%fused_computation | custom fusion | bytes 8388864 | tf_op jit(solution)/shard_map/gather | solution.py:144
  8.4 4.7 %pad_maximum_fusion.1.send_ref = bf16[16,576,256]{2,1,0:T(8,128)(2,1)} fusion(bf16[16,64,256]{2,1,0:T(8,128)(2,1)S(1)} %reshape.185, bf16[16,512,256]{2,1,0:T(8,128)(2,1)} %bitcast.35), kind=kLoop, calls=%fused_computation.9 | loop fusion | flops 9437184 | bytes 9437184 | tf_op jit(solution)/shard_map/concatenate | solution.py:153
  13.2 70.0 %shard_map.118 = bf16[16,576,256]{2,1,0:T(8,128)(2,1)} custom-call(bf16[16,576,256]{2,1,0:T(8,128)(2,1)} %pad_maximum_fusion.1.send_ref), custom_call_target="tpu_custom_call" | custom-call | tf_op jit(solution)/shard_map/pallas_call | solution.py:91
  83.2 1.1 slice.21
  84.5 2.9 %gather_fusion.3 = bf16[64,128,256]{2,1,0:T(8,128)(2,1)} fusion(bf16[32,128,256]{2,1,0:T(8,128)(2,1)S(1)} %copy-done.2, s32[1024]{0:T(1024)S(1)} %pad_clamp_fusion.2), kind=kCustom, calls=%fused_computation.3 | custom fusion | bytes 8388864 | tf_op jit(solution)/shard_map/gather | solution.py:157
  87.3 4.2 %fusion.13 = f32[16,4,32,256]{3,2,1,0:T(8,128)} fusion(bf16[16,4,32,128]{3,2,1,0:T(8,128)(2,1)S(1)} %reshape.187, bf16[16,4,128,256]{3,2,1,0:T(8,128)(2,1)} %bitcast.37), kind=kOutput, calls=%fused_computation.46 | convolution fusion | flops 134217728 | bytes 6815744 | tf_op jit(solution)/shard_map/qcsk,qckv->qcsv/dot_general | solution.py:158
  91.5 43.4 %all-to-all-start = ((f32[16,4,32,256]{3,2,1,0:T(8,128)}), f32[16,4,32,256]{3,2,1,0:T(8,128)}, u32[]{:S(2)}, u32[]{:S(2)}) async-start(f32[16,4,32,256]{3,2,1,0:T(8,128)} %fusion.13), calls=%async_computation | async-start | bytes 4194304 | tf_op jit(solution)/shard_map/all_to_all | solution.py:159
  135.1 0.6 gather_fusion.2
  135.7 0.7 fusion.12
  136.4 1.9 collective-permute-start
  138.3 3.6 %collective-permute-start.1 = (bf16[4,128,256]{2,1,0:T(8,128)(2,1)S(1)}, bf16[4,128,256]{2,1,0:T(8,128)(2,1)}, u32[]{:S(2)}, u32[]{:S(2)}) collective-permute-start(bf16[4,128,256]{2,1,0:T(8,128)(2,1)S(1)} %get-tuple-element.8), channel_id=1, source_target_pairs={{1,0},{2,1},{3,2},{4,3},{5,4},{6,5},{7,6},{9,8},{10,9},{11,10},{12... | collective-permute-start | bytes 786440 | tf_op jit(solution)/shard_map/ppermute | solution.py:17
  142.2 4.7 %slice.18 = bf16[16,512,256]{2,1,0:T(8,128)(2,1)} slice(bf16[16,576,256]{2,1,0:T(8,128)(2,1)} %shard_map.118), slice={[0:16], [0:512], [0:256]} | slice | bytes 8388608 | tf_op jit(solution)/shard_map/slice | solution.py:155
  147.9 0.7 reshape.181.cols_ref
  148.5 0.7 gather_fusion.6
  149.2 4.6 %broadcast_select_fusion = bf16[64,128,256]{2,1,0:T(8,128)(2,1)} fusion(bf16[64,128,256]{2,1,0:T(8,128)(2,1)} %bitcast.36, pred[64]{0:T(512)(128)(4,1)S(1)} %lt.83), kind=kLoop, calls=%fused_computation.13 | loop fusion | flops 2097152 | bytes 8388672 | tf_op jit(solution)/shard_map/jit(_where)/select_n | solution.py:176
  153.8 7.6 %all-to-all-done = f32[16,4,32,256]{3,2,1,0:T(8,128)} async-done(((f32[16,4,32,256]{3,2,1,0:T(8,128)}), f32[16,4,32,256]{3,2,1,0:T(8,128)}, u32[]{:S(2)}, u32[]{:S(2)}) %all-to-all-start) | async-done | bytes 2097184 | tf_op jit(solution)/shard_map/all_to_all | solution.py:159
  161.4 3.6 %gather_fusion.4 = f32[64,32,256]{2,1,0:T(8,128)} fusion(f32[64,32,256]{2,1,0:T(8,128)} %bitcast.9, s32[1024]{0:T(1024)S(1)} %pad_clamp_fusion.1), kind=kCustom, calls=%fused_computation.4 | custom fusion | bytes 4194560 | tf_op jit(solution)/shard_map/gather | solution.py:161
  165.0 1.8 bitcast_reduce_fusion
  166.9 0.6 fusion.3
  167.5 1.6 gather_fusion.5
  169.1 2.5 %pad_maximum_fusion.2 = bf16[64,32,384]{2,1,0:T(8,128)(2,1)} fusion(bf16[64,32,128]{2,1,0:T(8,128)(2,1)S(1)} %gather_fusion.6, bf16[64,32,256]{2,1,0:T(8,128)(2,1)} %gather_fusion.5), kind=kLoop, calls=%fused_computation.15 | loop fusion | flops 3145728 | bytes 3145728 | tf_op jit(solution)/shard_map/concatenate | solution.py:165
  171.6 6.9 %all-to-all-start.1 = ((bf16[16,4,32,384]{3,2,1,0:T(8,128)(2,1)}), bf16[16,4,32,384]{3,2,1,0:T(8,128)(2,1)}, u32[]{:S(2)}, u32[]{:S(2)}) async-start(bf16[16,4,32,384]{3,2,1,0:T(8,128)(2,1)} %bitcast.38), calls=%async_computation.1 | async-start | bytes 3145728 | tf_op jit(solution)/shard_map/all_to_all | solution.py:167
  178.6 6.0 %pad_maximum_fusion.ext_ref = bf16[104,128,256]{2,1,0:T(8,128)(2,1)} fusion(bf16[4,128,256]{2,1,0:T(8,128)(2,1)} %collective-permute-done.1, bf16[4,128,256]{2,1,0:T(8,128)(2,1)} %collective-permute-done, bf16[64,128,256]{2,1,0:T(8,128)(2,1)} %broadcast_select_fusion, bf16[32,128,256]{2,1,0:T(8,128)(2,1)S(1)} %copy-done.2), kind=kLoop, calls=%fused_computation.8 | loop fusion | flops 10223616 | bytes 13631488 | tf_op jit(solution)/shard_map/concatenate | solution.py:177
  184.6 17.0 %shard_map.119 = f32[32,128,256]{2,1,0:T(8,128)} custom-call(s32[512]{0:T(512)} %reshape.181.cols_ref, bf16[104,128,256]{2,1,0:T(8,128)(2,1)} %pad_maximum_fusion.ext_ref, bf16[32,16,128,128]{3,2,1,0:T(8,128)(2,1)} %tiles_ref.1), custom_call_target="tpu_custom_call" | custom-call | flops 4294967296 | bytes 27787264 | tf_op jit(solution)/shard_map/pallas_call | solution.py:48
  201.6 2.7 %fusion.4 = bf16[64,128,256]{2,1,0:T(8,128)(2,1)S(1)} fusion(bf16[64,32,384]{2,1,0:T(8,128)(2,1)} %bitcast.16), kind=kOutput, calls=%fused_computation.19 | convolution fusion | flops 134217728 | bytes 5767168 | tf_op jit(solution)/shard_map/qsk,qsv->qkv/dot_general | solution.py:169
  204.3 3.0 %fusion = f32[32,128,256]{2,0,1:T(8,128)S(1)} fusion(bf16[64,128,256]{2,1,0:T(8,128)(2,1)S(1)} %fusion.4, s32[64]{0:T(128)S(1)} %eq.15), kind=kOutput, calls=%fused_computation.10 | convolution fusion | flops 134219776 | bytes 8388864 | tf_op jit(solution)/shard_map/bq,qkv->bkv/dot_general | solution.py:116
  207.3 3.7 %fusion.1 = bf16[32,128,256]{2,1,0:T(8,128)(2,1)} fusion(f32[32,128,256]{2,1,0:T(8,128)S(1)} %copy-done.3, f32[32,128,256]{2,0,1:T(8,128)S(1)} %fusion), kind=kLoop, calls=%fused_computation.12 | loop fusion | flops 2097152 | bytes 10485760 | tf_op jit(solution)/shard_map/convert_element_type | solution.py:181
  (47 shorter events, 1.5 us)
Async XLA Ops:
  0.0 4.8 %copy-start = (bf16[16,4,32,128]{3,2,1,0:T(8,128)(2,1)S(1)}, bf16[16,4,32,128]{3,2,1,0:T(8,128)(2,1)}, u32[]{:S(2)}) copy-start(bf16[16,4,32,128]{3,2,1,0:T(8,128)(2,1)} %param.21) | copy-start | bytes 1572868
  0.0 5.7 %copy-start.2 = (bf16[32,128,256]{2,1,0:T(8,128)(2,1)S(1)}, bf16[32,128,256]{2,1,0:T(8,128)(2,1)}, u32[]{:S(2)}) copy-start(bf16[32,128,256]{2,1,0:T(8,128)(2,1)} %param.12) | copy-start | bytes 6291460
  87.3 47.7 %copy-start.9 = (s32[1,2,4]{2,1,0:T(2,128)S(1)}, s32[1,2,4]{2,1,0:T(2,128)}, u32[]{:S(2)}) copy-start(s32[1,2,4]{2,1,0:T(2,128)} %param.17) | copy-start | bytes 100
  91.5 50.5 %copy-start.7 = (s32[1,16,4]{1,2,0:T(4,128)S(1)}, s32[1,16,4]{1,2,0:T(4,128)}, u32[]{:S(2)}) copy-start(s32[1,16,4]{1,2,0:T(4,128)} %param.18) | copy-start | bytes 772
  91.5 69.9 %all-to-all-start = ((f32[16,4,32,256]{3,2,1,0:T(8,128)}), f32[16,4,32,256]{3,2,1,0:T(8,128)}, u32[]{:S(2)}, u32[]{:S(2)}) async-start(f32[16,4,32,256]{3,2,1,0:T(8,128)} %fusion.13), calls=%async_computation | async-start | bytes 4194304 | tf_op jit(solution)/shard_map/all_to_all | solution.py:159
  136.4 42.1 %collective-permute-start = (bf16[4,128,256]{2,1,0:T(8,128)(2,1)}, bf16[4,128,256]{2,1,0:T(8,128)(2,1)}, u32[]{:S(2)}, u32[]{:S(2)}) collective-permute-start(bf16[4,128,256]{2,1,0:T(8,128)(2,1)} %get-tuple-element.7), channel_id=1, source_target_pairs={{0,1},{1,2},{2,3},{3,4},{4,5},{5,6},{6,7},{8,9},{9,10},{10,11},{11... | collective-permute-start | bytes 786440 | tf_op jit(solution)/shard_map/ppermute | solution.py:16
  138.3 40.2 %collective-permute-start.1 = (bf16[4,128,256]{2,1,0:T(8,128)(2,1)S(1)}, bf16[4,128,256]{2,1,0:T(8,128)(2,1)}, u32[]{:S(2)}, u32[]{:S(2)}) collective-permute-start(bf16[4,128,256]{2,1,0:T(8,128)(2,1)S(1)} %get-tuple-element.8), channel_id=1, source_target_pairs={{1,0},{2,1},{3,2},{4,3},{5,4},{6,5},{7,6},{9,8},{10,9},{11,10},{12... | collective-permute-start | bytes 786440 | tf_op jit(solution)/shard_map/ppermute | solution.py:17
  142.2 5.3 %copy-start.8 = (s32[1,16]{1,0:T(1,128)S(1)}, s32[1,16]{1,0:T(1,128)}, u32[]{:S(2)}) copy-start(s32[1,16]{1,0:T(1,128)} %param.16) | copy-start | bytes 196
  142.2 5.6 %copy-start.6 = (s32[32,16]{0,1:T(8,128)S(1)}, s32[32,16]{0,1:T(8,128)}, u32[]{:S(2)}) copy-start(s32[32,16]{0,1:T(8,128)} %param.14) | copy-start | bytes 6148
  142.2 6.4 %copy-start.4 = (bf16[16,4,32,128]{3,2,1,0:T(8,128)(2,1)S(1)}, bf16[16,4,32,128]{3,2,1,0:T(8,128)(2,1)}, u32[]{:S(2)}) copy-start(bf16[16,4,32,128]{3,2,1,0:T(8,128)(2,1)} %param.22) | copy-start | bytes 1572868
  153.8 13.1 %copy-start.5 = (f32[16,32,32]{2,1,0:T(8,128)S(1)}, f32[16,32,32]{2,1,0:T(8,128)}, u32[]{:S(2)}) copy-start(f32[16,32,32]{2,1,0:T(8,128)} %param.23) | copy-start | bytes 196612
  171.6 30.0 %all-to-all-start.1 = ((bf16[16,4,32,384]{3,2,1,0:T(8,128)(2,1)}), bf16[16,4,32,384]{3,2,1,0:T(8,128)(2,1)}, u32[]{:S(2)}, u32[]{:S(2)}) async-start(bf16[16,4,32,384]{3,2,1,0:T(8,128)(2,1)} %bitcast.38), calls=%async_computation.1 | async-start | bytes 3145728 | tf_op jit(solution)/shard_map/all_to_all | solution.py:167
  204.3 3.1 %copy-start.3 = (f32[32,128,256]{2,1,0:T(8,128)S(1)}, f32[32,128,256]{2,1,0:T(8,128)}, u32[]{:S(2)}) copy-start(f32[32,128,256]{2,1,0:T(8,128)} %shard_map.119) | copy-start | bytes 12582916
  204.3 6.7 %copy-start.1 = (bf16[16,4,32,128]{3,2,1,0:T(8,128)(2,1)S(1)}, bf16[16,4,32,128]{3,2,1,0:T(8,128)(2,1)}, u32[]{:S(2)}) copy-start(bf16[16,4,32,128]{3,2,1,0:T(8,128)(2,1)} %param.21) | copy-start | bytes 1572868

commit v5 on v3

--- a/solution.py
+++ b/solution.py
@@ -107,8 +107,8 @@
     in_recv = recv_pack[:, halo_width * cell_count :].reshape(dom_count, slot_width, seg, cell_count)
     well_pack = blocks[well_send[0]]
     partial = jnp.einsum("qcsk,qckv->qcsv", in_recv, well_pack, preferred_element_type=jnp.float32)
-    partial_in = lax.all_to_all(partial, "dom", split_axis=0, concat_axis=0, tiled=True)
-    partial_in = partial_in.reshape(slot_total, seg, vec_count)
+    partial_in = lax.all_to_all(partial.astype(jnp.bfloat16), "dom", split_axis=0, concat_axis=0, tiled=True)
+    partial_in = partial_in.reshape(slot_total, seg, vec_count).astype(jnp.float32)
     summed = jnp.sum(partial_in[well_slot.reshape(-1)].reshape(wells, couplings, seg, vec_count), axis=1)
     well_state = well_states_of(summed, well_inverse, well_count)
     state_slots = well_state[slot_well]

time: 185 us -> 174 us (0.941)
  waiting for transfers between devices: 67.3 us -> 56.4 us
  other arithmetic: 24.3 us -> 27.1 us
    all_to_all x1, waiting for transfers between devices: 57.7 us -> 50.7 us  [on_device(): lax.all_to_all(send_pack, 'dom', split_axis=0, concat_axis=0, tiled=True)]
    all_to_all x1, waiting for transfers between devices: 9.63 us -> 5.72 us  [on_device(): lax.all_to_all(partial.astype(jnp.bfloat16), 'dom', split_axis=0, concat_...]
    convert_element_type x0 -> x1, other arithmetic: none -> 2.8 us  [on_device(): partial_in.reshape(slot_total, seg, vec_count).astype(jnp.float32)]
  transfers between devices with their start and end apart: 5 -> 5, of which waited for: 2 -> 2; matrix products, arithmetic and copies ran while one was open for 16% -> 20% of each run, Pallas kernels for 9% -> 10%
where the time goes in v5:
time: 174 us; the launch traced here: 173 us
  waiting for transfers between devices  56.4 us (32%)
  starting transfers between devices  41.7 us (24%)
  other arithmetic  27.1 us (16%)
  local copies, waits for them, and re-layouts  19.9 us (11%)
  Pallas kernels  17 us (10%)
  matrix products  10.2 us (6%)
    all_to_all x1, waiting for transfers between devices, on_device(): lax.all_to_all(send_pack, 'dom', split_axis=0, concat_axis=0, tiled=True)  50.7 us
    all_to_all x1, starting transfers between devices, on_device(): lax.all_to_all(partial.astype(jnp.bfloat16), 'dom', split_axis=0, concat_...  22.2 us
    pallas_call x1, Pallas kernels, local_product(): pl.pallas_call(product_kernel, out_shape=jax.ShapeDtypeStruct((block_rows...  17 us
    all_to_all x1, starting transfers between devices, on_device(): lax.all_to_all(send_pack, 'dom', split_axis=0, concat_axis=0, tiled=True)  7.61 us
    all_to_all x1, starting transfers between devices, on_device(): lax.all_to_all(state_pack, 'dom', split_axis=0, concat_axis=0, tiled=True)  6.37 us
    concatenate x1, other arithmetic, on_device(): jnp.concatenate([blocks, halo_rows.reshape(dom_count * halo_width, cell_c...  6.05 us
    all_to_all x1, waiting for transfers between devices, on_device(): lax.all_to_all(partial.astype(jnp.bfloat16), 'dom', split_axis=0, concat_...  5.72 us
    concatenate x1, other arithmetic, on_device(): send_pack = jnp.concatenate([halo_flat, in_slots], 1)  4.79 us
  transfers between devices with their start and end apart: 5, of which 2 were waited for; matrix products, arithmetic and copies ran while one was open for 20% of the time, Pallas kernels for 10%

profile of v5, /device:TPU:66, one launch (start us, length us, event | category | flops | bytes accessed | tf_op | source)
XLA Modules:
  0.0 173.2 jit_solution(2258035572245912242)
XLA Ops:
  0.0 0.8 compare_select_fusion.1
  1.0 0.8 copy.21
  1.9 2.0 %sort.17 = (s32[64]{0:T(128)}, s32[64]{0:T(128)S(1)}) sort(s32[64]{0:T(128)S(1)} %reshape.184, s32[64]{0:T(128)S(1)} %iota.21), dimensions={0}, to_apply=%region_0.0 | sort | flops 384 | bytes 1024 | tf_op jit(solution)/shard_map/jit(argsort)/sort | solution.py:99
  4.0 0.7 gather_fusion.1
  4.8 2.8 %gather_fusion = bf16[64,128,256]{2,1,0:T(8,128)(2,1)} fusion(bf16[32,128,256]{2,1,0:T(8,128)(2,1)S(1)} %copy-done.2, s32[1024]{0:T(1024)S(1)} %pad_clamp_fusion.5), kind=kCustom, calls=%fused_computation | custom fusion | bytes 8388864 | tf_op jit(solution)/shard_map/gather | solution.py:95
  7.6 4.8 %pad_maximum_fusion.1 = bf16[16,576,256]{2,1,0:T(8,128)(2,1)} fusion(bf16[16,64,256]{2,1,0:T(8,128)(2,1)S(1)} %reshape.185, bf16[16,512,256]{2,1,0:T(8,128)(2,1)} %bitcast.38), kind=kLoop, calls=%fused_computation.9 | loop fusion | flops 9437184 | bytes 9437184 | tf_op jit(solution)/shard_map/concatenate | solution.py:104
  12.4 7.6 %all-to-all-start = ((bf16[16,576,256]{2,1,0:T(8,128)(2,1)}), bf16[16,576,256]{2,1,0:T(8,128)(2,1)}, u32[]{:S(2)}, u32[]{:S(2)}) async-start(bf16[16,576,256]{2,1,0:T(8,128)(2,1)} %pad_maximum_fusion.1), calls=%async_computation | async-start | bytes 9437184 | tf_op jit(solution)/shard_map/all_to_all | solution.py:105
  20.7 0.7 fusion.12
  21.4 1.9 %collective-permute-start = (bf16[4,128,256]{2,1,0:T(8,128)(2,1)}, bf16[4,128,256]{2,1,0:T(8,128)(2,1)}, u32[]{:S(2)}, u32[]{:S(2)}) collective-permute-start(bf16[4,128,256]{2,1,0:T(8,128)(2,1)} %get-tuple-element.7), channel_id=1, source_target_pairs={{0,1},{1,2},{2,3},{3,4},{4,5},{5,6},{6,7},{8,9},{9,10},{10,11},{11... | collective-permute-start | bytes 786440 | tf_op jit(solution)/shard_map/ppermute | solution.py:16
  23.3 3.6 %collective-permute-start.1 = (bf16[4,128,256]{2,1,0:T(8,128)(2,1)S(1)}, bf16[4,128,256]{2,1,0:T(8,128)(2,1)}, u32[]{:S(2)}, u32[]{:S(2)}) collective-permute-start(bf16[4,128,256]{2,1,0:T(8,128)(2,1)S(1)} %get-tuple-element.8), channel_id=1, source_target_pairs={{1,0},{2,1},{3,2},{4,3},{5,4},{6,5},{7,6},{9,8},{10,9},{11,10},{12... | collective-permute-start | bytes 786440 | tf_op jit(solution)/shard_map/ppermute | solution.py:17
  27.2 2.9 %gather_fusion.3 = bf16[64,128,256]{2,1,0:T(8,128)(2,1)} fusion(bf16[32,128,256]{2,1,0:T(8,128)(2,1)S(1)} %copy-done.2, s32[1024]{0:T(1024)S(1)} %pad_clamp_fusion.2), kind=kCustom, calls=%fused_computation.3 | custom fusion | bytes 8388864 | tf_op jit(solution)/shard_map/gather | solution.py:108
  30.1 50.7 %all-to-all-done = bf16[16,576,256]{2,1,0:T(8,128)(2,1)} async-done(((bf16[16,576,256]{2,1,0:T(8,128)(2,1)}), bf16[16,576,256]{2,1,0:T(8,128)(2,1)}, u32[]{:S(2)}, u32[]{:S(2)}) %all-to-all-start) | async-done | bytes 4718624 | tf_op jit(solution)/shard_map/all_to_all | solution.py:105
  80.7 1.1 slice.41
  82.1 3.9 %convolution_convert_fusion = bf16[16,4,32,256]{3,2,1,0:T(8,128)(2,1)} fusion(bf16[16,4,32,128]{3,2,1,0:T(8,128)(2,1)S(1)} %reshape.187, bf16[16,4,128,256]{3,2,1,0:T(8,128)(2,1)} %bitcast.37), kind=kOutput, calls=%fused_computation.16 | convolution fusion | flops 134742016 | bytes 5767168 | tf_op jit(solution)/shard_map/qcsk,qckv->qcsv/dot_general | solution.py:109
  86.0 22.2 %all-to-all-start.1 = ((bf16[16,4,32,256]{3,2,1,0:T(8,128)(2,1)}), bf16[16,4,32,256]{3,2,1,0:T(8,128)(2,1)}, u32[]{:S(2)}, u32[]{:S(2)}) async-start(bf16[16,4,32,256]{3,2,1,0:T(8,128)(2,1)} %convolution_convert_fusion), calls=%async_computation.1 | async-start | bytes 2097152 | tf_op jit(solution)/shard_map/all_to_all | solution.py:110
  109.3 0.6 reshape.181.cols_ref
  109.9 0.7 gather_fusion.6
  110.6 2.6 %slice.38 = bf16[16,512,256]{2,1,0:T(8,128)(2,1)S(1)} slice(bf16[16,576,256]{2,1,0:T(8,128)(2,1)} %all-to-all-done), slice={[0:16], [0:512], [0:256]} | slice | bytes 8388608 | tf_op jit(solution)/shard_map/slice | solution.py:106
  113.2 2.4 %broadcast_select_fusion = bf16[64,128,256]{2,1,0:T(8,128)(2,1)} fusion(bf16[64,128,256]{2,1,0:T(8,128)(2,1)S(1)} %bitcast.39, pred[64]{0:T(512)(128)(4,1)S(1)} %lt.83), kind=kLoop, calls=%fused_computation.13 | loop fusion | flops 2097152 | bytes 8388672 | tf_op jit(solution)/shard_map/jit(_where)/select_n | solution.py:127
  115.6 5.7 %all-to-all-done.1 = bf16[16,4,32,256]{3,2,1,0:T(8,128)(2,1)} async-done(((bf16[16,4,32,256]{3,2,1,0:T(8,128)(2,1)}), bf16[16,4,32,256]{3,2,1,0:T(8,128)(2,1)}, u32[]{:S(2)}, u32[]{:S(2)}) %all-to-all-start.1) | async-done | bytes 1048608 | tf_op jit(solution)/shard_map/all_to_all | solution.py:110
  121.3 2.8 %bitcast_convert_fusion = f32[64,32,256]{2,1,0:T(8,128)} fusion(bf16[16,4,32,256]{3,2,1,0:T(8,128)(2,1)} %all-to-all-done.1), kind=kLoop, calls=%fused_computation.22 | loop fusion | flops 524288 | bytes 3145728 | tf_op jit(solution)/shard_map/convert_element_type | solution.py:111
  124.1 3.6 %gather_fusion.4 = f32[64,32,256]{2,1,0:T(8,128)} fusion(f32[64,32,256]{2,1,0:T(8,128)} %bitcast_convert_fusion, s32[1024]{0:T(1024)S(1)} %pad_clamp_fusion.1), kind=kCustom, calls=%fused_computation.4 | custom fusion | bytes 4194560 | tf_op jit(solution)/shard_map/gather | solution.py:112
  127.8 1.8 %bitcast_reduce_fusion = f32[16,32,256]{2,1,0:T(8,128)S(1)} fusion(f32[64,32,256]{2,1,0:T(8,128)} %gather_fusion.4), kind=kLoop, calls=%fused_computation.14 | loop fusion | flops 393216 | bytes 2621440 | tf_op jit(solution)/shard_map/reduce_sum | solution.py:112
  129.6 0.6 fusion.3
  130.2 1.6 gather_fusion.5
  131.8 2.5 %pad_maximum_fusion.2 = bf16[64,32,384]{2,1,0:T(8,128)(2,1)} fusion(bf16[64,32,128]{2,1,0:T(8,128)(2,1)S(1)} %gather_fusion.6, bf16[64,32,256]{2,1,0:T(8,128)(2,1)} %gather_fusion.5), kind=kLoop, calls=%fused_computation.15 | loop fusion | flops 3145728 | bytes 3145728 | tf_op jit(solution)/shard_map/concatenate | solution.py:116
  134.4 6.4 %all-to-all-start.2 = ((bf16[16,4,32,384]{3,2,1,0:T(8,128)(2,1)}), bf16[16,4,32,384]{3,2,1,0:T(8,128)(2,1)}, u32[]{:S(2)}, u32[]{:S(2)}) async-start(bf16[16,4,32,384]{3,2,1,0:T(8,128)(2,1)} %bitcast.40), calls=%async_computation.2 | async-start | bytes 3145728 | tf_op jit(solution)/shard_map/all_to_all | solution.py:118
  140.7 6.0 %pad_maximum_fusion.ext_ref = bf16[104,128,256]{2,1,0:T(8,128)(2,1)} fusion(bf16[4,128,256]{2,1,0:T(8,128)(2,1)} %collective-permute-done.1, bf16[4,128,256]{2,1,0:T(8,128)(2,1)} %collective-permute-done, bf16[64,128,256]{2,1,0:T(8,128)(2,1)} %broadcast_select_fusion, bf16[32,128,256]{2,1,0:T(8,128)(2,1)S(1)} %copy-done.2), kind=kLoop, calls=%fused_computation.8 | loop fusion | flops 10223616 | bytes 13631488 | tf_op jit(solution)/shard_map/concatenate | solution.py:128
  146.8 17.0 %shard_map.118 = f32[32,128,256]{2,1,0:T(8,128)} custom-call(s32[512]{0:T(512)} %reshape.181.cols_ref, bf16[104,128,256]{2,1,0:T(8,128)(2,1)} %pad_maximum_fusion.ext_ref, bf16[32,16,128,128]{3,2,1,0:T(8,128)(2,1)} %tiles_ref.1), custom_call_target="tpu_custom_call" | custom-call | flops 4294967296 | bytes 27787264 | tf_op jit(solution)/shard_map/pallas_call | solution.py:48
  163.8 2.7 %fusion.4 = bf16[64,128,256]{2,1,0:T(8,128)(2,1)S(1)} fusion(bf16[64,32,384]{2,1,0:T(8,128)(2,1)} %bitcast.16), kind=kOutput, calls=%fused_computation.20 | convolution fusion | flops 134217728 | bytes 5767168 | tf_op jit(solution)/shard_map/qsk,qsv->qkv/dot_general | solution.py:120
  166.5 3.0 %fusion = f32[32,128,256]{2,0,1:T(8,128)S(1)} fusion(bf16[64,128,256]{2,1,0:T(8,128)(2,1)S(1)} %fusion.4, s32[64]{0:T(128)S(1)} %eq.15), kind=kOutput, calls=%fused_computation.10 | convolution fusion | flops 134219776 | bytes 8388864 | tf_op jit(solution)/shard_map/bq,qkv->bkv/dot_general | solution.py:67
  169.5 3.7 %fusion.1 = bf16[32,128,256]{2,1,0:T(8,128)(2,1)} fusion(f32[32,128,256]{2,1,0:T(8,128)S(1)} %copy-done.3, f32[32,128,256]{2,0,1:T(8,128)S(1)} %fusion), kind=kLoop, calls=%fused_computation.12 | loop fusion | flops 2097152 | bytes 10485760 | tf_op jit(solution)/shard_map/convert_element_type | solution.py:132
  (49 shorter events, 2.1 us)
Async XLA Ops:
  0.0 4.0 %copy-start = (bf16[16,4,32,128]{3,2,1,0:T(8,128)(2,1)S(1)}, bf16[16,4,32,128]{3,2,1,0:T(8,128)(2,1)}, u32[]{:S(2)}) copy-start(bf16[16,4,32,128]{3,2,1,0:T(8,128)(2,1)} %param.21) | copy-start | bytes 1572868
  0.0 4.8 %copy-start.2 = (bf16[32,128,256]{2,1,0:T(8,128)(2,1)S(1)}, bf16[32,128,256]{2,1,0:T(8,128)(2,1)}, u32[]{:S(2)}) copy-start(bf16[32,128,256]{2,1,0:T(8,128)(2,1)} %param.12) | copy-start | bytes 6291460
  12.4 7.6 %copy-start.9 = (s32[1,2,4]{2,1,0:T(2,128)S(1)}, s32[1,2,4]{2,1,0:T(2,128)}, u32[]{:S(2)}) copy-start(s32[1,2,4]{2,1,0:T(2,128)} %param.17) | copy-start | bytes 100
  12.4 14.6 %copy-start.7 = (s32[1,16,4]{1,2,0:T(4,128)S(1)}, s32[1,16,4]{1,2,0:T(4,128)}, u32[]{:S(2)}) copy-start(s32[1,16,4]{1,2,0:T(4,128)} %param.18) | copy-start | bytes 772
  12.4 68.4 %all-to-all-start = ((bf16[16,576,256]{2,1,0:T(8,128)(2,1)}), bf16[16,576,256]{2,1,0:T(8,128)(2,1)}, u32[]{:S(2)}, u32[]{:S(2)}) async-start(bf16[16,576,256]{2,1,0:T(8,128)(2,1)} %pad_maximum_fusion.1), calls=%async_computation | async-start | bytes 9437184 | tf_op jit(solution)/shard_map/all_to_all | solution.py:105
  21.4 119.3 %collective-permute-start = (bf16[4,128,256]{2,1,0:T(8,128)(2,1)}, bf16[4,128,256]{2,1,0:T(8,128)(2,1)}, u32[]{:S(2)}, u32[]{:S(2)}) collective-permute-start(bf16[4,128,256]{2,1,0:T(8,128)(2,1)} %get-tuple-element.7), channel_id=1, source_target_pairs={{0,1},{1,2},{2,3},{3,4},{4,5},{5,6},{6,7},{8,9},{9,10},{10,11},{11... | collective-permute-start | bytes 786440 | tf_op jit(solution)/shard_map/ppermute | solution.py:16
  23.3 117.4 %collective-permute-start.1 = (bf16[4,128,256]{2,1,0:T(8,128)(2,1)S(1)}, bf16[4,128,256]{2,1,0:T(8,128)(2,1)}, u32[]{:S(2)}, u32[]{:S(2)}) collective-permute-start(bf16[4,128,256]{2,1,0:T(8,128)(2,1)S(1)} %get-tuple-element.8), channel_id=1, source_target_pairs={{1,0},{2,1},{3,2},{4,3},{5,4},{6,5},{7,6},{9,8},{10,9},{11,10},{12... | collective-permute-start | bytes 786440 | tf_op jit(solution)/shard_map/ppermute | solution.py:17
  82.0 26.1 %copy-start.8 = (s32[1,16]{1,0:T(1,128)S(1)}, s32[1,16]{1,0:T(1,128)}, u32[]{:S(2)}) copy-start(s32[1,16]{1,0:T(1,128)} %param.16) | copy-start | bytes 196
  82.0 27.2 %copy-start.6 = (s32[32,16]{0,1:T(8,128)S(1)}, s32[32,16]{0,1:T(8,128)}, u32[]{:S(2)}) copy-start(s32[32,16]{0,1:T(8,128)} %param.14) | copy-start | bytes 6148
  82.0 27.9 %copy-start.4 = (bf16[16,4,32,128]{3,2,1,0:T(8,128)(2,1)S(1)}, bf16[16,4,32,128]{3,2,1,0:T(8,128)(2,1)}, u32[]{:S(2)}) copy-start(bf16[16,4,32,128]{3,2,1,0:T(8,128)(2,1)} %param.22) | copy-start | bytes 1572868
  86.0 35.4 %all-to-all-start.1 = ((bf16[16,4,32,256]{3,2,1,0:T(8,128)(2,1)}), bf16[16,4,32,256]{3,2,1,0:T(8,128)(2,1)}, u32[]{:S(2)}, u32[]{:S(2)}) async-start(bf16[16,4,32,256]{3,2,1,0:T(8,128)(2,1)} %convolution_convert_fusion), calls=%async_computation.1 | async-start | bytes 2097152 | tf_op jit(solution)/shard_map/all_to_all | solution.py:110
  124.1 5.5 %copy-start.5 = (f32[16,32,32]{2,1,0:T(8,128)S(1)}, f32[16,32,32]{2,1,0:T(8,128)}, u32[]{:S(2)}) copy-start(f32[16,32,32]{2,1,0:T(8,128)} %param.23) | copy-start | bytes 196612
  134.4 29.4 %all-to-all-start.2 = ((bf16[16,4,32,384]{3,2,1,0:T(8,128)(2,1)}), bf16[16,4,32,384]{3,2,1,0:T(8,128)(2,1)}, u32[]{:S(2)}, u32[]{:S(2)}) async-start(bf16[16,4,32,384]{3,2,1,0:T(8,128)(2,1)} %bitcast.40), calls=%async_computation.2 | async-start | bytes 3145728 | tf_op jit(solution)/shard_map/all_to_all | solution.py:118
  166.5 3.0 %copy-start.3 = (f32[32,128,256]{2,1,0:T(8,128)S(1)}, f32[32,128,256]{2,1,0:T(8,128)}, u32[]{:S(2)}) copy-start(f32[32,128,256]{2,1,0:T(8,128)} %shard_map.118) | copy-start | bytes 12582916
  166.5 6.7 %copy-start.1 = (bf16[16,4,32,128]{3,2,1,0:T(8,128)(2,1)S(1)}, bf16[16,4,32,128]{3,2,1,0:T(8,128)(2,1)}, u32[]{:S(2)}) copy-start(bf16[16,4,32,128]{3,2,1,0:T(8,128)(2,1)} %param.21) | copy-start | bytes 1572868

commit v6 on v3

--- a/solution.py
+++ b/solution.py
@@ -51,6 +51,98 @@
         grid_spec=grid_spec,
         cost_estimate=pl.CostEstimate(flops=flops, transcendentals=0, bytes_accessed=moved),
     )(tile_cols.reshape(-1), extended, tile_values)
+
+
+SIDE = 4
+NEAR = ((1, 0), (3, 0), (0, 1), (0, 3), (1, 1), (1, 3), (3, 1), (3, 3))
+RELAYED = (
+    ((2, 0), (1, 0), 0), ((2, 0), (3, 0), 1),
+    ((2, 1), (1, 0), 0), ((2, 1), (3, 0), 1),
+    ((2, 3), (1, 0), 0), ((2, 3), (3, 0), 1),
+    ((0, 2), (0, 1), 0), ((0, 2), (0, 3), 1),
+    ((1, 2), (0, 1), 0), ((1, 2), (0, 3), 1),
+    ((3, 2), (0, 1), 0), ((3, 2), (0, 3), 1),
+    ((2, 2), (1, 1), 0), ((2, 2), (3, 3), 1),
+)
+
+
+def exchange_kernel(send_ref, recv_ref, relay_ref, near_send, near_recv, leg_send, leg_recv,
+                    fwd_send, fwd_recv, own_sem):
+    me = lax.axis_index("dom")
+    grp = lax.axis_index("grp")
+    row, col = me // SIDE, me % SIDE
+    half = send_ref.shape[1] // 2
+
+    def at(offset):
+        return ((row + offset[0]) % SIDE) * SIDE + (col + offset[1]) % SIDE
+
+    def remote(src, dst, send_sem, recv_sem, offset):
+        return pltpu.make_async_remote_copy(
+            src_ref=src, dst_ref=dst, send_sem=send_sem, recv_sem=recv_sem,
+            device_id=(at(offset), grp), device_id_type=pl.DeviceIdType.MESH,
+        )
+
+    barrier = pltpu.get_barrier_semaphore()
+    for offset in NEAR:
+        pl.semaphore_signal(
+            barrier, inc=1, device_id=(at(offset), grp), device_id_type=pl.DeviceIdType.MESH
+        )
+    pl.semaphore_wait(barrier, len(NEAR))
+    own = pltpu.make_async_copy(send_ref.at[me], recv_ref.at[me], own_sem)
+    own.start()
+    legs = []
+    for k, (target, relay, part) in enumerate(RELAYED):
+        leg = remote(send_ref.at[at(target), pl.ds(part * half, half)], relay_ref.at[k],
+                     leg_send.at[k], leg_recv.at[k], relay)
+        leg.start()
+        legs.append(leg)
+    nears = []
+    for k, offset in enumerate(NEAR):
+        near = remote(send_ref.at[at(offset)], recv_ref.at[me], near_send.at[k], near_recv.at[k], offset)
+        near.start()
+        nears.append(near)
+    fwds = []
+    for k, (target, relay, part) in enumerate(RELAYED):
+        legs[k].wait_recv()
+        source = at(((SIDE - relay[0]) % SIDE, (SIDE - relay[1]) % SIDE))
+        onward = ((target[0] - relay[0]) % SIDE, (target[1] - relay[1]) % SIDE)
+        fwd = remote(relay_ref.at[k], recv_ref.at[source, pl.ds(part * half, half)],
+                     fwd_send.at[k], fwd_recv.at[k], onward)
+        fwd.start()
+        fwds.append(fwd)
+    for leg in legs:
+        leg.wait_send()
+    for near in nears:
+        near.wait_send()
+    for near in nears:
+        near.wait_recv()
+    for fwd in fwds:
+        fwd.wait_send()
+    for fwd in fwds:
+        fwd.wait_recv()
+    own.wait()
+
+
+def dom_exchange(value, collective):
+    count, rows, lanes = value.shape
+    relay_shape = jax.ShapeDtypeStruct((len(RELAYED), rows // 2, lanes), value.dtype)
+    recv, _ = pl.pallas_call(
+        exchange_kernel,
+        out_shape=(jax.ShapeDtypeStruct(value.shape, value.dtype), relay_shape),
+        in_specs=[pl.BlockSpec(memory_space=pl.ANY)],
+        out_specs=(pl.BlockSpec(memory_space=pl.ANY), pl.BlockSpec(memory_space=pl.ANY)),
+        scratch_shapes=[
+            pltpu.SemaphoreType.DMA((len(NEAR),)),
+            pltpu.SemaphoreType.DMA((len(NEAR),)),
+            pltpu.SemaphoreType.DMA((len(RELAYED),)),
+            pltpu.SemaphoreType.DMA((len(RELAYED),)),
+            pltpu.SemaphoreType.DMA((len(RELAYED),)),
+            pltpu.SemaphoreType.DMA((len(RELAYED),)),
+            pltpu.SemaphoreType.DMA,
+        ],
+        compiler_params=pltpu.CompilerParams(collective_id=collective, has_side_effects=True),
+    )(value)
+    return recv
 
 
 def well_states_of(summed, well_inverse, well_count):
@@ -102,7 +194,7 @@
     in_slots = in_slots.reshape(dom_count, slot_width * seg * cell_count // vec_count, vec_count)
     halo_flat = halo_pack.reshape(dom_count, halo_width * cell_count, vec_count)
     send_pack = jnp.concatenate([halo_flat, in_slots], 1)
-    recv_pack = lax.all_to_all(send_pack, "dom", split_axis=0, concat_axis=0, tiled=True)
+    recv_pack = dom_exchange(send_pack, 0)
     halo_rows = recv_pack[:, : halo_width * cell_count].reshape(dom_count, halo_width, cell_count, vec_count)
     in_recv = recv_pack[:, halo_width * cell_count :].reshape(dom_count, slot_width, seg, cell_count)
     well_pack = blocks[well_send[0]]

time: 185 us -> 171 us (0.924)
  Pallas kernels: 17 us -> 83.1 us
  waiting for transfers between devices: 67.3 us -> 7.51 us
  starting transfers between devices: 42.5 us -> 18.7 us
  other arithmetic: 24.3 us -> 27.1 us
    pallas_call x0 -> x1, Pallas kernels: none -> 66.2 us  [dom_exchange(): pl.pallas_call(exchange_kernel, out_shape=(jax.ShapeDtypeStruct(value.sha...]
    all_to_all x1 -> x0, waiting for transfers between devices: 57.7 us -> none  [on_device(): lax.all_to_all(send_pack, 'dom', split_axis=0, concat_axis=0, tiled=True)]
    all_to_all x1, starting transfers between devices: 22.3 us -> 6.23 us  [on_device(): lax.all_to_all(partial, 'dom', split_axis=0, concat_axis=0, tiled=True)]
    all_to_all x1 -> x0, starting transfers between devices: 7.61 us -> none  [on_device(): lax.all_to_all(send_pack, 'dom', split_axis=0, concat_axis=0, tiled=True)]
    select_n x1, other arithmetic: 2.43 us -> 4.59 us  [on_device(): jnp.where(live_halo[:, :, None, None], halo_rows, jnp.zeros_like(halo_rows))]
    all_to_all x1, waiting for transfers between devices: 9.63 us -> 7.5 us  [on_device(): lax.all_to_all(partial, 'dom', split_axis=0, concat_axis=0, tiled=True)]
    slice x1, local copies, waits for them, and re-layouts: 2.56 us -> 4.66 us  [on_device(): recv_pack[:, :halo_width * cell_count]]
  transfers between devices with their start and end apart: 5 -> 4, of which waited for: 2 -> 1; matrix products, arithmetic and copies ran while one was open for 16% -> 17% of each run, Pallas kernels for 9% -> 10%
where the time goes in v6:
time: 171 us; the launch traced here: 170 us
  Pallas kernels  83.1 us (49%)
  other arithmetic  27.1 us (16%)
  local copies, waits for them, and re-layouts  22 us (13%)
  starting transfers between devices  18.7 us (11%)
  matrix products  10.5 us (6%)
  waiting for transfers between devices  7.51 us (4%)
    pallas_call x1, Pallas kernels, dom_exchange(): pl.pallas_call(exchange_kernel, out_shape=(jax.ShapeDtypeStruct(value.sha...  66.2 us
    pallas_call x1, Pallas kernels, local_product(): pl.pallas_call(product_kernel, out_shape=jax.ShapeDtypeStruct((block_rows...  17 us
    all_to_all x1, waiting for transfers between devices, on_device(): lax.all_to_all(partial, 'dom', split_axis=0, concat_axis=0, tiled=True)  7.5 us
    all_to_all x1, starting transfers between devices, on_device(): lax.all_to_all(state_pack, 'dom', split_axis=0, concat_axis=0, tiled=True)  6.95 us
    all_to_all x1, starting transfers between devices, on_device(): lax.all_to_all(partial, 'dom', split_axis=0, concat_axis=0, tiled=True)  6.23 us
    concatenate x1, other arithmetic, on_device(): jnp.concatenate([blocks, halo_rows.reshape(dom_count * halo_width, cell_c...  6.04 us
    concatenate x1, other arithmetic, on_device(): send_pack = jnp.concatenate([halo_flat, in_slots], 1)  4.74 us
    slice x1, local copies, waits for them, and re-layouts, on_device(): recv_pack[:, :halo_width * cell_count]  4.66 us
  transfers between devices with their start and end apart: 4, of which 1 were waited for; matrix products, arithmetic and copies ran while one was open for 17% of the time, Pallas kernels for 10%

profile of v6, /device:TPU:66, one launch (start us, length us, event | category | flops | bytes accessed | tf_op | source)
XLA Modules:
  0.0 169.8 jit_solution(9406599992930793816)
XLA Ops:
  0.0 0.8 compare_select_fusion.1
  0.8 0.7 compare_select_fusion
  1.9 0.8 copy.21
  2.8 2.0 %sort.17 = (s32[64]{0:T(128)}, s32[64]{0:T(128)S(1)}) sort(s32[64]{0:T(128)S(1)} %reshape.184, s32[64]{0:T(128)S(1)} %iota.21), dimensions={0}, to_apply=%region_0.0 | sort | flops 384 | bytes 1024 | tf_op jit(solution)/shard_map/jit(argsort)/sort | solution.py:191
  4.8 0.7 gather_fusion.1
  5.7 2.8 %gather_fusion = bf16[64,128,256]{2,1,0:T(8,128)(2,1)} fusion(bf16[32,128,256]{2,1,0:T(8,128)(2,1)S(1)} %copy-done.2, s32[1024]{0:T(1024)S(1)} %pad_clamp_fusion.5), kind=kCustom, calls=%fused_computation | custom fusion | bytes 8388864 | tf_op jit(solution)/shard_map/gather | solution.py:187
  8.4 4.7 %pad_maximum_fusion.1.send_ref = bf16[16,576,256]{2,1,0:T(8,128)(2,1)} fusion(bf16[16,64,256]{2,1,0:T(8,128)(2,1)S(1)} %reshape.185, bf16[16,512,256]{2,1,0:T(8,128)(2,1)} %bitcast.35), kind=kLoop, calls=%fused_computation.9 | loop fusion | flops 9437184 | bytes 9437184 | tf_op jit(solution)/shard_map/concatenate | solution.py:196
  13.2 66.2 %shard_map.118 = (bf16[16,576,256]{2,1,0:T(8,128)(2,1)}, bf16[14,288,256]{2,1,0:T(8,128)(2,1)}) custom-call(bf16[16,576,256]{2,1,0:T(8,128)(2,1)} %pad_maximum_fusion.1.send_ref), custom_call_target="tpu_custom_call" | custom-call | tf_op jit(solution)/shard_map/pallas_call | solution.py:129
  79.4 1.1 slice.21
  80.6 2.9 %gather_fusion.3 = bf16[64,128,256]{2,1,0:T(8,128)(2,1)} fusion(bf16[32,128,256]{2,1,0:T(8,128)(2,1)S(1)} %copy-done.2, s32[1024]{0:T(1024)S(1)} %pad_clamp_fusion.2), kind=kCustom, calls=%fused_computation.3 | custom fusion | bytes 8388864 | tf_op jit(solution)/shard_map/gather | solution.py:200
  83.5 4.2 %fusion.13 = f32[16,4,32,256]{3,2,1,0:T(8,128)} fusion(bf16[16,4,32,128]{3,2,1,0:T(8,128)(2,1)S(1)} %reshape.187, bf16[16,4,128,256]{3,2,1,0:T(8,128)(2,1)} %bitcast.37), kind=kOutput, calls=%fused_computation.46 | convolution fusion | flops 134217728 | bytes 6815744 | tf_op jit(solution)/shard_map/qcsk,qckv->qcsv/dot_general | solution.py:201
  87.7 6.2 %all-to-all-start = ((f32[16,4,32,256]{3,2,1,0:T(8,128)}), f32[16,4,32,256]{3,2,1,0:T(8,128)}, u32[]{:S(2)}, u32[]{:S(2)}) async-start(f32[16,4,32,256]{3,2,1,0:T(8,128)} %fusion.13), calls=%async_computation | async-start | bytes 4194304 | tf_op jit(solution)/shard_map/all_to_all | solution.py:202
  94.1 0.6 gather_fusion.2
  94.6 0.7 fusion.12
  95.4 1.9 %collective-permute-start = (bf16[4,128,256]{2,1,0:T(8,128)(2,1)}, bf16[4,128,256]{2,1,0:T(8,128)(2,1)}, u32[]{:S(2)}, u32[]{:S(2)}) collective-permute-start(bf16[4,128,256]{2,1,0:T(8,128)(2,1)} %get-tuple-element.9), channel_id=1, source_target_pairs={{0,1},{1,2},{2,3},{3,4},{4,5},{5,6},{6,7},{8,9},{9,10},{10,11},{11... | collective-permute-start | bytes 786440 | tf_op jit(solution)/shard_map/ppermute | solution.py:16
  97.3 3.6 %collective-permute-start.1 = (bf16[4,128,256]{2,1,0:T(8,128)(2,1)S(1)}, bf16[4,128,256]{2,1,0:T(8,128)(2,1)}, u32[]{:S(2)}, u32[]{:S(2)}) collective-permute-start(bf16[4,128,256]{2,1,0:T(8,128)(2,1)S(1)} %get-tuple-element.10), channel_id=1, source_target_pairs={{1,0},{2,1},{3,2},{4,3},{5,4},{6,5},{7,6},{9,8},{10,9},{11,10},{12... | collective-permute-start | bytes 786440 | tf_op jit(solution)/shard_map/ppermute | solution.py:17
  101.1 4.7 %slice.18 = bf16[16,512,256]{2,1,0:T(8,128)(2,1)} slice(bf16[16,576,256]{2,1,0:T(8,128)(2,1)} %get-tuple-element.8), slice={[0:16], [0:512], [0:256]} | slice | bytes 8388608 | tf_op jit(solution)/shard_map/slice | solution.py:198
  106.8 0.7 reshape.181.cols_ref
  107.5 0.7 gather_fusion.6
  108.2 4.6 %broadcast_select_fusion = bf16[64,128,256]{2,1,0:T(8,128)(2,1)} fusion(bf16[64,128,256]{2,1,0:T(8,128)(2,1)} %bitcast.36, pred[64]{0:T(512)(128)(4,1)S(1)} %lt.83), kind=kLoop, calls=%fused_computation.13 | loop fusion | flops 2097152 | bytes 8388672 | tf_op jit(solution)/shard_map/jit(_where)/select_n | solution.py:219
  112.8 7.5 %all-to-all-done = f32[16,4,32,256]{3,2,1,0:T(8,128)} async-done(((f32[16,4,32,256]{3,2,1,0:T(8,128)}), f32[16,4,32,256]{3,2,1,0:T(8,128)}, u32[]{:S(2)}, u32[]{:S(2)}) %all-to-all-start) | async-done | bytes 2097184 | tf_op jit(solution)/shard_map/all_to_all | solution.py:202
  120.3 3.6 %gather_fusion.4 = f32[64,32,256]{2,1,0:T(8,128)} fusion(f32[64,32,256]{2,1,0:T(8,128)} %bitcast.9, s32[1024]{0:T(1024)S(1)} %pad_clamp_fusion.1), kind=kCustom, calls=%fused_computation.4 | custom fusion | bytes 4194560 | tf_op jit(solution)/shard_map/gather | solution.py:204
  123.8 1.8 %bitcast_reduce_fusion = f32[16,32,256]{2,1,0:T(8,128)S(1)} fusion(f32[64,32,256]{2,1,0:T(8,128)} %gather_fusion.4), kind=kLoop, calls=%fused_computation.14 | loop fusion | flops 393216 | bytes 2621440 | tf_op jit(solution)/shard_map/reduce_sum | solution.py:204
  125.7 0.6 fusion.3
  126.3 1.6 gather_fusion.5
  127.9 2.5 %pad_maximum_fusion.2 = bf16[64,32,384]{2,1,0:T(8,128)(2,1)} fusion(bf16[64,32,128]{2,1,0:T(8,128)(2,1)S(1)} %gather_fusion.6, bf16[64,32,256]{2,1,0:T(8,128)(2,1)} %gather_fusion.5), kind=kLoop, calls=%fused_computation.15 | loop fusion | flops 3145728 | bytes 3145728 | tf_op jit(solution)/shard_map/concatenate | solution.py:208
  130.5 6.9 %all-to-all-start.1 = ((bf16[16,4,32,384]{3,2,1,0:T(8,128)(2,1)}), bf16[16,4,32,384]{3,2,1,0:T(8,128)(2,1)}, u32[]{:S(2)}, u32[]{:S(2)}) async-start(bf16[16,4,32,384]{3,2,1,0:T(8,128)(2,1)} %bitcast.38), calls=%async_computation.1 | async-start | bytes 3145728 | tf_op jit(solution)/shard_map/all_to_all | solution.py:210
  137.4 6.0 %pad_maximum_fusion.ext_ref = bf16[104,128,256]{2,1,0:T(8,128)(2,1)} fusion(bf16[4,128,256]{2,1,0:T(8,128)(2,1)} %collective-permute-done.1, bf16[4,128,256]{2,1,0:T(8,128)(2,1)} %collective-permute-done, bf16[64,128,256]{2,1,0:T(8,128)(2,1)} %broadcast_select_fusion, bf16[32,128,256]{2,1,0:T(8,128)(2,1)S(1)} %copy-done.2), kind=kLoop, calls=%fused_computation.8 | loop fusion | flops 10223616 | bytes 13631488 | tf_op jit(solution)/shard_map/concatenate | solution.py:220
  143.5 17.0 %shard_map.119 = f32[32,128,256]{2,1,0:T(8,128)} custom-call(s32[512]{0:T(512)} %reshape.181.cols_ref, bf16[104,128,256]{2,1,0:T(8,128)(2,1)} %pad_maximum_fusion.ext_ref, bf16[32,16,128,128]{3,2,1,0:T(8,128)(2,1)} %tiles_ref.1), custom_call_target="tpu_custom_call" | custom-call | flops 4294967296 | bytes 27787264 | tf_op jit(solution)/shard_map/pallas_call | solution.py:48
  160.4 2.7 %fusion.4 = bf16[64,128,256]{2,1,0:T(8,128)(2,1)S(1)} fusion(bf16[64,32,384]{2,1,0:T(8,128)(2,1)} %bitcast.16), kind=kOutput, calls=%fused_computation.19 | convolution fusion | flops 134217728 | bytes 5767168 | tf_op jit(solution)/shard_map/qsk,qsv->qkv/dot_general | solution.py:212
  163.2 3.0 %fusion = f32[32,128,256]{2,0,1:T(8,128)S(1)} fusion(bf16[64,128,256]{2,1,0:T(8,128)(2,1)S(1)} %fusion.4, s32[64]{0:T(128)S(1)} %eq.15), kind=kOutput, calls=%fused_computation.10 | convolution fusion | flops 134219776 | bytes 8388864 | tf_op jit(solution)/shard_map/bq,qkv->bkv/dot_general | solution.py:159
  166.2 3.7 %fusion.1 = bf16[32,128,256]{2,1,0:T(8,128)(2,1)} fusion(f32[32,128,256]{2,1,0:T(8,128)S(1)} %copy-done.3, f32[32,128,256]{2,0,1:T(8,128)S(1)} %fusion), kind=kLoop, calls=%fused_computation.12 | loop fusion | flops 2097152 | bytes 10485760 | tf_op jit(solution)/shard_map/convert_element_type | solution.py:224
  (47 shorter events, 1.5 us)
Async XLA Ops:
  0.0 4.8 %copy-start = (bf16[16,4,32,128]{3,2,1,0:T(8,128)(2,1)S(1)}, bf16[16,4,32,128]{3,2,1,0:T(8,128)(2,1)}, u32[]{:S(2)}) copy-start(bf16[16,4,32,128]{3,2,1,0:T(8,128)(2,1)} %param.21) | copy-start | bytes 1572868
  0.0 5.7 %copy-start.2 = (bf16[32,128,256]{2,1,0:T(8,128)(2,1)S(1)}, bf16[32,128,256]{2,1,0:T(8,128)(2,1)}, u32[]{:S(2)}) copy-start(bf16[32,128,256]{2,1,0:T(8,128)(2,1)} %param.12) | copy-start | bytes 6291460
  83.5 10.5 %copy-start.9 = (s32[1,2,4]{2,1,0:T(2,128)S(1)}, s32[1,2,4]{2,1,0:T(2,128)}, u32[]{:S(2)}) copy-start(s32[1,2,4]{2,1,0:T(2,128)} %param.17) | copy-start | bytes 100
  87.7 13.3 %copy-start.7 = (s32[1,16,4]{1,2,0:T(4,128)S(1)}, s32[1,16,4]{1,2,0:T(4,128)}, u32[]{:S(2)}) copy-start(s32[1,16,4]{1,2,0:T(4,128)} %param.18) | copy-start | bytes 772
  87.7 32.5 %all-to-all-start = ((f32[16,4,32,256]{3,2,1,0:T(8,128)}), f32[16,4,32,256]{3,2,1,0:T(8,128)}, u32[]{:S(2)}, u32[]{:S(2)}) async-start(f32[16,4,32,256]{3,2,1,0:T(8,128)} %fusion.13), calls=%async_computation | async-start | bytes 4194304 | tf_op jit(solution)/shard_map/all_to_all | solution.py:202
  95.4 42.0 %collective-permute-start = (bf16[4,128,256]{2,1,0:T(8,128)(2,1)}, bf16[4,128,256]{2,1,0:T(8,128)(2,1)}, u32[]{:S(2)}, u32[]{:S(2)}) collective-permute-start(bf16[4,128,256]{2,1,0:T(8,128)(2,1)} %get-tuple-element.9), channel_id=1, source_target_pairs={{0,1},{1,2},{2,3},{3,4},{4,5},{5,6},{6,7},{8,9},{9,10},{10,11},{11... | collective-permute-start | bytes 786440 | tf_op jit(solution)/shard_map/ppermute | solution.py:16
  97.3 40.1 %collective-permute-start.1 = (bf16[4,128,256]{2,1,0:T(8,128)(2,1)S(1)}, bf16[4,128,256]{2,1,0:T(8,128)(2,1)}, u32[]{:S(2)}, u32[]{:S(2)}) collective-permute-start(bf16[4,128,256]{2,1,0:T(8,128)(2,1)S(1)} %get-tuple-element.10), channel_id=1, source_target_pairs={{1,0},{2,1},{3,2},{4,3},{5,4},{6,5},{7,6},{9,8},{10,9},{11,10},{12... | collective-permute-start | bytes 786440 | tf_op jit(solution)/shard_map/ppermute | solution.py:17
  101.1 5.3 %copy-start.8 = (s32[1,16]{1,0:T(1,128)S(1)}, s32[1,16]{1,0:T(1,128)}, u32[]{:S(2)}) copy-start(s32[1,16]{1,0:T(1,128)} %param.16) | copy-start | bytes 196
  101.1 5.6 %copy-start.6 = (s32[32,16]{0,1:T(8,128)S(1)}, s32[32,16]{0,1:T(8,128)}, u32[]{:S(2)}) copy-start(s32[32,16]{0,1:T(8,128)} %param.14) | copy-start | bytes 6148
  101.1 6.3 %copy-start.4 = (bf16[16,4,32,128]{3,2,1,0:T(8,128)(2,1)S(1)}, bf16[16,4,32,128]{3,2,1,0:T(8,128)(2,1)}, u32[]{:S(2)}) copy-start(bf16[16,4,32,128]{3,2,1,0:T(8,128)(2,1)} %param.22) | copy-start | bytes 1572868
  112.8 12.9 %copy-start.5 = (f32[16,32,32]{2,1,0:T(8,128)S(1)}, f32[16,32,32]{2,1,0:T(8,128)}, u32[]{:S(2)}) copy-start(f32[16,32,32]{2,1,0:T(8,128)} %param.23) | copy-start | bytes 196612
  130.5 30.0 %all-to-all-start.1 = ((bf16[16,4,32,384]{3,2,1,0:T(8,128)(2,1)}), bf16[16,4,32,384]{3,2,1,0:T(8,128)(2,1)}, u32[]{:S(2)}, u32[]{:S(2)}) async-start(bf16[16,4,32,384]{3,2,1,0:T(8,128)(2,1)} %bitcast.38), calls=%async_computation.1 | async-start | bytes 3145728 | tf_op jit(solution)/shard_map/all_to_all | solution.py:210
  163.1 3.1 %copy-start.3 = (f32[32,128,256]{2,1,0:T(8,128)S(1)}, f32[32,128,256]{2,1,0:T(8,128)}, u32[]{:S(2)}) copy-start(f32[32,128,256]{2,1,0:T(8,128)} %shard_map.119) | copy-start | bytes 12582916
  163.1 6.7 %copy-start.1 = (bf16[16,4,32,128]{3,2,1,0:T(8,128)(2,1)S(1)}, bf16[16,4,32,128]{3,2,1,0:T(8,128)(2,1)}, u32[]{:S(2)}) copy-start(bf16[16,4,32,128]{3,2,1,0:T(8,128)(2,1)} %param.21) | copy-start | bytes 1572868

commit v7 on v6

--- a/solution.py
+++ b/solution.py
@@ -66,12 +66,13 @@
 )
 
 
-def exchange_kernel(send_ref, recv_ref, relay_ref, near_send, near_recv, leg_send, leg_recv,
-                    fwd_send, fwd_recv, own_sem):
+def exchange_kernel(*refs):
+    parts = (len(refs) - 7) // 3
+    send_refs, recv_refs, relay_refs = refs[:parts], refs[parts : 2 * parts], refs[2 * parts : 3 * parts]
+    near_send, near_recv, leg_send, leg_recv, fwd_send, fwd_recv, own_sems = refs[3 * parts :]
     me = lax.axis_index("dom")
     grp = lax.axis_index("grp")
     row, col = me // SIDE, me % SIDE
-    half = send_ref.shape[1] // 2
 
     def at(offset):
         return ((row + offset[0]) % SIDE) * SIDE + (col + offset[1]) % SIDE
@@ -88,28 +89,37 @@
             barrier, inc=1, device_id=(at(offset), grp), device_id_type=pl.DeviceIdType.MESH
         )
     pl.semaphore_wait(barrier, len(NEAR))
-    own = pltpu.make_async_copy(send_ref.at[me], recv_ref.at[me], own_sem)
-    own.start()
+    owns = []
+    for p in range(parts):
+        own = pltpu.make_async_copy(send_refs[p].at[me], recv_refs[p].at[me], own_sems.at[p])
+        own.start()
+        owns.append(own)
     legs = []
     for k, (target, relay, part) in enumerate(RELAYED):
-        leg = remote(send_ref.at[at(target), pl.ds(part * half, half)], relay_ref.at[k],
-                     leg_send.at[k], leg_recv.at[k], relay)
-        leg.start()
-        legs.append(leg)
+        for p in range(parts):
+            half = send_refs[p].shape[1] // 2
+            leg = remote(send_refs[p].at[at(target), pl.ds(part * half, half)], relay_refs[p].at[k],
+                         leg_send.at[p, k], leg_recv.at[p, k], relay)
+            leg.start()
+            legs.append(leg)
     nears = []
     for k, offset in enumerate(NEAR):
-        near = remote(send_ref.at[at(offset)], recv_ref.at[me], near_send.at[k], near_recv.at[k], offset)
-        near.start()
-        nears.append(near)
+        for p in range(parts):
+            near = remote(send_refs[p].at[at(offset)], recv_refs[p].at[me],
+                          near_send.at[p, k], near_recv.at[p, k], offset)
+            near.start()
+            nears.append(near)
     fwds = []
     for k, (target, relay, part) in enumerate(RELAYED):
-        legs[k].wait_recv()
         source = at(((SIDE - relay[0]) % SIDE, (SIDE - relay[1]) % SIDE))
         onward = ((target[0] - relay[0]) % SIDE, (target[1] - relay[1]) % SIDE)
-        fwd = remote(relay_ref.at[k], recv_ref.at[source, pl.ds(part * half, half)],
-                     fwd_send.at[k], fwd_recv.at[k], onward)
-        fwd.start()
-        fwds.append(fwd)
+        for p in range(parts):
+            half = send_refs[p].shape[1] // 2
+            legs[k * parts + p].wait_recv()
+            fwd = remote(relay_refs[p].at[k], recv_refs[p].at[source, pl.ds(part * half, half)],
+                         fwd_send.at[p, k], fwd_recv.at[p, k], onward)
+            fwd.start()
+            fwds.append(fwd)
     for leg in legs:
         leg.wait_send()
     for near in nears:
@@ -120,29 +130,62 @@
         fwd.wait_send()
     for fwd in fwds:
         fwd.wait_recv()
-    own.wait()
-
-
-def dom_exchange(value, collective):
-    count, rows, lanes = value.shape
-    relay_shape = jax.ShapeDtypeStruct((len(RELAYED), rows // 2, lanes), value.dtype)
-    recv, _ = pl.pallas_call(
+    for own in owns:
+        own.wait()
+
+
+def dom_exchange(values, collective):
+    parts = len(values)
+    outs = [jax.ShapeDtypeStruct(v.shape, v.dtype) for v in values]
+    relays = [jax.ShapeDtypeStruct((len(RELAYED), v.shape[1] // 2, v.shape[2]), v.dtype) for v in values]
+    any_spec = pl.BlockSpec(memory_space=pl.ANY)
+    result = pl.pallas_call(
         exchange_kernel,
-        out_shape=(jax.ShapeDtypeStruct(value.shape, value.dtype), relay_shape),
-        in_specs=[pl.BlockSpec(memory_space=pl.ANY)],
-        out_specs=(pl.BlockSpec(memory_space=pl.ANY), pl.BlockSpec(memory_space=pl.ANY)),
+        out_shape=tuple(outs + relays),
+        in_specs=[any_spec] * parts,
+        out_specs=tuple([any_spec] * (2 * parts)),
         scratch_shapes=[
-            pltpu.SemaphoreType.DMA((len(NEAR),)),
-            pltpu.SemaphoreType.DMA((len(NEAR),)),
-            pltpu.SemaphoreType.DMA((len(RELAYED),)),
-            pltpu.SemaphoreType.DMA((len(RELAYED),)),
-            pltpu.SemaphoreType.DMA((len(RELAYED),)),
-            pltpu.SemaphoreType.DMA((len(RELAYED),)),
-            pltpu.SemaphoreType.DMA,
+            pltpu.SemaphoreType.DMA((parts, len(NEAR))),
+            pltpu.SemaphoreType.DMA((parts, len(NEAR))),
+            pltpu.SemaphoreType.DMA((parts, len(RELAYED))),
+            pltpu.SemaphoreType.DMA((parts, len(RELAYED))),
+            pltpu.SemaphoreType.DMA((parts, len(RELAYED))),
+            pltpu.SemaphoreType.DMA((parts, len(RELAYED))),
+            pltpu.SemaphoreType.DMA((parts,)),
         ],
         compiler_params=pltpu.CompilerParams(collective_id=collective, has_side_effects=True),
-    )(value)
-    return recv
+    )(*values)
+    return result[:parts]
+
+
+def finish_kernel(targets_ref, product_ref, state_ref, out_ref, acc_ref):
+    vecs = out_ref.shape[2]
+    acc_ref[...] = product_ref[...]
+
+    def subtract(q, carry):
+        state = state_ref[q]
+        contrib = lax.dot_general(
+            state[:, vecs:], state[:, :vecs], (((0,), (0,)), ((), ())),
+            preferred_element_type=jnp.float32,
+        ).astype(jnp.bfloat16)
+        target = targets_ref[q]
+        acc_ref[target] = acc_ref[target] - contrib.astype(jnp.float32)
+        return carry
+
+    lax.fori_loop(0, state_ref.shape[0], subtract, 0)
+    out_ref[...] = acc_ref[...].astype(out_ref.dtype)
+
+
+def finish(product, state_in, targets):
+    vmem = pl.BlockSpec(memory_space=pltpu.VMEM)
+    smem = pl.BlockSpec(memory_space=pltpu.SMEM)
+    return pl.pallas_call(
+        finish_kernel,
+        out_shape=jax.ShapeDtypeStruct(product.shape, jnp.bfloat16),
+        in_specs=[smem, vmem, vmem],
+        out_specs=vmem,
+        scratch_shapes=[pltpu.VMEM(product.shape, jnp.float32)],
+    )(targets, product, state_in)
 
 
 def well_states_of(summed, well_inverse, well_count):
@@ -193,10 +236,9 @@
     in_slots = couple_in.reshape(wells * couplings, seg, cell_count)[slot_order]
     in_slots = in_slots.reshape(dom_count, slot_width * seg * cell_count // vec_count, vec_count)
     halo_flat = halo_pack.reshape(dom_count, halo_width * cell_count, vec_count)
-    send_pack = jnp.concatenate([halo_flat, in_slots], 1)
-    recv_pack = dom_exchange(send_pack, 0)
-    halo_rows = recv_pack[:, : halo_width * cell_count].reshape(dom_count, halo_width, cell_count, vec_count)
-    in_recv = recv_pack[:, halo_width * cell_count :].reshape(dom_count, slot_width, seg, cell_count)
+    halo_recv, in_recv = dom_exchange([halo_flat, in_slots], 0)
+    halo_rows = halo_recv.reshape(dom_count, halo_width, cell_count, vec_count)
+    in_recv = in_recv.reshape(dom_count, slot_width, seg, cell_count)
     well_pack = blocks[well_send[0]]
     partial = jnp.einsum("qcsk,qckv->qcsv", in_recv, well_pack, preferred_element_type=jnp.float32)
     partial_in = lax.all_to_all(partial, "dom", split_axis=0, concat_axis=0, tiled=True)
@@ -209,19 +251,13 @@
     state_pack = state_pack.reshape(dom_count, slot_width, seg, vec_count + cell_count)
     state_in = lax.all_to_all(state_pack, "dom", split_axis=0, concat_axis=0, tiled=True)
     state_in = state_in.reshape(slot_total, seg, vec_count + cell_count)
-    incoming = jnp.einsum(
-        "qsk,qsv->qkv",
-        state_in[:, :, vec_count:],
-        state_in[:, :, :vec_count],
-        preferred_element_type=jnp.float32,
-    ).astype(jnp.bfloat16)
     live_halo = jnp.arange(halo_width)[None, :] < halo_counts[0][:, None]
     halo_rows = jnp.where(live_halo[:, :, None, None], halo_rows, jnp.zeros_like(halo_rows))
     extended = jnp.concatenate(
         [blocks, halo_rows.reshape(dom_count * halo_width, cell_count, vec_count), rim_rows], 0
     )
     product = local_product(extended, tile_values, tile_cols)
-    return subtract_incoming(product, well_send, incoming).astype(jnp.bfloat16)
+    return finish(product, state_in, well_send[0].reshape(-1))
 
 
 def solution(mesh):

time: 171 us -> 175 us (1.023)
  Pallas kernels: 83.1 us -> 101 us
  other arithmetic: 27.1 us -> 18.1 us
  matrix products: 10.5 us -> 4.81 us
  waiting for transfers between devices: 7.51 us -> 11.9 us
  local copies, waits for them, and re-layouts: 22 us -> 19.5 us
    pallas_call x1 -> x2, Pallas kernels: 66.2 us -> 84.2 us  [the longest x1 66.8 us: dom_exchange(): pl.pallas_call(exchange_kernel, out_shape=tuple(outs + relays), in_specs=...]
    slice x2 -> x0, local copies, waits for them, and re-layouts: 5.75 us -> none  [the longest x1 4.66 us: on_device(): recv_pack[:, :halo_width * cell_count]]
    dot_general x2 -> x0, matrix products: 5.71 us -> none  [the longest x1 3.03 us: subtract_incoming(): jnp.einsum('bq,qkv->bkv', selector, flat_rows, preferred_element_type=jnp...]
    concatenate x1 -> x0, other arithmetic: 4.74 us -> none  [on_device(): send_pack = jnp.concatenate([halo_flat, in_slots], 1)]
    all_to_all x1, waiting for transfers between devices: 7.5 us -> 11.9 us  [on_device(): lax.all_to_all(partial, 'dom', split_axis=0, concat_axis=0, tiled=True)]
    convert_element_type x1 -> x0, other arithmetic: 3.65 us -> none  [on_device(): return subtract_incoming(product, well_send, incoming).astype(jnp.bfloat16)]
  transfers between devices with their start and end apart: 4 -> 4, of which waited for: 1 -> 1; matrix products, arithmetic and copies ran while one was open for 17% -> 15% of each run, Pallas kernels for 10% -> 10%
where the time goes in v7:
time: 175 us; the launch traced here: 174 us
  Pallas kernels  101 us (58%)
  local copies, waits for them, and re-layouts  19.5 us (11%)
  other arithmetic  18.1 us (10%)
  starting transfers between devices  17.5 us (10%)
  waiting for transfers between devices  11.9 us (7%)
  matrix products  4.81 us (3%)
    pallas_call x1, Pallas kernels, dom_exchange(): pl.pallas_call(exchange_kernel, out_shape=tuple(outs + relays), in_specs=...  66.8 us
    pallas_call x1, Pallas kernels, finish(): pl.pallas_call(finish_kernel, out_shape=jax.ShapeDtypeStruct(product.shap...  17.4 us
    pallas_call x1, Pallas kernels, local_product(): pl.pallas_call(product_kernel, out_shape=jax.ShapeDtypeStruct((block_rows...  17.1 us
    all_to_all x1, waiting for transfers between devices, on_device(): lax.all_to_all(partial, 'dom', split_axis=0, concat_axis=0, tiled=True)  11.9 us
    all_to_all x1, starting transfers between devices, on_device(): lax.all_to_all(state_pack, 'dom', split_axis=0, concat_axis=0, tiled=True)  6.93 us
    all_to_all x1, starting transfers between devices, on_device(): lax.all_to_all(partial, 'dom', split_axis=0, concat_axis=0, tiled=True)  6.23 us
    concatenate x1, other arithmetic, on_device(): jnp.concatenate([blocks, halo_rows.reshape(dom_count * halo_width, cell_c...  6.07 us
    select_n x1, other arithmetic, on_device(): jnp.where(live_halo[:, :, None, None], halo_rows, jnp.zeros_like(halo_rows))  4.61 us
  transfers between devices with their start and end apart: 4, of which 1 were waited for; matrix products, arithmetic and copies ran while one was open for 15% of the time, Pallas kernels for 10%

profile of v7, /device:TPU:66, one launch (start us, length us, event | category | flops | bytes accessed | tf_op | source)
XLA Modules:
  0.0 173.9 jit_solution(14976642940461495708)
XLA Ops:
  0.0 0.8 compare_select_fusion.1
  0.9 0.1 reshape.195
  1.0 0.8 copy.21
  1.9 2.0 %sort.17 = (s32[64]{0:T(128)}, s32[64]{0:T(128)S(1)}) sort(s32[64]{0:T(128)S(1)} %reshape.183, s32[64]{0:T(128)S(1)} %iota.17), dimensions={0}, to_apply=%region_0.0 | sort | flops 384 | bytes 1024 | tf_op jit(solution)/shard_map/jit(argsort)/sort | solution.py:234
  4.0 0.7 gather_fusion.1
  4.6 1.0 reshape.184.refs_1_
  5.6 2.8 %gather_fusion = bf16[64,128,256]{2,1,0:T(8,128)(2,1)} fusion(bf16[32,128,256]{2,1,0:T(8,128)(2,1)S(1)} %copy-done.2, s32[1024]{0:T(1024)S(1)} %pad_clamp_fusion.5), kind=kCustom, calls=%fused_computation | custom fusion | bytes 8388864 | tf_op jit(solution)/shard_map/gather | solution.py:230
  8.4 66.8 %shard_map.118 = (bf16[16,512,256]{2,1,0:T(8,128)(2,1)}, bf16[16,64,256]{2,1,0:T(8,128)(2,1)}, bf16[14,256,256]{2,1,0:T(8,128)(2,1)}, bf16[14,32,256]{2,1,0:T(8,128)(2,1)}) custom-call(bf16[16,512,256]{2,1,0:T(8,128)(2,1)} %bitcast.32, bf16[16,64,256]{2,1,0:T(8,128)(2,1)} %reshape.184.refs_1_), custom_call_target="tpu_custom_call" | custom-call | tf_op jit(solution)/shard_map/pallas_call | solution.py:142
  75.2 1.2 reshape.186
  76.5 0.1 reshape.219
  76.6 2.8 %gather_fusion.3 = bf16[64,128,256]{2,1,0:T(8,128)(2,1)} fusion(bf16[32,128,256]{2,1,0:T(8,128)(2,1)S(1)} %copy-done.2, s32[1024]{0:T(1024)S(1)} %pad_clamp_fusion.2), kind=kCustom, calls=%fused_computation.3 | custom fusion | bytes 8388864 | tf_op jit(solution)/shard_map/gather | solution.py:242
  79.4 4.2 %fusion.5 = f32[16,4,32,256]{3,2,1,0:T(8,128)} fusion(bf16[16,4,32,128]{3,2,1,0:T(8,128)(2,1)S(1)} %reshape.186, bf16[16,4,128,256]{3,2,1,0:T(8,128)(2,1)} %bitcast.33), kind=kOutput, calls=%fused_computation.35 | convolution fusion | flops 134217728 | bytes 6815744 | tf_op jit(solution)/shard_map/qcsk,qckv->qcsv/dot_general | solution.py:243
  83.7 6.2 %all-to-all-start = ((f32[16,4,32,256]{3,2,1,0:T(8,128)}), f32[16,4,32,256]{3,2,1,0:T(8,128)}, u32[]{:S(2)}, u32[]{:S(2)}) async-start(f32[16,4,32,256]{3,2,1,0:T(8,128)} %fusion.5), calls=%async_computation | async-start | bytes 4194304 | tf_op jit(solution)/shard_map/all_to_all | solution.py:244
  90.0 0.6 gather_fusion.2
  90.6 0.7 fusion.4
  91.3 1.9 %collective-permute-start.1 = (bf16[4,128,256]{2,1,0:T(8,128)(2,1)}, bf16[4,128,256]{2,1,0:T(8,128)(2,1)}, u32[]{:S(2)}, u32[]{:S(2)}) collective-permute-start(bf16[4,128,256]{2,1,0:T(8,128)(2,1)} %get-tuple-element.12), channel_id=1, source_target_pairs={{1,0},{2,1},{3,2},{4,3},{5,4},{6,5},{7,6},{9,8},{10,9},{11,10},{12... | collective-permute-start | bytes 786440 | tf_op jit(solution)/shard_map/ppermute | solution.py:17
  93.2 2.4 %collective-permute-start = (bf16[4,128,256]{2,1,0:T(8,128)(2,1)S(1)}, bf16[4,128,256]{2,1,0:T(8,128)(2,1)}, u32[]{:S(2)}, u32[]{:S(2)}) collective-permute-start(bf16[4,128,256]{2,1,0:T(8,128)(2,1)S(1)} %get-tuple-element.11), channel_id=1, source_target_pairs={{0,1},{1,2},{2,3},{3,4},{4,5},{5,6},{6,7},{8,9},{9,10},{10,11},{11... | collective-permute-start | bytes 786440 | tf_op jit(solution)/shard_map/ppermute | solution.py:16
  95.8 0.6 reshape_squeeze.6.targets_ref
  96.5 0.7 reshape.180.cols_ref
  97.3 0.1 lt.83
  97.4 1.7 gather_fusion.6
  99.7 4.6 %broadcast_select_fusion = bf16[64,128,256]{2,1,0:T(8,128)(2,1)} fusion(bf16[64,128,256]{2,1,0:T(8,128)(2,1)} %bitcast.35, pred[64]{0:T(512)(128)(4,1)S(1)} %lt.83), kind=kLoop, calls=%fused_computation.8 | loop fusion | flops 2097152 | bytes 8388672 | tf_op jit(solution)/shard_map/jit(_where)/select_n | solution.py:255
  104.4 11.9 %all-to-all-done = f32[16,4,32,256]{3,2,1,0:T(8,128)} async-done(((f32[16,4,32,256]{3,2,1,0:T(8,128)}), f32[16,4,32,256]{3,2,1,0:T(8,128)}, u32[]{:S(2)}, u32[]{:S(2)}) %all-to-all-start) | async-done | bytes 2097184 | tf_op jit(solution)/shard_map/all_to_all | solution.py:244
  116.2 3.6 %gather_fusion.4 = f32[64,32,256]{2,1,0:T(8,128)} fusion(f32[64,32,256]{2,1,0:T(8,128)} %bitcast.8, s32[1024]{0:T(1024)S(1)} %pad_clamp_fusion.1), kind=kCustom, calls=%fused_computation.4 | custom fusion | bytes 4194560 | tf_op jit(solution)/shard_map/gather | solution.py:246
  119.8 1.8 %bitcast_reduce_fusion = f32[16,32,256]{2,1,0:T(8,128)S(1)} fusion(f32[64,32,256]{2,1,0:T(8,128)} %gather_fusion.4), kind=kLoop, calls=%fused_computation.9 | loop fusion | flops 393216 | bytes 2621440 | tf_op jit(solution)/shard_map/reduce_sum | solution.py:246
  121.7 0.6 fusion.1
  122.2 1.6 gather_fusion.5
  123.8 2.5 %pad_maximum_fusion.1 = bf16[64,32,384]{2,1,0:T(8,128)(2,1)} fusion(bf16[64,32,128]{2,1,0:T(8,128)(2,1)S(1)} %gather_fusion.6, bf16[64,32,256]{2,1,0:T(8,128)(2,1)} %gather_fusion.5), kind=kLoop, calls=%fused_computation.10 | loop fusion | flops 3145728 | bytes 3145728 | tf_op jit(solution)/shard_map/concatenate | solution.py:250
  126.4 6.9 %all-to-all-start.1 = ((bf16[16,4,32,384]{3,2,1,0:T(8,128)(2,1)}), bf16[16,4,32,384]{3,2,1,0:T(8,128)(2,1)}, u32[]{:S(2)}, u32[]{:S(2)}) async-start(bf16[16,4,32,384]{3,2,1,0:T(8,128)(2,1)} %bitcast.34), calls=%async_computation.1 | async-start | bytes 3145728 | tf_op jit(solution)/shard_map/all_to_all | solution.py:252
  133.3 6.1 %pad_maximum_fusion.ext_ref = bf16[104,128,256]{2,1,0:T(8,128)(2,1)} fusion(bf16[4,128,256]{2,1,0:T(8,128)(2,1)} %collective-permute-done.1, bf16[4,128,256]{2,1,0:T(8,128)(2,1)} %collective-permute-done, bf16[64,128,256]{2,1,0:T(8,128)(2,1)} %broadcast_select_fusion, bf16[32,128,256]{2,1,0:T(8,128)(2,1)S(1)} %copy-done.2), kind=kLoop, calls=%fused_computation.7 | loop fusion | flops 10223616 | bytes 13631488 | tf_op jit(solution)/shard_map/concatenate | solution.py:256
  139.4 17.1 %shard_map.119.product_ref = f32[32,128,256]{2,1,0:T(8,128)} custom-call(s32[512]{0:T(512)} %reshape.180.cols_ref, bf16[104,128,256]{2,1,0:T(8,128)(2,1)} %pad_maximum_fusion.ext_ref, bf16[32,16,128,128]{3,2,1,0:T(8,128)(2,1)} %tiles_ref.1), custom_call_target="tpu_custom_call" | custom-call | flops 4294967296 | bytes 27787264 | tf_op jit(solution)/shard_map/pallas_call | solution.py:48
  156.5 17.4 %shard_map.120 = bf16[32,128,256]{2,1,0:T(8,128)(2,1)} custom-call(s32[64]{0:T(128)} %reshape_squeeze.6.targets_ref, f32[32,128,256]{2,1,0:T(8,128)} %shard_map.119.product_ref, bf16[64,32,384]{2,1,0:T(8,128)(2,1)} %bitcast.15.state_ref), custom_call_target="tpu_custom_call" | custom-call | tf_op jit(solution)/shard_map/pallas_call | solution.py:182
  (38 shorter events, 0.8 us)
Async XLA Ops:
  0.0 4.0 %copy-start = (bf16[16,4,32,128]{3,2,1,0:T(8,128)(2,1)S(1)}, bf16[16,4,32,128]{3,2,1,0:T(8,128)(2,1)}, u32[]{:S(2)}) copy-start(bf16[16,4,32,128]{3,2,1,0:T(8,128)(2,1)} %param.21) | copy-start | bytes 1572868
  0.0 5.6 %copy-start.2 = (bf16[32,128,256]{2,1,0:T(8,128)(2,1)S(1)}, bf16[32,128,256]{2,1,0:T(8,128)(2,1)}, u32[]{:S(2)}) copy-start(bf16[32,128,256]{2,1,0:T(8,128)(2,1)} %param.12) | copy-start | bytes 6291460
  8.4 68.0 %copy-start.5 = (s32[1,16,4]{1,2,0:T(4,128)S(1)}, s32[1,16,4]{1,2,0:T(4,128)}, u32[]{:S(2)}) copy-start(s32[1,16,4]{1,2,0:T(4,128)} %param.18) | copy-start | bytes 772
  79.4 10.5 %copy-start.7 = (s32[1,2,4]{2,1,0:T(2,128)S(1)}, s32[1,2,4]{2,1,0:T(2,128)}, u32[]{:S(2)}) copy-start(s32[1,2,4]{2,1,0:T(2,128)} %param.17) | copy-start | bytes 100
  83.7 12.8 %copy-start.4 = (s32[32,16]{0,1:T(8,128)S(1)}, s32[32,16]{0,1:T(8,128)}, u32[]{:S(2)}) copy-start(s32[32,16]{0,1:T(8,128)} %param.14) | copy-start | bytes 6148
  83.7 13.5 %copy-start.6 = (s32[1,16]{1,0:T(1,128)S(1)}, s32[1,16]{1,0:T(1,128)}, u32[]{:S(2)}) copy-start(s32[1,16]{1,0:T(1,128)} %param.16) | copy-start | bytes 196
  83.7 32.5 %all-to-all-start = ((f32[16,4,32,256]{3,2,1,0:T(8,128)}), f32[16,4,32,256]{3,2,1,0:T(8,128)}, u32[]{:S(2)}, u32[]{:S(2)}) async-start(f32[16,4,32,256]{3,2,1,0:T(8,128)} %fusion.5), calls=%async_computation | async-start | bytes 4194304 | tf_op jit(solution)/shard_map/all_to_all | solution.py:244
  91.3 42.0 %collective-permute-start.1 = (bf16[4,128,256]{2,1,0:T(8,128)(2,1)}, bf16[4,128,256]{2,1,0:T(8,128)(2,1)}, u32[]{:S(2)}, u32[]{:S(2)}) collective-permute-start(bf16[4,128,256]{2,1,0:T(8,128)(2,1)} %get-tuple-element.12), channel_id=1, source_target_pairs={{1,0},{2,1},{3,2},{4,3},{5,4},{6,5},{7,6},{9,8},{10,9},{11,10},{12... | collective-permute-start | bytes 786440 | tf_op jit(solution)/shard_map/ppermute | solution.py:17
  93.2 40.1 %collective-permute-start = (bf16[4,128,256]{2,1,0:T(8,128)(2,1)S(1)}, bf16[4,128,256]{2,1,0:T(8,128)(2,1)}, u32[]{:S(2)}, u32[]{:S(2)}) collective-permute-start(bf16[4,128,256]{2,1,0:T(8,128)(2,1)S(1)} %get-tuple-element.11), channel_id=1, source_target_pairs={{0,1},{1,2},{2,3},{3,4},{4,5},{5,6},{6,7},{8,9},{9,10},{10,11},{11... | collective-permute-start | bytes 786440 | tf_op jit(solution)/shard_map/ppermute | solution.py:16
  104.4 17.3 %copy-start.3 = (f32[16,32,32]{2,1,0:T(8,128)S(1)}, f32[16,32,32]{2,1,0:T(8,128)}, u32[]{:S(2)}) copy-start(f32[16,32,32]{2,1,0:T(8,128)} %param.23) | copy-start | bytes 196612
  126.4 30.1 %all-to-all-start.1 = ((bf16[16,4,32,384]{3,2,1,0:T(8,128)(2,1)}), bf16[16,4,32,384]{3,2,1,0:T(8,128)(2,1)}, u32[]{:S(2)}, u32[]{:S(2)}) async-start(bf16[16,4,32,384]{3,2,1,0:T(8,128)(2,1)} %bitcast.34), calls=%async_computation.1 | async-start | bytes 3145728 | tf_op jit(solution)/shard_map/all_to_all | solution.py:252
  139.4 34.5 %copy-start.1 = (bf16[16,4,32,128]{3,2,1,0:T(8,128)(2,1)S(1)}, bf16[16,4,32,128]{3,2,1,0:T(8,128)(2,1)}, u32[]{:S(2)}) copy-start(bf16[16,4,32,128]{3,2,1,0:T(8,128)(2,1)} %param.21) | copy-start | bytes 1572868

commit v8 on v7

--- a/solution.py
+++ b/solution.py
@@ -158,36 +158,6 @@
     return result[:parts]
 
 
-def finish_kernel(targets_ref, product_ref, state_ref, out_ref, acc_ref):
-    vecs = out_ref.shape[2]
-    acc_ref[...] = product_ref[...]
-
-    def subtract(q, carry):
-        state = state_ref[q]
-        contrib = lax.dot_general(
-            state[:, vecs:], state[:, :vecs], (((0,), (0,)), ((), ())),
-            preferred_element_type=jnp.float32,
-        ).astype(jnp.bfloat16)
-        target = targets_ref[q]
-        acc_ref[target] = acc_ref[target] - contrib.astype(jnp.float32)
-        return carry
-
-    lax.fori_loop(0, state_ref.shape[0], subtract, 0)
-    out_ref[...] = acc_ref[...].astype(out_ref.dtype)
-
-
-def finish(product, state_in, targets):
-    vmem = pl.BlockSpec(memory_space=pltpu.VMEM)
-    smem = pl.BlockSpec(memory_space=pltpu.SMEM)
-    return pl.pallas_call(
-        finish_kernel,
-        out_shape=jax.ShapeDtypeStruct(product.shape, jnp.bfloat16),
-        in_specs=[smem, vmem, vmem],
-        out_specs=vmem,
-        scratch_shapes=[pltpu.VMEM(product.shape, jnp.float32)],
-    )(targets, product, state_in)
-
-
 def well_states_of(summed, well_inverse, well_count):
     wells = summed.shape[0]
     live_mask = (jnp.arange(wells) < well_count[0]).astype(jnp.float32)
@@ -236,12 +206,12 @@
     in_slots = couple_in.reshape(wells * couplings, seg, cell_count)[slot_order]
     in_slots = in_slots.reshape(dom_count, slot_width * seg * cell_count // vec_count, vec_count)
     halo_flat = halo_pack.reshape(dom_count, halo_width * cell_count, vec_count)
-    halo_recv, in_recv = dom_exchange([halo_flat, in_slots], 0)
-    halo_rows = halo_recv.reshape(dom_count, halo_width, cell_count, vec_count)
+    (in_recv,) = dom_exchange([in_slots], 0)
     in_recv = in_recv.reshape(dom_count, slot_width, seg, cell_count)
     well_pack = blocks[well_send[0]]
     partial = jnp.einsum("qcsk,qckv->qcsv", in_recv, well_pack, preferred_element_type=jnp.float32)
     partial_in = lax.all_to_all(partial, "dom", split_axis=0, concat_axis=0, tiled=True)
+    (halo_recv,) = dom_exchange([halo_flat], 1)
     partial_in = partial_in.reshape(slot_total, seg, vec_count)
     summed = jnp.sum(partial_in[well_slot.reshape(-1)].reshape(wells, couplings, seg, vec_count), axis=1)
     well_state = well_states_of(summed, well_inverse, well_count)
@@ -251,13 +221,20 @@
     state_pack = state_pack.reshape(dom_count, slot_width, seg, vec_count + cell_count)
     state_in = lax.all_to_all(state_pack, "dom", split_axis=0, concat_axis=0, tiled=True)
     state_in = state_in.reshape(slot_total, seg, vec_count + cell_count)
+    halo_rows = halo_recv.reshape(dom_count, halo_width, cell_count, vec_count)
     live_halo = jnp.arange(halo_width)[None, :] < halo_counts[0][:, None]
     halo_rows = jnp.where(live_halo[:, :, None, None], halo_rows, jnp.zeros_like(halo_rows))
     extended = jnp.concatenate(
         [blocks, halo_rows.reshape(dom_count * halo_width, cell_count, vec_count), rim_rows], 0
     )
     product = local_product(extended, tile_values, tile_cols)
-    return finish(product, state_in, well_send[0].reshape(-1))
+    incoming = jnp.einsum(
+        "qsk,qsv->qkv",
+        state_in[:, :, vec_count:],
+        state_in[:, :, :vec_count],
+        preferred_element_type=jnp.float32,
+    ).astype(jnp.bfloat16)
+    return subtract_incoming(product, well_send, incoming).astype(jnp.bfloat16)
 
 
 def solution(mesh):

time: 175 us -> 163 us (0.931)
  waiting for transfers between devices: 11.9 us -> 0.01 us
  matrix products: 4.81 us -> 10.5 us
  Pallas kernels: 101 us -> 95.5 us
  other arithmetic: 18.1 us -> 21.6 us
    pallas_call x1 -> x0, Pallas kernels: 17.4 us -> none  [finish(): pl.pallas_call(finish_kernel, out_shape=jax.ShapeDtypeStruct(product.shap...]
    all_to_all x1, waiting for transfers between devices: 11.9 us -> 0.01 us  [on_device(): lax.all_to_all(partial, 'dom', split_axis=0, concat_axis=0, tiled=True)]
    pallas_call x1 -> x2, Pallas kernels: 66.8 us -> 78.5 us  [dom_exchange(): pl.pallas_call(exchange_kernel, out_shape=tuple(outs + relays), in_specs=...]
    dot_general x0 -> x2, matrix products: none -> 5.71 us  [the longest x1 3.02 us: subtract_incoming(): jnp.einsum('bq,qkv->bkv', selector, flat_rows, preferred_element_type=jnp...]
    convert_element_type x0 -> x1, other arithmetic: none -> 3.65 us  [on_device(): return subtract_incoming(product, well_send, incoming).astype(jnp.bfloat16)]
    all_to_all x1, starting transfers between devices: 6.93 us -> 5.15 us  [on_device(): lax.all_to_all(state_pack, 'dom', split_axis=0, concat_axis=0, tiled=True)]
  transfers between devices with their start and end apart: 4 -> 4, of which waited for: 1 -> 0; matrix products, arithmetic and copies ran while one was open for 15% -> 17% of each run, Pallas kernels for 10% -> 50%
where the time goes in v8:
time: 163 us
  Pallas kernels  95.5 us (59%)
  other arithmetic  21.6 us (13%)
  local copies, waits for them, and re-layouts  18.1 us (11%)
  starting transfers between devices  16 us (10%)
  matrix products  10.5 us (6%)
    pallas_call x2, Pallas kernels, dom_exchange(): pl.pallas_call(exchange_kernel, out_shape=tuple(outs + relays), in_specs=...  78.5 us
    pallas_call x1, Pallas kernels, local_product(): pl.pallas_call(product_kernel, out_shape=jax.ShapeDtypeStruct((block_rows...  17 us
    all_to_all x1, starting transfers between devices, on_device(): lax.all_to_all(partial, 'dom', split_axis=0, concat_axis=0, tiled=True)  6.51 us
    concatenate x1, other arithmetic, on_device(): jnp.concatenate([blocks, halo_rows.reshape(dom_count * halo_width, cell_c...  6.07 us
    all_to_all x1, starting transfers between devices, on_device(): lax.all_to_all(state_pack, 'dom', split_axis=0, concat_axis=0, tiled=True)  5.15 us
    select_n x1, other arithmetic, on_device(): jnp.where(live_halo[:, :, None, None], halo_rows, jnp.zeros_like(halo_rows))  4.61 us
    dot_general x1, matrix products, on_device(): jnp.einsum('qcsk,qckv->qcsv', in_recv, well_pack, preferred_element_type=...  4.22 us
    convert_element_type x1, other arithmetic, on_device(): return subtract_incoming(product, well_send, incoming).astype(jnp.bfloat16)  3.65 us
  transfers between devices with their start and end apart: 4, of which 0 were waited for; matrix products, arithmetic and copies ran while one was open for 17% of the time, Pallas kernels for 50%

profile of v8, /device:TPU:66, one launch (start us, length us, event | category | flops | bytes accessed | tf_op | source)
XLA Modules:
  0.0 162.5 jit_solution(7380036816780864816)
XLA Ops:
  0.0 0.9 copy.22
  1.0 2.0 %sort.17 = (s32[64]{0:T(128)}, s32[64]{0:T(128)S(1)}) sort(s32[64]{0:T(128)S(1)} %reshape.185, s32[64]{0:T(128)S(1)} %iota.21), dimensions={0}, to_apply=%region_0.0 | sort | flops 384 | bytes 1024 | tf_op jit(solution)/shard_map/jit(argsort)/sort | solution.py:204
  3.1 0.7 gather_fusion.2
  3.7 1.0 reshape.186.refs_0_
  4.7 14.3 %shard_map.120 = (bf16[16,64,256]{2,1,0:T(8,128)(2,1)}, bf16[14,32,256]{2,1,0:T(8,128)(2,1)}) custom-call(bf16[16,64,256]{2,1,0:T(8,128)(2,1)} %reshape.186.refs_0_), custom_call_target="tpu_custom_call" | custom-call | tf_op jit(solution)/shard_map/pallas_call | solution.py:142
  19.0 1.2 reshape.187
  20.3 0.7 compare_select_fusion
  21.1 2.8 %gather_fusion.3 = bf16[64,128,256]{2,1,0:T(8,128)(2,1)} fusion(bf16[32,128,256]{2,1,0:T(8,128)(2,1)S(1)} %copy-done.2, s32[1024]{0:T(1024)S(1)} %pad_clamp_fusion.2), kind=kCustom, calls=%fused_computation.3 | custom fusion | bytes 8388864 | tf_op jit(solution)/shard_map/gather | solution.py:211
  23.9 4.2 %fusion.13 = f32[16,4,32,256]{3,2,1,0:T(8,128)} fusion(bf16[16,4,32,128]{3,2,1,0:T(8,128)(2,1)S(1)} %reshape.187, bf16[16,4,128,256]{3,2,1,0:T(8,128)(2,1)} %bitcast.36), kind=kOutput, calls=%fused_computation.45 | convolution fusion | flops 134217728 | bytes 6815744 | tf_op jit(solution)/shard_map/qcsk,qckv->qcsv/dot_general | solution.py:212
  28.1 6.5 %all-to-all-start = ((f32[16,4,32,256]{3,2,1,0:T(8,128)}), f32[16,4,32,256]{3,2,1,0:T(8,128)}, u32[]{:S(2)}, u32[]{:S(2)}) async-start(f32[16,4,32,256]{3,2,1,0:T(8,128)} %fusion.13), calls=%async_computation | async-start | bytes 4194304 | tf_op jit(solution)/shard_map/all_to_all | solution.py:213
  34.8 0.6 gather_fusion.1
  35.3 0.7 fusion.12
  36.1 1.9 %collective-permute-start.1 = (bf16[4,128,256]{2,1,0:T(8,128)(2,1)}, bf16[4,128,256]{2,1,0:T(8,128)(2,1)}, u32[]{:S(2)}, u32[]{:S(2)}) collective-permute-start(bf16[4,128,256]{2,1,0:T(8,128)(2,1)} %get-tuple-element.12), channel_id=1, source_target_pairs={{1,0},{2,1},{3,2},{4,3},{5,4},{6,5},{7,6},{9,8},{10,9},{11,10},{12... | collective-permute-start | bytes 786440 | tf_op jit(solution)/shard_map/ppermute | solution.py:17
  38.0 2.4 %collective-permute-start = (bf16[4,128,256]{2,1,0:T(8,128)(2,1)S(1)}, bf16[4,128,256]{2,1,0:T(8,128)(2,1)}, u32[]{:S(2)}, u32[]{:S(2)}) collective-permute-start(bf16[4,128,256]{2,1,0:T(8,128)(2,1)S(1)} %get-tuple-element.11), channel_id=1, source_target_pairs={{0,1},{1,2},{2,3},{3,4},{4,5},{5,6},{6,7},{8,9},{9,10},{10,11},{11... | collective-permute-start | bytes 786440 | tf_op jit(solution)/shard_map/ppermute | solution.py:16
  40.7 0.7 reshape.181.cols_ref
  41.4 0.1 reshape.196
  41.5 2.8 %gather_fusion = bf16[64,128,256]{2,1,0:T(8,128)(2,1)} fusion(bf16[32,128,256]{2,1,0:T(8,128)(2,1)S(1)} %copy-done.2, s32[1024]{0:T(1024)S(1)} %pad_clamp_fusion.5), kind=kCustom, calls=%fused_computation | custom fusion | bytes 8388864 | tf_op jit(solution)/shard_map/gather | solution.py:200
  44.3 64.2 %shard_map.118 = (bf16[16,512,256]{2,1,0:T(8,128)(2,1)}, bf16[14,256,256]{2,1,0:T(8,128)(2,1)}) custom-call(bf16[16,512,256]{2,1,0:T(8,128)(2,1)} %bitcast.35), custom_call_target="tpu_custom_call" | custom-call | tf_op jit(solution)/shard_map/pallas_call | solution.py:142
  108.6 0.1 lt.83
  108.7 0.7 gather_fusion.6
  110.1 4.6 %broadcast_select_fusion = bf16[64,128,256]{2,1,0:T(8,128)(2,1)} fusion(bf16[64,128,256]{2,1,0:T(8,128)(2,1)} %bitcast.38, pred[64]{0:T(512)(128)(4,1)S(1)} %lt.83), kind=kLoop, calls=%fused_computation.12 | loop fusion | flops 2097152 | bytes 8388672 | tf_op jit(solution)/shard_map/jit(_where)/select_n | solution.py:226
  114.7 3.6 %gather_fusion.4 = f32[64,32,256]{2,1,0:T(8,128)} fusion(f32[64,32,256]{2,1,0:T(8,128)} %bitcast.9, s32[1024]{0:T(1024)S(1)} %pad_clamp_fusion.1), kind=kCustom, calls=%fused_computation.4 | custom fusion | bytes 4194560 | tf_op jit(solution)/shard_map/gather | solution.py:216
  118.4 1.8 %bitcast_reduce_fusion = f32[16,32,256]{2,1,0:T(8,128)S(1)} fusion(f32[64,32,256]{2,1,0:T(8,128)} %gather_fusion.4), kind=kLoop, calls=%fused_computation.13 | loop fusion | flops 393216 | bytes 2621440 | tf_op jit(solution)/shard_map/reduce_sum | solution.py:216
  120.2 0.6 fusion.3
  120.8 1.6 gather_fusion.5
  122.4 2.5 %pad_maximum_fusion.1 = bf16[64,32,384]{2,1,0:T(8,128)(2,1)} fusion(bf16[64,32,128]{2,1,0:T(8,128)(2,1)S(1)} %gather_fusion.6, bf16[64,32,256]{2,1,0:T(8,128)(2,1)} %gather_fusion.5), kind=kLoop, calls=%fused_computation.14 | loop fusion | flops 3145728 | bytes 3145728 | tf_op jit(solution)/shard_map/concatenate | solution.py:220
  124.9 5.2 %all-to-all-start.1 = ((bf16[16,4,32,384]{3,2,1,0:T(8,128)(2,1)}), bf16[16,4,32,384]{3,2,1,0:T(8,128)(2,1)}, u32[]{:S(2)}, u32[]{:S(2)}) async-start(bf16[16,4,32,384]{3,2,1,0:T(8,128)(2,1)} %bitcast.37), calls=%async_computation.1 | async-start | bytes 3145728 | tf_op jit(solution)/shard_map/all_to_all | solution.py:222
  130.1 6.1 %pad_maximum_fusion.ext_ref = bf16[104,128,256]{2,1,0:T(8,128)(2,1)} fusion(bf16[4,128,256]{2,1,0:T(8,128)(2,1)} %collective-permute-done.1, bf16[4,128,256]{2,1,0:T(8,128)(2,1)} %collective-permute-done, bf16[64,128,256]{2,1,0:T(8,128)(2,1)} %broadcast_select_fusion, bf16[32,128,256]{2,1,0:T(8,128)(2,1)S(1)} %copy-done.2), kind=kLoop, calls=%fused_computation.8 | loop fusion | flops 10223616 | bytes 13631488 | tf_op jit(solution)/shard_map/concatenate | solution.py:227
  136.2 17.0 %shard_map.119 = f32[32,128,256]{2,1,0:T(8,128)} custom-call(s32[512]{0:T(512)} %reshape.181.cols_ref, bf16[104,128,256]{2,1,0:T(8,128)(2,1)} %pad_maximum_fusion.ext_ref, bf16[32,16,128,128]{3,2,1,0:T(8,128)(2,1)} %tiles_ref.1), custom_call_target="tpu_custom_call" | custom-call | flops 4294967296 | bytes 27787264 | tf_op jit(solution)/shard_map/pallas_call | solution.py:48
  153.1 2.7 %fusion.4 = bf16[64,128,256]{2,1,0:T(8,128)(2,1)S(1)} fusion(bf16[64,32,384]{2,1,0:T(8,128)(2,1)} %bitcast.16), kind=kOutput, calls=%fused_computation.18 | convolution fusion | flops 134217728 | bytes 5767168 | tf_op jit(solution)/shard_map/qsk,qsv->qkv/dot_general | solution.py:231
  155.8 3.0 %fusion = f32[32,128,256]{2,0,1:T(8,128)S(1)} fusion(bf16[64,128,256]{2,1,0:T(8,128)(2,1)S(1)} %fusion.4, s32[64]{0:T(128)S(1)} %eq.15), kind=kOutput, calls=%fused_computation.9 | convolution fusion | flops 134219776 | bytes 8388864 | tf_op jit(solution)/shard_map/bq,qkv->bkv/dot_general | solution.py:172
  158.9 3.7 %fusion.1 = bf16[32,128,256]{2,1,0:T(8,128)(2,1)} fusion(f32[32,128,256]{2,1,0:T(8,128)S(1)} %copy-done.3, f32[32,128,256]{2,0,1:T(8,128)S(1)} %fusion), kind=kLoop, calls=%fused_computation.11 | loop fusion | flops 2097152 | bytes 10485760 | tf_op jit(solution)/shard_map/convert_element_type | solution.py:237
  (47 shorter events, 0.9 us)
Async XLA Ops:
  0.0 3.1 %copy-start = (bf16[16,4,32,128]{3,2,1,0:T(8,128)(2,1)S(1)}, bf16[16,4,32,128]{3,2,1,0:T(8,128)(2,1)}, u32[]{:S(2)}) copy-start(bf16[16,4,32,128]{3,2,1,0:T(8,128)(2,1)} %param.21) | copy-start | bytes 1572868
  0.0 21.1 %copy-start.2 = (bf16[32,128,256]{2,1,0:T(8,128)(2,1)S(1)}, bf16[32,128,256]{2,1,0:T(8,128)(2,1)}, u32[]{:S(2)}) copy-start(bf16[32,128,256]{2,1,0:T(8,128)(2,1)} %param.12) | copy-start | bytes 6291460
  23.9 10.7 %copy-start.10 = (s32[1,2,4]{2,1,0:T(2,128)S(1)}, s32[1,2,4]{2,1,0:T(2,128)}, u32[]{:S(2)}) copy-start(s32[1,2,4]{2,1,0:T(2,128)} %param.17) | copy-start | bytes 100
  28.1 12.4 %copy-start.7 = (s32[1,16,4]{1,2,0:T(4,128)S(1)}, s32[1,16,4]{1,2,0:T(4,128)}, u32[]{:S(2)}) copy-start(s32[1,16,4]{1,2,0:T(4,128)} %param.18) | copy-start | bytes 772
  28.1 12.4 %copy-start.6 = (s32[32,16]{0,1:T(8,128)S(1)}, s32[32,16]{0,1:T(8,128)}, u32[]{:S(2)}) copy-start(s32[32,16]{0,1:T(8,128)} %param.14) | copy-start | bytes 6148
  28.1 13.2 %copy-start.8 = (s32[1,16,4]{1,2,0:T(4,128)S(1)}, s32[1,16,4]{1,2,0:T(4,128)}, u32[]{:S(2)}) copy-start(s32[1,16,4]{1,2,0:T(4,128)} %param.15) | copy-start | bytes 772
  28.1 86.6 %all-to-all-start = ((f32[16,4,32,256]{3,2,1,0:T(8,128)}), f32[16,4,32,256]{3,2,1,0:T(8,128)}, u32[]{:S(2)}, u32[]{:S(2)}) async-start(f32[16,4,32,256]{3,2,1,0:T(8,128)} %fusion.13), calls=%async_computation | async-start | bytes 4194304 | tf_op jit(solution)/shard_map/all_to_all | solution.py:213
  36.1 94.0 %collective-permute-start.1 = (bf16[4,128,256]{2,1,0:T(8,128)(2,1)}, bf16[4,128,256]{2,1,0:T(8,128)(2,1)}, u32[]{:S(2)}, u32[]{:S(2)}) collective-permute-start(bf16[4,128,256]{2,1,0:T(8,128)(2,1)} %get-tuple-element.12), channel_id=1, source_target_pairs={{1,0},{2,1},{3,2},{4,3},{5,4},{6,5},{7,6},{9,8},{10,9},{11,10},{12... | collective-permute-start | bytes 786440 | tf_op jit(solution)/shard_map/ppermute | solution.py:17
  38.0 92.1 %collective-permute-start = (bf16[4,128,256]{2,1,0:T(8,128)(2,1)S(1)}, bf16[4,128,256]{2,1,0:T(8,128)(2,1)}, u32[]{:S(2)}, u32[]{:S(2)}) collective-permute-start(bf16[4,128,256]{2,1,0:T(8,128)(2,1)S(1)} %get-tuple-element.11), channel_id=1, source_target_pairs={{0,1},{1,2},{2,3},{3,4},{4,5},{5,6},{6,7},{8,9},{9,10},{10,11},{11... | collective-permute-start | bytes 786440 | tf_op jit(solution)/shard_map/ppermute | solution.py:16
  44.3 64.2 %copy-start.9 = (s32[1,16]{1,0:T(1,128)S(1)}, s32[1,16]{1,0:T(1,128)}, u32[]{:S(2)}) copy-start(s32[1,16]{1,0:T(1,128)} %param.16) | copy-start | bytes 196
  44.3 64.4 %copy-start.4 = (bf16[16,4,32,128]{3,2,1,0:T(8,128)(2,1)S(1)}, bf16[16,4,32,128]{3,2,1,0:T(8,128)(2,1)}, u32[]{:S(2)}) copy-start(bf16[16,4,32,128]{3,2,1,0:T(8,128)(2,1)} %param.22) | copy-start | bytes 1572868
  114.7 5.5 %copy-start.5 = (f32[16,32,32]{2,1,0:T(8,128)S(1)}, f32[16,32,32]{2,1,0:T(8,128)}, u32[]{:S(2)}) copy-start(f32[16,32,32]{2,1,0:T(8,128)} %param.23) | copy-start | bytes 196612
  124.9 28.2 %all-to-all-start.1 = ((bf16[16,4,32,384]{3,2,1,0:T(8,128)(2,1)}), bf16[16,4,32,384]{3,2,1,0:T(8,128)(2,1)}, u32[]{:S(2)}, u32[]{:S(2)}) async-start(bf16[16,4,32,384]{3,2,1,0:T(8,128)(2,1)} %bitcast.37), calls=%async_computation.1 | async-start | bytes 3145728 | tf_op jit(solution)/shard_map/all_to_all | solution.py:222
  155.8 3.0 %copy-start.3 = (f32[32,128,256]{2,1,0:T(8,128)S(1)}, f32[32,128,256]{2,1,0:T(8,128)}, u32[]{:S(2)}) copy-start(f32[32,128,256]{2,1,0:T(8,128)} %shard_map.119) | copy-start | bytes 12582916
  155.8 6.7 %copy-start.1 = (bf16[16,4,32,128]{3,2,1,0:T(8,128)(2,1)S(1)}, bf16[16,4,32,128]{3,2,1,0:T(8,128)(2,1)}, u32[]{:S(2)}) copy-start(bf16[16,4,32,128]{3,2,1,0:T(8,128)(2,1)} %param.21) | copy-start | bytes 1572868

commit v9 on v8

--- a/solution.py
+++ b/solution.py
@@ -19,29 +19,30 @@
     return value
 
 
-def product_kernel(cols_ref, ext_ref, tiles_ref, out_ref):
+def product_kernel(cols_ref, live_ref, ext_ref, tiles_ref, out_ref):
     rows, tiles_per_row = tiles_ref.shape[0], tiles_ref.shape[1]
     first = pl.program_id(0) * rows
     for r in range(rows):
         acc = jnp.zeros(out_ref.shape[1:], jnp.float32)
         for t in range(tiles_per_row):
             col = cols_ref[(first + r) * tiles_per_row + t]
-            acc = acc + jnp.dot(tiles_ref[r, t], ext_ref[col], preferred_element_type=jnp.float32)
+            scale = live_ref[col].astype(jnp.float32)
+            acc = acc + scale * jnp.dot(tiles_ref[r, t], ext_ref[col], preferred_element_type=jnp.float32)
         out_ref[r] = acc
 
 
-def local_product(extended, tile_values, tile_cols):
+def local_product(extended, live, tile_values, tile_cols):
     block_rows, tiles_per_row, cells, _ = tile_values.shape
     ext_blocks, _, vecs = extended.shape
     rows = 4
     grid_spec = pltpu.PrefetchScalarGridSpec(
-        num_scalar_prefetch=1,
+        num_scalar_prefetch=2,
         grid=(block_rows // rows,),
         in_specs=[
-            pl.BlockSpec((ext_blocks, cells, vecs), lambda k, cols: (0, 0, 0)),
-            pl.BlockSpec((rows, tiles_per_row, cells, cells), lambda k, cols: (k, 0, 0, 0)),
+            pl.BlockSpec((ext_blocks, cells, vecs), lambda k, cols, live: (0, 0, 0)),
+            pl.BlockSpec((rows, tiles_per_row, cells, cells), lambda k, cols, live: (k, 0, 0, 0)),
         ],
-        out_specs=pl.BlockSpec((rows, cells, vecs), lambda k, cols: (k, 0, 0)),
+        out_specs=pl.BlockSpec((rows, cells, vecs), lambda k, cols, live: (k, 0, 0)),
     )
     flops = 2 * block_rows * tiles_per_row * cells * cells * vecs
     moved = tile_values.size * 2 + extended.size * 2 + block_rows * cells * vecs * 4
@@ -50,7 +51,25 @@
         out_shape=jax.ShapeDtypeStruct((block_rows, cells, vecs), jnp.float32),
         grid_spec=grid_spec,
         cost_estimate=pl.CostEstimate(flops=flops, transcendentals=0, bytes_accessed=moved),
-    )(tile_cols.reshape(-1), extended, tile_values)
+    )(tile_cols.reshape(-1), live, extended, tile_values)
+
+
+def partial_kernel(index_ref, couple_ref, blocks_ref, out_ref):
+    for q in range(out_ref.shape[0]):
+        out_ref[q] = jnp.dot(
+            couple_ref[q], blocks_ref[index_ref[q]], preferred_element_type=jnp.float32
+        )
+
+
+def partial_sums(index, couple, blocks):
+    slots, seg, _ = couple.shape
+    vmem = pl.BlockSpec(memory_space=pltpu.VMEM)
+    return pl.pallas_call(
+        partial_kernel,
+        out_shape=jax.ShapeDtypeStruct((slots, seg, blocks.shape[2]), jnp.float32),
+        in_specs=[pl.BlockSpec(memory_space=pltpu.SMEM), vmem, vmem],
+        out_specs=vmem,
+    )(index, couple, blocks)
 
 
 SIDE = 4
@@ -208,8 +227,9 @@
     halo_flat = halo_pack.reshape(dom_count, halo_width * cell_count, vec_count)
     (in_recv,) = dom_exchange([in_slots], 0)
     in_recv = in_recv.reshape(dom_count, slot_width, seg, cell_count)
-    well_pack = blocks[well_send[0]]
-    partial = jnp.einsum("qcsk,qckv->qcsv", in_recv, well_pack, preferred_element_type=jnp.float32)
+    partial = partial_sums(
+        well_send[0].reshape(-1), in_recv.reshape(slot_total, seg, cell_count), blocks
+    ).reshape(dom_count, slot_width, seg, vec_count)
     partial_in = lax.all_to_all(partial, "dom", split_axis=0, concat_axis=0, tiled=True)
     (halo_recv,) = dom_exchange([halo_flat], 1)
     partial_in = partial_in.reshape(slot_total, seg, vec_count)
@@ -222,12 +242,14 @@
     state_in = lax.all_to_all(state_pack, "dom", split_axis=0, concat_axis=0, tiled=True)
     state_in = state_in.reshape(slot_total, seg, vec_count + cell_count)
     halo_rows = halo_recv.reshape(dom_count, halo_width, cell_count, vec_count)
-    live_halo = jnp.arange(halo_width)[None, :] < halo_counts[0][:, None]
-    halo_rows = jnp.where(live_halo[:, :, None, None], halo_rows, jnp.zeros_like(halo_rows))
+    live_halo = (jnp.arange(halo_width)[None, :] < halo_counts[0][:, None]).astype(jnp.int32)
+    live = jnp.concatenate(
+        [jnp.ones((blocks.shape[0],), jnp.int32), live_halo.reshape(-1), jnp.ones((2 * rim_width,), jnp.int32)]
+    )
     extended = jnp.concatenate(
         [blocks, halo_rows.reshape(dom_count * halo_width, cell_count, vec_count), rim_rows], 0
     )
-    product = local_product(extended, tile_values, tile_cols)
+    product = local_product(extended, live, tile_values, tile_cols)
     incoming = jnp.einsum(
         "qsk,qsv->qkv",
         state_in[:, :, vec_count:],

time: 163 us -> 157 us (0.963)
  other arithmetic: 21.6 us -> 16.7 us
  Pallas kernels: 95.5 us -> 99.7 us
  matrix products: 10.5 us -> 6.3 us
    select_n x2 -> x0, other arithmetic: 5.3 us -> none  [the longest x1 4.61 us: on_device(): jnp.where(live_halo[:, :, None, None], halo_rows, jnp.zeros_like(halo_rows))]
    dot_general x1 -> x0, matrix products: 4.22 us -> none  [on_device(): jnp.einsum('qcsk,qckv->qcsv', in_recv, well_pack, preferred_element_type=...]
    pallas_call x0 -> x1, Pallas kernels: none -> 3.91 us  [partial_sums(): pl.pallas_call(partial_kernel, out_shape=jax.ShapeDtypeStruct((slots, seg...]
    gather x1 -> x0, local copies, waits for them, and re-layouts: 2.77 us -> none  [on_device(): well_pack = blocks[well_send[0]]]
    another operation x0 -> x2, local copies, waits for them, and re-layouts: none -> 2 us  [the longest x1 2 us: on_device(): in_recv.reshape(slot_total, seg, cell_count)]
  transfers between devices with their start and end apart: 4 -> 4, of which waited for: 0 -> 0; matrix products, arithmetic and copies ran while one was open for 17% -> 14% of each run, Pallas kernels for 50% -> 52%
where the time goes in v9:
time: 157 us; the launch traced here: 156 us
  Pallas kernels  99.7 us (64%)
  local copies, waits for them, and re-layouts  16.9 us (11%)
  other arithmetic  16.7 us (11%)
  starting transfers between devices  15.3 us (10%)
  matrix products  6.3 us (4%)
    pallas_call x2, Pallas kernels, dom_exchange(): pl.pallas_call(exchange_kernel, out_shape=tuple(outs + relays), in_specs=...  78.8 us
    pallas_call x1, Pallas kernels, local_product(): pl.pallas_call(product_kernel, out_shape=jax.ShapeDtypeStruct((block_rows...  17.1 us
    all_to_all x1, starting transfers between devices, on_device(): lax.all_to_all(partial, 'dom', split_axis=0, concat_axis=0, tiled=True)  6.51 us
    concatenate x1, other arithmetic, on_device(): jnp.concatenate([blocks, halo_rows.reshape(dom_count * halo_width, cell_c...  6.07 us
    all_to_all x1, starting transfers between devices, on_device(): lax.all_to_all(state_pack, 'dom', split_axis=0, concat_axis=0, tiled=True)  4.51 us
    pallas_call x1, Pallas kernels, partial_sums(): pl.pallas_call(partial_kernel, out_shape=jax.ShapeDtypeStruct((slots, seg...  3.91 us
    convert_element_type x1, other arithmetic, on_device(): return subtract_incoming(product, well_send, incoming).astype(jnp.bfloat16)  3.65 us
    gather x1, local copies, waits for them, and re-layouts, on_device(): partial_in[well_slot.reshape(-1)].reshape(wells, couplings, seg, vec_count)  3.59 us
  transfers between devices with their start and end apart: 4, of which 0 were waited for; matrix products, arithmetic and copies ran while one was open for 14% of the time, Pallas kernels for 52%

profile of v9, /device:TPU:66, one launch (start us, length us, event | category | flops | bytes accessed | tf_op | source)
XLA Modules:
  0.0 155.9 jit_solution(8332131868146371962)
XLA Ops:
  0.0 0.8 copy.21
  0.9 2.0 %sort.17 = (s32[64]{0:T(128)}, s32[64]{0:T(128)S(1)}) sort(s32[64]{0:T(128)S(1)} %reshape.136, s32[64]{0:T(128)S(1)} %iota.17), dimensions={0}, to_apply=%region_0.0 | sort | flops 384 | bytes 1024 | tf_op jit(solution)/shard_map/jit(argsort)/sort | solution.py:223
  3.0 0.8 copy.20
  3.7 0.6 eq.15.index_ref
  4.4 0.7 gather_fusion.2
  5.0 1.0 reshape.137.refs_0_
  6.0 14.3 %shard_map.120 = (bf16[16,64,256]{2,1,0:T(8,128)(2,1)}, bf16[14,32,256]{2,1,0:T(8,128)(2,1)}) custom-call(bf16[16,64,256]{2,1,0:T(8,128)(2,1)} %reshape.137.refs_0_), custom_call_target="tpu_custom_call" | custom-call | tf_op jit(solution)/shard_map/pallas_call | solution.py:161
  20.3 2.0 %reshape_reshape.7.couple_ref = bf16[64,32,128]{2,1,0:T(8,128)(2,1)} reshape(bf16[16,64,256]{2,1,0:T(8,128)(2,1)} %get-tuple-element.10) | data formatting | bytes 1048576 | tf_op jit(solution)/shard_map/reshape;reshape | solution.py:231
  22.3 3.9 %shard_map.121 = f32[64,32,256]{2,1,0:T(8,128)} custom-call(s32[64]{0:T(128)} %eq.15.index_ref, bf16[64,32,128]{2,1,0:T(8,128)(2,1)} %reshape_reshape.7.couple_ref, bf16[32,128,256]{2,1,0:T(8,128)(2,1)} %blocks_ref.1), custom_call_target="tpu_custom_call" | custom-call | tf_op jit(solution)/shard_map/pallas_call | solution.py:67
  26.2 6.5 %all-to-all-start = ((f32[16,4,32,256]{3,2,1,0:T(8,128)}), f32[16,4,32,256]{3,2,1,0:T(8,128)}, u32[]{:S(2)}, u32[]{:S(2)}) async-start(f32[16,4,32,256]{3,2,1,0:T(8,128)} %bitcast.30), calls=%async_computation | async-start | bytes 4194304 | tf_op jit(solution)/shard_map/all_to_all | solution.py:233
  32.9 0.6 gather_fusion.1
  33.4 0.8 fusion.13
  34.3 1.9 %collective-permute-start.1 = (bf16[4,128,256]{2,1,0:T(8,128)(2,1)}, bf16[4,128,256]{2,1,0:T(8,128)(2,1)}, u32[]{:S(2)}, u32[]{:S(2)}) collective-permute-start(bf16[4,128,256]{2,1,0:T(8,128)(2,1)} %get-tuple-element.12), channel_id=1, source_target_pairs={{1,0},{2,1},{3,2},{4,3},{5,4},{6,5},{7,6},{9,8},{10,9},{11,10},{12... | collective-permute-start | bytes 786440 | tf_op jit(solution)/shard_map/ppermute | solution.py:17
  36.2 2.4 %collective-permute-start = (bf16[4,128,256]{2,1,0:T(8,128)(2,1)}, bf16[4,128,256]{2,1,0:T(8,128)(2,1)}, u32[]{:S(2)}, u32[]{:S(2)}) collective-permute-start(bf16[4,128,256]{2,1,0:T(8,128)(2,1)} %get-tuple-element.11), channel_id=1, source_target_pairs={{0,1},{1,2},{2,3},{3,4},{4,5},{5,6},{6,7},{8,9},{9,10},{10,11},{11... | collective-permute-start | bytes 786440 | tf_op jit(solution)/shard_map/ppermute | solution.py:16
  38.8 0.7 reshape.133.cols_ref
  39.5 0.1 reshape.145
  39.7 0.1 reshape.148
  39.8 2.8 %gather_fusion = bf16[64,128,256]{2,1,0:T(8,128)(2,1)} fusion(bf16[32,128,256]{2,1,0:T(8,128)(2,1)S(1)} %copy-done.2, s32[1024]{0:T(1024)S(1)} %pad_clamp_fusion.4), kind=kCustom, calls=%fused_computation | custom fusion | bytes 8388864 | tf_op jit(solution)/shard_map/gather | solution.py:219
  42.6 64.5 %shard_map.118 = (bf16[16,512,256]{2,1,0:T(8,128)(2,1)}, bf16[14,256,256]{2,1,0:T(8,128)(2,1)}) custom-call(bf16[16,512,256]{2,1,0:T(8,128)(2,1)} %bitcast.29), custom_call_target="tpu_custom_call" | custom-call | tf_op jit(solution)/shard_map/pallas_call | solution.py:161
  107.1 1.4 gather_fusion.5
  109.2 0.6 pad_add_fusion.live_ref
  109.8 3.6 %gather_fusion.3 = f32[64,32,256]{2,1,0:T(8,128)} fusion(f32[64,32,256]{2,1,0:T(8,128)} %bitcast.8, s32[1024]{0:T(1024)S(1)} %pad_clamp_fusion.1), kind=kCustom, calls=%fused_computation.3 | custom fusion | bytes 4194560 | tf_op jit(solution)/shard_map/gather | solution.py:236
  113.4 1.8 %bitcast_reduce_fusion = f32[16,32,256]{2,1,0:T(8,128)S(1)} fusion(f32[64,32,256]{2,1,0:T(8,128)} %gather_fusion.3), kind=kLoop, calls=%fused_computation.11 | loop fusion | flops 393216 | bytes 2621440 | tf_op jit(solution)/shard_map/reduce_sum | solution.py:236
  115.3 0.6 fusion.3
  115.9 0.6 gather_fusion.4
  116.5 2.4 %pad_maximum_fusion.1 = bf16[64,32,384]{2,1,0:T(8,128)(2,1)} fusion(bf16[64,32,128]{2,1,0:T(8,128)(2,1)} %gather_fusion.5, bf16[64,32,256]{2,1,0:T(8,128)(2,1)S(1)} %gather_fusion.4), kind=kLoop, calls=%fused_computation.12 | loop fusion | flops 3145728 | bytes 3145728 | tf_op jit(solution)/shard_map/concatenate | solution.py:240
  118.8 4.5 %all-to-all-start.1 = ((bf16[16,4,32,384]{3,2,1,0:T(8,128)(2,1)}), bf16[16,4,32,384]{3,2,1,0:T(8,128)(2,1)}, u32[]{:S(2)}, u32[]{:S(2)}) async-start(bf16[16,4,32,384]{3,2,1,0:T(8,128)(2,1)} %bitcast.31), calls=%async_computation.1 | async-start | bytes 3145728 | tf_op jit(solution)/shard_map/all_to_all | solution.py:242
  123.4 6.1 %pad_maximum_fusion.ext_ref = bf16[104,128,256]{2,1,0:T(8,128)(2,1)} fusion(bf16[4,128,256]{2,1,0:T(8,128)(2,1)} %collective-permute-done.1, bf16[4,128,256]{2,1,0:T(8,128)(2,1)} %collective-permute-done, bf16[64,128,256]{2,1,0:T(8,128)(2,1)} %bitcast.32, bf16[32,128,256]{2,1,0:T(8,128)(2,1)S(1)} %copy-done.2), kind=kLoop, calls=%fused_computation.7 | loop fusion | flops 10223616 | bytes 13631488 | tf_op jit(solution)/shard_map/concatenate | solution.py:249
  129.4 17.1 %shard_map.119 = f32[32,128,256]{2,1,0:T(8,128)} custom-call(s32[512]{0:T(512)} %reshape.133.cols_ref, s32[104]{0:T(128)} %pad_add_fusion.live_ref, bf16[104,128,256]{2,1,0:T(8,128)(2,1)} %pad_maximum_fusion.ext_ref, bf16[32,16,128,128]{3,2,1,0:T(8,128)(2,1)} %tiles_ref.1), custom_call_target="tpu_custom_call" | custom-call | flops 4294967296 | bytes 27787264 | tf_op jit(solution)/shard_map/pallas_call | solution.py:49
  146.5 2.7 %fusion.4 = bf16[64,128,256]{2,1,0:T(8,128)(2,1)S(1)} fusion(bf16[64,32,384]{2,1,0:T(8,128)(2,1)} %bitcast.15), kind=kOutput, calls=%fused_computation.16 | convolution fusion | flops 134217728 | bytes 5767168 | tf_op jit(solution)/shard_map/qsk,qsv->qkv/dot_general | solution.py:253
  149.2 3.0 %fusion = f32[32,128,256]{2,0,1:T(8,128)S(1)} fusion(bf16[64,128,256]{2,1,0:T(8,128)(2,1)S(1)} %fusion.4, s32[64]{0:T(128)S(1)} %copy-done.7), kind=kOutput, calls=%fused_computation.8 | convolution fusion | flops 134219776 | bytes 8388864 | tf_op jit(solution)/shard_map/bq,qkv->bkv/dot_general | solution.py:191
  152.2 3.7 %fusion.1 = bf16[32,128,256]{2,1,0:T(8,128)(2,1)} fusion(f32[32,128,256]{2,1,0:T(8,128)S(1)} %copy-done.3, f32[32,128,256]{2,0,1:T(8,128)S(1)} %fusion), kind=kLoop, calls=%fused_computation.10 | loop fusion | flops 2097152 | bytes 10485760 | tf_op jit(solution)/shard_map/convert_element_type | solution.py:259
  (44 shorter events, 0.6 us)
Async XLA Ops:
  0.0 4.4 %copy-start = (bf16[16,4,32,128]{3,2,1,0:T(8,128)(2,1)S(1)}, bf16[16,4,32,128]{3,2,1,0:T(8,128)(2,1)}, u32[]{:S(2)}) copy-start(bf16[16,4,32,128]{3,2,1,0:T(8,128)(2,1)} %param.21) | copy-start | bytes 1572868
  22.3 10.4 %copy-start.10 = (s32[1,2,4]{2,1,0:T(2,128)S(1)}, s32[1,2,4]{2,1,0:T(2,128)}, u32[]{:S(2)}) copy-start(s32[1,2,4]{2,1,0:T(2,128)} %param.17) | copy-start | bytes 100
  22.3 10.5 %copy-start.2 = (bf16[32,128,256]{2,1,0:T(8,128)(2,1)S(1)}, bf16[32,128,256]{2,1,0:T(8,128)(2,1)}, u32[]{:S(2)}) copy-start(bf16[32,128,256]{2,1,0:T(8,128)(2,1)} %blocks_ref.1) | copy-start | bytes 6291460
  26.2 12.5 %copy-start.6 = (s32[32,16]{0,1:T(8,128)S(1)}, s32[32,16]{0,1:T(8,128)}, u32[]{:S(2)}) copy-start(s32[32,16]{0,1:T(8,128)} %param.14) | copy-start | bytes 6148
  26.2 13.2 %copy-start.9 = (s32[1,16]{1,0:T(1,128)S(1)}, s32[1,16]{1,0:T(1,128)}, u32[]{:S(2)}) copy-start(s32[1,16]{1,0:T(1,128)} %param.16) | copy-start | bytes 196
  26.2 13.4 %copy-start.8 = (s32[1,16,4]{1,2,0:T(4,128)S(1)}, s32[1,16,4]{1,2,0:T(4,128)}, u32[]{:S(2)}) copy-start(s32[1,16,4]{1,2,0:T(4,128)} %param.15) | copy-start | bytes 772
  26.2 83.6 %all-to-all-start = ((f32[16,4,32,256]{3,2,1,0:T(8,128)}), f32[16,4,32,256]{3,2,1,0:T(8,128)}, u32[]{:S(2)}, u32[]{:S(2)}) async-start(f32[16,4,32,256]{3,2,1,0:T(8,128)} %bitcast.30), calls=%async_computation | async-start | bytes 4194304 | tf_op jit(solution)/shard_map/all_to_all | solution.py:233
  34.3 89.1 %collective-permute-start.1 = (bf16[4,128,256]{2,1,0:T(8,128)(2,1)}, bf16[4,128,256]{2,1,0:T(8,128)(2,1)}, u32[]{:S(2)}, u32[]{:S(2)}) collective-permute-start(bf16[4,128,256]{2,1,0:T(8,128)(2,1)} %get-tuple-element.12), channel_id=1, source_target_pairs={{1,0},{2,1},{3,2},{4,3},{5,4},{6,5},{7,6},{9,8},{10,9},{11,10},{12... | collective-permute-start | bytes 786440 | tf_op jit(solution)/shard_map/ppermute | solution.py:17
  36.2 87.2 %collective-permute-start = (bf16[4,128,256]{2,1,0:T(8,128)(2,1)}, bf16[4,128,256]{2,1,0:T(8,128)(2,1)}, u32[]{:S(2)}, u32[]{:S(2)}) collective-permute-start(bf16[4,128,256]{2,1,0:T(8,128)(2,1)} %get-tuple-element.11), channel_id=1, source_target_pairs={{0,1},{1,2},{2,3},{3,4},{4,5},{5,6},{6,7},{8,9},{9,10},{10,11},{11... | collective-permute-start | bytes 786440 | tf_op jit(solution)/shard_map/ppermute | solution.py:16
  42.6 64.5 %copy-start.4 = (bf16[16,4,32,128]{3,2,1,0:T(8,128)(2,1)S(1)}, bf16[16,4,32,128]{3,2,1,0:T(8,128)(2,1)}, u32[]{:S(2)}) copy-start(bf16[16,4,32,128]{3,2,1,0:T(8,128)(2,1)} %param.22) | copy-start | bytes 1572868
  107.1 8.2 %copy-start.5 = (f32[16,32,32]{2,1,0:T(8,128)S(1)}, f32[16,32,32]{2,1,0:T(8,128)}, u32[]{:S(2)}) copy-start(f32[16,32,32]{2,1,0:T(8,128)} %param.23) | copy-start | bytes 196612
  118.8 27.7 %all-to-all-start.1 = ((bf16[16,4,32,384]{3,2,1,0:T(8,128)(2,1)}), bf16[16,4,32,384]{3,2,1,0:T(8,128)(2,1)}, u32[]{:S(2)}, u32[]{:S(2)}) async-start(bf16[16,4,32,384]{3,2,1,0:T(8,128)(2,1)} %bitcast.31), calls=%async_computation.1 | async-start | bytes 3145728 | tf_op jit(solution)/shard_map/all_to_all | solution.py:242
  146.5 2.7 %copy-start.7 = (s32[64]{0:T(128)S(1)}, s32[64]{0:T(128)}, u32[]{:S(2)}) copy-start(s32[64]{0:T(128)} %eq.15.index_ref) | copy-start | bytes 772
  149.2 3.0 %copy-start.3 = (f32[32,128,256]{2,1,0:T(8,128)S(1)}, f32[32,128,256]{2,1,0:T(8,128)}, u32[]{:S(2)}) copy-start(f32[32,128,256]{2,1,0:T(8,128)} %shard_map.119) | copy-start | bytes 12582916
  149.2 6.7 %copy-start.1 = (bf16[16,4,32,128]{3,2,1,0:T(8,128)(2,1)S(1)}, bf16[16,4,32,128]{3,2,1,0:T(8,128)(2,1)}, u32[]{:S(2)}) copy-start(bf16[16,4,32,128]{3,2,1,0:T(8,128)(2,1)} %param.21) | copy-start | bytes 1572868

commit v10 on v9

--- a/solution.py
+++ b/solution.py
@@ -52,6 +52,25 @@
         grid_spec=grid_spec,
         cost_estimate=pl.CostEstimate(flops=flops, transcendentals=0, bytes_accessed=moved),
     )(tile_cols.reshape(-1), live, extended, tile_values)
+
+
+def sums_kernel(slot_ref, partial_ref, out_ref):
+    couplings = slot_ref.shape[0] // out_ref.shape[0]
+    for w in range(out_ref.shape[0]):
+        acc = partial_ref[slot_ref[w * couplings]]
+        for c in range(1, couplings):
+            acc = acc + partial_ref[slot_ref[w * couplings + c]]
+        out_ref[w] = acc
+
+
+def well_sums(slots, partial, wells):
+    vmem = pl.BlockSpec(memory_space=pltpu.VMEM)
+    return pl.pallas_call(
+        sums_kernel,
+        out_shape=jax.ShapeDtypeStruct((wells,) + partial.shape[1:], jnp.float32),
+        in_specs=[pl.BlockSpec(memory_space=pltpu.SMEM), vmem],
+        out_specs=vmem,
+    )(slots, partial)
 
 
 def partial_kernel(index_ref, couple_ref, blocks_ref, out_ref):
@@ -223,7 +242,7 @@
     slot_order = jnp.argsort(well_slot.reshape(-1))
     slot_well = slot_order // couplings
     in_slots = couple_in.reshape(wells * couplings, seg, cell_count)[slot_order]
-    in_slots = in_slots.reshape(dom_count, slot_width * seg * cell_count // vec_count, vec_count)
+    in_slots = in_slots.reshape(dom_count, slot_width * seg, cell_count)
     halo_flat = halo_pack.reshape(dom_count, halo_width * cell_count, vec_count)
     (in_recv,) = dom_exchange([in_slots], 0)
     in_recv = in_recv.reshape(dom_count, slot_width, seg, cell_count)
@@ -233,7 +252,7 @@
     partial_in = lax.all_to_all(partial, "dom", split_axis=0, concat_axis=0, tiled=True)
     (halo_recv,) = dom_exchange([halo_flat], 1)
     partial_in = partial_in.reshape(slot_total, seg, vec_count)
-    summed = jnp.sum(partial_in[well_slot.reshape(-1)].reshape(wells, couplings, seg, vec_count), axis=1)
+    summed = well_sums(well_slot.reshape(-1), partial_in, wells)
     well_state = well_states_of(summed, well_inverse, well_count)
     state_slots = well_state[slot_well]
     out_slots = couple_out.reshape(wells * couplings, seg, cell_count)[slot_order]

time: 157 us -> 154 us (0.981)
  local copies, waits for them, and re-layouts: 16.9 us -> 12.2 us
  Pallas kernels: 99.7 us -> 102 us
  other arithmetic: 16.7 us -> 15.1 us
    gather x1 -> x0, local copies, waits for them, and re-layouts: 3.59 us -> none  [on_device(): partial_in[well_slot.reshape(-1)].reshape(wells, couplings, seg, vec_count)]
    pallas_call x0 -> x1, Pallas kernels: none -> 2.49 us  [well_sums(): pl.pallas_call(sums_kernel, out_shape=jax.ShapeDtypeStruct((wells,) + par...]
    another operation x2 -> x1, local copies, waits for them, and re-layouts: 2 us -> 0.01 us  [the longest x1 2 us: on_device(): in_recv.reshape(slot_total, seg, cell_count)]
    reduce_sum x1 -> x0, other arithmetic: 1.84 us -> none  [on_device(): jnp.sum(partial_in[well_slot.reshape(-1)].reshape(wells, couplings, seg,...]
  transfers between devices with their start and end apart: 4 -> 4, of which waited for: 0 -> 0; matrix products, arithmetic and copies ran while one was open for 14% -> 13% of each run, Pallas kernels for 52% -> 55%
where the time goes in v10:
time: 154 us; the launch traced here: 153 us
  Pallas kernels  102 us (66%)
  starting transfers between devices  15.8 us (10%)
  other arithmetic  15.1 us (10%)
  local copies, waits for them, and re-layouts  12.2 us (8%)
  matrix products  7.41 us (5%)
    pallas_call x2, Pallas kernels, dom_exchange(): pl.pallas_call(exchange_kernel, out_shape=tuple(outs + relays), in_specs=...  78.6 us
    pallas_call x1, Pallas kernels, local_product(): pl.pallas_call(product_kernel, out_shape=jax.ShapeDtypeStruct((block_rows...  17.1 us
    all_to_all x1, starting transfers between devices, on_device(): lax.all_to_all(partial, 'dom', split_axis=0, concat_axis=0, tiled=True)  6.5 us
    concatenate x1, other arithmetic, on_device(): jnp.concatenate([blocks, halo_rows.reshape(dom_count * halo_width, cell_c...  6.11 us
    all_to_all x1, starting transfers between devices, on_device(): lax.all_to_all(state_pack, 'dom', split_axis=0, concat_axis=0, tiled=True)  4.98 us
    pallas_call x1, Pallas kernels, partial_sums(): pl.pallas_call(partial_kernel, out_shape=jax.ShapeDtypeStruct((slots, seg...  3.91 us
    convert_element_type x1, other arithmetic, on_device(): return subtract_incoming(product, well_send, incoming).astype(jnp.bfloat16)  3.65 us
  transfers between devices with their start and end apart: 4, of which 0 were waited for; matrix products, arithmetic and copies ran while one was open for 13% of the time, Pallas kernels for 55%

profile of v10, /device:TPU:66, one launch (start us, length us, event | category | flops | bytes accessed | tf_op | source)
XLA Modules:
  0.0 153.4 jit_solution(9764148369376291853)
XLA Ops:
  0.0 0.8 copy.20
  0.8 0.1 reshape.102.slot_ref
  0.9 2.0 %sort.17 = (s32[64]{0:T(128)}, s32[64]{0:T(128)S(1)}) sort(s32[64]{0:T(128)S(1)} %reshape.102.slot_ref, s32[64]{0:T(128)S(1)} %iota.17), dimensions={0}, to_apply=%region_0.0 | sort | flops 384 | bytes 1024 | tf_op jit(solution)/shard_map/jit(argsort)/sort | solution.py:242
  3.0 0.8 copy.19
  3.7 0.6 eq.15.index_ref
  4.4 1.4 gather_fusion.2
  5.8 14.3 %shard_map.120 = (bf16[16,128,128]{2,1,0:T(8,128)(2,1)}, bf16[14,64,128]{2,1,0:T(8,128)(2,1)}) custom-call(bf16[16,128,128]{2,1,0:T(8,128)(2,1)} %bitcast.31), custom_call_target="tpu_custom_call" | custom-call | tf_op jit(solution)/shard_map/pallas_call | solution.py:180
  20.1 3.9 %shard_map.121 = f32[64,32,256]{2,1,0:T(8,128)} custom-call(s32[64]{0:T(128)} %eq.15.index_ref, bf16[64,32,128]{2,1,0:T(8,128)(2,1)} %bitcast.32, bf16[32,128,256]{2,1,0:T(8,128)(2,1)} %blocks_ref.1), custom_call_target="tpu_custom_call" | custom-call | tf_op jit(solution)/shard_map/pallas_call | solution.py:86
  24.1 6.5 %all-to-all-start = ((f32[16,4,32,256]{3,2,1,0:T(8,128)}), f32[16,4,32,256]{3,2,1,0:T(8,128)}, u32[]{:S(2)}, u32[]{:S(2)}) async-start(f32[16,4,32,256]{3,2,1,0:T(8,128)} %bitcast.28), calls=%async_computation | async-start | bytes 4194304 | tf_op jit(solution)/shard_map/all_to_all | solution.py:252
  30.6 0.1 reshape_squeeze.4
  30.7 0.6 gather_fusion.1
  31.3 0.8 fusion.12
  32.1 1.9 %collective-permute-start.1 = (bf16[4,128,256]{2,1,0:T(8,128)(2,1)}, bf16[4,128,256]{2,1,0:T(8,128)(2,1)}, u32[]{:S(2)}, u32[]{:S(2)}) collective-permute-start(bf16[4,128,256]{2,1,0:T(8,128)(2,1)} %get-tuple-element.12), channel_id=1, source_target_pairs={{1,0},{2,1},{3,2},{4,3},{5,4},{6,5},{7,6},{9,8},{10,9},{11,10},{12... | collective-permute-start | bytes 786440 | tf_op jit(solution)/shard_map/ppermute | solution.py:17
  34.0 2.4 %collective-permute-start = (bf16[4,128,256]{2,1,0:T(8,128)(2,1)}, bf16[4,128,256]{2,1,0:T(8,128)(2,1)}, u32[]{:S(2)}, u32[]{:S(2)}) collective-permute-start(bf16[4,128,256]{2,1,0:T(8,128)(2,1)} %get-tuple-element.11), channel_id=1, source_target_pairs={{0,1},{1,2},{2,3},{3,4},{4,5},{5,6},{6,7},{8,9},{9,10},{10,11},{11... | collective-permute-start | bytes 786440 | tf_op jit(solution)/shard_map/ppermute | solution.py:16
  36.5 0.6 reshape.100.cols_ref
  37.2 0.1 reshape.110
  37.3 0.1 copy.18
  37.4 0.1 reshape.113
  37.5 2.8 %gather_fusion = bf16[64,128,256]{2,1,0:T(8,128)(2,1)} fusion(bf16[32,128,256]{2,1,0:T(8,128)(2,1)S(1)} %copy-done.1, s32[1024]{0:T(1024)S(1)} %pad_clamp_fusion.3), kind=kCustom, calls=%fused_computation | custom fusion | bytes 8388864 | tf_op jit(solution)/shard_map/gather | solution.py:238
  40.3 64.2 %shard_map.118 = (bf16[16,512,256]{2,1,0:T(8,128)(2,1)}, bf16[14,256,256]{2,1,0:T(8,128)(2,1)}) custom-call(bf16[16,512,256]{2,1,0:T(8,128)(2,1)} %bitcast.27), custom_call_target="tpu_custom_call" | custom-call | tf_op jit(solution)/shard_map/pallas_call | solution.py:180
  104.5 1.7 %gather_fusion.4 = bf16[64,32,128]{2,1,0:T(8,128)(2,1)S(1)} fusion(bf16[64,32,128]{2,1,0:T(8,128)(2,1)} %bitcast.33, s32[1024]{0:T(1024)S(1)} %get-tuple-element.16), kind=kCustom, calls=%fused_computation.4 | custom fusion | bytes 1048832 | tf_op jit(solution)/shard_map/gather | solution.py:258
  106.9 0.6 pad_add_fusion.live_ref
  107.5 2.5 %shard_map.122 = f32[16,32,256]{2,1,0:T(8,128)} custom-call(s32[64]{0:T(128)} %copy-done.6, f32[64,32,256]{2,1,0:T(8,128)} %bitcast.10.partial_ref), custom_call_target="tpu_custom_call" | custom-call | tf_op jit(solution)/shard_map/pallas_call | solution.py:68
  110.0 1.7 %fusion.3 = bf16[16,32,256]{2,1,0:T(8,128)(2,1)S(1)} fusion(f32[16,32,256]{2,1,0:T(8,128)} %shard_map.122, f32[16,32,32]{2,1,0:T(8,128)} %param.23, f32[16]{0:T(128)S(1)} %compare_convert_fusion), kind=kOutput, calls=%fused_computation.13 | convolution fusion | flops 50593792 | bytes 852032 | tf_op jit(solution)/shard_map/wst,wtv->wsv/dot_general | solution.py:202
  111.7 1.6 %gather_fusion.3 = bf16[64,32,256]{2,1,0:T(8,128)(2,1)} fusion(bf16[16,32,256]{2,1,0:T(8,128)(2,1)S(1)} %fusion.3, s32[1024]{0:T(1024)S(1)} %get-tuple-element.15), kind=kCustom, calls=%fused_computation.3 | custom fusion | bytes 2097408 | tf_op jit(solution)/shard_map/gather | solution.py:257
  113.3 2.5 %pad_maximum_fusion.1 = bf16[64,32,384]{2,1,0:T(8,128)(2,1)} fusion(bf16[64,32,128]{2,1,0:T(8,128)(2,1)S(1)} %gather_fusion.4, bf16[64,32,256]{2,1,0:T(8,128)(2,1)} %gather_fusion.3), kind=kLoop, calls=%fused_computation.10 | loop fusion | flops 3145728 | bytes 3145728 | tf_op jit(solution)/shard_map/concatenate | solution.py:259
  115.8 5.0 %all-to-all-start.1 = ((bf16[16,4,32,384]{3,2,1,0:T(8,128)(2,1)}), bf16[16,4,32,384]{3,2,1,0:T(8,128)(2,1)}, u32[]{:S(2)}, u32[]{:S(2)}) async-start(bf16[16,4,32,384]{3,2,1,0:T(8,128)(2,1)} %bitcast.29), calls=%async_computation.1 | async-start | bytes 3145728 | tf_op jit(solution)/shard_map/all_to_all | solution.py:261
  120.8 6.1 %pad_maximum_fusion.ext_ref = bf16[104,128,256]{2,1,0:T(8,128)(2,1)} fusion(bf16[4,128,256]{2,1,0:T(8,128)(2,1)} %collective-permute-done.1, bf16[4,128,256]{2,1,0:T(8,128)(2,1)} %collective-permute-done, bf16[64,128,256]{2,1,0:T(8,128)(2,1)} %bitcast.30, bf16[32,128,256]{2,1,0:T(8,128)(2,1)S(1)} %copy-done.1), kind=kLoop, calls=%fused_computation.6 | loop fusion | flops 10223616 | bytes 13631488 | tf_op jit(solution)/shard_map/concatenate | solution.py:268
  126.9 17.1 %shard_map.119 = f32[32,128,256]{2,1,0:T(8,128)} custom-call(s32[512]{0:T(512)} %reshape.100.cols_ref, s32[104]{0:T(128)} %pad_add_fusion.live_ref, bf16[104,128,256]{2,1,0:T(8,128)(2,1)} %pad_maximum_fusion.ext_ref, bf16[32,16,128,128]{3,2,1,0:T(8,128)(2,1)} %tiles_ref.1), custom_call_target="tpu_custom_call" | custom-call | flops 4294967296 | bytes 27787264 | tf_op jit(solution)/shard_map/pallas_call | solution.py:49
  144.0 2.7 %fusion.4 = bf16[64,128,256]{2,1,0:T(8,128)(2,1)S(1)} fusion(bf16[64,32,384]{2,1,0:T(8,128)(2,1)} %bitcast.15), kind=kOutput, calls=%fused_computation.14 | convolution fusion | flops 134217728 | bytes 5767168 | tf_op jit(solution)/shard_map/qsk,qsv->qkv/dot_general | solution.py:272
  146.7 3.0 %fusion = f32[32,128,256]{2,0,1:T(8,128)S(1)} fusion(bf16[64,128,256]{2,1,0:T(8,128)(2,1)S(1)} %fusion.4, s32[64]{0:T(128)S(1)} %copy-done.4), kind=kOutput, calls=%fused_computation.7 | convolution fusion | flops 134219776 | bytes 8388864 | tf_op jit(solution)/shard_map/bq,qkv->bkv/dot_general | solution.py:210
  149.8 3.7 %fusion.1 = bf16[32,128,256]{2,1,0:T(8,128)(2,1)} fusion(f32[32,128,256]{2,1,0:T(8,128)S(1)} %copy-done.2, f32[32,128,256]{2,0,1:T(8,128)S(1)} %fusion), kind=kLoop, calls=%fused_computation.9 | loop fusion | flops 2097152 | bytes 10485760 | tf_op jit(solution)/shard_map/convert_element_type | solution.py:278
  (34 shorter events, 0.2 us)
Async XLA Ops:
  0.0 4.4 %copy-start = (bf16[16,4,32,128]{3,2,1,0:T(8,128)(2,1)S(1)}, bf16[16,4,32,128]{3,2,1,0:T(8,128)(2,1)}, u32[]{:S(2)}) copy-start(bf16[16,4,32,128]{3,2,1,0:T(8,128)(2,1)} %param.21) | copy-start | bytes 1572868
  0.9 23.2 %copy-start.6 = (s32[64]{0:T(128)}, s32[64]{0:T(128)S(1)}, u32[]{:S(2)}) copy-start(s32[64]{0:T(128)S(1)} %reshape.102.slot_ref) | copy-start | bytes 772
  20.1 10.5 %copy-start.8 = (s32[1,2,4]{2,1,0:T(2,128)S(1)}, s32[1,2,4]{2,1,0:T(2,128)}, u32[]{:S(2)}) copy-start(s32[1,2,4]{2,1,0:T(2,128)} %param.17) | copy-start | bytes 100
  20.1 10.5 %copy-start.1 = (bf16[32,128,256]{2,1,0:T(8,128)(2,1)S(1)}, bf16[32,128,256]{2,1,0:T(8,128)(2,1)}, u32[]{:S(2)}) copy-start(bf16[32,128,256]{2,1,0:T(8,128)(2,1)} %blocks_ref.1) | copy-start | bytes 6291460
  24.1 12.4 %copy-start.3 = (s32[32,16]{0,1:T(8,128)S(1)}, s32[32,16]{0,1:T(8,128)}, u32[]{:S(2)}) copy-start(s32[32,16]{0,1:T(8,128)} %param.14) | copy-start | bytes 6148
  24.1 13.1 %copy-start.7 = (s32[1,16]{1,0:T(1,128)S(1)}, s32[1,16]{1,0:T(1,128)}, u32[]{:S(2)}) copy-start(s32[1,16]{1,0:T(1,128)} %param.16) | copy-start | bytes 196
  24.1 13.3 %copy-start.5 = (s32[1,16,4]{1,2,0:T(4,128)S(1)}, s32[1,16,4]{1,2,0:T(4,128)}, u32[]{:S(2)}) copy-start(s32[1,16,4]{1,2,0:T(4,128)} %param.15) | copy-start | bytes 772
  24.1 83.4 %all-to-all-start = ((f32[16,4,32,256]{3,2,1,0:T(8,128)}), f32[16,4,32,256]{3,2,1,0:T(8,128)}, u32[]{:S(2)}, u32[]{:S(2)}) async-start(f32[16,4,32,256]{3,2,1,0:T(8,128)} %bitcast.28), calls=%async_computation | async-start | bytes 4194304 | tf_op jit(solution)/shard_map/all_to_all | solution.py:252
  32.1 88.7 %collective-permute-start.1 = (bf16[4,128,256]{2,1,0:T(8,128)(2,1)}, bf16[4,128,256]{2,1,0:T(8,128)(2,1)}, u32[]{:S(2)}, u32[]{:S(2)}) collective-permute-start(bf16[4,128,256]{2,1,0:T(8,128)(2,1)} %get-tuple-element.12), channel_id=1, source_target_pairs={{1,0},{2,1},{3,2},{4,3},{5,4},{6,5},{7,6},{9,8},{10,9},{11,10},{12... | collective-permute-start | bytes 786440 | tf_op jit(solution)/shard_map/ppermute | solution.py:17
  34.0 86.8 %collective-permute-start = (bf16[4,128,256]{2,1,0:T(8,128)(2,1)}, bf16[4,128,256]{2,1,0:T(8,128)(2,1)}, u32[]{:S(2)}, u32[]{:S(2)}) collective-permute-start(bf16[4,128,256]{2,1,0:T(8,128)(2,1)} %get-tuple-element.11), channel_id=1, source_target_pairs={{0,1},{1,2},{2,3},{3,4},{4,5},{5,6},{6,7},{8,9},{9,10},{10,11},{11... | collective-permute-start | bytes 786440 | tf_op jit(solution)/shard_map/ppermute | solution.py:16
  115.8 28.2 %all-to-all-start.1 = ((bf16[16,4,32,384]{3,2,1,0:T(8,128)(2,1)}), bf16[16,4,32,384]{3,2,1,0:T(8,128)(2,1)}, u32[]{:S(2)}, u32[]{:S(2)}) async-start(bf16[16,4,32,384]{3,2,1,0:T(8,128)(2,1)} %bitcast.29), calls=%async_computation.1 | async-start | bytes 3145728 | tf_op jit(solution)/shard_map/all_to_all | solution.py:261
  144.0 2.7 %copy-start.4 = (s32[64]{0:T(128)S(1)}, s32[64]{0:T(128)}, u32[]{:S(2)}) copy-start(s32[64]{0:T(128)} %eq.15.index_ref) | copy-start | bytes 772
  146.7 3.0 %copy-start.2 = (f32[32,128,256]{2,1,0:T(8,128)S(1)}, f32[32,128,256]{2,1,0:T(8,128)}, u32[]{:S(2)}) copy-start(f32[32,128,256]{2,1,0:T(8,128)} %shard_map.119) | copy-start | bytes 12582916

commit v11 on v10

--- a/solution.py
+++ b/solution.py
@@ -1,3 +1,5 @@
+import functools
+
 import jax
 import jax.numpy as jnp
 from jax import lax
@@ -23,18 +25,22 @@
     rows, tiles_per_row = tiles_ref.shape[0], tiles_ref.shape[1]
     first = pl.program_id(0) * rows
     for r in range(rows):
-        acc = jnp.zeros(out_ref.shape[1:], jnp.float32)
-        for t in range(tiles_per_row):
-            col = cols_ref[(first + r) * tiles_per_row + t]
-            scale = live_ref[col].astype(jnp.float32)
-            acc = acc + scale * jnp.dot(tiles_ref[r, t], ext_ref[col], preferred_element_type=jnp.float32)
+        acc = None
+        for t in range(0, tiles_per_row, 2):
+            pair = [cols_ref[(first + r) * tiles_per_row + t + u] for u in range(2)]
+            lhs = jnp.concatenate(
+                [tiles_ref[r, t + u] * live_ref[pair[u]].astype(tiles_ref.dtype) for u in range(2)], axis=1
+            )
+            rhs = jnp.concatenate([ext_ref[c] for c in pair], axis=0)
+            term = jnp.dot(lhs, rhs, preferred_element_type=jnp.float32)
+            acc = term if acc is None else acc + term
         out_ref[r] = acc
 
 
 def local_product(extended, live, tile_values, tile_cols):
     block_rows, tiles_per_row, cells, _ = tile_values.shape
     ext_blocks, _, vecs = extended.shape
-    rows = 4
+    rows = 16
     grid_spec = pltpu.PrefetchScalarGridSpec(
         num_scalar_prefetch=2,
         grid=(block_rows // rows,),
@@ -104,7 +110,7 @@
 )
 
 
-def exchange_kernel(*refs):
+def exchange_kernel(offsets, *refs):
     parts = (len(refs) - 7) // 3
     send_refs, recv_refs, relay_refs = refs[:parts], refs[parts : 2 * parts], refs[2 * parts : 3 * parts]
     near_send, near_recv, leg_send, leg_recv, fwd_send, fwd_recv, own_sems = refs[3 * parts :]
@@ -129,7 +135,7 @@
     pl.semaphore_wait(barrier, len(NEAR))
     owns = []
     for p in range(parts):
-        own = pltpu.make_async_copy(send_refs[p].at[me], recv_refs[p].at[me], own_sems.at[p])
+        own = pltpu.make_async_copy(send_refs[p].at[me], recv_refs[p].at[offsets[p] + me], own_sems.at[p])
         own.start()
         owns.append(own)
     legs = []
@@ -143,7 +149,7 @@
     nears = []
     for k, offset in enumerate(NEAR):
         for p in range(parts):
-            near = remote(send_refs[p].at[at(offset)], recv_refs[p].at[me],
+            near = remote(send_refs[p].at[at(offset)], recv_refs[p].at[offsets[p] + me],
                           near_send.at[p, k], near_recv.at[p, k], offset)
             near.start()
             nears.append(near)
@@ -154,7 +160,7 @@
         for p in range(parts):
             half = send_refs[p].shape[1] // 2
             legs[k * parts + p].wait_recv()
-            fwd = remote(relay_refs[p].at[k], recv_refs[p].at[source, pl.ds(part * half, half)],
+            fwd = remote(relay_refs[p].at[k], recv_refs[p].at[offsets[p] + source, pl.ds(part * half, half)],
                          fwd_send.at[p, k], fwd_recv.at[p, k], onward)
             fwd.start()
             fwds.append(fwd)
@@ -172,13 +178,14 @@
         own.wait()
 
 
-def dom_exchange(values, collective):
+def dom_exchange(values, collective, frames=None):
     parts = len(values)
-    outs = [jax.ShapeDtypeStruct(v.shape, v.dtype) for v in values]
+    frames = frames or [(0, v.shape[0]) for v in values]
+    outs = [jax.ShapeDtypeStruct((n,) + v.shape[1:], v.dtype) for v, (_, n) in zip(values, frames)]
     relays = [jax.ShapeDtypeStruct((len(RELAYED), v.shape[1] // 2, v.shape[2]), v.dtype) for v in values]
     any_spec = pl.BlockSpec(memory_space=pl.ANY)
     result = pl.pallas_call(
-        exchange_kernel,
+        functools.partial(exchange_kernel, tuple(f[0] for f in frames)),
         out_shape=tuple(outs + relays),
         in_specs=[any_spec] * parts,
         out_specs=tuple([any_spec] * (2 * parts)),
@@ -250,7 +257,9 @@
         well_send[0].reshape(-1), in_recv.reshape(slot_total, seg, cell_count), blocks
     ).reshape(dom_count, slot_width, seg, vec_count)
     partial_in = lax.all_to_all(partial, "dom", split_axis=0, concat_axis=0, tiled=True)
-    (halo_recv,) = dom_exchange([halo_flat], 1)
+    own_slots = blocks.shape[0] // halo_width
+    ext_slots = own_slots + dom_count + 2 * rim_width // halo_width
+    (ext_frame,) = dom_exchange([halo_flat], 1, [(own_slots, ext_slots)])
     partial_in = partial_in.reshape(slot_total, seg, vec_count)
     summed = well_sums(well_slot.reshape(-1), partial_in, wells)
     well_state = well_states_of(summed, well_inverse, well_count)
@@ -260,14 +269,13 @@
     state_pack = state_pack.reshape(dom_count, slot_width, seg, vec_count + cell_count)
     state_in = lax.all_to_all(state_pack, "dom", split_axis=0, concat_axis=0, tiled=True)
     state_in = state_in.reshape(slot_total, seg, vec_count + cell_count)
-    halo_rows = halo_recv.reshape(dom_count, halo_width, cell_count, vec_count)
     live_halo = (jnp.arange(halo_width)[None, :] < halo_counts[0][:, None]).astype(jnp.int32)
     live = jnp.concatenate(
         [jnp.ones((blocks.shape[0],), jnp.int32), live_halo.reshape(-1), jnp.ones((2 * rim_width,), jnp.int32)]
     )
-    extended = jnp.concatenate(
-        [blocks, halo_rows.reshape(dom_count * halo_width, cell_count, vec_count), rim_rows], 0
-    )
+    extended = ext_frame.reshape(ext_slots * halo_width, cell_count, vec_count)
+    extended = lax.dynamic_update_slice_in_dim(extended, blocks, 0, 0)
+    extended = lax.dynamic_update_slice_in_dim(extended, rim_rows, extended.shape[0] - 2 * rim_width, 0)
     product = local_product(extended, live, tile_values, tile_cols)
     incoming = jnp.einsum(
         "qsk,qsv->qkv",

time: 154 us -> 174 us (1.13)
  the two profiles are of different devices: /device:TPU:66 before, /device:TPU:91 now
where the time goes in v11:
time: 174 us; the launch traced here: 173 us
  Pallas kernels  96.7 us (56%)
  waiting for transfers between devices  21.8 us (13%)
  starting transfers between devices  21.7 us (12%)
  local copies, waits for them, and re-layouts  14.7 us (8%)
  other arithmetic  9.97 us (6%)
  matrix products  7.4 us (4%)
    pallas_call x2, Pallas kernels, dom_exchange(): pl.pallas_call(functools.partial(exchange_kernel, tuple((f[0] for f in fr...  78.2 us
    all_to_all x1, waiting for transfers between devices, on_device(): lax.all_to_all(partial, 'dom', split_axis=0, concat_axis=0, tiled=True)  21.8 us
    pallas_call x1, Pallas kernels, local_product(): pl.pallas_call(product_kernel, out_shape=jax.ShapeDtypeStruct((block_rows...  12.1 us
    all_to_all x1, starting transfers between devices, on_device(): lax.all_to_all(partial, 'dom', split_axis=0, concat_axis=0, tiled=True)  6.42 us
    all_to_all x1, starting transfers between devices, on_device(): lax.all_to_all(state_pack, 'dom', split_axis=0, concat_axis=0, tiled=True)  6.39 us
    ppermute x1, starting transfers between devices, padded(): after = lax.ppermute(leading, axis, down)  5.57 us
    pallas_call x1, Pallas kernels, partial_sums(): pl.pallas_call(partial_kernel, out_shape=jax.ShapeDtypeStruct((slots, seg...  3.91 us
    convert_element_type x1, other arithmetic, on_device(): return subtract_incoming(product, well_send, incoming).astype(jnp.bfloat16)  3.65 us
  transfers between devices with their start and end apart: 4, of which 1 were waited for; matrix products, arithmetic and copies ran while one was open for 6% of the time, Pallas kernels for 46%

profile of v11, /device:TPU:91, one launch (start us, length us, event | category | flops | bytes accessed | tf_op | source)
XLA Modules:
  0.0 173.1 jit_solution(3997934829328496998)
XLA Ops:
  0.0 0.8 copy.20
  0.8 0.1 reshape.106.slot_ref
  0.9 2.0 %sort.17 = (s32[64]{0:T(128)}, s32[64]{0:T(128)S(1)}) sort(s32[64]{0:T(128)S(1)} %reshape.106.slot_ref, s32[64]{0:T(128)S(1)} %iota.17), dimensions={0}, to_apply=%region_0.0 | sort | flops 384 | bytes 1024 | tf_op jit(solution)/shard_map/jit(argsort)/sort | solution.py:249
  3.0 0.8 copy.19
  3.7 0.7 eq.15.index_ref
  4.4 1.4 gather_fusion.2
  5.8 11.2 %shard_map.120 = (bf16[16,128,128]{2,1,0:T(8,128)(2,1)}, bf16[14,64,128]{2,1,0:T(8,128)(2,1)}) custom-call(bf16[16,128,128]{2,1,0:T(8,128)(2,1)} %bitcast.31), custom_call_target="tpu_custom_call" | custom-call | tf_op jit(solution)/shard_map/pallas_call | solution.py:187
  17.0 3.9 %shard_map.121 = f32[64,32,256]{2,1,0:T(8,128)} custom-call(s32[64]{0:T(128)} %eq.15.index_ref, bf16[64,32,128]{2,1,0:T(8,128)(2,1)} %bitcast.32, bf16[32,128,256]{2,1,0:T(8,128)(2,1)} %blocks_ref.1), custom_call_target="tpu_custom_call" | custom-call | tf_op jit(solution)/shard_map/pallas_call | solution.py:92
  21.0 6.4 %all-to-all-start = ((f32[16,4,32,256]{3,2,1,0:T(8,128)}), f32[16,4,32,256]{3,2,1,0:T(8,128)}, u32[]{:S(2)}, u32[]{:S(2)}) async-start(f32[16,4,32,256]{3,2,1,0:T(8,128)} %bitcast.28), calls=%async_computation | async-start | bytes 4194304 | tf_op jit(solution)/shard_map/all_to_all | solution.py:259
  27.5 0.6 gather_fusion.1
  28.1 2.5 %gather_fusion.4 = bf16[64,32,128]{2,1,0:T(8,128)(2,1)} fusion(bf16[64,32,128]{2,1,0:T(8,128)(2,1)} %bitcast.33, s32[1024]{0:T(1024)S(1)} %get-tuple-element.16), kind=kCustom, calls=%fused_computation.4 | custom fusion | bytes 1048832 | tf_op jit(solution)/shard_map/gather | solution.py:267
  31.2 21.8 %all-to-all-done = f32[16,4,32,256]{3,2,1,0:T(8,128)} async-done(((f32[16,4,32,256]{3,2,1,0:T(8,128)}), f32[16,4,32,256]{3,2,1,0:T(8,128)}, u32[]{:S(2)}, u32[]{:S(2)}) %all-to-all-start) | async-done | bytes 2097184 | tf_op jit(solution)/shard_map/all_to_all | solution.py:259
  53.0 2.5 %shard_map.122 = f32[16,32,256]{2,1,0:T(8,128)} custom-call(s32[64]{0:T(128)} %copy-done.6, f32[64,32,256]{2,1,0:T(8,128)} %bitcast.10.partial_ref), custom_call_target="tpu_custom_call" | custom-call | tf_op jit(solution)/shard_map/pallas_call | solution.py:74
  55.5 1.7 fusion.3
  57.2 1.6 gather_fusion.3
  58.8 2.7 %pad_maximum_fusion = bf16[64,32,384]{2,1,0:T(8,128)(2,1)} fusion(bf16[64,32,128]{2,1,0:T(8,128)(2,1)} %gather_fusion.4, bf16[64,32,256]{2,1,0:T(8,128)(2,1)} %gather_fusion.3), kind=kLoop, calls=%fused_computation.9 | loop fusion | flops 3145728 | bytes 3145728 | tf_op jit(solution)/shard_map/concatenate | solution.py:268
  61.5 6.4 %all-to-all-start.1 = ((bf16[16,4,32,384]{3,2,1,0:T(8,128)(2,1)}), bf16[16,4,32,384]{3,2,1,0:T(8,128)(2,1)}, u32[]{:S(2)}, u32[]{:S(2)}) async-start(bf16[16,4,32,384]{3,2,1,0:T(8,128)(2,1)} %bitcast.30), calls=%async_computation.1 | async-start | bytes 3145728 | tf_op jit(solution)/shard_map/all_to_all | solution.py:270
  67.9 0.7 fusion.12
  68.7 5.6 %collective-permute-start.1 = (bf16[4,128,256]{2,1,0:T(8,128)(2,1)}, bf16[4,128,256]{2,1,0:T(8,128)(2,1)S(1)}, u32[]{:S(2)}, u32[]{:S(2)}) collective-permute-start(bf16[4,128,256]{2,1,0:T(8,128)(2,1)} %get-tuple-element.12), channel_id=1, source_target_pairs={{1,0},{2,1},{3,2},{4,3},{5,4},{6,5},{7,6},{9,8},{10,9},{11,10},{12... | collective-permute-start | bytes 786440 | tf_op jit(solution)/shard_map/ppermute | solution.py:19
  74.2 3.3 %collective-permute-start = (bf16[4,128,256]{2,1,0:T(8,128)(2,1)S(1)}, bf16[4,128,256]{2,1,0:T(8,128)(2,1)S(1)}, u32[]{:S(2)}, u32[]{:S(2)}) collective-permute-start(bf16[4,128,256]{2,1,0:T(8,128)(2,1)S(1)} %get-tuple-element.11), channel_id=1, source_target_pairs={{0,1},{1,2},{2,3},{3,4},{4,5},{5,6},{6,7},{8,9},{9,10},{10,11},{11... | collective-permute-start | bytes 786440 | tf_op jit(solution)/shard_map/ppermute | solution.py:18
  77.7 0.7 reshape.103.cols_ref
  78.4 0.1 reshape.114
  78.6 0.1 reshape.117
  78.7 2.9 %gather_fusion = bf16[64,128,256]{2,1,0:T(8,128)(2,1)} fusion(bf16[32,128,256]{2,1,0:T(8,128)(2,1)S(1)} %copy-done.1, s32[1024]{0:T(1024)S(1)} %pad_clamp_fusion.3), kind=kCustom, calls=%fused_computation | custom fusion | bytes 8388864 | tf_op jit(solution)/shard_map/gather | solution.py:245
  81.6 67.0 %shard_map.118 = (bf16[26,512,256]{2,1,0:T(8,128)(2,1)}, bf16[14,256,256]{2,1,0:T(8,128)(2,1)}) custom-call(bf16[16,512,256]{2,1,0:T(8,128)(2,1)} %bitcast.27), custom_call_target="tpu_custom_call" | custom-call | tf_op jit(solution)/shard_map/pallas_call | solution.py:187
  148.6 0.6 pad_add_fusion.live_ref
  149.2 1.6 constant_dynamic-update-slice_fusion
  150.8 0.8 maximum_dynamic-update-slice_fusion.ext_ref
  151.6 12.1 %shard_map.119 = f32[32,128,256]{2,1,0:T(8,128)} custom-call(s32[512]{0:T(512)} %reshape.103.cols_ref, s32[104]{0:T(128)} %pad_add_fusion.live_ref, bf16[104,128,256]{2,1,0:T(8,128)(2,1)} %maximum_dynamic-update-slice_fusion.ext_ref, bf16[32,16,128,128]{3,2,1,0:T(8,128)(2,1)} %tiles_ref.1), custom_call_target="tpu_custom_call" | custom-call | flops 4294967296 | bytes 27787264 | tf_op jit(solution)/shard_map/pallas_call | solution.py:55
  163.7 2.7 %fusion.4 = bf16[64,128,256]{2,1,0:T(8,128)(2,1)S(1)} fusion(bf16[64,32,384]{2,1,0:T(8,128)(2,1)} %bitcast.15), kind=kOutput, calls=%fused_computation.13 | convolution fusion | flops 134217728 | bytes 5767168 | tf_op jit(solution)/shard_map/qsk,qsv->qkv/dot_general | solution.py:280
  166.4 3.0 %fusion = f32[32,128,256]{2,0,1:T(8,128)S(1)} fusion(bf16[64,128,256]{2,1,0:T(8,128)(2,1)S(1)} %fusion.4, s32[64]{0:T(128)S(1)} %copy-done.4), kind=kOutput, calls=%fused_computation.6 | convolution fusion | flops 134219776 | bytes 8388864 | tf_op jit(solution)/shard_map/bq,qkv->bkv/dot_general | solution.py:217
  169.4 3.7 %fusion.1 = bf16[32,128,256]{2,1,0:T(8,128)(2,1)} fusion(f32[32,128,256]{2,1,0:T(8,128)S(1)} %copy-done.2, f32[32,128,256]{2,0,1:T(8,128)S(1)} %fusion), kind=kLoop, calls=%fused_computation.8 | loop fusion | flops 2097152 | bytes 10485760 | tf_op jit(solution)/shard_map/convert_element_type | solution.py:286
  (35 shorter events, 0.4 us)
Async XLA Ops:
  0.0 4.4 %copy-start = (bf16[16,4,32,128]{3,2,1,0:T(8,128)(2,1)S(1)}, bf16[16,4,32,128]{3,2,1,0:T(8,128)(2,1)}, u32[]{:S(2)}) copy-start(bf16[16,4,32,128]{3,2,1,0:T(8,128)(2,1)} %param.21) | copy-start | bytes 1572868
  0.9 20.0 %copy-start.6 = (s32[64]{0:T(128)}, s32[64]{0:T(128)S(1)}, u32[]{:S(2)}) copy-start(s32[64]{0:T(128)S(1)} %reshape.106.slot_ref) | copy-start | bytes 772
  17.0 10.4 %copy-start.8 = (s32[1,2,4]{2,1,0:T(2,128)S(1)}, s32[1,2,4]{2,1,0:T(2,128)}, u32[]{:S(2)}) copy-start(s32[1,2,4]{2,1,0:T(2,128)} %param.17) | copy-start | bytes 100
  17.0 10.5 %copy-start.1 = (bf16[32,128,256]{2,1,0:T(8,128)(2,1)S(1)}, bf16[32,128,256]{2,1,0:T(8,128)(2,1)}, u32[]{:S(2)}) copy-start(bf16[32,128,256]{2,1,0:T(8,128)(2,1)} %blocks_ref.1) | copy-start | bytes 6291460
  21.0 32.1 %all-to-all-start = ((f32[16,4,32,256]{3,2,1,0:T(8,128)}), f32[16,4,32,256]{3,2,1,0:T(8,128)}, u32[]{:S(2)}, u32[]{:S(2)}) async-start(f32[16,4,32,256]{3,2,1,0:T(8,128)} %bitcast.28), calls=%async_computation | async-start | bytes 4194304 | tf_op jit(solution)/shard_map/all_to_all | solution.py:259
  58.8 18.8 %copy-start.3 = (s32[32,16]{0,1:T(8,128)S(1)}, s32[32,16]{0,1:T(8,128)}, u32[]{:S(2)}) copy-start(s32[32,16]{0,1:T(8,128)} %param.14) | copy-start | bytes 6148
  58.8 19.5 %copy-start.7 = (s32[1,16]{1,0:T(1,128)S(1)}, s32[1,16]{1,0:T(1,128)}, u32[]{:S(2)}) copy-start(s32[1,16]{1,0:T(1,128)} %param.16) | copy-start | bytes 196
  58.8 19.7 %copy-start.5 = (s32[1,16,4]{1,2,0:T(4,128)S(1)}, s32[1,16,4]{1,2,0:T(4,128)}, u32[]{:S(2)}) copy-start(s32[1,16,4]{1,2,0:T(4,128)} %param.15) | copy-start | bytes 772
  61.5 102.2 %all-to-all-start.1 = ((bf16[16,4,32,384]{3,2,1,0:T(8,128)(2,1)}), bf16[16,4,32,384]{3,2,1,0:T(8,128)(2,1)}, u32[]{:S(2)}, u32[]{:S(2)}) async-start(bf16[16,4,32,384]{3,2,1,0:T(8,128)(2,1)} %bitcast.30), calls=%async_computation.1 | async-start | bytes 3145728 | tf_op jit(solution)/shard_map/all_to_all | solution.py:270
  68.7 82.1 %collective-permute-start.1 = (bf16[4,128,256]{2,1,0:T(8,128)(2,1)}, bf16[4,128,256]{2,1,0:T(8,128)(2,1)S(1)}, u32[]{:S(2)}, u32[]{:S(2)}) collective-permute-start(bf16[4,128,256]{2,1,0:T(8,128)(2,1)} %get-tuple-element.12), channel_id=1, source_target_pairs={{1,0},{2,1},{3,2},{4,3},{5,4},{6,5},{7,6},{9,8},{10,9},{11,10},{12... | collective-permute-start | bytes 786440 | tf_op jit(solution)/shard_map/ppermute | solution.py:19
  74.2 76.5 %collective-permute-start = (bf16[4,128,256]{2,1,0:T(8,128)(2,1)S(1)}, bf16[4,128,256]{2,1,0:T(8,128)(2,1)S(1)}, u32[]{:S(2)}, u32[]{:S(2)}) collective-permute-start(bf16[4,128,256]{2,1,0:T(8,128)(2,1)S(1)} %get-tuple-element.11), channel_id=1, source_target_pairs={{0,1},{1,2},{2,3},{3,4},{4,5},{5,6},{6,7},{8,9},{9,10},{10,11},{11... | collective-permute-start | bytes 786440 | tf_op jit(solution)/shard_map/ppermute | solution.py:18
  163.7 2.7 %copy-start.4 = (s32[64]{0:T(128)S(1)}, s32[64]{0:T(128)}, u32[]{:S(2)}) copy-start(s32[64]{0:T(128)} %eq.15.index_ref) | copy-start | bytes 772
  166.4 3.0 %copy-start.2 = (f32[32,128,256]{2,1,0:T(8,128)S(1)}, f32[32,128,256]{2,1,0:T(8,128)}, u32[]{:S(2)}) copy-start(f32[32,128,256]{2,1,0:T(8,128)} %shard_map.119) | copy-start | bytes 12582916

commit v12 on v11

--- a/solution.py
+++ b/solution.py
@@ -260,6 +260,7 @@
     own_slots = blocks.shape[0] // halo_width
     ext_slots = own_slots + dom_count + 2 * rim_width // halo_width
     (ext_frame,) = dom_exchange([halo_flat], 1, [(own_slots, ext_slots)])
+    partial_in, ext_frame = lax.optimization_barrier((partial_in, ext_frame))
     partial_in = partial_in.reshape(slot_total, seg, vec_count)
     summed = well_sums(well_slot.reshape(-1), partial_in, wells)
     well_state = well_states_of(summed, well_inverse, well_count)

time: 174 us -> 154 us (0.89)
  the two profiles are of different devices: /device:TPU:91 before, /device:TPU:66 now
where the time goes in v12:
time: 154 us
  Pallas kernels  104 us (68%)
  starting transfers between devices  15.9 us (10%)
  local copies, waits for them, and re-layouts  13.9 us (9%)
  other arithmetic  9.8 us (6%)
  matrix products  7.41 us (5%)
  waiting for transfers between devices  2.02 us (1%)
    pallas_call x2, Pallas kernels, dom_exchange(): pl.pallas_call(functools.partial(exchange_kernel, tuple((f[0] for f in fr...  85.2 us
    pallas_call x1, Pallas kernels, local_product(): pl.pallas_call(product_kernel, out_shape=jax.ShapeDtypeStruct((block_rows...  12.1 us
    all_to_all x1, starting transfers between devices, on_device(): lax.all_to_all(partial, 'dom', split_axis=0, concat_axis=0, tiled=True)  6.38 us
    all_to_all x1, starting transfers between devices, on_device(): lax.all_to_all(state_pack, 'dom', split_axis=0, concat_axis=0, tiled=True)  4.98 us
    pallas_call x1, Pallas kernels, partial_sums(): pl.pallas_call(partial_kernel, out_shape=jax.ShapeDtypeStruct((slots, seg...  3.91 us
    convert_element_type x1, other arithmetic, on_device(): return subtract_incoming(product, well_send, incoming).astype(jnp.bfloat16)  3.65 us
  transfers between devices with their start and end apart: 4, of which 1 were waited for; matrix products, arithmetic and copies ran while one was open for 7% of the time, Pallas kernels for 54%

profile of v12, /device:TPU:66, one launch (start us, length us, event | category | flops | bytes accessed | tf_op | source)
XLA Modules:
  0.0 153.5 jit_solution(13716426311112019180)
XLA Ops:
  0.0 0.8 copy.18
  0.8 0.7 reshape_squeeze.6.index_ref
  1.5 0.8 copy.19
  2.2 0.1 reshape.105.slot_ref
  2.4 2.0 %sort.17 = (s32[64]{0:T(128)}, s32[64]{0:T(128)S(1)}) sort(s32[64]{0:T(128)S(1)} %reshape.105.slot_ref, s32[64]{0:T(128)S(1)} %iota.17), dimensions={0}, to_apply=%region_0.0 | sort | flops 384 | bytes 1024 | tf_op jit(solution)/shard_map/jit(argsort)/sort | solution.py:249
  4.4 1.4 gather_fusion
  5.8 14.3 %shard_map.118 = (bf16[16,128,128]{2,1,0:T(8,128)(2,1)}, bf16[14,64,128]{2,1,0:T(8,128)(2,1)}) custom-call(bf16[16,128,128]{2,1,0:T(8,128)(2,1)} %bitcast.31), custom_call_target="tpu_custom_call" | custom-call | tf_op jit(solution)/shard_map/pallas_call | solution.py:187
  20.2 3.9 %shard_map.119 = f32[64,32,256]{2,1,0:T(8,128)} custom-call(s32[64]{0:T(128)} %reshape_squeeze.6.index_ref, bf16[64,32,128]{2,1,0:T(8,128)(2,1)} %bitcast.32, bf16[32,128,256]{2,1,0:T(8,128)(2,1)} %blocks_ref.1), custom_call_target="tpu_custom_call" | custom-call | tf_op jit(solution)/shard_map/pallas_call | solution.py:92
  24.1 6.4 %all-to-all-start = ((f32[16,4,32,256]{3,2,1,0:T(8,128)}), f32[16,4,32,256]{3,2,1,0:T(8,128)}, u32[]{:S(2)}, u32[]{:S(2)}) async-start(f32[16,4,32,256]{3,2,1,0:T(8,128)} %bitcast.28), calls=%async_computation | async-start | bytes 4194304 | tf_op jit(solution)/shard_map/all_to_all | solution.py:259
  30.6 0.1 reshape.125
  30.7 2.9 %gather_fusion.1 = bf16[64,128,256]{2,1,0:T(8,128)(2,1)} fusion(bf16[32,128,256]{2,1,0:T(8,128)(2,1)S(1)} %copy-done.1, s32[1024]{0:T(1024)S(1)} %pad_clamp_fusion.2), kind=kCustom, calls=%fused_computation.1 | custom fusion | bytes 8388864 | tf_op jit(solution)/shard_map/gather | solution.py:245
  33.6 70.8 %shard_map.120 = (bf16[26,512,256]{2,1,0:T(8,128)(2,1)}, bf16[14,256,256]{2,1,0:T(8,128)(2,1)}) custom-call(bf16[16,512,256]{2,1,0:T(8,128)(2,1)} %bitcast.27), custom_call_target="tpu_custom_call" | custom-call | tf_op jit(solution)/shard_map/pallas_call | solution.py:187
  104.5 1.7 %gather_fusion.4 = bf16[64,32,128]{2,1,0:T(8,128)(2,1)S(1)} fusion(bf16[64,32,128]{2,1,0:T(8,128)(2,1)} %bitcast.33, s32[1024]{0:T(1024)S(1)} %get-tuple-element.20), kind=kCustom, calls=%fused_computation.4 | custom fusion | bytes 1048832 | tf_op jit(solution)/shard_map/gather | solution.py:268
  106.9 2.5 %shard_map.122 = f32[16,32,256]{2,1,0:T(8,128)} custom-call(s32[64]{0:T(128)} %copy-done.6, f32[64,32,256]{2,1,0:T(8,128)} %bitcast.10.partial_ref), custom_call_target="tpu_custom_call" | custom-call | tf_op jit(solution)/shard_map/pallas_call | solution.py:74
  109.4 1.7 %fusion.3 = bf16[16,32,256]{2,1,0:T(8,128)(2,1)S(1)} fusion(f32[16,32,256]{2,1,0:T(8,128)} %shard_map.122, f32[16,32,32]{2,1,0:T(8,128)} %param.23, f32[16]{0:T(128)S(1)} %compare_convert_fusion), kind=kOutput, calls=%fused_computation.12 | convolution fusion | flops 50593792 | bytes 852032 | tf_op jit(solution)/shard_map/wst,wtv->wsv/dot_general | solution.py:209
  111.1 1.6 %gather_fusion.3 = bf16[64,32,256]{2,1,0:T(8,128)(2,1)} fusion(bf16[16,32,256]{2,1,0:T(8,128)(2,1)S(1)} %fusion.3, s32[1024]{0:T(1024)S(1)} %get-tuple-element.19), kind=kCustom, calls=%fused_computation.3 | custom fusion | bytes 2097408 | tf_op jit(solution)/shard_map/gather | solution.py:267
  112.7 2.6 %pad_maximum_fusion = bf16[64,32,384]{2,1,0:T(8,128)(2,1)} fusion(bf16[64,32,128]{2,1,0:T(8,128)(2,1)S(1)} %gather_fusion.4, bf16[64,32,256]{2,1,0:T(8,128)(2,1)} %gather_fusion.3), kind=kLoop, calls=%fused_computation.9 | loop fusion | flops 3145728 | bytes 3145728 | tf_op jit(solution)/shard_map/concatenate | solution.py:269
  115.3 5.0 %all-to-all-start.1 = ((bf16[16,4,32,384]{3,2,1,0:T(8,128)(2,1)}), bf16[16,4,32,384]{3,2,1,0:T(8,128)(2,1)}, u32[]{:S(2)}, u32[]{:S(2)}) async-start(bf16[16,4,32,384]{3,2,1,0:T(8,128)(2,1)} %bitcast.30), calls=%async_computation.1 | async-start | bytes 3145728 | tf_op jit(solution)/shard_map/all_to_all | solution.py:271
  120.2 0.6 gather_fusion.2
  120.8 0.7 fusion.12
  121.6 1.9 %collective-permute-start.1 = (bf16[4,128,256]{2,1,0:T(8,128)(2,1)}, bf16[4,128,256]{2,1,0:T(8,128)(2,1)S(1)}, u32[]{:S(2)}, u32[]{:S(2)}) collective-permute-start(bf16[4,128,256]{2,1,0:T(8,128)(2,1)} %get-tuple-element.16), channel_id=1, source_target_pairs={{1,0},{2,1},{3,2},{4,3},{5,4},{6,5},{7,6},{9,8},{10,9},{11,10},{12... | collective-permute-start | bytes 786440 | tf_op jit(solution)/shard_map/ppermute | solution.py:19
  123.5 2.6 %collective-permute-start = (bf16[4,128,256]{2,1,0:T(8,128)(2,1)S(1)}, bf16[4,128,256]{2,1,0:T(8,128)(2,1)S(1)}, u32[]{:S(2)}, u32[]{:S(2)}) collective-permute-start(bf16[4,128,256]{2,1,0:T(8,128)(2,1)S(1)} %get-tuple-element.15), channel_id=1, source_target_pairs={{0,1},{1,2},{2,3},{3,4},{4,5},{5,6},{6,7},{8,9},{9,10},{10,11},{11... | collective-permute-start | bytes 786440 | tf_op jit(solution)/shard_map/ppermute | solution.py:18
  126.2 0.7 reshape.103.cols_ref
  126.9 0.1 reshape.114
  127.0 0.6 pad_add_fusion.live_ref
  127.6 1.6 %constant_dynamic-update-slice_fusion = bf16[104,128,256]{2,1,0:T(8,128)(2,1)} fusion(bf16[104,128,256]{2,1,0:T(8,128)(2,1)} %bitcast.29, bf16[32,128,256]{2,1,0:T(8,128)(2,1)S(1)} %copy-done.1), kind=kLoop, calls=%fused_computation.37 | loop fusion | bytes 4194304 | tf_op jit(solution)/shard_map/dynamic_update_slice | solution.py:278
  129.2 2.0 %collective-permute-done = bf16[4,128,256]{2,1,0:T(8,128)(2,1)S(1)} collective-permute-done((bf16[4,128,256]{2,1,0:T(8,128)(2,1)S(1)}, bf16[4,128,256]{2,1,0:T(8,128)(2,1)S(1)}, u32[]{:S(2)}, u32[]{:S(2)}) %collective-permute-start) | collective-permute-done | bytes 262176 | tf_op jit(solution)/shard_map/ppermute | solution.py:18
  131.2 0.8 maximum_dynamic-update-slice_fusion.ext_ref
  132.0 12.1 %shard_map.121 = f32[32,128,256]{2,1,0:T(8,128)} custom-call(s32[512]{0:T(512)} %reshape.103.cols_ref, s32[104]{0:T(128)} %pad_add_fusion.live_ref, bf16[104,128,256]{2,1,0:T(8,128)(2,1)} %maximum_dynamic-update-slice_fusion.ext_ref, bf16[32,16,128,128]{3,2,1,0:T(8,128)(2,1)} %tiles_ref.1), custom_call_target="tpu_custom_call" | custom-call | flops 4294967296 | bytes 27787264 | tf_op jit(solution)/shard_map/pallas_call | solution.py:55
  144.1 2.7 %fusion.4 = bf16[64,128,256]{2,1,0:T(8,128)(2,1)S(1)} fusion(bf16[64,32,384]{2,1,0:T(8,128)(2,1)} %bitcast.15), kind=kOutput, calls=%fused_computation.13 | convolution fusion | flops 134217728 | bytes 5767168 | tf_op jit(solution)/shard_map/qsk,qsv->qkv/dot_general | solution.py:281
  146.9 3.0 %fusion = f32[32,128,256]{2,0,1:T(8,128)S(1)} fusion(bf16[64,128,256]{2,1,0:T(8,128)(2,1)S(1)} %fusion.4, s32[64]{0:T(128)S(1)} %copy-done.4), kind=kOutput, calls=%fused_computation.6 | convolution fusion | flops 134219776 | bytes 8388864 | tf_op jit(solution)/shard_map/bq,qkv->bkv/dot_general | solution.py:217
  149.9 3.7 %fusion.1 = bf16[32,128,256]{2,1,0:T(8,128)(2,1)} fusion(f32[32,128,256]{2,1,0:T(8,128)S(1)} %copy-done.2, f32[32,128,256]{2,0,1:T(8,128)S(1)} %fusion), kind=kLoop, calls=%fused_computation.8 | loop fusion | flops 2097152 | bytes 10485760 | tf_op jit(solution)/shard_map/convert_element_type | solution.py:287
  (35 shorter events, 0.4 us)
Async XLA Ops:
  0.0 4.4 %copy-start = (bf16[16,4,32,128]{3,2,1,0:T(8,128)(2,1)S(1)}, bf16[16,4,32,128]{3,2,1,0:T(8,128)(2,1)}, u32[]{:S(2)}) copy-start(bf16[16,4,32,128]{3,2,1,0:T(8,128)(2,1)} %param.21) | copy-start | bytes 1572868
  2.3 21.8 %copy-start.6 = (s32[64]{0:T(128)}, s32[64]{0:T(128)S(1)}, u32[]{:S(2)}) copy-start(s32[64]{0:T(128)S(1)} %reshape.105.slot_ref) | copy-start | bytes 772
  20.2 10.3 %copy-start.5 = (s32[1,16,4]{1,2,0:T(4,128)S(1)}, s32[1,16,4]{1,2,0:T(4,128)}, u32[]{:S(2)}) copy-start(s32[1,16,4]{1,2,0:T(4,128)} %param.15) | copy-start | bytes 772
  20.2 10.5 %copy-start.1 = (bf16[32,128,256]{2,1,0:T(8,128)(2,1)S(1)}, bf16[32,128,256]{2,1,0:T(8,128)(2,1)}, u32[]{:S(2)}) copy-start(bf16[32,128,256]{2,1,0:T(8,128)(2,1)} %blocks_ref.1) | copy-start | bytes 6291460
  24.1 82.8 %all-to-all-start = ((f32[16,4,32,256]{3,2,1,0:T(8,128)}), f32[16,4,32,256]{3,2,1,0:T(8,128)}, u32[]{:S(2)}, u32[]{:S(2)}) async-start(f32[16,4,32,256]{3,2,1,0:T(8,128)} %bitcast.28), calls=%async_computation | async-start | bytes 4194304 | tf_op jit(solution)/shard_map/all_to_all | solution.py:259
  33.6 70.8 %copy-start.8 = (s32[1,2,4]{2,1,0:T(2,128)S(1)}, s32[1,2,4]{2,1,0:T(2,128)}, u32[]{:S(2)}) copy-start(s32[1,2,4]{2,1,0:T(2,128)} %param.17) | copy-start | bytes 100
  112.7 13.4 %copy-start.3 = (s32[32,16]{0,1:T(8,128)S(1)}, s32[32,16]{0,1:T(8,128)}, u32[]{:S(2)}) copy-start(s32[32,16]{0,1:T(8,128)} %param.14) | copy-start | bytes 6148
  112.7 14.2 %copy-start.7 = (s32[1,16]{1,0:T(1,128)S(1)}, s32[1,16]{1,0:T(1,128)}, u32[]{:S(2)}) copy-start(s32[1,16]{1,0:T(1,128)} %param.16) | copy-start | bytes 196
  115.3 28.9 %all-to-all-start.1 = ((bf16[16,4,32,384]{3,2,1,0:T(8,128)(2,1)}), bf16[16,4,32,384]{3,2,1,0:T(8,128)(2,1)}, u32[]{:S(2)}, u32[]{:S(2)}) async-start(bf16[16,4,32,384]{3,2,1,0:T(8,128)(2,1)} %bitcast.30), calls=%async_computation.1 | async-start | bytes 3145728 | tf_op jit(solution)/shard_map/all_to_all | solution.py:271
  121.6 7.6 %collective-permute-start.1 = (bf16[4,128,256]{2,1,0:T(8,128)(2,1)}, bf16[4,128,256]{2,1,0:T(8,128)(2,1)S(1)}, u32[]{:S(2)}, u32[]{:S(2)}) collective-permute-start(bf16[4,128,256]{2,1,0:T(8,128)(2,1)} %get-tuple-element.16), channel_id=1, source_target_pairs={{1,0},{2,1},{3,2},{4,3},{5,4},{6,5},{7,6},{9,8},{10,9},{11,10},{12... | collective-permute-start | bytes 786440 | tf_op jit(solution)/shard_map/ppermute | solution.py:19
  123.5 7.7 %collective-permute-start = (bf16[4,128,256]{2,1,0:T(8,128)(2,1)S(1)}, bf16[4,128,256]{2,1,0:T(8,128)(2,1)S(1)}, u32[]{:S(2)}, u32[]{:S(2)}) collective-permute-start(bf16[4,128,256]{2,1,0:T(8,128)(2,1)S(1)} %get-tuple-element.15), channel_id=1, source_target_pairs={{0,1},{1,2},{2,3},{3,4},{4,5},{5,6},{6,7},{8,9},{9,10},{10,11},{11... | collective-permute-start | bytes 786440 | tf_op jit(solution)/shard_map/ppermute | solution.py:18
  144.1 2.7 %copy-start.4 = (s32[64]{0:T(128)S(1)}, s32[64]{0:T(128)}, u32[]{:S(2)}) copy-start(s32[64]{0:T(128)} %reshape_squeeze.6.index_ref) | copy-start | bytes 772
  146.8 3.0 %copy-start.2 = (f32[32,128,256]{2,1,0:T(8,128)S(1)}, f32[32,128,256]{2,1,0:T(8,128)}, u32[]{:S(2)}) copy-start(f32[32,128,256]{2,1,0:T(8,128)} %shard_map.121) | copy-start | bytes 12582916

commit v13 on v12

--- a/solution.py
+++ b/solution.py
@@ -251,7 +251,9 @@
     in_slots = couple_in.reshape(wells * couplings, seg, cell_count)[slot_order]
     in_slots = in_slots.reshape(dom_count, slot_width * seg, cell_count)
     halo_flat = halo_pack.reshape(dom_count, halo_width * cell_count, vec_count)
-    (in_recv,) = dom_exchange([in_slots], 0)
+    out_slots = couple_out.reshape(wells * couplings, seg, cell_count)[slot_order]
+    out_slots = out_slots.reshape(dom_count, slot_width * seg, cell_count)
+    in_recv, out_recv = dom_exchange([in_slots, out_slots], 0)
     in_recv = in_recv.reshape(dom_count, slot_width, seg, cell_count)
     partial = partial_sums(
         well_send[0].reshape(-1), in_recv.reshape(slot_total, seg, cell_count), blocks
@@ -264,12 +266,9 @@
     partial_in = partial_in.reshape(slot_total, seg, vec_count)
     summed = well_sums(well_slot.reshape(-1), partial_in, wells)
     well_state = well_states_of(summed, well_inverse, well_count)
-    state_slots = well_state[slot_well]
-    out_slots = couple_out.reshape(wells * couplings, seg, cell_count)[slot_order]
-    state_pack = jnp.concatenate([state_slots, out_slots], 2)
-    state_pack = state_pack.reshape(dom_count, slot_width, seg, vec_count + cell_count)
+    state_pack = well_state[slot_well].reshape(dom_count, slot_width, seg, vec_count)
     state_in = lax.all_to_all(state_pack, "dom", split_axis=0, concat_axis=0, tiled=True)
-    state_in = state_in.reshape(slot_total, seg, vec_count + cell_count)
+    state_in = state_in.reshape(slot_total, seg, vec_count)
     live_halo = (jnp.arange(halo_width)[None, :] < halo_counts[0][:, None]).astype(jnp.int32)
     live = jnp.concatenate(
         [jnp.ones((blocks.shape[0],), jnp.int32), live_halo.reshape(-1), jnp.ones((2 * rim_width,), jnp.int32)]
@@ -280,8 +279,8 @@
     product = local_product(extended, live, tile_values, tile_cols)
     incoming = jnp.einsum(
         "qsk,qsv->qkv",
-        state_in[:, :, vec_count:],
-        state_in[:, :, :vec_count],
+        out_recv.reshape(slot_total, seg, cell_count),
+        state_in,
         preferred_element_type=jnp.float32,
     ).astype(jnp.bfloat16)
     return subtract_incoming(product, well_send, incoming).astype(jnp.bfloat16)

time: 154 us -> 151 us (0.981)
  waiting for transfers between devices: 2.02 us -> 0.01 us
    concatenate x1 -> x0, other arithmetic: 2.56 us -> none  [on_device(): state_pack = jnp.concatenate([state_slots, out_slots], 2)]
    ppermute x1, waiting for transfers between devices: 2.01 us -> 0.01 us  [padded(): before = lax.ppermute(last, axis, up)]
  transfers between devices with their start and end apart: 4 -> 4, of which waited for: 1 -> 0; matrix products, arithmetic and copies ran while one was open for 7% -> 8% of each run, Pallas kernels for 54% -> 53%
where the time goes in v13:
time: 151 us
  Pallas kernels  103 us (68%)
  starting transfers between devices  16.4 us (11%)
  local copies, waits for them, and re-layouts  14.5 us (10%)
  other arithmetic  8.29 us (5%)
  matrix products  7.18 us (5%)
    pallas_call x2, Pallas kernels, dom_exchange(): pl.pallas_call(functools.partial(exchange_kernel, tuple((f[0] for f in fr...  84.7 us
    pallas_call x1, Pallas kernels, local_product(): pl.pallas_call(product_kernel, out_shape=jax.ShapeDtypeStruct((block_rows...  12.2 us
    all_to_all x1, starting transfers between devices, on_device(): lax.all_to_all(partial, 'dom', split_axis=0, concat_axis=0, tiled=True)  6.6 us
    all_to_all x1, starting transfers between devices, on_device(): lax.all_to_all(state_pack, 'dom', split_axis=0, concat_axis=0, tiled=True)  5.5 us
    pallas_call x1, Pallas kernels, partial_sums(): pl.pallas_call(partial_kernel, out_shape=jax.ShapeDtypeStruct((slots, seg...  3.91 us
    convert_element_type x1, other arithmetic, on_device(): return subtract_incoming(product, well_send, incoming).astype(jnp.bfloat16)  3.65 us
    dot_general x1, matrix products, subtract_incoming(): jnp.einsum('bq,qkv->bkv', selector, flat_rows, preferred_element_type=jnp...  3.02 us
  transfers between devices with their start and end apart: 4, of which 0 were waited for; matrix products, arithmetic and copies ran while one was open for 8% of the time, Pallas kernels for 53%

profile of v13, /device:TPU:66, one launch (start us, length us, event | category | flops | bytes accessed | tf_op | source)
XLA Modules:
  0.0 150.6 jit_solution(3952186864693610061)
XLA Ops:
  0.0 0.8 copy.18
  0.8 0.6 reshape_squeeze.6.index_ref
  1.4 0.8 copy.19
  2.1 0.1 reshape.111.slot_ref
  2.3 2.0 %sort.17 = (s32[64]{0:T(128)}, s32[64]{0:T(128)S(1)}) sort(s32[64]{0:T(128)S(1)} %reshape.111.slot_ref, s32[64]{0:T(128)S(1)} %iota.17), dimensions={0}, to_apply=%region_0.0 | sort | flops 384 | bytes 1024 | tf_op jit(solution)/shard_map/jit(argsort)/sort | solution.py:249
  4.3 1.4 gather_fusion
  5.7 2.5 %gather_fusion.1 = bf16[64,32,128]{2,1,0:T(8,128)(2,1)} fusion(bf16[64,32,128]{2,1,0:T(8,128)(2,1)} %bitcast.38, s32[1024]{0:T(1024)S(1)} %get-tuple-element.22), kind=kCustom, calls=%fused_computation.1 | custom fusion | bytes 1048832 | tf_op jit(solution)/shard_map/gather | solution.py:254
  8.2 19.2 %shard_map.118 = (bf16[16,128,128]{2,1,0:T(8,128)(2,1)}, bf16[16,128,128]{2,1,0:T(8,128)(2,1)}, bf16[14,64,128]{2,1,0:T(8,128)(2,1)}, bf16[14,64,128]{2,1,0:T(8,128)(2,1)}) custom-call(bf16[16,128,128]{2,1,0:T(8,128)(2,1)} %bitcast.35, bf16[16,128,128]{2,1,0:T(8,128)(2,1)} %bitcast.36), custom_call_target="tpu_custom_call" | custom-call | tf_op jit(solution)/shard_map/pallas_call | solution.py:187
  27.4 3.9 %shard_map.119 = f32[64,32,256]{2,1,0:T(8,128)} custom-call(s32[64]{0:T(128)} %reshape_squeeze.6.index_ref, bf16[64,32,128]{2,1,0:T(8,128)(2,1)} %bitcast.37, bf16[32,128,256]{2,1,0:T(8,128)(2,1)} %blocks_ref.1), custom_call_target="tpu_custom_call" | custom-call | tf_op jit(solution)/shard_map/pallas_call | solution.py:92
  31.3 6.6 %all-to-all-start = ((f32[16,4,32,256]{3,2,1,0:T(8,128)}), f32[16,4,32,256]{3,2,1,0:T(8,128)}, u32[]{:S(2)}, u32[]{:S(2)}) async-start(f32[16,4,32,256]{3,2,1,0:T(8,128)} %bitcast.32), calls=%async_computation | async-start | bytes 4194304 | tf_op jit(solution)/shard_map/all_to_all | solution.py:261
  38.0 0.1 reshape_squeeze.7
  38.1 0.6 gather_fusion.3
  38.6 0.7 fusion.9
  39.4 1.9 %collective-permute-start.1 = (bf16[4,128,256]{2,1,0:T(8,128)(2,1)}, bf16[4,128,256]{2,1,0:T(8,128)(2,1)}, u32[]{:S(2)}, u32[]{:S(2)}) collective-permute-start(bf16[4,128,256]{2,1,0:T(8,128)(2,1)} %get-tuple-element.18), channel_id=1, source_target_pairs={{1,0},{2,1},{3,2},{4,3},{5,4},{6,5},{7,6},{9,8},{10,9},{11,10},{12... | collective-permute-start | bytes 786440 | tf_op jit(solution)/shard_map/ppermute | solution.py:19
  41.3 2.4 %collective-permute-start = (bf16[4,128,256]{2,1,0:T(8,128)(2,1)S(1)}, bf16[4,128,256]{2,1,0:T(8,128)(2,1)}, u32[]{:S(2)}, u32[]{:S(2)}) collective-permute-start(bf16[4,128,256]{2,1,0:T(8,128)(2,1)S(1)} %get-tuple-element.17), channel_id=1, source_target_pairs={{0,1},{1,2},{2,3},{3,4},{4,5},{5,6},{6,7},{8,9},{9,10},{10,11},{11... | collective-permute-start | bytes 786440 | tf_op jit(solution)/shard_map/ppermute | solution.py:18
  43.8 0.7 reshape.109.cols_ref
  44.5 0.1 copy.20
  44.6 0.1 reshape.141
  44.7 2.9 %gather_fusion.2 = bf16[64,128,256]{2,1,0:T(8,128)(2,1)} fusion(bf16[32,128,256]{2,1,0:T(8,128)(2,1)S(1)} %copy-done.1, s32[1024]{0:T(1024)S(1)} %pad_clamp_fusion.2), kind=kCustom, calls=%fused_computation.2 | custom fusion | bytes 8388864 | tf_op jit(solution)/shard_map/gather | solution.py:245
  47.6 65.5 %shard_map.120 = (bf16[26,512,256]{2,1,0:T(8,128)(2,1)}, bf16[14,256,256]{2,1,0:T(8,128)(2,1)}) custom-call(bf16[16,512,256]{2,1,0:T(8,128)(2,1)} %bitcast.31), custom_call_target="tpu_custom_call" | custom-call | tf_op jit(solution)/shard_map/pallas_call | solution.py:187
  113.7 2.5 %shard_map.122 = f32[16,32,256]{2,1,0:T(8,128)} custom-call(s32[64]{0:T(128)} %copy-done.8, f32[64,32,256]{2,1,0:T(8,128)} %bitcast.13.partial_ref), custom_call_target="tpu_custom_call" | custom-call | tf_op jit(solution)/shard_map/pallas_call | solution.py:74
  116.2 1.6 %fusion.3 = bf16[16,32,256]{2,1,0:T(8,128)(2,1)S(1)} fusion(f32[16,32,256]{2,1,0:T(8,128)} %shard_map.122, f32[16,32,32]{2,1,0:T(8,128)S(1)} %copy-done.4, f32[16]{0:T(128)S(1)} %compare_convert_fusion), kind=kOutput, calls=%fused_computation.11 | convolution fusion | flops 50593792 | bytes 852032 | tf_op jit(solution)/shard_map/wst,wtv->wsv/dot_general | solution.py:209
  117.9 1.6 %gather_fusion.4 = bf16[64,32,256]{2,1,0:T(8,128)(2,1)} fusion(bf16[16,32,256]{2,1,0:T(8,128)(2,1)S(1)} %fusion.3, s32[1024]{0:T(1024)S(1)} %get-tuple-element.21), kind=kCustom, calls=%fused_computation.4 | custom fusion | bytes 2097408 | tf_op jit(solution)/shard_map/gather | solution.py:269
  119.4 5.5 %all-to-all-start.1 = ((bf16[16,4,32,256]{3,2,1,0:T(8,128)(2,1)}), bf16[16,4,32,256]{3,2,1,0:T(8,128)(2,1)}, u32[]{:S(2)}, u32[]{:S(2)}) async-start(bf16[16,4,32,256]{3,2,1,0:T(8,128)(2,1)} %bitcast.34), calls=%async_computation.1 | async-start | bytes 2097152 | tf_op jit(solution)/shard_map/all_to_all | solution.py:270
  125.0 0.1 reshape.122
  125.1 0.6 pad_add_fusion.live_ref
  125.8 1.5 constant_dynamic-update-slice_fusion
  127.2 1.9 %maximum_dynamic-update-slice_fusion.ext_ref = bf16[104,128,256]{2,1,0:T(8,128)(2,1)} fusion(bf16[104,128,256]{2,1,0:T(8,128)(2,1)} %constant_dynamic-update-slice_fusion, bf16[4,128,256]{2,1,0:T(8,128)(2,1)} %collective-permute-done.1, bf16[4,128,256]{2,1,0:T(8,128)(2,1)} %collective-permute-done), kind=kLoop, calls=%fused_computation.12 | loop fusion | flops 1048576 | bytes 1048576 | tf_op jit(solution)/shard_map/dynamic_update_slice | solution.py:278
  129.1 12.2 %shard_map.121 = f32[32,128,256]{2,1,0:T(8,128)} custom-call(s32[512]{0:T(512)} %reshape.109.cols_ref, s32[104]{0:T(128)} %pad_add_fusion.live_ref, bf16[104,128,256]{2,1,0:T(8,128)(2,1)} %maximum_dynamic-update-slice_fusion.ext_ref, bf16[32,16,128,128]{3,2,1,0:T(8,128)(2,1)} %tiles_ref.1), custom_call_target="tpu_custom_call" | custom-call | flops 4294967296 | bytes 27787264 | tf_op jit(solution)/shard_map/pallas_call | solution.py:55
  141.3 2.5 %fusion.10 = bf16[64,128,256]{2,1,0:T(8,128)(2,1)S(1)} fusion(bf16[64,32,128]{2,1,0:T(8,128)(2,1)S(1)} %bitcast.39, bf16[64,32,256]{2,1,0:T(8,128)(2,1)} %bitcast.17), kind=kOutput, calls=%fused_computation.35 | convolution fusion | flops 134217728 | bytes 5767168 | tf_op jit(solution)/shard_map/qsk,qsv->qkv/dot_general | solution.py:280
  143.9 3.0 %fusion = f32[32,128,256]{2,0,1:T(8,128)S(1)} fusion(bf16[64,128,256]{2,1,0:T(8,128)(2,1)S(1)} %fusion.10, s32[64]{0:T(128)S(1)} %copy-done.6), kind=kOutput, calls=%fused_computation.6 | convolution fusion | flops 134219776 | bytes 8388864 | tf_op jit(solution)/shard_map/bq,qkv->bkv/dot_general | solution.py:217
  146.9 3.7 %fusion.1 = bf16[32,128,256]{2,1,0:T(8,128)(2,1)} fusion(f32[32,128,256]{2,1,0:T(8,128)S(1)} %copy-done.2, f32[32,128,256]{2,0,1:T(8,128)S(1)} %fusion), kind=kLoop, calls=%fused_computation.8 | loop fusion | flops 2097152 | bytes 10485760 | tf_op jit(solution)/shard_map/convert_element_type | solution.py:286
  (38 shorter events, 0.3 us)
Async XLA Ops:
  0.0 4.3 %copy-start = (bf16[16,4,32,128]{3,2,1,0:T(8,128)(2,1)S(1)}, bf16[16,4,32,128]{3,2,1,0:T(8,128)(2,1)}, u32[]{:S(2)}) copy-start(bf16[16,4,32,128]{3,2,1,0:T(8,128)(2,1)} %param.21) | copy-start | bytes 1572868
  2.2 29.1 %copy-start.8 = (s32[64]{0:T(128)}, s32[64]{0:T(128)S(1)}, u32[]{:S(2)}) copy-start(s32[64]{0:T(128)S(1)} %reshape.111.slot_ref) | copy-start | bytes 772
  27.4 10.5 %copy-start.10 = (s32[1,2,4]{2,1,0:T(2,128)S(1)}, s32[1,2,4]{2,1,0:T(2,128)}, u32[]{:S(2)}) copy-start(s32[1,2,4]{2,1,0:T(2,128)} %param.17) | copy-start | bytes 100
  27.4 10.6 %copy-start.1 = (bf16[32,128,256]{2,1,0:T(8,128)(2,1)S(1)}, bf16[32,128,256]{2,1,0:T(8,128)(2,1)}, u32[]{:S(2)}) copy-start(bf16[32,128,256]{2,1,0:T(8,128)(2,1)} %blocks_ref.1) | copy-start | bytes 6291460
  31.3 12.4 %copy-start.5 = (s32[32,16]{0,1:T(8,128)S(1)}, s32[32,16]{0,1:T(8,128)}, u32[]{:S(2)}) copy-start(s32[32,16]{0,1:T(8,128)} %param.14) | copy-start | bytes 6148
  31.3 13.2 %copy-start.7 = (s32[1,16,4]{1,2,0:T(4,128)S(1)}, s32[1,16,4]{1,2,0:T(4,128)}, u32[]{:S(2)}) copy-start(s32[1,16,4]{1,2,0:T(4,128)} %param.15) | copy-start | bytes 772
  31.3 82.4 %all-to-all-start = ((f32[16,4,32,256]{3,2,1,0:T(8,128)}), f32[16,4,32,256]{3,2,1,0:T(8,128)}, u32[]{:S(2)}, u32[]{:S(2)}) async-start(f32[16,4,32,256]{3,2,1,0:T(8,128)} %bitcast.32), calls=%async_computation | async-start | bytes 4194304 | tf_op jit(solution)/shard_map/all_to_all | solution.py:261
  39.4 87.8 %collective-permute-start.1 = (bf16[4,128,256]{2,1,0:T(8,128)(2,1)}, bf16[4,128,256]{2,1,0:T(8,128)(2,1)}, u32[]{:S(2)}, u32[]{:S(2)}) collective-permute-start(bf16[4,128,256]{2,1,0:T(8,128)(2,1)} %get-tuple-element.18), channel_id=1, source_target_pairs={{1,0},{2,1},{3,2},{4,3},{5,4},{6,5},{7,6},{9,8},{10,9},{11,10},{12... | collective-permute-start | bytes 786440 | tf_op jit(solution)/shard_map/ppermute | solution.py:19
  41.3 85.9 %collective-permute-start = (bf16[4,128,256]{2,1,0:T(8,128)(2,1)S(1)}, bf16[4,128,256]{2,1,0:T(8,128)(2,1)}, u32[]{:S(2)}, u32[]{:S(2)}) collective-permute-start(bf16[4,128,256]{2,1,0:T(8,128)(2,1)S(1)} %get-tuple-element.17), channel_id=1, source_target_pairs={{0,1},{1,2},{2,3},{3,4},{4,5},{5,6},{6,7},{8,9},{9,10},{10,11},{11... | collective-permute-start | bytes 786440 | tf_op jit(solution)/shard_map/ppermute | solution.py:18
  47.6 68.7 %copy-start.4 = (f32[16,32,32]{2,1,0:T(8,128)S(1)}, f32[16,32,32]{2,1,0:T(8,128)}, u32[]{:S(2)}) copy-start(f32[16,32,32]{2,1,0:T(8,128)} %param.23) | copy-start | bytes 196612
  113.0 11.9 %copy-start.9 = (s32[1,16]{1,0:T(1,128)S(1)}, s32[1,16]{1,0:T(1,128)}, u32[]{:S(2)}) copy-start(s32[1,16]{1,0:T(1,128)} %param.16) | copy-start | bytes 196
  119.4 21.9 %all-to-all-start.1 = ((bf16[16,4,32,256]{3,2,1,0:T(8,128)(2,1)}), bf16[16,4,32,256]{3,2,1,0:T(8,128)(2,1)}, u32[]{:S(2)}, u32[]{:S(2)}) async-start(bf16[16,4,32,256]{3,2,1,0:T(8,128)(2,1)} %bitcast.34), calls=%async_computation.1 | async-start | bytes 2097152 | tf_op jit(solution)/shard_map/all_to_all | solution.py:270
  129.1 12.2 %copy-start.3 = (bf16[16,128,128]{2,1,0:T(8,128)(2,1)S(1)}, bf16[16,128,128]{2,1,0:T(8,128)(2,1)}, u32[]{:S(2)}) copy-start(bf16[16,128,128]{2,1,0:T(8,128)(2,1)} %get-tuple-element.15) | copy-start | bytes 1572868
  141.3 2.5 %copy-start.6 = (s32[64]{0:T(128)S(1)}, s32[64]{0:T(128)}, u32[]{:S(2)}) copy-start(s32[64]{0:T(128)} %reshape_squeeze.6.index_ref) | copy-start | bytes 772
  143.9 3.0 %copy-start.2 = (f32[32,128,256]{2,1,0:T(8,128)S(1)}, f32[32,128,256]{2,1,0:T(8,128)}, u32[]{:S(2)}) copy-start(f32[32,128,256]{2,1,0:T(8,128)} %shard_map.121) | copy-start | bytes 12582916

commit v14 on v13

--- a/solution.py
+++ b/solution.py
@@ -201,6 +201,25 @@
         compiler_params=pltpu.CompilerParams(collective_id=collective, has_side_effects=True),
     )(*values)
     return result[:parts]
+
+
+def finish_kernel(targets_ref, product_ref, incoming_ref, out_ref, acc_ref):
+    acc_ref[...] = product_ref[...]
+    for q in range(incoming_ref.shape[0]):
+        target = targets_ref[q]
+        acc_ref[target] = acc_ref[target] - incoming_ref[q].astype(jnp.float32)
+    out_ref[...] = acc_ref[...].astype(out_ref.dtype)
+
+
+def finish(product, incoming, targets):
+    vmem = pl.BlockSpec(memory_space=pltpu.VMEM)
+    return pl.pallas_call(
+        finish_kernel,
+        out_shape=jax.ShapeDtypeStruct(product.shape, jnp.bfloat16),
+        in_specs=[pl.BlockSpec(memory_space=pltpu.SMEM), vmem, vmem],
+        out_specs=vmem,
+        scratch_shapes=[pltpu.VMEM(product.shape, jnp.float32)],
+    )(targets, product, incoming)
 
 
 def well_states_of(summed, well_inverse, well_count):
@@ -283,7 +302,7 @@
         state_in,
         preferred_element_type=jnp.float32,
     ).astype(jnp.bfloat16)
-    return subtract_incoming(product, well_send, incoming).astype(jnp.bfloat16)
+    return finish(product, incoming, well_send[0].reshape(-1))
 
 
 def solution(mesh):

time: 151 us -> 153 us (1.013)
  Pallas kernels: 103 us -> 109 us
  other arithmetic: 8.29 us -> 4.66 us
    pallas_call x0 -> x1, Pallas kernels: none -> 6.13 us  [finish(): pl.pallas_call(finish_kernel, out_shape=jax.ShapeDtypeStruct(product.shap...]
    convert_element_type x1 -> x0, other arithmetic: 3.65 us -> none  [on_device(): return subtract_incoming(product, well_send, incoming).astype(jnp.bfloat16)]
    dot_general x1 -> x0, matrix products: 3.02 us -> none  [subtract_incoming(): jnp.einsum('bq,qkv->bkv', selector, flat_rows, preferred_element_type=jnp...]
    dot_general x1, matrix products: 2.53 us -> 4.48 us  [on_device(): jnp.einsum('qsk,qsv->qkv', out_recv.reshape(slot_total, seg, cell_count),...]
where the time goes in v14:
time: 153 us; the launch traced here: 152 us
  Pallas kernels  109 us (71%)
  starting transfers between devices  16.4 us (11%)
  local copies, waits for them, and re-layouts  14.7 us (10%)
  matrix products  6.1 us (4%)
  other arithmetic  4.66 us (3%)
    pallas_call x2, Pallas kernels, dom_exchange(): pl.pallas_call(functools.partial(exchange_kernel, tuple((f[0] for f in fr...  84.7 us
    pallas_call x1, Pallas kernels, local_product(): pl.pallas_call(product_kernel, out_shape=jax.ShapeDtypeStruct((block_rows...  12.2 us
    all_to_all x1, starting transfers between devices, on_device(): lax.all_to_all(partial, 'dom', split_axis=0, concat_axis=0, tiled=True)  6.6 us
    pallas_call x1, Pallas kernels, finish(): pl.pallas_call(finish_kernel, out_shape=jax.ShapeDtypeStruct(product.shap...  6.13 us
    all_to_all x1, starting transfers between devices, on_device(): lax.all_to_all(state_pack, 'dom', split_axis=0, concat_axis=0, tiled=True)  5.49 us
    dot_general x1, matrix products, on_device(): jnp.einsum('qsk,qsv->qkv', out_recv.reshape(slot_total, seg, cell_count),...  4.48 us
    pallas_call x1, Pallas kernels, partial_sums(): pl.pallas_call(partial_kernel, out_shape=jax.ShapeDtypeStruct((slots, seg...  3.91 us
  transfers between devices with their start and end apart: 4, of which 0 were waited for; matrix products, arithmetic and copies ran while one was open for 8% of the time, Pallas kernels for 53%

profile of v14, /device:TPU:66, one launch (start us, length us, event | category | flops | bytes accessed | tf_op | source)
XLA Modules:
  0.0 152.2 jit_solution(11794979691760086569)
XLA Ops:
  0.0 0.8 copy.16
  0.8 0.7 reshape_squeeze.7.index_ref.targets_ref
  1.5 0.8 copy.18
  2.2 0.1 reshape.110.slot_ref
  2.4 2.0 %sort.17 = (s32[64]{0:T(128)}, s32[64]{0:T(128)S(1)}) sort(s32[64]{0:T(128)S(1)} %reshape.110.slot_ref, s32[64]{0:T(128)S(1)} %iota.13), dimensions={0}, to_apply=%region_0.0 | sort | flops 384 | bytes 1024 | tf_op jit(solution)/shard_map/jit(argsort)/sort | solution.py:268
  4.4 1.4 gather_fusion
  5.8 2.5 %gather_fusion.1 = bf16[64,32,128]{2,1,0:T(8,128)(2,1)} fusion(bf16[64,32,128]{2,1,0:T(8,128)(2,1)} %bitcast.35, s32[1024]{0:T(1024)S(1)} %get-tuple-element.22), kind=kCustom, calls=%fused_computation.1 | custom fusion | bytes 1048832 | tf_op jit(solution)/shard_map/gather | solution.py:273
  8.3 19.2 %shard_map.118 = (bf16[16,128,128]{2,1,0:T(8,128)(2,1)}, bf16[16,128,128]{2,1,0:T(8,128)(2,1)}, bf16[14,64,128]{2,1,0:T(8,128)(2,1)}, bf16[14,64,128]{2,1,0:T(8,128)(2,1)}) custom-call(bf16[16,128,128]{2,1,0:T(8,128)(2,1)} %bitcast.32, bf16[16,128,128]{2,1,0:T(8,128)(2,1)} %bitcast.33), custom_call_target="tpu_custom_call" | custom-call | tf_op jit(solution)/shard_map/pallas_call | solution.py:187
  27.5 3.9 %shard_map.119 = f32[64,32,256]{2,1,0:T(8,128)} custom-call(s32[64]{0:T(128)} %reshape_squeeze.7.index_ref.targets_ref, bf16[64,32,128]{2,1,0:T(8,128)(2,1)} %bitcast.34, bf16[32,128,256]{2,1,0:T(8,128)(2,1)} %blocks_ref.1), custom_call_target="tpu_custom_call" | custom-call | tf_op jit(solution)/shard_map/pallas_call | solution.py:92
  31.5 6.6 %all-to-all-start = ((f32[16,4,32,256]{3,2,1,0:T(8,128)}), f32[16,4,32,256]{3,2,1,0:T(8,128)}, u32[]{:S(2)}, u32[]{:S(2)}) async-start(f32[16,4,32,256]{3,2,1,0:T(8,128)} %bitcast.29), calls=%async_computation | async-start | bytes 4194304 | tf_op jit(solution)/shard_map/all_to_all | solution.py:280
  38.1 0.1 reshape_squeeze.8
  38.2 0.6 gather_fusion.3
  38.7 0.8 fusion.4
  39.5 1.9 %collective-permute-start.1 = (bf16[4,128,256]{2,1,0:T(8,128)(2,1)}, bf16[4,128,256]{2,1,0:T(8,128)(2,1)}, u32[]{:S(2)}, u32[]{:S(2)}) collective-permute-start(bf16[4,128,256]{2,1,0:T(8,128)(2,1)} %get-tuple-element.18), channel_id=1, source_target_pairs={{1,0},{2,1},{3,2},{4,3},{5,4},{6,5},{7,6},{9,8},{10,9},{11,10},{12... | collective-permute-start | bytes 786440 | tf_op jit(solution)/shard_map/ppermute | solution.py:19
  41.4 2.4 %collective-permute-start = (bf16[4,128,256]{2,1,0:T(8,128)(2,1)S(1)}, bf16[4,128,256]{2,1,0:T(8,128)(2,1)}, u32[]{:S(2)}, u32[]{:S(2)}) collective-permute-start(bf16[4,128,256]{2,1,0:T(8,128)(2,1)S(1)} %get-tuple-element.17), channel_id=1, source_target_pairs={{0,1},{1,2},{2,3},{3,4},{4,5},{5,6},{6,7},{8,9},{9,10},{10,11},{11... | collective-permute-start | bytes 786440 | tf_op jit(solution)/shard_map/ppermute | solution.py:18
  43.9 0.1 copy.17
  43.9 0.6 reshape.108.cols_ref
  44.6 0.1 copy.19
  44.7 0.1 reshape.140
  44.8 2.9 %gather_fusion.2 = bf16[64,128,256]{2,1,0:T(8,128)(2,1)} fusion(bf16[32,128,256]{2,1,0:T(8,128)(2,1)S(1)} %copy-done.1, s32[1024]{0:T(1024)S(1)} %pad_clamp_fusion.2), kind=kCustom, calls=%fused_computation.2 | custom fusion | bytes 8388864 | tf_op jit(solution)/shard_map/gather | solution.py:264
  47.6 65.5 %shard_map.120 = (bf16[26,512,256]{2,1,0:T(8,128)(2,1)}, bf16[14,256,256]{2,1,0:T(8,128)(2,1)}) custom-call(bf16[16,512,256]{2,1,0:T(8,128)(2,1)} %bitcast.28), custom_call_target="tpu_custom_call" | custom-call | tf_op jit(solution)/shard_map/pallas_call | solution.py:187
  113.8 2.5 %shard_map.122 = f32[16,32,256]{2,1,0:T(8,128)} custom-call(s32[64]{0:T(128)} %copy-done.6, f32[64,32,256]{2,1,0:T(8,128)} %bitcast.12.partial_ref), custom_call_target="tpu_custom_call" | custom-call | tf_op jit(solution)/shard_map/pallas_call | solution.py:74
  116.3 1.6 %fusion.1 = bf16[16,32,256]{2,1,0:T(8,128)(2,1)S(1)} fusion(f32[16,32,256]{2,1,0:T(8,128)} %shard_map.122, f32[16,32,32]{2,1,0:T(8,128)S(1)} %copy-done.3, f32[16]{0:T(128)S(1)} %compare_convert_fusion), kind=kOutput, calls=%fused_computation.8 | convolution fusion | flops 50593792 | bytes 852032 | tf_op jit(solution)/shard_map/wst,wtv->wsv/dot_general | solution.py:228
  118.0 1.6 %gather_fusion.4 = bf16[64,32,256]{2,1,0:T(8,128)(2,1)} fusion(bf16[16,32,256]{2,1,0:T(8,128)(2,1)S(1)} %fusion.1, s32[1024]{0:T(1024)S(1)} %get-tuple-element.21), kind=kCustom, calls=%fused_computation.4 | custom fusion | bytes 2097408 | tf_op jit(solution)/shard_map/gather | solution.py:288
  119.6 5.5 %all-to-all-start.1 = ((bf16[16,4,32,256]{3,2,1,0:T(8,128)(2,1)}), bf16[16,4,32,256]{3,2,1,0:T(8,128)(2,1)}, u32[]{:S(2)}, u32[]{:S(2)}) async-start(bf16[16,4,32,256]{3,2,1,0:T(8,128)(2,1)} %bitcast.31), calls=%async_computation.1 | async-start | bytes 2097152 | tf_op jit(solution)/shard_map/all_to_all | solution.py:289
  125.1 0.1 reshape.121
  125.2 0.6 pad_add_fusion.live_ref
  125.9 1.6 %constant_dynamic-update-slice_fusion = bf16[104,128,256]{2,1,0:T(8,128)(2,1)} fusion(bf16[104,128,256]{2,1,0:T(8,128)(2,1)} %bitcast.30, bf16[32,128,256]{2,1,0:T(8,128)(2,1)S(1)} %copy-done.1), kind=kLoop, calls=%fused_computation.27 | loop fusion | bytes 4194304 | tf_op jit(solution)/shard_map/dynamic_update_slice | solution.py:296
  127.4 1.9 %maximum_dynamic-update-slice_fusion.ext_ref = bf16[104,128,256]{2,1,0:T(8,128)(2,1)} fusion(bf16[104,128,256]{2,1,0:T(8,128)(2,1)} %constant_dynamic-update-slice_fusion, bf16[4,128,256]{2,1,0:T(8,128)(2,1)} %collective-permute-done.1, bf16[4,128,256]{2,1,0:T(8,128)(2,1)} %collective-permute-done), kind=kLoop, calls=%fused_computation.9 | loop fusion | flops 1048576 | bytes 1048576 | tf_op jit(solution)/shard_map/dynamic_update_slice | solution.py:297
  129.3 12.2 %shard_map.121.product_ref = f32[32,128,256]{2,1,0:T(8,128)} custom-call(s32[512]{0:T(512)} %reshape.108.cols_ref, s32[104]{0:T(128)} %pad_add_fusion.live_ref, bf16[104,128,256]{2,1,0:T(8,128)(2,1)} %maximum_dynamic-update-slice_fusion.ext_ref, bf16[32,16,128,128]{3,2,1,0:T(8,128)(2,1)} %tiles_ref.1), custom_call_target="tpu_custom_call" | custom-call | flops 4294967296 | bytes 27787264 | tf_op jit(solution)/shard_map/pallas_call | solution.py:55
  141.5 4.5 %convolution_convert_fusion.incoming_ref = bf16[64,128,256]{2,1,0:T(8,128)(2,1)} fusion(bf16[64,32,128]{2,1,0:T(8,128)(2,1)S(1)} %bitcast.36, bf16[64,32,256]{2,1,0:T(8,128)(2,1)} %bitcast.16), kind=kOutput, calls=%fused_computation.5 | convolution fusion | flops 136314880 | bytes 5767168 | tf_op jit(solution)/shard_map/qsk,qsv->qkv/dot_general | solution.py:299
  146.0 6.1 %shard_map.123 = bf16[32,128,256]{2,1,0:T(8,128)(2,1)} custom-call(s32[64]{0:T(128)} %reshape_squeeze.7.index_ref.targets_ref, f32[32,128,256]{2,1,0:T(8,128)} %shard_map.121.product_ref, bf16[64,128,256]{2,1,0:T(8,128)(2,1)} %convolution_convert_fusion.incoming_ref), custom_call_target="tpu_custom_call" | custom-call | tf_op jit(solution)/shard_map/pallas_call | solution.py:216
  (33 shorter events, 0.2 us)
Async XLA Ops:
  0.0 4.4 %copy-start = (bf16[16,4,32,128]{3,2,1,0:T(8,128)(2,1)S(1)}, bf16[16,4,32,128]{3,2,1,0:T(8,128)(2,1)}, u32[]{:S(2)}) copy-start(bf16[16,4,32,128]{3,2,1,0:T(8,128)(2,1)} %param.21) | copy-start | bytes 1572868
  2.3 29.1 %copy-start.6 = (s32[64]{0:T(128)}, s32[64]{0:T(128)S(1)}, u32[]{:S(2)}) copy-start(s32[64]{0:T(128)S(1)} %reshape.110.slot_ref) | copy-start | bytes 772
  27.5 10.5 %copy-start.8 = (s32[1,2,4]{2,1,0:T(2,128)S(1)}, s32[1,2,4]{2,1,0:T(2,128)}, u32[]{:S(2)}) copy-start(s32[1,2,4]{2,1,0:T(2,128)} %param.17) | copy-start | bytes 100
  27.5 10.6 %copy-start.1 = (bf16[32,128,256]{2,1,0:T(8,128)(2,1)S(1)}, bf16[32,128,256]{2,1,0:T(8,128)(2,1)}, u32[]{:S(2)}) copy-start(bf16[32,128,256]{2,1,0:T(8,128)(2,1)} %blocks_ref.1) | copy-start | bytes 6291460
  31.4 12.4 %copy-start.4 = (s32[32,16]{0,1:T(8,128)S(1)}, s32[32,16]{0,1:T(8,128)}, u32[]{:S(2)}) copy-start(s32[32,16]{0,1:T(8,128)} %param.14) | copy-start | bytes 6148
  31.4 13.1 %copy-start.5 = (s32[1,16,4]{1,2,0:T(4,128)S(1)}, s32[1,16,4]{1,2,0:T(4,128)}, u32[]{:S(2)}) copy-start(s32[1,16,4]{1,2,0:T(4,128)} %param.15) | copy-start | bytes 772
  31.5 82.4 %all-to-all-start = ((f32[16,4,32,256]{3,2,1,0:T(8,128)}), f32[16,4,32,256]{3,2,1,0:T(8,128)}, u32[]{:S(2)}, u32[]{:S(2)}) async-start(f32[16,4,32,256]{3,2,1,0:T(8,128)} %bitcast.29), calls=%async_computation | async-start | bytes 4194304 | tf_op jit(solution)/shard_map/all_to_all | solution.py:280
  39.5 87.9 %collective-permute-start.1 = (bf16[4,128,256]{2,1,0:T(8,128)(2,1)}, bf16[4,128,256]{2,1,0:T(8,128)(2,1)}, u32[]{:S(2)}, u32[]{:S(2)}) collective-permute-start(bf16[4,128,256]{2,1,0:T(8,128)(2,1)} %get-tuple-element.18), channel_id=1, source_target_pairs={{1,0},{2,1},{3,2},{4,3},{5,4},{6,5},{7,6},{9,8},{10,9},{11,10},{12... | collective-permute-start | bytes 786440 | tf_op jit(solution)/shard_map/ppermute | solution.py:19
  41.4 86.0 %collective-permute-start = (bf16[4,128,256]{2,1,0:T(8,128)(2,1)S(1)}, bf16[4,128,256]{2,1,0:T(8,128)(2,1)}, u32[]{:S(2)}, u32[]{:S(2)}) collective-permute-start(bf16[4,128,256]{2,1,0:T(8,128)(2,1)S(1)} %get-tuple-element.17), channel_id=1, source_target_pairs={{0,1},{1,2},{2,3},{3,4},{4,5},{5,6},{6,7},{8,9},{9,10},{10,11},{11... | collective-permute-start | bytes 786440 | tf_op jit(solution)/shard_map/ppermute | solution.py:18
  47.6 68.7 %copy-start.3 = (f32[16,32,32]{2,1,0:T(8,128)S(1)}, f32[16,32,32]{2,1,0:T(8,128)}, u32[]{:S(2)}) copy-start(f32[16,32,32]{2,1,0:T(8,128)} %param.23) | copy-start | bytes 196612
  113.1 11.9 %copy-start.7 = (s32[1,16]{1,0:T(1,128)S(1)}, s32[1,16]{1,0:T(1,128)}, u32[]{:S(2)}) copy-start(s32[1,16]{1,0:T(1,128)} %param.16) | copy-start | bytes 196
  119.6 22.0 %all-to-all-start.1 = ((bf16[16,4,32,256]{3,2,1,0:T(8,128)(2,1)}), bf16[16,4,32,256]{3,2,1,0:T(8,128)(2,1)}, u32[]{:S(2)}, u32[]{:S(2)}) async-start(bf16[16,4,32,256]{3,2,1,0:T(8,128)(2,1)} %bitcast.31), calls=%async_computation.1 | async-start | bytes 2097152 | tf_op jit(solution)/shard_map/all_to_all | solution.py:289
  129.3 12.2 %copy-start.2 = (bf16[16,128,128]{2,1,0:T(8,128)(2,1)S(1)}, bf16[16,128,128]{2,1,0:T(8,128)(2,1)}, u32[]{:S(2)}) copy-start(bf16[16,128,128]{2,1,0:T(8,128)(2,1)} %get-tuple-element.15) | copy-start | bytes 1572868

commit v15 on v13

--- a/solution.py
+++ b/solution.py
@@ -246,15 +246,17 @@
     rim_pack = blocks[grp_send[0].reshape(-1)]
     rim_ext = padded(rim_pack, (("grp", 0),), rim_width)
     rim_rows = jnp.concatenate([rim_ext[:rim_width], rim_ext[rim_ext.shape[0] - rim_width :]], 0)
-    slot_order = jnp.argsort(well_slot.reshape(-1))
+    slot_flat = well_slot.reshape(-1)
+    slot_order = jnp.zeros_like(slot_flat).at[slot_flat].set(jnp.arange(slot_flat.shape[0], dtype=slot_flat.dtype))
     slot_well = slot_order // couplings
-    in_slots = couple_in.reshape(wells * couplings, seg, cell_count)[slot_order]
-    in_slots = in_slots.reshape(dom_count, slot_width * seg, cell_count)
+    couple_both = jnp.concatenate(
+        [couple_in.reshape(wells * couplings, seg, cell_count), couple_out.reshape(wells * couplings, seg, cell_count)], 2
+    )[slot_order]
     halo_flat = halo_pack.reshape(dom_count, halo_width * cell_count, vec_count)
-    out_slots = couple_out.reshape(wells * couplings, seg, cell_count)[slot_order]
-    out_slots = out_slots.reshape(dom_count, slot_width * seg, cell_count)
-    in_recv, out_recv = dom_exchange([in_slots, out_slots], 0)
-    in_recv = in_recv.reshape(dom_count, slot_width, seg, cell_count)
+    (both_recv,) = dom_exchange([couple_both.reshape(dom_count, slot_width * seg, 2 * cell_count)], 0)
+    both_recv = both_recv.reshape(slot_total, seg, 2 * cell_count)
+    in_recv = both_recv[:, :, :cell_count]
+    out_recv = both_recv[:, :, cell_count:]
     partial = partial_sums(
         well_send[0].reshape(-1), in_recv.reshape(slot_total, seg, cell_count), blocks
     ).reshape(dom_count, slot_width, seg, vec_count)

time: 151 us -> 149 us (0.987)
  Pallas kernels: 103 us -> 101 us
    pallas_call x2, Pallas kernels: 84.7 us -> 82.2 us  [dom_exchange(): pl.pallas_call(functools.partial(exchange_kernel, tuple((f[0] for f in fr...]
    gather x2 -> x1, local copies, waits for them, and re-layouts: 3.87 us -> 1.58 us  [on_device(): jnp.concatenate([couple_in.reshape(wells * couplings, seg, cell_count), c...]
    sort x1 -> x0, other arithmetic: 2.03 us -> none  [on_device(): slot_order = jnp.argsort(well_slot.reshape(-1))]
    slice x0 -> x1, local copies, waits for them, and re-layouts: none -> 1.88 us  [on_device(): in_recv = both_recv[:, :, :cell_count]]
    ppermute x1, starting transfers between devices: 1.91 us -> 3.64 us  [padded(): after = lax.ppermute(leading, axis, down)]
  transfers between devices with their start and end apart: 4 -> 4, of which waited for: 0 -> 0; matrix products, arithmetic and copies ran while one was open for 8% -> 9% of each run, Pallas kernels for 53% -> 53%
where the time goes in v15:
time: 149 us
  Pallas kernels  101 us (68%)
  starting transfers between devices  17.6 us (12%)
  local copies, waits for them, and re-layouts  15.7 us (11%)
  other arithmetic  7.62 us (5%)
  matrix products  5.95 us (4%)
    pallas_call x2, Pallas kernels, dom_exchange(): pl.pallas_call(functools.partial(exchange_kernel, tuple((f[0] for f in fr...  82.2 us
    pallas_call x1, Pallas kernels, local_product(): pl.pallas_call(product_kernel, out_shape=jax.ShapeDtypeStruct((block_rows...  12.2 us
    all_to_all x1, starting transfers between devices, on_device(): lax.all_to_all(partial, 'dom', split_axis=0, concat_axis=0, tiled=True)  6.59 us
    all_to_all x1, starting transfers between devices, on_device(): lax.all_to_all(state_pack, 'dom', split_axis=0, concat_axis=0, tiled=True)  5.42 us
    pallas_call x1, Pallas kernels, partial_sums(): pl.pallas_call(partial_kernel, out_shape=jax.ShapeDtypeStruct((slots, seg...  3.91 us
    convert_element_type x1, other arithmetic, on_device(): return subtract_incoming(product, well_send, incoming).astype(jnp.bfloat16)  3.65 us
    ppermute x1, starting transfers between devices, padded(): after = lax.ppermute(leading, axis, down)  3.64 us
    dot_general x1, matrix products, subtract_incoming(): jnp.einsum('bq,qkv->bkv', selector, flat_rows, preferred_element_type=jnp...  3.03 us
  transfers between devices with their start and end apart: 4, of which 0 were waited for; matrix products, arithmetic and copies ran while one was open for 9% of the time, Pallas kernels for 53%

profile of v15, /device:TPU:66, one launch (start us, length us, event | category | flops | bytes accessed | tf_op | source)
XLA Modules:
  0.0 148.5 jit_solution(13086187464037967247)
XLA Ops:
  0.0 0.8 copy.20
  0.8 0.1 reshape.139
  0.9 0.8 scatter_custom_fusion
  1.7 0.8 copy.19
  2.5 0.7 reshape_squeeze.6.index_ref
  3.1 1.3 pad_maximum_fusion
  4.5 1.6 %gather_fusion = bf16[64,32,256]{2,1,0:T(8,128)(2,1)} fusion(bf16[64,32,256]{2,1,0:T(8,128)(2,1)S(1)} %pad_maximum_fusion, s32[1024]{0:T(1024)S(1)} %get-tuple-element.18), kind=kCustom, calls=%fused_computation | custom fusion | bytes 2097408 | tf_op jit(solution)/shard_map/gather | solution.py:252
  6.1 18.5 %shard_map.118 = (bf16[16,128,256]{2,1,0:T(8,128)(2,1)}, bf16[14,64,256]{2,1,0:T(8,128)(2,1)}) custom-call(bf16[16,128,256]{2,1,0:T(8,128)(2,1)} %bitcast.34), custom_call_target="tpu_custom_call" | custom-call | tf_op jit(solution)/shard_map/pallas_call | solution.py:187
  24.6 1.9 %slice.24.couple_ref = bf16[64,32,128]{2,1,0:T(8,128)(2,1)} slice(bf16[64,32,256]{2,1,0:T(8,128)(2,1)} %bitcast.36), slice={[0:64], [0:32], [0:128]} | slice | bytes 1048576 | tf_op jit(solution)/shard_map/slice | solution.py:258
  26.5 3.9 %shard_map.119 = f32[64,32,256]{2,1,0:T(8,128)} custom-call(s32[64]{0:T(128)} %reshape_squeeze.6.index_ref, bf16[64,32,128]{2,1,0:T(8,128)(2,1)} %slice.24.couple_ref, bf16[32,128,256]{2,1,0:T(8,128)(2,1)} %blocks_ref.1), custom_call_target="tpu_custom_call" | custom-call | tf_op jit(solution)/shard_map/pallas_call | solution.py:92
  30.4 6.6 %all-to-all-start = ((f32[16,4,32,256]{3,2,1,0:T(8,128)}), f32[16,4,32,256]{3,2,1,0:T(8,128)}, u32[]{:S(2)}, u32[]{:S(2)}) async-start(f32[16,4,32,256]{3,2,1,0:T(8,128)} %bitcast.31), calls=%async_computation | async-start | bytes 4194304 | tf_op jit(solution)/shard_map/all_to_all | solution.py:263
  37.1 0.6 gather_fusion.2
  37.7 0.8 fusion.14
  38.5 1.9 %collective-permute-start = (bf16[4,128,256]{2,1,0:T(8,128)(2,1)}, bf16[4,128,256]{2,1,0:T(8,128)(2,1)}, u32[]{:S(2)}, u32[]{:S(2)}) collective-permute-start(bf16[4,128,256]{2,1,0:T(8,128)(2,1)} %get-tuple-element.13), channel_id=1, source_target_pairs={{0,1},{1,2},{2,3},{3,4},{4,5},{5,6},{6,7},{8,9},{9,10},{10,11},{11... | collective-permute-start | bytes 786440 | tf_op jit(solution)/shard_map/ppermute | solution.py:18
  40.5 3.6 %collective-permute-start.1 = (bf16[4,128,256]{2,1,0:T(8,128)(2,1)}, bf16[4,128,256]{2,1,0:T(8,128)(2,1)}, u32[]{:S(2)}, u32[]{:S(2)}) collective-permute-start(bf16[4,128,256]{2,1,0:T(8,128)(2,1)} %get-tuple-element.14), channel_id=1, source_target_pairs={{1,0},{2,1},{3,2},{4,3},{5,4},{6,5},{7,6},{9,8},{10,9},{11,10},{12... | collective-permute-start | bytes 786440 | tf_op jit(solution)/shard_map/ppermute | solution.py:19
  44.1 0.7 reshape.145.slot_ref
  45.5 0.1 reshape.160
  45.6 2.9 %gather_fusion.1 = bf16[64,128,256]{2,1,0:T(8,128)(2,1)} fusion(bf16[32,128,256]{2,1,0:T(8,128)(2,1)S(1)} %copy-done.1, s32[1024]{0:T(1024)S(1)} %pad_clamp_fusion.2), kind=kCustom, calls=%fused_computation.1 | custom fusion | bytes 8388864 | tf_op jit(solution)/shard_map/gather | solution.py:245
  48.5 63.6 %shard_map.120 = (bf16[26,512,256]{2,1,0:T(8,128)(2,1)}, bf16[14,256,256]{2,1,0:T(8,128)(2,1)}) custom-call(bf16[16,512,256]{2,1,0:T(8,128)(2,1)} %bitcast.30), custom_call_target="tpu_custom_call" | custom-call | tf_op jit(solution)/shard_map/pallas_call | solution.py:187
  112.2 2.5 %shard_map.122 = f32[16,32,256]{2,1,0:T(8,128)} custom-call(s32[64]{0:T(128)} %reshape.145.slot_ref, f32[64,32,256]{2,1,0:T(8,128)} %bitcast.12.partial_ref), custom_call_target="tpu_custom_call" | custom-call | tf_op jit(solution)/shard_map/pallas_call | solution.py:74
  114.7 1.6 %fusion.3 = bf16[16,32,256]{2,1,0:T(8,128)(2,1)S(1)} fusion(f32[16,32,256]{2,1,0:T(8,128)} %shard_map.122, f32[16,32,32]{2,1,0:T(8,128)S(1)} %copy-done, f32[16]{0:T(128)S(1)} %compare_convert_fusion), kind=kOutput, calls=%fused_computation.11 | convolution fusion | flops 50593792 | bytes 852032 | tf_op jit(solution)/shard_map/wst,wtv->wsv/dot_general | solution.py:209
  116.4 1.6 %gather_fusion.3 = bf16[64,32,256]{2,1,0:T(8,128)(2,1)} fusion(bf16[16,32,256]{2,1,0:T(8,128)(2,1)S(1)} %fusion.3, s32[1024]{0:T(1024)S(1)} %get-tuple-element.17), kind=kCustom, calls=%fused_computation.3 | custom fusion | bytes 2097408 | tf_op jit(solution)/shard_map/gather | solution.py:271
  117.9 5.4 %all-to-all-start.1 = ((bf16[16,4,32,256]{3,2,1,0:T(8,128)(2,1)}), bf16[16,4,32,256]{3,2,1,0:T(8,128)(2,1)S(1)}, u32[]{:S(2)}, u32[]{:S(2)}) async-start(bf16[16,4,32,256]{3,2,1,0:T(8,128)(2,1)} %bitcast.33), calls=%async_computation.1 | async-start | bytes 2097152 | tf_op jit(solution)/shard_map/all_to_all | solution.py:272
  123.4 0.1 reshape.149
  123.6 0.6 reshape.136.cols_ref
  124.2 0.6 pad_add_fusion.live_ref
  124.9 1.6 %constant_dynamic-update-slice_fusion = bf16[104,128,256]{2,1,0:T(8,128)(2,1)} fusion(bf16[104,128,256]{2,1,0:T(8,128)(2,1)} %bitcast.32, bf16[32,128,256]{2,1,0:T(8,128)(2,1)S(1)} %copy-done.1), kind=kLoop, calls=%fused_computation.38 | loop fusion | bytes 4194304 | tf_op jit(solution)/shard_map/dynamic_update_slice | solution.py:279
  126.4 1.9 %maximum_dynamic-update-slice_fusion.ext_ref = bf16[104,128,256]{2,1,0:T(8,128)(2,1)} fusion(bf16[104,128,256]{2,1,0:T(8,128)(2,1)} %constant_dynamic-update-slice_fusion, bf16[4,128,256]{2,1,0:T(8,128)(2,1)} %collective-permute-done.1, bf16[4,128,256]{2,1,0:T(8,128)(2,1)} %collective-permute-done), kind=kLoop, calls=%fused_computation.15 | loop fusion | flops 1048576 | bytes 1048576 | tf_op jit(solution)/shard_map/dynamic_update_slice | solution.py:280
  128.3 12.2 %shard_map.121 = f32[32,128,256]{2,1,0:T(8,128)} custom-call(s32[512]{0:T(512)} %reshape.136.cols_ref, s32[104]{0:T(128)} %pad_add_fusion.live_ref, bf16[104,128,256]{2,1,0:T(8,128)(2,1)} %maximum_dynamic-update-slice_fusion.ext_ref, bf16[32,16,128,128]{3,2,1,0:T(8,128)(2,1)} %tiles_ref.1), custom_call_target="tpu_custom_call" | custom-call | flops 4294967296 | bytes 27787264 | tf_op jit(solution)/shard_map/pallas_call | solution.py:55
  140.5 1.3 fusion.4
  141.9 3.0 %fusion = f32[32,128,256]{2,0,1:T(8,128)S(1)} fusion(bf16[64,128,256]{2,1,0:T(8,128)(2,1)S(1)} %fusion.4, s32[64]{0:T(128)S(1)} %copy-done.5), kind=kOutput, calls=%fused_computation.6 | convolution fusion | flops 134219776 | bytes 8388864 | tf_op jit(solution)/shard_map/bq,qkv->bkv/dot_general | solution.py:217
  144.9 3.7 %fusion.1 = bf16[32,128,256]{2,1,0:T(8,128)(2,1)} fusion(f32[32,128,256]{2,1,0:T(8,128)S(1)} %copy-done.2, f32[32,128,256]{2,0,1:T(8,128)S(1)} %fusion), kind=kLoop, calls=%fused_computation.8 | loop fusion | flops 2097152 | bytes 10485760 | tf_op jit(solution)/shard_map/convert_element_type | solution.py:288
  (37 shorter events, 0.4 us)
Async XLA Ops:
  0.0 114.7 %copy-start = (f32[16,32,32]{2,1,0:T(8,128)S(1)}, f32[16,32,32]{2,1,0:T(8,128)}, u32[]{:S(2)}) copy-start(f32[16,32,32]{2,1,0:T(8,128)} %param.23) | copy-start | bytes 196612
  26.5 10.5 %copy-start.8 = (s32[1,2,4]{2,1,0:T(2,128)S(1)}, s32[1,2,4]{2,1,0:T(2,128)}, u32[]{:S(2)}) copy-start(s32[1,2,4]{2,1,0:T(2,128)} %param.17) | copy-start | bytes 100
  26.5 10.6 %copy-start.1 = (bf16[32,128,256]{2,1,0:T(8,128)(2,1)S(1)}, bf16[32,128,256]{2,1,0:T(8,128)(2,1)}, u32[]{:S(2)}) copy-start(bf16[32,128,256]{2,1,0:T(8,128)(2,1)} %blocks_ref.1) | copy-start | bytes 6291460
  30.4 15.0 %copy-start.6 = (s32[1,16,4]{1,2,0:T(4,128)S(1)}, s32[1,16,4]{1,2,0:T(4,128)}, u32[]{:S(2)}) copy-start(s32[1,16,4]{1,2,0:T(4,128)} %param.15) | copy-start | bytes 772
  30.4 81.8 %all-to-all-start = ((f32[16,4,32,256]{3,2,1,0:T(8,128)}), f32[16,4,32,256]{3,2,1,0:T(8,128)}, u32[]{:S(2)}, u32[]{:S(2)}) async-start(f32[16,4,32,256]{3,2,1,0:T(8,128)} %bitcast.31), calls=%async_computation | async-start | bytes 4194304 | tf_op jit(solution)/shard_map/all_to_all | solution.py:263
  38.5 87.9 %collective-permute-start = (bf16[4,128,256]{2,1,0:T(8,128)(2,1)}, bf16[4,128,256]{2,1,0:T(8,128)(2,1)}, u32[]{:S(2)}, u32[]{:S(2)}) collective-permute-start(bf16[4,128,256]{2,1,0:T(8,128)(2,1)} %get-tuple-element.13), channel_id=1, source_target_pairs={{0,1},{1,2},{2,3},{3,4},{4,5},{5,6},{6,7},{8,9},{9,10},{10,11},{11... | collective-permute-start | bytes 786440 | tf_op jit(solution)/shard_map/ppermute | solution.py:18
  40.5 86.0 %collective-permute-start.1 = (bf16[4,128,256]{2,1,0:T(8,128)(2,1)}, bf16[4,128,256]{2,1,0:T(8,128)(2,1)}, u32[]{:S(2)}, u32[]{:S(2)}) collective-permute-start(bf16[4,128,256]{2,1,0:T(8,128)(2,1)} %get-tuple-element.14), channel_id=1, source_target_pairs={{1,0},{2,1},{3,2},{4,3},{5,4},{6,5},{7,6},{9,8},{10,9},{11,10},{12... | collective-permute-start | bytes 786440 | tf_op jit(solution)/shard_map/ppermute | solution.py:19
  112.2 11.2 %copy-start.7 = (s32[1,16]{1,0:T(1,128)S(1)}, s32[1,16]{1,0:T(1,128)}, u32[]{:S(2)}) copy-start(s32[1,16]{1,0:T(1,128)} %param.16) | copy-start | bytes 196
  112.2 11.3 %copy-start.4 = (s32[32,16]{0,1:T(8,128)S(1)}, s32[32,16]{0,1:T(8,128)}, u32[]{:S(2)}) copy-start(s32[32,16]{0,1:T(8,128)} %param.14) | copy-start | bytes 6148
  117.9 22.6 %all-to-all-start.1 = ((bf16[16,4,32,256]{3,2,1,0:T(8,128)(2,1)}), bf16[16,4,32,256]{3,2,1,0:T(8,128)(2,1)S(1)}, u32[]{:S(2)}, u32[]{:S(2)}) async-start(bf16[16,4,32,256]{3,2,1,0:T(8,128)(2,1)} %bitcast.33), calls=%async_computation.1 | async-start | bytes 2097152 | tf_op jit(solution)/shard_map/all_to_all | solution.py:272
  128.3 12.2 %copy-start.3 = (bf16[16,128,256]{2,1,0:T(8,128)(2,1)S(1)}, bf16[16,128,256]{2,1,0:T(8,128)(2,1)}, u32[]{:S(2)}) copy-start(bf16[16,128,256]{2,1,0:T(8,128)(2,1)} %get-tuple-element.9) | copy-start | bytes 3145732
  140.5 1.3 copy-start.5
  141.9 3.0 %copy-start.2 = (f32[32,128,256]{2,1,0:T(8,128)S(1)}, f32[32,128,256]{2,1,0:T(8,128)}, u32[]{:S(2)}) copy-start(f32[32,128,256]{2,1,0:T(8,128)} %shard_map.121) | copy-start | bytes 12582916

commit v16 on v15

--- a/solution.py
+++ b/solution.py
@@ -82,7 +82,7 @@
 def partial_kernel(index_ref, couple_ref, blocks_ref, out_ref):
     for q in range(out_ref.shape[0]):
         out_ref[q] = jnp.dot(
-            couple_ref[q], blocks_ref[index_ref[q]], preferred_element_type=jnp.float32
+            couple_ref[q][:, : blocks_ref.shape[1]], blocks_ref[index_ref[q]], preferred_element_type=jnp.float32
         )
 
 
@@ -255,11 +255,8 @@
     halo_flat = halo_pack.reshape(dom_count, halo_width * cell_count, vec_count)
     (both_recv,) = dom_exchange([couple_both.reshape(dom_count, slot_width * seg, 2 * cell_count)], 0)
     both_recv = both_recv.reshape(slot_total, seg, 2 * cell_count)
-    in_recv = both_recv[:, :, :cell_count]
     out_recv = both_recv[:, :, cell_count:]
-    partial = partial_sums(
-        well_send[0].reshape(-1), in_recv.reshape(slot_total, seg, cell_count), blocks
-    ).reshape(dom_count, slot_width, seg, vec_count)
+    partial = partial_sums(well_send[0].reshape(-1), both_recv, blocks).reshape(dom_count, slot_width, seg, vec_count)
     partial_in = lax.all_to_all(partial, "dom", split_axis=0, concat_axis=0, tiled=True)
     own_slots = blocks.shape[0] // halo_width
     ext_slots = own_slots + dom_count + 2 * rim_width // halo_width

time: 149 us -> 147 us (0.987)
  local copies, waits for them, and re-layouts: 15.7 us -> 13.9 us
    slice x1 -> x0, local copies, waits for them, and re-layouts: 1.88 us -> none  [on_device(): in_recv = both_recv[:, :, :cell_count]]
where the time goes in v16:
time: 147 us
  Pallas kernels  101 us (69%)
  starting transfers between devices  17.5 us (12%)
  local copies, waits for them, and re-layouts  13.9 us (9%)
  other arithmetic  7.62 us (5%)
  matrix products  5.95 us (4%)
    pallas_call x2, Pallas kernels, dom_exchange(): pl.pallas_call(functools.partial(exchange_kernel, tuple((f[0] for f in fr...  82.2 us
    pallas_call x1, Pallas kernels, local_product(): pl.pallas_call(product_kernel, out_shape=jax.ShapeDtypeStruct((block_rows...  12.2 us
    all_to_all x1, starting transfers between devices, on_device(): lax.all_to_all(partial, 'dom', split_axis=0, concat_axis=0, tiled=True)  6.59 us
    all_to_all x1, starting transfers between devices, on_device(): lax.all_to_all(state_pack, 'dom', split_axis=0, concat_axis=0, tiled=True)  5.41 us
    pallas_call x1, Pallas kernels, partial_sums(): pl.pallas_call(partial_kernel, out_shape=jax.ShapeDtypeStruct((slots, seg...  4.07 us
    convert_element_type x1, other arithmetic, on_device(): return subtract_incoming(product, well_send, incoming).astype(jnp.bfloat16)  3.65 us
    ppermute x1, starting transfers between devices, padded(): after = lax.ppermute(leading, axis, down)  3.64 us
    dot_general x1, matrix products, subtract_incoming(): jnp.einsum('bq,qkv->bkv', selector, flat_rows, preferred_element_type=jnp...  3.03 us
  transfers between devices with their start and end apart: 4, of which 0 were waited for; matrix products, arithmetic and copies ran while one was open for 9% of the time, Pallas kernels for 53%

profile of v16, /device:TPU:66, one launch (start us, length us, event | category | flops | bytes accessed | tf_op | source)
XLA Modules:
  0.0 146.8 jit_solution(9044194001282926854)
XLA Ops:
  0.0 0.8 copy.20
  0.8 0.1 reshape.139
  0.9 0.8 scatter_custom_fusion
  1.7 0.8 copy.19
  2.5 0.7 reshape_squeeze.6.index_ref
  3.1 1.3 pad_maximum_fusion
  4.5 1.6 %gather_fusion = bf16[64,32,256]{2,1,0:T(8,128)(2,1)} fusion(bf16[64,32,256]{2,1,0:T(8,128)(2,1)S(1)} %pad_maximum_fusion, s32[1024]{0:T(1024)S(1)} %get-tuple-element.18), kind=kCustom, calls=%fused_computation | custom fusion | bytes 2097408 | tf_op jit(solution)/shard_map/gather | solution.py:252
  6.1 18.5 %shard_map.118 = (bf16[16,128,256]{2,1,0:T(8,128)(2,1)}, bf16[14,64,256]{2,1,0:T(8,128)(2,1)}) custom-call(bf16[16,128,256]{2,1,0:T(8,128)(2,1)} %bitcast.34), custom_call_target="tpu_custom_call" | custom-call | tf_op jit(solution)/shard_map/pallas_call | solution.py:187
  24.6 4.1 %shard_map.119 = f32[64,32,256]{2,1,0:T(8,128)} custom-call(s32[64]{0:T(128)} %reshape_squeeze.6.index_ref, bf16[64,32,256]{2,1,0:T(8,128)(2,1)} %bitcast.36, bf16[32,128,256]{2,1,0:T(8,128)(2,1)} %blocks_ref.1), custom_call_target="tpu_custom_call" | custom-call | tf_op jit(solution)/shard_map/pallas_call | solution.py:92
  28.7 6.6 %all-to-all-start = ((f32[16,4,32,256]{3,2,1,0:T(8,128)}), f32[16,4,32,256]{3,2,1,0:T(8,128)}, u32[]{:S(2)}, u32[]{:S(2)}) async-start(f32[16,4,32,256]{3,2,1,0:T(8,128)} %bitcast.31), calls=%async_computation | async-start | bytes 4194304 | tf_op jit(solution)/shard_map/all_to_all | solution.py:260
  35.4 0.6 gather_fusion.2
  36.0 0.8 fusion.14
  36.8 1.9 %collective-permute-start = (bf16[4,128,256]{2,1,0:T(8,128)(2,1)}, bf16[4,128,256]{2,1,0:T(8,128)(2,1)}, u32[]{:S(2)}, u32[]{:S(2)}) collective-permute-start(bf16[4,128,256]{2,1,0:T(8,128)(2,1)} %get-tuple-element.13), channel_id=1, source_target_pairs={{0,1},{1,2},{2,3},{3,4},{4,5},{5,6},{6,7},{8,9},{9,10},{10,11},{11... | collective-permute-start | bytes 786440 | tf_op jit(solution)/shard_map/ppermute | solution.py:18
  38.8 3.6 %collective-permute-start.1 = (bf16[4,128,256]{2,1,0:T(8,128)(2,1)}, bf16[4,128,256]{2,1,0:T(8,128)(2,1)}, u32[]{:S(2)}, u32[]{:S(2)}) collective-permute-start(bf16[4,128,256]{2,1,0:T(8,128)(2,1)} %get-tuple-element.14), channel_id=1, source_target_pairs={{1,0},{2,1},{3,2},{4,3},{5,4},{6,5},{7,6},{9,8},{10,9},{11,10},{12... | collective-permute-start | bytes 786440 | tf_op jit(solution)/shard_map/ppermute | solution.py:19
  42.4 0.7 reshape.145.slot_ref
  43.7 0.1 copy.21
  43.8 0.1 reshape.160
  43.9 2.9 %gather_fusion.1 = bf16[64,128,256]{2,1,0:T(8,128)(2,1)} fusion(bf16[32,128,256]{2,1,0:T(8,128)(2,1)S(1)} %copy-done.1, s32[1024]{0:T(1024)S(1)} %pad_clamp_fusion.2), kind=kCustom, calls=%fused_computation.1 | custom fusion | bytes 8388864 | tf_op jit(solution)/shard_map/gather | solution.py:245
  46.8 63.7 %shard_map.120 = (bf16[26,512,256]{2,1,0:T(8,128)(2,1)}, bf16[14,256,256]{2,1,0:T(8,128)(2,1)}) custom-call(bf16[16,512,256]{2,1,0:T(8,128)(2,1)} %bitcast.30), custom_call_target="tpu_custom_call" | custom-call | tf_op jit(solution)/shard_map/pallas_call | solution.py:187
  110.5 2.5 %shard_map.122 = f32[16,32,256]{2,1,0:T(8,128)} custom-call(s32[64]{0:T(128)} %reshape.145.slot_ref, f32[64,32,256]{2,1,0:T(8,128)} %bitcast.12.partial_ref), custom_call_target="tpu_custom_call" | custom-call | tf_op jit(solution)/shard_map/pallas_call | solution.py:74
  113.0 1.6 %fusion.3 = bf16[16,32,256]{2,1,0:T(8,128)(2,1)S(1)} fusion(f32[16,32,256]{2,1,0:T(8,128)} %shard_map.122, f32[16,32,32]{2,1,0:T(8,128)S(1)} %copy-done, f32[16]{0:T(128)S(1)} %compare_convert_fusion), kind=kOutput, calls=%fused_computation.11 | convolution fusion | flops 50593792 | bytes 852032 | tf_op jit(solution)/shard_map/wst,wtv->wsv/dot_general | solution.py:209
  114.7 1.6 %gather_fusion.3 = bf16[64,32,256]{2,1,0:T(8,128)(2,1)} fusion(bf16[16,32,256]{2,1,0:T(8,128)(2,1)S(1)} %fusion.3, s32[1024]{0:T(1024)S(1)} %get-tuple-element.17), kind=kCustom, calls=%fused_computation.3 | custom fusion | bytes 2097408 | tf_op jit(solution)/shard_map/gather | solution.py:268
  116.3 5.4 %all-to-all-start.1 = ((bf16[16,4,32,256]{3,2,1,0:T(8,128)(2,1)}), bf16[16,4,32,256]{3,2,1,0:T(8,128)(2,1)S(1)}, u32[]{:S(2)}, u32[]{:S(2)}) async-start(bf16[16,4,32,256]{3,2,1,0:T(8,128)(2,1)} %bitcast.33), calls=%async_computation.1 | async-start | bytes 2097152 | tf_op jit(solution)/shard_map/all_to_all | solution.py:269
  121.7 0.1 reshape.149
  121.9 0.6 reshape.136.cols_ref
  122.5 0.6 pad_add_fusion.live_ref
  123.2 1.6 %constant_dynamic-update-slice_fusion = bf16[104,128,256]{2,1,0:T(8,128)(2,1)} fusion(bf16[104,128,256]{2,1,0:T(8,128)(2,1)} %bitcast.32, bf16[32,128,256]{2,1,0:T(8,128)(2,1)S(1)} %copy-done.1), kind=kLoop, calls=%fused_computation.38 | loop fusion | bytes 4194304 | tf_op jit(solution)/shard_map/dynamic_update_slice | solution.py:276
  124.7 1.9 %maximum_dynamic-update-slice_fusion.ext_ref = bf16[104,128,256]{2,1,0:T(8,128)(2,1)} fusion(bf16[104,128,256]{2,1,0:T(8,128)(2,1)} %constant_dynamic-update-slice_fusion, bf16[4,128,256]{2,1,0:T(8,128)(2,1)} %collective-permute-done.1, bf16[4,128,256]{2,1,0:T(8,128)(2,1)} %collective-permute-done), kind=kLoop, calls=%fused_computation.15 | loop fusion | flops 1048576 | bytes 1048576 | tf_op jit(solution)/shard_map/dynamic_update_slice | solution.py:277
  126.6 12.2 %shard_map.121 = f32[32,128,256]{2,1,0:T(8,128)} custom-call(s32[512]{0:T(512)} %reshape.136.cols_ref, s32[104]{0:T(128)} %pad_add_fusion.live_ref, bf16[104,128,256]{2,1,0:T(8,128)(2,1)} %maximum_dynamic-update-slice_fusion.ext_ref, bf16[32,16,128,128]{3,2,1,0:T(8,128)(2,1)} %tiles_ref.1), custom_call_target="tpu_custom_call" | custom-call | flops 4294967296 | bytes 27787264 | tf_op jit(solution)/shard_map/pallas_call | solution.py:55
  138.8 1.3 fusion.4
  140.2 3.0 %fusion = f32[32,128,256]{2,0,1:T(8,128)S(1)} fusion(bf16[64,128,256]{2,1,0:T(8,128)(2,1)S(1)} %fusion.4, s32[64]{0:T(128)S(1)} %copy-done.5), kind=kOutput, calls=%fused_computation.6 | convolution fusion | flops 134219776 | bytes 8388864 | tf_op jit(solution)/shard_map/bq,qkv->bkv/dot_general | solution.py:217
  143.2 3.7 %fusion.1 = bf16[32,128,256]{2,1,0:T(8,128)(2,1)} fusion(f32[32,128,256]{2,1,0:T(8,128)S(1)} %copy-done.2, f32[32,128,256]{2,0,1:T(8,128)S(1)} %fusion), kind=kLoop, calls=%fused_computation.8 | loop fusion | flops 2097152 | bytes 10485760 | tf_op jit(solution)/shard_map/convert_element_type | solution.py:285
  (36 shorter events, 0.3 us)
Async XLA Ops:
  0.0 113.0 %copy-start = (f32[16,32,32]{2,1,0:T(8,128)S(1)}, f32[16,32,32]{2,1,0:T(8,128)}, u32[]{:S(2)}) copy-start(f32[16,32,32]{2,1,0:T(8,128)} %param.23) | copy-start | bytes 196612
  24.6 10.7 %copy-start.8 = (s32[1,2,4]{2,1,0:T(2,128)S(1)}, s32[1,2,4]{2,1,0:T(2,128)}, u32[]{:S(2)}) copy-start(s32[1,2,4]{2,1,0:T(2,128)} %param.17) | copy-start | bytes 100
  24.6 10.8 %copy-start.1 = (bf16[32,128,256]{2,1,0:T(8,128)(2,1)S(1)}, bf16[32,128,256]{2,1,0:T(8,128)(2,1)}, u32[]{:S(2)}) copy-start(bf16[32,128,256]{2,1,0:T(8,128)(2,1)} %blocks_ref.1) | copy-start | bytes 6291460
  28.7 15.0 %copy-start.6 = (s32[1,16,4]{1,2,0:T(4,128)S(1)}, s32[1,16,4]{1,2,0:T(4,128)}, u32[]{:S(2)}) copy-start(s32[1,16,4]{1,2,0:T(4,128)} %param.15) | copy-start | bytes 772
  28.7 81.8 %all-to-all-start = ((f32[16,4,32,256]{3,2,1,0:T(8,128)}), f32[16,4,32,256]{3,2,1,0:T(8,128)}, u32[]{:S(2)}, u32[]{:S(2)}) async-start(f32[16,4,32,256]{3,2,1,0:T(8,128)} %bitcast.31), calls=%async_computation | async-start | bytes 4194304 | tf_op jit(solution)/shard_map/all_to_all | solution.py:260
  36.8 87.9 %collective-permute-start = (bf16[4,128,256]{2,1,0:T(8,128)(2,1)}, bf16[4,128,256]{2,1,0:T(8,128)(2,1)}, u32[]{:S(2)}, u32[]{:S(2)}) collective-permute-start(bf16[4,128,256]{2,1,0:T(8,128)(2,1)} %get-tuple-element.13), channel_id=1, source_target_pairs={{0,1},{1,2},{2,3},{3,4},{4,5},{5,6},{6,7},{8,9},{9,10},{10,11},{11... | collective-permute-start | bytes 786440 | tf_op jit(solution)/shard_map/ppermute | solution.py:18
  38.8 86.0 %collective-permute-start.1 = (bf16[4,128,256]{2,1,0:T(8,128)(2,1)}, bf16[4,128,256]{2,1,0:T(8,128)(2,1)}, u32[]{:S(2)}, u32[]{:S(2)}) collective-permute-start(bf16[4,128,256]{2,1,0:T(8,128)(2,1)} %get-tuple-element.14), channel_id=1, source_target_pairs={{1,0},{2,1},{3,2},{4,3},{5,4},{6,5},{7,6},{9,8},{10,9},{11,10},{12... | collective-permute-start | bytes 786440 | tf_op jit(solution)/shard_map/ppermute | solution.py:19
  110.5 11.2 %copy-start.7 = (s32[1,16]{1,0:T(1,128)S(1)}, s32[1,16]{1,0:T(1,128)}, u32[]{:S(2)}) copy-start(s32[1,16]{1,0:T(1,128)} %param.16) | copy-start | bytes 196
  110.5 11.3 %copy-start.4 = (s32[32,16]{0,1:T(8,128)S(1)}, s32[32,16]{0,1:T(8,128)}, u32[]{:S(2)}) copy-start(s32[32,16]{0,1:T(8,128)} %param.14) | copy-start | bytes 6148
  116.3 22.6 %all-to-all-start.1 = ((bf16[16,4,32,256]{3,2,1,0:T(8,128)(2,1)}), bf16[16,4,32,256]{3,2,1,0:T(8,128)(2,1)S(1)}, u32[]{:S(2)}, u32[]{:S(2)}) async-start(bf16[16,4,32,256]{3,2,1,0:T(8,128)(2,1)} %bitcast.33), calls=%async_computation.1 | async-start | bytes 2097152 | tf_op jit(solution)/shard_map/all_to_all | solution.py:269
  126.6 12.2 %copy-start.3 = (bf16[16,128,256]{2,1,0:T(8,128)(2,1)S(1)}, bf16[16,128,256]{2,1,0:T(8,128)(2,1)}, u32[]{:S(2)}) copy-start(bf16[16,128,256]{2,1,0:T(8,128)(2,1)} %get-tuple-element.9) | copy-start | bytes 3145732
  138.8 1.3 copy-start.5
  140.2 3.0 %copy-start.2 = (f32[32,128,256]{2,1,0:T(8,128)S(1)}, f32[32,128,256]{2,1,0:T(8,128)}, u32[]{:S(2)}) copy-start(f32[32,128,256]{2,1,0:T(8,128)} %shard_map.121) | copy-start | bytes 12582916

commit v17 on v16

--- a/solution.py
+++ b/solution.py
@@ -110,7 +110,9 @@
 )
 
 
-def exchange_kernel(offsets, *refs):
+def exchange_kernel(offsets, local, *refs):
+    if local:
+        local_ref, refs = refs[0], refs[1:]
     parts = (len(refs) - 7) // 3
     send_refs, recv_refs, relay_refs = refs[:parts], refs[parts : 2 * parts], refs[2 * parts : 3 * parts]
     near_send, near_recv, leg_send, leg_recv, fwd_send, fwd_recv, own_sems = refs[3 * parts :]
@@ -134,6 +136,10 @@
         )
     pl.semaphore_wait(barrier, len(NEAR))
     owns = []
+    if local:
+        own = pltpu.make_async_copy(local_ref, recv_refs[0].at[pl.ds(0, local_ref.shape[0])], own_sems.at[parts])
+        own.start()
+        owns.append(own)
     for p in range(parts):
         own = pltpu.make_async_copy(send_refs[p].at[me], recv_refs[p].at[offsets[p] + me], own_sems.at[p])
         own.start()
@@ -178,16 +184,17 @@
         own.wait()
 
 
-def dom_exchange(values, collective, frames=None):
+def dom_exchange(values, collective, frames=None, local=None):
     parts = len(values)
+    lead = [] if local is None else [local]
     frames = frames or [(0, v.shape[0]) for v in values]
     outs = [jax.ShapeDtypeStruct((n,) + v.shape[1:], v.dtype) for v, (_, n) in zip(values, frames)]
     relays = [jax.ShapeDtypeStruct((len(RELAYED), v.shape[1] // 2, v.shape[2]), v.dtype) for v in values]
     any_spec = pl.BlockSpec(memory_space=pl.ANY)
     result = pl.pallas_call(
-        functools.partial(exchange_kernel, tuple(f[0] for f in frames)),
+        functools.partial(exchange_kernel, tuple(f[0] for f in frames), local is not None),
         out_shape=tuple(outs + relays),
-        in_specs=[any_spec] * parts,
+        in_specs=[any_spec] * (parts + len(lead)),
         out_specs=tuple([any_spec] * (2 * parts)),
         scratch_shapes=[
             pltpu.SemaphoreType.DMA((parts, len(NEAR))),
@@ -196,10 +203,10 @@
             pltpu.SemaphoreType.DMA((parts, len(RELAYED))),
             pltpu.SemaphoreType.DMA((parts, len(RELAYED))),
             pltpu.SemaphoreType.DMA((parts, len(RELAYED))),
-            pltpu.SemaphoreType.DMA((parts,)),
+            pltpu.SemaphoreType.DMA((parts + len(lead),)),
         ],
         compiler_params=pltpu.CompilerParams(collective_id=collective, has_side_effects=True),
-    )(*values)
+    )(*lead, *values)
     return result[:parts]
 
 
@@ -260,7 +267,8 @@
     partial_in = lax.all_to_all(partial, "dom", split_axis=0, concat_axis=0, tiled=True)
     own_slots = blocks.shape[0] // halo_width
     ext_slots = own_slots + dom_count + 2 * rim_width // halo_width
-    (ext_frame,) = dom_exchange([halo_flat], 1, [(own_slots, ext_slots)])
+    own_frame = blocks.reshape(own_slots, halo_width * cell_count, vec_count)
+    (ext_frame,) = dom_exchange([halo_flat], 1, [(own_slots, ext_slots)], own_frame)
     partial_in, ext_frame = lax.optimization_barrier((partial_in, ext_frame))
     partial_in = partial_in.reshape(slot_total, seg, vec_count)
     summed = well_sums(well_slot.reshape(-1), partial_in, wells)
@@ -273,7 +281,6 @@
         [jnp.ones((blocks.shape[0],), jnp.int32), live_halo.reshape(-1), jnp.ones((2 * rim_width,), jnp.int32)]
     )
     extended = ext_frame.reshape(ext_slots * halo_width, cell_count, vec_count)
-    extended = lax.dynamic_update_slice_in_dim(extended, blocks, 0, 0)
     extended = lax.dynamic_update_slice_in_dim(extended, rim_rows, extended.shape[0] - 2 * rim_width, 0)
     product = local_product(extended, live, tile_values, tile_cols)
     incoming = jnp.einsum(

time: 147 us -> 162 us (1.10)
  the two profiles are of different devices: /device:TPU:66 before, /device:TPU:1 now
where the time goes in v17:
time: 162 us
  Pallas kernels  115 us (71%)
  starting transfers between devices  17.3 us (11%)
  local copies, waits for them, and re-layouts  11.4 us (7%)
  other arithmetic  6.58 us (4%)
  matrix products  5.95 us (4%)
  waiting for transfers between devices  4.36 us (3%)
    pallas_call x2, Pallas kernels, dom_exchange(): pl.pallas_call(functools.partial(exchange_kernel, tuple((f[0] for f in fr...  96.5 us
    pallas_call x1, Pallas kernels, local_product(): pl.pallas_call(product_kernel, out_shape=jax.ShapeDtypeStruct((block_rows...  12.2 us
    ppermute x1, starting transfers between devices, padded(): before = lax.ppermute(last, axis, up)  5.91 us
    all_to_all x1, starting transfers between devices, on_device(): lax.all_to_all(partial, 'dom', split_axis=0, concat_axis=0, tiled=True)  5.66 us
    ppermute x1, waiting for transfers between devices, padded(): after = lax.ppermute(leading, axis, down)  4.35 us
    pallas_call x1, Pallas kernels, partial_sums(): pl.pallas_call(partial_kernel, out_shape=jax.ShapeDtypeStruct((slots, seg...  4.07 us
    all_to_all x1, starting transfers between devices, on_device(): lax.all_to_all(state_pack, 'dom', split_axis=0, concat_axis=0, tiled=True)  3.66 us
    convert_element_type x1, other arithmetic, on_device(): return subtract_incoming(product, well_send, incoming).astype(jnp.bfloat16)  3.65 us
  transfers between devices with their start and end apart: 4, of which 1 were waited for; matrix products, arithmetic and copies ran while one was open for 4% of the time, Pallas kernels for 56%

profile of v17, /device:TPU:1, one launch (start us, length us, event | category | flops | bytes accessed | tf_op | source)
XLA Modules:
  0.0 161.8 jit_solution(4862773367428524855)
XLA Ops:
  0.0 0.8 copy.20
  0.8 0.1 reshape.142
  0.9 0.8 scatter_custom_fusion
  1.7 0.8 copy.19
  2.5 0.6 reshape_squeeze.6.index_ref
  3.1 1.3 pad_maximum_fusion
  4.4 1.6 gather_fusion
  6.0 18.6 %shard_map.118 = (bf16[16,128,256]{2,1,0:T(8,128)(2,1)}, bf16[14,64,256]{2,1,0:T(8,128)(2,1)}) custom-call(bf16[16,128,256]{2,1,0:T(8,128)(2,1)} %bitcast.35), custom_call_target="tpu_custom_call" | custom-call | tf_op jit(solution)/shard_map/pallas_call | solution.py:194
  24.7 4.1 %shard_map.119 = f32[64,32,256]{2,1,0:T(8,128)} custom-call(s32[64]{0:T(128)} %reshape_squeeze.6.index_ref, bf16[64,32,256]{2,1,0:T(8,128)(2,1)} %bitcast.37, bf16[32,128,256]{2,1,0:T(8,128)(2,1)} %blocks_ref.1), custom_call_target="tpu_custom_call" | custom-call | tf_op jit(solution)/shard_map/pallas_call | solution.py:92
  28.7 5.7 %all-to-all-start = ((f32[16,4,32,256]{3,2,1,0:T(8,128)}), f32[16,4,32,256]{3,2,1,0:T(8,128)}, u32[]{:S(2)}, u32[]{:S(2)}) async-start(f32[16,4,32,256]{3,2,1,0:T(8,128)} %bitcast.33), calls=%async_computation | async-start | bytes 4194304 | tf_op jit(solution)/shard_map/all_to_all | solution.py:267
  34.4 0.6 reshape.149.slot_ref
  35.7 0.1 reshape_squeeze.7
  35.8 0.1 copy.21
  35.8 0.1 reshape.164
  36.0 0.6 gather_fusion.2
  36.6 2.9 %gather_fusion.1 = bf16[64,128,256]{2,1,0:T(8,128)(2,1)} fusion(bf16[32,128,256]{2,1,0:T(8,128)(2,1)S(1)} %copy-done.1, s32[1024]{0:T(1024)S(1)} %pad_clamp_fusion.2), kind=kCustom, calls=%fused_computation.1 | custom fusion | bytes 8388864 | tf_op jit(solution)/shard_map/gather | solution.py:252
  39.5 77.9 %shard_map.120 = (bf16[26,512,256]{2,1,0:T(8,128)(2,1)}, bf16[14,256,256]{2,1,0:T(8,128)(2,1)}) custom-call(bf16[8,512,256]{2,1,0:T(8,128)(2,1)} %bitcast.31, bf16[16,512,256]{2,1,0:T(8,128)(2,1)} %bitcast.32), custom_call_target="tpu_custom_call" | custom-call | tf_op jit(solution)/shard_map/pallas_call | solution.py:194
  117.4 2.5 %shard_map.122 = f32[16,32,256]{2,1,0:T(8,128)} custom-call(s32[64]{0:T(128)} %reshape.149.slot_ref, f32[64,32,256]{2,1,0:T(8,128)} %bitcast.13.partial_ref), custom_call_target="tpu_custom_call" | custom-call | tf_op jit(solution)/shard_map/pallas_call | solution.py:74
  119.9 1.6 %fusion.3 = bf16[16,32,256]{2,1,0:T(8,128)(2,1)S(1)} fusion(f32[16,32,256]{2,1,0:T(8,128)} %shard_map.122, f32[16,32,32]{2,1,0:T(8,128)S(1)} %copy-done, f32[16]{0:T(128)S(1)} %compare_convert_fusion), kind=kOutput, calls=%fused_computation.11 | convolution fusion | flops 50593792 | bytes 852032 | tf_op jit(solution)/shard_map/wst,wtv->wsv/dot_general | solution.py:216
  121.5 1.6 gather_fusion.3
  123.1 3.7 %all-to-all-start.1 = ((bf16[16,4,32,256]{3,2,1,0:T(8,128)(2,1)}), bf16[16,4,32,256]{3,2,1,0:T(8,128)(2,1)S(1)}, u32[]{:S(2)}, u32[]{:S(2)}) async-start(bf16[16,4,32,256]{3,2,1,0:T(8,128)(2,1)} %bitcast.16), calls=%async_computation.1 | async-start | bytes 2097152 | tf_op jit(solution)/shard_map/all_to_all | solution.py:277
  126.8 5.9 %collective-permute-start = (bf16[4,128,256]{2,1,0:T(8,128)(2,1)S(1)}, bf16[4,128,256]{2,1,0:T(8,128)(2,1)S(1)}, u32[]{:S(2)}, u32[]{:S(2)}) collective-permute-start(bf16[4,128,256]{2,1,0:T(8,128)(2,1)S(1)} %get-tuple-element.13), channel_id=1, source_target_pairs={{0,1},{1,2},{2,3},{3,4},{4,5},{5,6},{6,7},{8,9},{9,10},{10,11},{11... | collective-permute-start | bytes 786440 | tf_op jit(solution)/shard_map/ppermute | solution.py:18
  132.7 2.1 %collective-permute-start.1 = (bf16[4,128,256]{2,1,0:T(8,128)(2,1)S(1)}, bf16[4,128,256]{2,1,0:T(8,128)(2,1)S(1)}, u32[]{:S(2)}, u32[]{:S(2)}) collective-permute-start(bf16[4,128,256]{2,1,0:T(8,128)(2,1)S(1)} %get-tuple-element.14), channel_id=1, source_target_pairs={{1,0},{2,1},{3,2},{4,3},{5,4},{6,5},{7,6},{9,8},{10,9},{11,10},{12... | collective-permute-start | bytes 786440 | tf_op jit(solution)/shard_map/ppermute | solution.py:19
  134.9 0.1 reshape.153
  135.1 0.6 reshape.139.cols_ref
  135.7 0.6 pad_add_fusion.live_ref
  136.4 4.4 %collective-permute-done.1 = bf16[4,128,256]{2,1,0:T(8,128)(2,1)S(1)} collective-permute-done((bf16[4,128,256]{2,1,0:T(8,128)(2,1)S(1)}, bf16[4,128,256]{2,1,0:T(8,128)(2,1)S(1)}, u32[]{:S(2)}, u32[]{:S(2)}) %collective-permute-start.1) | collective-permute-done | bytes 262176 | tf_op jit(solution)/shard_map/ppermute | solution.py:19
  140.7 0.8 maximum_dynamic-update-slice_fusion.ext_ref
  141.5 12.2 %shard_map.121 = f32[32,128,256]{2,1,0:T(8,128)} custom-call(s32[512]{0:T(512)} %reshape.139.cols_ref, s32[104]{0:T(128)} %pad_add_fusion.live_ref, bf16[104,128,256]{2,1,0:T(8,128)(2,1)} %maximum_dynamic-update-slice_fusion.ext_ref, bf16[32,16,128,128]{3,2,1,0:T(8,128)(2,1)} %tiles_ref.1), custom_call_target="tpu_custom_call" | custom-call | flops 4294967296 | bytes 27787264 | tf_op jit(solution)/shard_map/pallas_call | solution.py:55
  153.8 1.3 fusion.4
  155.1 3.0 %fusion = f32[32,128,256]{2,0,1:T(8,128)S(1)} fusion(bf16[64,128,256]{2,1,0:T(8,128)(2,1)S(1)} %fusion.4, s32[64]{0:T(128)S(1)} %copy-done.5), kind=kOutput, calls=%fused_computation.6 | convolution fusion | flops 134219776 | bytes 8388864 | tf_op jit(solution)/shard_map/bq,qkv->bkv/dot_general | solution.py:224
  158.1 3.7 %fusion.1 = bf16[32,128,256]{2,1,0:T(8,128)(2,1)} fusion(f32[32,128,256]{2,1,0:T(8,128)S(1)} %copy-done.2, f32[32,128,256]{2,0,1:T(8,128)S(1)} %fusion), kind=kLoop, calls=%fused_computation.8 | loop fusion | flops 2097152 | bytes 10485760 | tf_op jit(solution)/shard_map/convert_element_type | solution.py:292
  (35 shorter events, 0.3 us)
Async XLA Ops:
  0.0 119.9 %copy-start = (f32[16,32,32]{2,1,0:T(8,128)S(1)}, f32[16,32,32]{2,1,0:T(8,128)}, u32[]{:S(2)}) copy-start(f32[16,32,32]{2,1,0:T(8,128)} %param.23) | copy-start | bytes 196612
  24.6 11.0 %copy-start.8 = (s32[1,2,4]{2,1,0:T(2,128)S(1)}, s32[1,2,4]{2,1,0:T(2,128)}, u32[]{:S(2)}) copy-start(s32[1,2,4]{2,1,0:T(2,128)} %param.17) | copy-start | bytes 100
  24.6 11.1 %copy-start.6 = (s32[1,16,4]{1,2,0:T(4,128)S(1)}, s32[1,16,4]{1,2,0:T(4,128)}, u32[]{:S(2)}) copy-start(s32[1,16,4]{1,2,0:T(4,128)} %param.15) | copy-start | bytes 772
  24.6 11.3 %copy-start.1 = (bf16[32,128,256]{2,1,0:T(8,128)(2,1)S(1)}, bf16[32,128,256]{2,1,0:T(8,128)(2,1)}, u32[]{:S(2)}) copy-start(bf16[32,128,256]{2,1,0:T(8,128)(2,1)} %blocks_ref.1) | copy-start | bytes 6291460
  28.7 88.6 %all-to-all-start = ((f32[16,4,32,256]{3,2,1,0:T(8,128)}), f32[16,4,32,256]{3,2,1,0:T(8,128)}, u32[]{:S(2)}, u32[]{:S(2)}) async-start(f32[16,4,32,256]{3,2,1,0:T(8,128)} %bitcast.33), calls=%async_computation | async-start | bytes 4194304 | tf_op jit(solution)/shard_map/all_to_all | solution.py:267
  117.4 17.5 %copy-start.7 = (s32[1,16]{1,0:T(1,128)S(1)}, s32[1,16]{1,0:T(1,128)}, u32[]{:S(2)}) copy-start(s32[1,16]{1,0:T(1,128)} %param.16) | copy-start | bytes 196
  117.4 17.6 %copy-start.4 = (s32[32,16]{0,1:T(8,128)S(1)}, s32[32,16]{0,1:T(8,128)}, u32[]{:S(2)}) copy-start(s32[32,16]{0,1:T(8,128)} %param.14) | copy-start | bytes 6148
  123.1 30.7 %all-to-all-start.1 = ((bf16[16,4,32,256]{3,2,1,0:T(8,128)(2,1)}), bf16[16,4,32,256]{3,2,1,0:T(8,128)(2,1)S(1)}, u32[]{:S(2)}, u32[]{:S(2)}) async-start(bf16[16,4,32,256]{3,2,1,0:T(8,128)(2,1)} %bitcast.16), calls=%async_computation.1 | async-start | bytes 2097152 | tf_op jit(solution)/shard_map/all_to_all | solution.py:277
  126.8 9.5 %collective-permute-start = (bf16[4,128,256]{2,1,0:T(8,128)(2,1)S(1)}, bf16[4,128,256]{2,1,0:T(8,128)(2,1)S(1)}, u32[]{:S(2)}, u32[]{:S(2)}) collective-permute-start(bf16[4,128,256]{2,1,0:T(8,128)(2,1)S(1)} %get-tuple-element.13), channel_id=1, source_target_pairs={{0,1},{1,2},{2,3},{3,4},{4,5},{5,6},{6,7},{8,9},{9,10},{10,11},{11... | collective-permute-start | bytes 786440 | tf_op jit(solution)/shard_map/ppermute | solution.py:18
  132.7 8.0 %collective-permute-start.1 = (bf16[4,128,256]{2,1,0:T(8,128)(2,1)S(1)}, bf16[4,128,256]{2,1,0:T(8,128)(2,1)S(1)}, u32[]{:S(2)}, u32[]{:S(2)}) collective-permute-start(bf16[4,128,256]{2,1,0:T(8,128)(2,1)S(1)} %get-tuple-element.14), channel_id=1, source_target_pairs={{1,0},{2,1},{3,2},{4,3},{5,4},{6,5},{7,6},{9,8},{10,9},{11,10},{12... | collective-permute-start | bytes 786440 | tf_op jit(solution)/shard_map/ppermute | solution.py:19
  141.5 12.2 %copy-start.3 = (bf16[16,128,256]{2,1,0:T(8,128)(2,1)S(1)}, bf16[16,128,256]{2,1,0:T(8,128)(2,1)}, u32[]{:S(2)}) copy-start(bf16[16,128,256]{2,1,0:T(8,128)(2,1)} %get-tuple-element.9) | copy-start | bytes 3145732
  153.8 1.3 copy-start.5
  155.1 3.0 %copy-start.2 = (f32[32,128,256]{2,1,0:T(8,128)S(1)}, f32[32,128,256]{2,1,0:T(8,128)}, u32[]{:S(2)}) copy-start(f32[32,128,256]{2,1,0:T(8,128)} %shard_map.121) | copy-start | bytes 12582916

commit v18 on v16

--- a/solution.py
+++ b/solution.py
@@ -282,7 +282,8 @@
         state_in,
         preferred_element_type=jnp.float32,
     ).astype(jnp.bfloat16)
-    return subtract_incoming(product, well_send, incoming).astype(jnp.bfloat16)
+    targets = well_send[0].reshape(-1)
+    return product.at[targets].add(-incoming.astype(jnp.float32)).astype(jnp.bfloat16)
 
 
 def solution(mesh):

time: 147 us -> 168 us (1.14)
  other arithmetic: 7.62 us -> 27.1 us
    scatter-add x0 -> x1, other arithmetic: none -> 19.4 us  [on_device(): product.at[targets].add(-incoming.astype(jnp.float32)).astype(jnp.bfloat16)]
    dot_general x1, matrix products: 1.3 us -> 4.53 us  [on_device(): jnp.einsum('qsk,qsv->qkv', out_recv.reshape(slot_total, seg, cell_count),...]
    dot_general x1 -> x0, matrix products: 3.03 us -> none  [subtract_incoming(): jnp.einsum('bq,qkv->bkv', selector, flat_rows, preferred_element_type=jnp...]
  transfers between devices with their start and end apart: 4 -> 4, of which waited for: 0 -> 0; matrix products, arithmetic and copies ran while one was open for 9% -> 8% of each run, Pallas kernels for 53% -> 47%
where the time goes in v18:
time: 168 us; the launch traced here: 166 us
  Pallas kernels  100 us (60%)
  other arithmetic  27.1 us (16%)
  starting transfers between devices  18.2 us (11%)
  local copies, waits for them, and re-layouts  13.9 us (8%)
  matrix products  6.16 us (4%)
    pallas_call x2, Pallas kernels, dom_exchange(): pl.pallas_call(functools.partial(exchange_kernel, tuple((f[0] for f in fr...  81.3 us
    scatter-add x1, other arithmetic, on_device(): product.at[targets].add(-incoming.astype(jnp.float32)).astype(jnp.bfloat16)  19.4 us
    pallas_call x1, Pallas kernels, local_product(): pl.pallas_call(product_kernel, out_shape=jax.ShapeDtypeStruct((block_rows...  12.2 us
    all_to_all x1, starting transfers between devices, on_device(): lax.all_to_all(partial, 'dom', split_axis=0, concat_axis=0, tiled=True)  6.59 us
    all_to_all x1, starting transfers between devices, on_device(): lax.all_to_all(state_pack, 'dom', split_axis=0, concat_axis=0, tiled=True)  6.02 us
    dot_general x1, matrix products, on_device(): jnp.einsum('qsk,qsv->qkv', out_recv.reshape(slot_total, seg, cell_count),...  4.53 us
    pallas_call x1, Pallas kernels, partial_sums(): pl.pallas_call(partial_kernel, out_shape=jax.ShapeDtypeStruct((slots, seg...  4.07 us
    convert_element_type x1, other arithmetic, on_device(): product.at[targets].add(-incoming.astype(jnp.float32)).astype(jnp.bfloat16)  3.8 us
  transfers between devices with their start and end apart: 4, of which 0 were waited for; matrix products, arithmetic and copies ran while one was open for 8% of the time, Pallas kernels for 47%

profile of v18, /device:TPU:66, one launch (start us, length us, event | category | flops | bytes accessed | tf_op | source)
XLA Modules:
  0.0 166.3 jit_solution(15865829688755486288)
XLA Ops:
  0.0 0.8 copy.19
  0.8 0.6 reshape_squeeze.9.index_ref
  1.4 0.8 copy.20
  2.2 0.1 reshape.166
  2.3 0.8 scatter_custom_fusion
  3.1 1.3 pad_maximum_fusion
  4.5 1.6 gather_fusion
  6.1 18.5 %shard_map.118 = (bf16[16,128,256]{2,1,0:T(8,128)(2,1)}, bf16[14,64,256]{2,1,0:T(8,128)(2,1)}) custom-call(bf16[16,128,256]{2,1,0:T(8,128)(2,1)} %bitcast.34), custom_call_target="tpu_custom_call" | custom-call | tf_op jit(solution)/shard_map/pallas_call | solution.py:187
  24.6 4.1 %shard_map.119 = f32[64,32,256]{2,1,0:T(8,128)} custom-call(s32[64]{0:T(128)} %reshape_squeeze.9.index_ref, bf16[64,32,256]{2,1,0:T(8,128)(2,1)} %bitcast.35, bf16[32,128,256]{2,1,0:T(8,128)(2,1)} %blocks_ref.1), custom_call_target="tpu_custom_call" | custom-call | tf_op jit(solution)/shard_map/pallas_call | solution.py:92
  28.7 6.6 %all-to-all-start = ((f32[16,4,32,256]{3,2,1,0:T(8,128)}), f32[16,4,32,256]{3,2,1,0:T(8,128)}, u32[]{:S(2)}, u32[]{:S(2)}) async-start(f32[16,4,32,256]{3,2,1,0:T(8,128)} %bitcast.30), calls=%async_computation | async-start | bytes 4194304 | tf_op jit(solution)/shard_map/all_to_all | solution.py:260
  35.4 0.6 gather_fusion.2
  36.0 0.8 fusion.9
  36.8 1.9 %collective-permute-start = (bf16[4,128,256]{2,1,0:T(8,128)(2,1)}, bf16[4,128,256]{2,1,0:T(8,128)(2,1)}, u32[]{:S(2)}, u32[]{:S(2)}) collective-permute-start(bf16[4,128,256]{2,1,0:T(8,128)(2,1)} %get-tuple-element.13), channel_id=1, source_target_pairs={{0,1},{1,2},{2,3},{3,4},{4,5},{5,6},{6,7},{8,9},{9,10},{10,11},{11... | collective-permute-start | bytes 786440 | tf_op jit(solution)/shard_map/ppermute | solution.py:18
  38.7 3.6 %collective-permute-start.1 = (bf16[4,128,256]{2,1,0:T(8,128)(2,1)}, bf16[4,128,256]{2,1,0:T(8,128)(2,1)}, u32[]{:S(2)}, u32[]{:S(2)}) collective-permute-start(bf16[4,128,256]{2,1,0:T(8,128)(2,1)} %get-tuple-element.14), channel_id=1, source_target_pairs={{1,0},{2,1},{3,2},{4,3},{5,4},{6,5},{7,6},{9,8},{10,9},{11,10},{12... | collective-permute-start | bytes 786440 | tf_op jit(solution)/shard_map/ppermute | solution.py:19
  42.4 0.1 reshape_squeeze.11
  42.5 0.6 reshape.172.slot_ref
  43.9 0.1 reshape.187
  44.0 0.1 reshape.176
  44.2 0.7 reshape.163.cols_ref
  44.9 2.9 %gather_fusion.1 = bf16[64,128,256]{2,1,0:T(8,128)(2,1)} fusion(bf16[32,128,256]{2,1,0:T(8,128)(2,1)S(1)} %copy-done.1, s32[1024]{0:T(1024)S(1)} %pad_clamp_fusion.2), kind=kCustom, calls=%fused_computation.1 | custom fusion | bytes 8388864 | tf_op jit(solution)/shard_map/gather | solution.py:245
  47.7 62.7 %shard_map.120 = (bf16[26,512,256]{2,1,0:T(8,128)(2,1)}, bf16[14,256,256]{2,1,0:T(8,128)(2,1)}) custom-call(bf16[16,512,256]{2,1,0:T(8,128)(2,1)} %bitcast.29), custom_call_target="tpu_custom_call" | custom-call | tf_op jit(solution)/shard_map/pallas_call | solution.py:187
  110.5 2.5 %shard_map.122 = f32[16,32,256]{2,1,0:T(8,128)} custom-call(s32[64]{0:T(128)} %reshape.172.slot_ref, f32[64,32,256]{2,1,0:T(8,128)} %bitcast.12.partial_ref), custom_call_target="tpu_custom_call" | custom-call | tf_op jit(solution)/shard_map/pallas_call | solution.py:74
  113.0 1.6 fusion.1
  114.6 1.6 gather_fusion.3
  116.2 6.0 %all-to-all-start.1 = ((bf16[16,4,32,256]{3,2,1,0:T(8,128)(2,1)}), bf16[16,4,32,256]{3,2,1,0:T(8,128)(2,1)S(1)}, u32[]{:S(2)}, u32[]{:S(2)}) async-start(bf16[16,4,32,256]{3,2,1,0:T(8,128)(2,1)} %bitcast.33), calls=%async_computation.1 | async-start | bytes 2097152 | tf_op jit(solution)/shard_map/all_to_all | solution.py:269
  122.3 0.6 pad_add_fusion.live_ref
  122.9 1.5 constant_dynamic-update-slice_fusion
  124.5 1.9 %maximum_dynamic-update-slice_fusion.ext_ref = bf16[104,128,256]{2,1,0:T(8,128)(2,1)} fusion(bf16[104,128,256]{2,1,0:T(8,128)(2,1)} %constant_dynamic-update-slice_fusion, bf16[4,128,256]{2,1,0:T(8,128)(2,1)} %collective-permute-done.1, bf16[4,128,256]{2,1,0:T(8,128)(2,1)} %collective-permute-done), kind=kLoop, calls=%fused_computation.12 | loop fusion | flops 1048576 | bytes 1048576 | tf_op jit(solution)/shard_map/dynamic_update_slice | solution.py:277
  126.3 12.2 %shard_map.121 = f32[32,128,256]{2,1,0:T(8,128)} custom-call(s32[512]{0:T(512)} %reshape.163.cols_ref, s32[104]{0:T(128)} %pad_add_fusion.live_ref, bf16[104,128,256]{2,1,0:T(8,128)(2,1)} %maximum_dynamic-update-slice_fusion.ext_ref, bf16[32,16,128,128]{3,2,1,0:T(8,128)(2,1)} %tiles_ref.1), custom_call_target="tpu_custom_call" | custom-call | flops 4294967296 | bytes 27787264 | tf_op jit(solution)/shard_map/pallas_call | solution.py:55
  138.6 4.5 %convert_negate_fusion = f32[64,128,256]{2,1,0:T(8,128)} fusion(bf16[64,32,256]{2,1,0:T(8,128)(2,1)S(1)} %bitcast.32, bf16[64,32,256]{2,1,0:T(8,128)(2,1)S(1)} %bitcast.36), kind=kOutput, calls=%fused_computation.6 | convolution fusion | flops 140509184 | bytes 9961472 | tf_op jit(solution)/shard_map/qsk,qsv->qkv/dot_general | solution.py:279
  143.1 19.4 %scatter_fusion = f32[32,128,256]{2,1,0:T(8,128)} fusion(f32[32,128,256]{2,1,0:T(8,128)} %shard_map.121, s32[64]{0:T(128)S(1)} %fusion.6, f32[64,128,256]{2,1,0:T(8,128)} %convert_negate_fusion), kind=kCustom, calls=%fused_computation.5 | custom fusion | flops 2097152 | bytes 25166080 | tf_op jit(solution)/shard_map/scatter-add | solution.py:286
  162.5 3.8 %convert_element_type.36 = bf16[32,128,256]{2,1,0:T(8,128)(2,1)} convert(f32[32,128,256]{2,1,0:T(8,128)} %scatter_fusion) | non-fusion elementwise | flops 1048576 | bytes 6291456 | tf_op jit(solution)/shard_map/convert_element_type | solution.py:286
  (34 shorter events, 0.4 us)
Async XLA Ops:
  0.0 113.0 %copy-start = (f32[16,32,32]{2,1,0:T(8,128)S(1)}, f32[16,32,32]{2,1,0:T(8,128)}, u32[]{:S(2)}) copy-start(f32[16,32,32]{2,1,0:T(8,128)} %param.23) | copy-start | bytes 196612
  24.6 10.7 %copy-start.6 = (s32[1,2,4]{2,1,0:T(2,128)S(1)}, s32[1,2,4]{2,1,0:T(2,128)}, u32[]{:S(2)}) copy-start(s32[1,2,4]{2,1,0:T(2,128)} %param.17) | copy-start | bytes 100
  24.6 10.8 %copy-start.1 = (bf16[32,128,256]{2,1,0:T(8,128)(2,1)S(1)}, bf16[32,128,256]{2,1,0:T(8,128)(2,1)}, u32[]{:S(2)}) copy-start(bf16[32,128,256]{2,1,0:T(8,128)(2,1)} %blocks_ref.1) | copy-start | bytes 6291460
  28.7 15.1 %copy-start.4 = (s32[1,16,4]{1,2,0:T(4,128)S(1)}, s32[1,16,4]{1,2,0:T(4,128)}, u32[]{:S(2)}) copy-start(s32[1,16,4]{1,2,0:T(4,128)} %param.15) | copy-start | bytes 772
  28.7 15.2 %copy-start.5 = (s32[1,16]{1,0:T(1,128)S(1)}, s32[1,16]{1,0:T(1,128)}, u32[]{:S(2)}) copy-start(s32[1,16]{1,0:T(1,128)} %param.16) | copy-start | bytes 196
  28.7 15.4 %copy-start.3 = (s32[32,16]{0,1:T(8,128)S(1)}, s32[32,16]{0,1:T(8,128)}, u32[]{:S(2)}) copy-start(s32[32,16]{0,1:T(8,128)} %param.14) | copy-start | bytes 6148
  28.7 81.8 %all-to-all-start = ((f32[16,4,32,256]{3,2,1,0:T(8,128)}), f32[16,4,32,256]{3,2,1,0:T(8,128)}, u32[]{:S(2)}, u32[]{:S(2)}) async-start(f32[16,4,32,256]{3,2,1,0:T(8,128)} %bitcast.30), calls=%async_computation | async-start | bytes 4194304 | tf_op jit(solution)/shard_map/all_to_all | solution.py:260
  36.8 87.6 %collective-permute-start = (bf16[4,128,256]{2,1,0:T(8,128)(2,1)}, bf16[4,128,256]{2,1,0:T(8,128)(2,1)}, u32[]{:S(2)}, u32[]{:S(2)}) collective-permute-start(bf16[4,128,256]{2,1,0:T(8,128)(2,1)} %get-tuple-element.13), channel_id=1, source_target_pairs={{0,1},{1,2},{2,3},{3,4},{4,5},{5,6},{6,7},{8,9},{9,10},{10,11},{11... | collective-permute-start | bytes 786440 | tf_op jit(solution)/shard_map/ppermute | solution.py:18
  38.7 85.7 %collective-permute-start.1 = (bf16[4,128,256]{2,1,0:T(8,128)(2,1)}, bf16[4,128,256]{2,1,0:T(8,128)(2,1)}, u32[]{:S(2)}, u32[]{:S(2)}) collective-permute-start(bf16[4,128,256]{2,1,0:T(8,128)(2,1)} %get-tuple-element.14), channel_id=1, source_target_pairs={{1,0},{2,1},{3,2},{4,3},{5,4},{6,5},{7,6},{9,8},{10,9},{11,10},{12... | collective-permute-start | bytes 786440 | tf_op jit(solution)/shard_map/ppermute | solution.py:19
  116.2 22.3 %all-to-all-start.1 = ((bf16[16,4,32,256]{3,2,1,0:T(8,128)(2,1)}), bf16[16,4,32,256]{3,2,1,0:T(8,128)(2,1)S(1)}, u32[]{:S(2)}, u32[]{:S(2)}) async-start(bf16[16,4,32,256]{3,2,1,0:T(8,128)(2,1)} %bitcast.33), calls=%async_computation.1 | async-start | bytes 2097152 | tf_op jit(solution)/shard_map/all_to_all | solution.py:269
  126.3 12.2 %copy-start.2 = (bf16[16,128,256]{2,1,0:T(8,128)(2,1)S(1)}, bf16[16,128,256]{2,1,0:T(8,128)(2,1)}, u32[]{:S(2)}) copy-start(bf16[16,128,256]{2,1,0:T(8,128)(2,1)} %get-tuple-element.9) | copy-start | bytes 3145732
